TPU v7x, 256 devices: a whole 4x4x8 slice. The times are simulated.
256 devices in a mesh: frame: 32 (over z, x), row: 8 (over y, core).
Axes of the slice: x: 4, y: 4, z: 8, core: 2. Of those that a mesh axis runs over, the one named last changes fastest.
Arguments:
- query_tokens: bfloat16 [64, 24, 40, 2240], P('frame', 'row'), may hold values from -6 to 6
- key_tokens: bfloat16 [64, 24, 40, 2240], P('frame', 'row'), may hold values from -6 to 6
- value_tokens: bfloat16 [64, 24, 40, 2240], P('frame', 'row'), may hold values from -6 to 6
- norm_gain: float32 [2240], replicated, may hold values from 0.1 to 1.9
- hidden: bfloat16 [64, 24, 40, 11200], P('frame', 'row'), may hold values from -6 to 6
- time_weight: float32 [2, 11200], replicated, may hold values from -4 to 4
- space_weight: float32 [3, 3, 11200], replicated, may hold values from -2 to 2
- conv_bias: float32 [11200], replicated, may hold values from -3 to 3
Outputs:
- attention: bfloat16 [64, 24, 40, 2240], P('frame', 'row')
- ffn_out: bfloat16 [64, 24, 40, 5600], P('frame', 'row')
All inputs are finite; a program needn't handle non-finite values.
Results may differ from a plain program's by a relative error of at most 0.0056.
Values may be sent and summed in bfloat16 or wider, within the bound.
No kernel may reach another device: no remote copies, remote signals or barrier semaphores. Data moves between devices by JAX's collectives and lax.ppermute only.
A program may use at most 128 MiB of HBM per device.

v0:
```python
import jax
import jax.numpy as jnp
from jax import lax
from jax.sharding import PartitionSpec as P

HD = 112
FF = 5600


epsilon = 1e-06


def entering(value, axis, join, neutral):
    count, mine = (lax.axis_size(axis), lax.axis_index(axis))
    pieces = lax.all_gather(value, axis)
    total = jnp.full_like(value, 0) + jnp.asarray(neutral, value.dtype)

    def turn(position, total):
        longer = join(total, pieces[position])
        return jnp.where(position < mine, longer, total)

    return lax.fori_loop(0, count - 1, turn, total)


def from_behind(value, axis, steps):
    count = lax.axis_size(axis)
    leading, last = (max(0, -steps), min(count, count - steps))
    return lax.ppermute(value, axis, [(source, source + steps) for source in range(leading, last)])


def extended(cells, sides, width):
    for axis, dim in sides:
        count = lax.axis_size(axis)
        ends = count - 1
        head = lax.slice_in_dim(cells, 0, width, axis=dim)
        tail = lax.slice_in_dim(cells, cells.shape[dim] - width, cells.shape[dim], axis=dim)
        cells = jnp.concatenate(
            [
                lax.ppermute(tail, axis, [(i, (i + 1) % count) for i in range(ends)]),
                cells,
                lax.ppermute(head, axis, [((i + 1) % count, i) for i in range(ends)]),
            ],
            axis=dim,
        )
    return cells


def add_states(earlier, later):
    return earlier + later


def per_device(
    query_tokens, key_tokens, value_tokens, norm_gain, hidden, time_weight, space_weight, conv_bias
):
    frames_here, rows_here, columns, model_width = query_tokens.shape
    head_count = model_width // HD
    tok_count = frames_here * rows_here * columns
    key_feat = jax.nn.relu(key_tokens.reshape(tok_count, head_count, HD))
    value_rows = value_tokens.reshape(tok_count, head_count, HD)
    partial_value = jnp.einsum(
        "thd,the->hde", key_feat, value_rows, preferred_element_type=jnp.float32
    )
    partial_value = partial_value.reshape(head_count * HD, HD)
    group_state = lax.psum(partial_value, "row")
    before = entering(group_state, "frame", add_states, jnp.zeros_like(group_state))
    kv_state = (before + group_state).astype(jnp.bfloat16)
    query_feat = jax.nn.relu(query_tokens.reshape(tok_count, head_count, HD))
    mixed = jnp.einsum(
        "thd,hde->the",
        query_feat,
        kv_state.reshape(head_count, HD, HD),
        preferred_element_type=jnp.float32,
    )
    mean_square = jnp.mean(mixed * mixed, axis=-1, keepdims=True)
    normed = mixed * lax.rsqrt(mean_square + epsilon) * norm_gain.reshape(head_count, HD)
    attention = normed.astype(jnp.bfloat16).reshape(frames_here, rows_here, columns, model_width)
    earlier_last = from_behind(hidden[frames_here - 1 :], "frame", 1)
    earlier = jnp.concatenate([earlier_last, hidden[: frames_here - 1]], axis=0)
    blended = (time_weight[0] * hidden + time_weight[1] * earlier).astype(jnp.bfloat16)
    padded_rows = extended(blended, (("row", 1),), 1)
    padded = jnp.pad(padded_rows, ((0, 0), (0, 0), (1, 1), (0, 0)))
    summed = conv_bias + jnp.zeros((frames_here, rows_here, columns, padded.shape[3]), jnp.float32)
    for row_off in range(3):
        for col_off in range(3):
            summed = (
                summed
                + space_weight[row_off, col_off]
                * padded[:, row_off : row_off + rows_here, col_off : col_off + columns]
            )
    ffn_out = (summed[..., :FF] * jax.nn.silu(summed[..., FF:])).astype(jnp.bfloat16)
    return (attention, ffn_out)


def solution(mesh):
    placed = (
        P("frame", "row", None, None),
        P("frame", "row", None, None),
        P("frame", "row", None, None),
        P(),
        P("frame", "row", None, None),
        P(),
        P(),
        P(),
    )
    return jax.shard_map(
        per_device,
        mesh=mesh,
        in_specs=placed,
        out_specs=(P("frame", "row", None, None), P("frame", "row", None, None)),
        check_vma=False,
    )
```

profile of v0, /device:TPU:1, one launch (start us, length us, event | category | flops | bytes accessed | tf_op | source)
XLA Modules:
  0.0 434.7 jit_solution(3798013161863862858)
XLA Ops:
  7.2 3.0 reshape.43
  10.2 1.3 broadcast_maximum_fusion.1
  11.5 2.5 max.20
  14.0 3.0 fusion.12
  17.0 69.7 %all-reduce.3.cloned.1.call-done = f32[2240,112]{1,0:T(8,128)} async-done(((f32[2240,112]{1,0:T(8,128)}), f32[2240,112]{1,0:T(8,128)}) %all-reduce.3.cloned.1.call-update) | async-done | bytes 1003536 | tf_op jit(solution)/shard_map/psum | solution.py:64
  86.7 2.6 copy.30
  89.4 5.4 %fusion.16 = (bf16[1,3,40,11200]{3,2,1,0:T(8,128)(2,1)}, bf16[1,3,40,11200]{3,2,1,0:T(8,128)(2,1)}) fusion(bf16[2,3,40,11200]{3,2,1,0:T(8,128)(2,1)} %param.14), kind=kLoop, calls=%fused_computation.31 | loop fusion | bytes 10752000 | tf_op jit(solution)/shard_map/slice | solution.py:77
  94.8 4.7 %collective-permute-start = (bf16[1,3,40,11200]{3,2,1,0:T(8,128)(2,1)}, bf16[1,3,40,11200]{3,2,1,0:T(8,128)(2,1)}, u32[]{:S(2)}, u32[]{:S(2)}) collective-permute-start(bf16[1,3,40,11200]{3,2,1,0:T(8,128)(2,1)} %get-tuple-element.117), channel_id=1, source_target_pairs={{0,8},{8,16},{16,24},{24,32},{32,40},{40,48},{48,56},{56,64},{64,7... | collective-permute-start | bytes 8064008 | tf_op jit(solution)/shard_map/ppermute | solution.py:28
  99.5 2.5 max.22
  102.1 67.6 %collective-permute-done = bf16[1,3,40,11200]{3,2,1,0:T(8,128)(2,1)} collective-permute-done((bf16[1,3,40,11200]{3,2,1,0:T(8,128)(2,1)}, bf16[1,3,40,11200]{3,2,1,0:T(8,128)(2,1)}, u32[]{:S(2)}, u32[]{:S(2)}) %collective-permute-start) | collective-permute-done | bytes 2688032 | tf_op jit(solution)/shard_map/ppermute | solution.py:28
  169.7 5.4 %add_convert_fusion = bf16[2,3,40,11200]{3,2,1,0:T(8,128)(2,1)S(1)} fusion(bf16[2,3,40,11200]{3,2,1,0:T(8,128)(2,1)} %param.14, bf16[1,3,40,11200]{3,2,1,0:T(8,128)(2,1)} %get-tuple-element.118, bf16[1,3,40,11200]{3,2,1,0:T(8,128)(2,1)} %collective-permute-done, f32[11200]{0:T(1024)S(1)} %bitcast.47, f32[11200]{0:T(1024)S(1)} %bitcast.46), kind=kLoop, calls=%fused_computation.11 | loop fusion | flops 18816000 | bytes 16217600 | tf_op jit(solution)/shard_map/convert_element_type | solution.py:79
  175.4 5.8 %collective-permute-start.2 = (bf16[2,1,40,11200]{3,2,1,0:T(8,128)(2,1)S(1)}, bf16[2,1,40,11200]{3,2,1,0:T(8,128)(2,1)S(1)}, u32[]{:S(2)}, u32[]{:S(2)}) collective-permute-start(bf16[2,1,40,11200]{3,2,1,0:T(8,128)(2,1)S(1)} %get-tuple-element.116), channel_id=1, source_target_pairs={{1,0},{2,1},{3,2},{4,3},{5,4},{6,5},{7,6},{9,8},{10,9},{11,10},{12... | collective-permute-start | bytes 5376008 | tf_op jit(solution)/shard_map/ppermute | solution.py:41
  181.2 2.1 collective-permute-start.1
  183.6 17.7 %collective-permute-done.2 = bf16[2,1,40,11200]{3,2,1,0:T(8,128)(2,1)S(1)} collective-permute-done((bf16[2,1,40,11200]{3,2,1,0:T(8,128)(2,1)S(1)}, bf16[2,1,40,11200]{3,2,1,0:T(8,128)(2,1)S(1)}, u32[]{:S(2)}, u32[]{:S(2)}) %collective-permute-start.2) | collective-permute-done | bytes 1792032 | tf_op jit(solution)/shard_map/ppermute | solution.py:41
  201.3 1.6 collective-permute-done.1
  202.9 4.6 %fusion.5 = bf16[2,5,42,11200]{3,2,1,0:T(8,128)(2,1)S(1)} fusion(bf16[2,1,40,11200]{3,2,1,0:T(8,128)(2,1)S(1)} %collective-permute-done.2, bf16[2,3,40,11200]{3,2,1,0:T(8,128)(2,1)S(1)} %add_convert_fusion, bf16[2,1,40,11200]{3,2,1,0:T(8,128)(2,1)S(1)} %collective-permute-done.1), kind=kLoop, calls=%fused_computation.9 | loop fusion | flops 56448000 | bytes 18368000 | tf_op jit(solution)/shard_map/concatenate | solution.py:37
  207.5 12.8 %multiply_add_fusion = f32[2,3,40,11200]{3,2,1,0:T(8,128)} fusion(bf16[2,3,40,11200]{3,2,1,0:T(8,128)(2,1)S(1)} %add_convert_fusion, bf16[2,5,42,11200]{3,2,1,0:T(8,128)(2,1)S(1)} %fusion.5, bf16[2,1,40,11200]{3,2,1,0:T(8,128)(2,1)S(1)} %collective-permute-done.2, bf16[2,1,40,11200]{3,2,1,0:T(8,128)(2,1)S(1)} %collective-permute-done.1, ...), kind=kLoop, calls=%fused_computation.10 | loop fusion | flops 77952000 | bytes 52416000 | tf_op jit(solution)/shard_map/add | solution.py:86
  220.3 6.3 %fusion.6 = bf16[2,3,40,5600]{3,2,1,0:T(8,128)(2,1)} fusion(f32[2,3,40,11200]{3,2,1,0:T(8,128)} %multiply_add_fusion), kind=kLoop, calls=%fused_computation.13 | loop fusion | flops 8064000 | bytes 13440000 | tf_op jit(solution)/shard_map/convert_element_type | solution.py:90
  226.6 132.6 %all-gather.4.cloned.1.call-done = f32[32,2240,112]{1,2,0:T(8,128)} async-done(((f32[1,2240,112]{1,2,0:T(8,128)}), f32[32,2240,112]{1,2,0:T(8,128)}) %all-gather.4.cloned.1.call-update) | async-done | bytes 32112656 | tf_op jit(solution)/shard_map/all_gather | solution.py:15
  359.2 61.2 %while.14 = (s32[]{:T(128)}, f32[2240,112]{1,0:T(8,128)S(1)}, s32[]{:T(128)}, f32[32,2240,112]{1,2,0:T(8,128)}, s32[]{:T(128)}, /*index=5*/s32[]{:T(128)}) while((s32[]{:T(128)}, f32[2240,112]{1,0:T(8,128)S(1)}, s32[]{:T(128)}, f32[32,2240,112]{1,2,0:T(8,128)}, s32[]{:T(128)}, /*index=5*/s32[]{:T(128)}) %tuple.51), condition=%wide.region_2.3_spmd.clone, body=%wide.region_1.2_spmd.clone.sunk | while | flops 752644 | bytes 7024741 | solution.py:22
  361.2 1.3 constant_dynamic-slice_fusion.2
  363.2 1.3 constant_dynamic-slice_fusion.2
  365.1 1.3 constant_dynamic-slice_fusion.2
  367.1 1.3 constant_dynamic-slice_fusion.2
  369.1 1.3 constant_dynamic-slice_fusion.2
  371.1 1.3 constant_dynamic-slice_fusion.2
  373.0 1.3 constant_dynamic-slice_fusion.2
  375.0 1.3 constant_dynamic-slice_fusion.2
  420.5 1.4 add_convert_fusion.1
  421.8 2.3 fusion.7
  424.6 1.4 copy.34
  425.9 1.9 reshape.46
  (107 shorter events, 51.1 us)
Async XLA Ops:
  7.2 79.5 %all-reduce.3.cloned.1.call-start = ((), (), s32[]{:S(2)}) async-start(), calls=%async_computation | async-start | bytes 2293760 | tf_op jit(solution)/shard_map/psum | solution.py:64
  16.9 342.3 %all-gather.4.cloned.1.call-start = ((), (), s32[]{:S(2)}) async-start(), calls=%async_computation.1 | async-start | bytes 34062336 | tf_op jit(solution)/shard_map/all_gather | solution.py:15
  89.3 10.1 %copy-start = (bf16[2,3,40,2240]{3,2,1,0:T(8,128)(2,1)S(1)}, bf16[2,3,40,2240]{3,2,1,0:T(8,128)(2,1)}, u32[]{:S(2)}) copy-start(bf16[2,3,40,2240]{3,2,1,0:T(8,128)(2,1)} %param.10) | copy-start | bytes 3225604
  89.3 12.7 %copy-start.4 = (f32[2240]{0:T(1024)S(1)}, f32[2240]{0:T(1024)}, u32[]{:S(2)}) copy-start(f32[2240]{0:T(1024)} %param.13) | copy-start | bytes 26884
  89.3 12.7 %copy-start.2 = (f32[2,11200]{1,0:T(2,128)S(1)}, f32[2,11200]{1,0:T(2,128)}, u32[]{:S(2)}) copy-start(f32[2,11200]{1,0:T(2,128)} %param.15) | copy-start | bytes 268804
  94.8 75.0 %collective-permute-start = (bf16[1,3,40,11200]{3,2,1,0:T(8,128)(2,1)}, bf16[1,3,40,11200]{3,2,1,0:T(8,128)(2,1)}, u32[]{:S(2)}, u32[]{:S(2)}) collective-permute-start(bf16[1,3,40,11200]{3,2,1,0:T(8,128)(2,1)} %get-tuple-element.117), channel_id=1, source_target_pairs={{0,8},{8,16},{16,24},{24,32},{32,40},{40,48},{48,56},{56,64},{64,7... | collective-permute-start | bytes 8064008 | tf_op jit(solution)/shard_map/ppermute | solution.py:28
  175.1 8.1 %copy-start.1 = (f32[3,3,11200]{2,1,0:T(4,128)S(1)}, f32[3,3,11200]{2,1,0:T(4,128)}, u32[]{:S(2)}) copy-start(f32[3,3,11200]{2,1,0:T(4,128)} %param.16) | copy-start | bytes 1209604
  175.4 25.9 %collective-permute-start.2 = (bf16[2,1,40,11200]{3,2,1,0:T(8,128)(2,1)S(1)}, bf16[2,1,40,11200]{3,2,1,0:T(8,128)(2,1)S(1)}, u32[]{:S(2)}, u32[]{:S(2)}) collective-permute-start(bf16[2,1,40,11200]{3,2,1,0:T(8,128)(2,1)S(1)} %get-tuple-element.116), channel_id=1, source_target_pairs={{1,0},{2,1},{3,2},{4,3},{5,4},{6,5},{7,6},{9,8},{10,9},{11,10},{12... | collective-permute-start | bytes 5376008 | tf_op jit(solution)/shard_map/ppermute | solution.py:41
  181.2 21.7 %collective-permute-start.1 = (bf16[2,1,40,11200]{3,2,1,0:T(8,128)(2,1)S(1)}, bf16[2,1,40,11200]{3,2,1,0:T(8,128)(2,1)S(1)}, u32[]{:S(2)}, u32[]{:S(2)}) collective-permute-start(bf16[2,1,40,11200]{3,2,1,0:T(8,128)(2,1)S(1)} %get-tuple-element.115), channel_id=1, source_target_pairs={{0,1},{1,2},{2,3},{3,4},{4,5},{5,6},{6,7},{8,9},{9,10},{10,11},{11... | collective-permute-start | bytes 5376008 | tf_op jit(solution)/shard_map/ppermute | solution.py:39
  183.6 23.9 %copy-start.3 = (f32[11200]{0:T(1024)S(1)}, f32[11200]{0:T(1024)}, u32[]{:S(2)}) copy-start(f32[11200]{0:T(1024)} %param.17) | copy-start | bytes 134404
Sparse Core Ops, SparseCore 0:
  17.1 69.6 all-reduce.2
  89.9 269.2 all-gather.3
where the time goes:
time: 436 us; the launch traced here: 435 us
  waiting for transfers between devices  289 us (66%)
  local copies, waits for them, and re-layouts  71.1 us (16%)
  other arithmetic  41.1 us (9%)
  between operations  14.2 us (3%)
  starting transfers between devices  12.6 us (3%)
  matrix products  5.26 us (1%)
    all_gather x1, waiting for transfers between devices, entering(): pieces = lax.all_gather(value, axis)  133 us
    psum x1, waiting for transfers between devices, per_device(): group_state = lax.psum(partial_value, 'row')  69.7 us
    ppermute x1, waiting for transfers between devices, from_behind(): lax.ppermute(value, axis, [(source, source + steps) for source in range(l...  67.6 us
    dynamic_slice x62, local copies, waits for them, and re-layouts, turn(): longer = join(total, pieces[position])  51.3 us
    ppermute x1, waiting for transfers between devices, extended(): lax.ppermute(head, axis, [((i + 1) % count, i) for i in range(ends)])  17.7 us
    add x1, other arithmetic, per_device(): summed + space_weight[row_off, col_off] * padded[:, row_off:row_off + row...  12.8 us
    select_n x31, other arithmetic, turn(): return jnp.where(position < mine, longer, total)  8.86 us
  transfers between devices with their start and end apart: 5, of which 5 were waited for; matrix products, arithmetic and copies ran while one was open for 9% of the time, Pallas kernels for 0%

commit v1 on v0

v1 whole, which is shorter than its diff:
```python
import functools

import jax
import jax.numpy as jnp
from jax import lax
from jax.experimental import pallas as pl
from jax.experimental.pallas import tpu as pltpu
from jax.sharding import Mesh, PartitionSpec as P

HD = 112
FF = 5600
LANES = 128
UNIT = 16
SHARES = 8
SHARE_ROWS = 256
INNER = 4
BLOCK = 11 * LANES
epsilon = 1e-06


def windows(width):
    out = []
    for head in range(width // HD):
        tile, offset = divmod(head * HD, LANES)
        span = LANES if offset + HD <= LANES else 2 * LANES
        out.append((tile, offset, min(span, width - tile * LANES)))
    return out


def unit_row(unit, row):
    share, inside = divmod(unit, UNIT)
    return pl.multiple_of((share ^ row) * SHARE_ROWS + inside * UNIT, UNIT)


def partial_kernel(row_ref, key_ref, value_ref, out_ref):
    row = row_ref[0]
    width = key_ref.shape[1]
    pending = {}

    def flush(tile):
        rounded = pending.pop(tile).astype(jnp.bfloat16)
        for piece in range(HD // UNIT):
            out_ref[pl.ds(unit_row(tile * (HD // UNIT) + piece, row), UNIT), :] = rounded[
                piece * UNIT : (piece + 1) * UNIT
            ]

    for tile, offset, span in windows(width):
        lanes = slice(tile * LANES, tile * LANES + span)
        keys = jnp.maximum(key_ref[:, lanes], 0)
        product = lax.dot_general(
            keys, value_ref[:, lanes], (((0,), (0,)), ((), ())), preferred_element_type=jnp.float32
        )
        block = product[offset : offset + HD]
        lane = lax.broadcasted_iota(jnp.int32, block.shape, 1)
        block = jnp.where((lane >= offset) & (lane < offset + HD), block, 0.0)
        for old in [done for done in pending if done < tile]:
            flush(old)
        for step in range(pl.cdiv(span, LANES)):
            part = block[:, step * LANES : min(span, (step + 1) * LANES)]
            if part.shape[1] < LANES:
                part = jnp.concatenate(
                    [part, jnp.zeros((HD, LANES - part.shape[1]), jnp.float32)], axis=1
                )
            at = tile + step
            pending[at] = pending[at] + part if at in pending else part
    tiles = max(pending) + 1
    for old in sorted(pending):
        flush(old)
    for unit in range(tiles * (HD // UNIT), SHARES * UNIT):
        out_ref[pl.ds(unit_row(unit, row), UNIT), :] = jnp.zeros((UNIT, LANES), jnp.bfloat16)


def mixed_kernel(row_ref, query_ref, state_ref, gain_ref, out_ref):
    row = row_ref[0]
    tokens, width = query_ref.shape
    pending = {}

    def state_tile(tile):
        return jnp.concatenate(
            [
                state_ref[pl.ds(unit_row(tile * (HD // UNIT) + piece, row), UNIT), :]
                for piece in range(HD // UNIT)
            ],
            axis=0,
        )

    def flush(tile):
        lanes = slice(tile * LANES, min(width, (tile + 1) * LANES))
        count = lanes.stop - lanes.start
        out_ref[:, lanes] = (pending.pop(tile)[:, :count] * gain_ref[:, lanes]).astype(jnp.bfloat16)

    for tile, offset, span in windows(width):
        lanes = slice(tile * LANES, tile * LANES + span)
        steps = pl.cdiv(span, LANES)
        block = jnp.concatenate([state_tile(tile + step) for step in range(steps)], axis=1)
        lane = lax.broadcasted_iota(jnp.int32, block.shape, 1)
        block = jnp.where((lane >= offset) & (lane < offset + HD), block, jnp.zeros_like(block))
        pieces = [block]
        if offset:
            pieces.insert(0, jnp.zeros((offset, block.shape[1]), jnp.bfloat16))
        if span - offset - HD:
            pieces.append(jnp.zeros((span - offset - HD, block.shape[1]), jnp.bfloat16))
        right = jnp.concatenate(pieces, axis=0) if len(pieces) > 1 else block
        mixed = jnp.dot(
            jnp.maximum(query_ref[:, lanes], 0), right, preferred_element_type=jnp.float32
        )
        mean_square = jnp.sum(mixed * mixed, axis=1, keepdims=True) * (1.0 / HD)
        normed = mixed * lax.rsqrt(mean_square + epsilon)
        for old in [done for done in pending if done < tile]:
            flush(old)
        for step in range(steps):
            part = normed[:, step * LANES : (step + 1) * LANES]
            at = tile + step
            pending[at] = pending[at] + part if at in pending else part
    for old in sorted(pending):
        flush(old)


def conv_kernel(cur_ref, prev0_ref, prev1_ref, prev2_ref, top_ref, bottom_ref, weight_ref, *rest):
    out_ref, gate_ref = rest[-2:]
    step = pl.program_id(0)
    blocks = pl.num_programs(0)
    block = blocks - 1 - step
    first_gate = FF // BLOCK
    prev_refs = (prev0_ref, prev1_ref, prev2_ref)
    rows = cur_ref.shape[0]

    def conv_tile(lanes):
        weights = weight_ref[:, lanes]
        pick = lambda index: weights[index : index + 1]
        columns = cur_ref.shape[1]
        spread = [
            (
                pick(0) * cur_ref[r, :, lanes].astype(jnp.float32)
                + pick(1) * prev_refs[r][:, lanes].astype(jnp.float32)
            )
            .astype(jnp.bfloat16)
            .astype(jnp.float32)
            for r in range(rows)
        ]
        spread = [top_ref[:, lanes].astype(jnp.float32)] + spread
        spread = spread + [bottom_ref[:, lanes].astype(jnp.float32)]
        column = lax.broadcasted_iota(jnp.int32, (columns, LANES), 0)
        out = []
        for r in range(rows):
            sums = []
            for b in range(3):
                total = pick(2 + b) * spread[r]
                for a in (1, 2):
                    total = total + pick(2 + 3 * a + b) * spread[r + a]
                sums.append(total)
            left = jnp.where(column == 0, 0.0, pltpu.roll(sums[0], 1, 0))
            right = jnp.where(column == columns - 1, 0.0, pltpu.roll(sums[2], columns - 1, 0))
            out.append(pick(11) + sums[1] + left + right)
        return out

    @pl.when(block >= first_gate)
    def _():
        @pl.loop(0, BLOCK // LANES)
        def _(tile):
            lanes = pl.ds(pl.multiple_of(tile * LANES, LANES), LANES)
            base = pl.multiple_of((block - first_gate) * BLOCK + tile * LANES, LANES)
            for r, summed in enumerate(conv_tile(lanes)):
                gate_ref[r, :, pl.ds(base, LANES)] = summed * (1.0 / (1.0 + jnp.exp(-summed)))

    @pl.when(block <= first_gate)
    def _():
        skew = FF % LANES
        start = FF - skew - first_gate * BLOCK

        @pl.loop(0, BLOCK // LANES)
        def _(tile):
            lanes = pl.ds(pl.multiple_of(tile * LANES, LANES), LANES)
            base = pl.multiple_of(block * BLOCK + tile * LANES + start, LANES)
            for r, summed in enumerate(conv_tile(lanes)):
                near = pltpu.roll(gate_ref[r, :, pl.ds(base, LANES)], LANES - skew, 1)
                far = pltpu.roll(gate_ref[r, :, pl.ds(base + LANES, LANES)], LANES - skew, 1)
                lane = lax.broadcasted_iota(jnp.int32, near.shape, 1)
                gate = jnp.where(lane < LANES - skew, near, far)
                out_ref[r, :, lanes] = (summed * gate).astype(jnp.bfloat16)


def conv_frame(hidden, frame, prev, top, bottom, weights, into=None):
    frames, rows, columns, channels = hidden.shape
    blocks = pl.cdiv(channels, BLOCK)
    first_gate = FF // BLOCK
    flat = pl.BlockSpec((pl.Squeezed(), columns, BLOCK), lambda i: (0, 0, blocks - 1 - i))
    specs = [
        pl.BlockSpec(
            (pl.Squeezed(), rows, columns, BLOCK), lambda i: (frame, 0, 0, blocks - 1 - i)
        )
    ]
    if prev is None:
        args = [hidden] * (1 + rows)
        for r in range(rows):
            specs.append(
                pl.BlockSpec(
                    (pl.Squeezed(), pl.Squeezed(), columns, BLOCK),
                    functools.partial(lambda r, i: (frame - 1, r, 0, blocks - 1 - i), r),
                )
            )
    else:
        args = [hidden, *prev]
        specs += [flat] * rows
    args += [top, bottom, weights]
    specs += [flat, flat, pl.BlockSpec((weights.shape[0], BLOCK), lambda i: (0, blocks - 1 - i))]
    aliases = {}
    if into is not None:
        aliases = {len(args): 0}
        args.append(into)
        specs.append(pl.BlockSpec(memory_space=pl.ANY))
    elements = rows * columns * channels
    return pl.pallas_call(
        conv_kernel,
        out_shape=jax.ShapeDtypeStruct((frames, rows, columns, FF), jnp.bfloat16),
        grid=(blocks,),
        in_specs=specs,
        out_specs=pl.BlockSpec(
            (pl.Squeezed(), rows, columns, BLOCK),
            lambda i: (frame, 0, 0, jnp.minimum(blocks - 1 - i, first_gate)),
        ),
        scratch_shapes=[
            pltpu.VMEM((rows, columns, (blocks - first_gate) * BLOCK + LANES), jnp.float32)
        ],
        input_output_aliases=aliases,
        compiler_params=pltpu.CompilerParams(vmem_limit_bytes=32 << 20),
        cost_estimate=pl.CostEstimate(
            flops=elements * 40, bytes_accessed=elements * 6, transcendentals=elements // 2
        ),
        name="conv_frame",
    )(*args)


def whole(body, out_shape, flops, *args):
    specs = [pl.BlockSpec(memory_space=pltpu.SMEM)]
    specs += [pl.BlockSpec(memory_space=pltpu.VMEM)] * (len(args) - 1)
    return pl.pallas_call(
        body,
        out_shape=out_shape,
        in_specs=specs,
        out_specs=pl.BlockSpec(memory_space=pltpu.VMEM),
        compiler_params=pltpu.CompilerParams(vmem_limit_bytes=32 << 20),
        cost_estimate=pl.CostEstimate(flops=flops, bytes_accessed=3 << 20, transcendentals=0),
        name=body.__name__,
    )(*args)


def exchange(value, axis, flip):
    return lax.ppermute(value, axis, [(i, i ^ flip) for i in range(lax.axis_size(axis))])


def ahead(value, axis, steps, wrap=False):
    count = lax.axis_size(axis)
    pairs = [(i, (i + steps) % count) for i in range(count) if wrap or 0 <= i + steps < count]
    return lax.ppermute(value, axis, pairs)


def per_device(
    query_tokens, key_tokens, value_tokens, norm_gain, hidden, time_weight, space_weight, conv_bias
):
    frames, rows, columns, width = query_tokens.shape
    tokens = frames * rows * columns
    channels = hidden.shape[3]
    frame_axes = ("z", "x")
    row = lax.axis_index("row").astype(jnp.int32).reshape(1)
    x = lax.axis_index("x")
    narrow = lambda value: value.astype(jnp.bfloat16)
    wide = lambda value: value.astype(jnp.float32)

    def last_frame_row(r, after=None):
        piece = hidden[frames - 1, r : r + 1]
        if after is not None:
            piece, _ = lax.optimization_barrier((piece, after))
        return ahead(piece, frame_axes, 1)

    def edge(frame, r, before):
        now = wide(hidden[frame, r : r + 1])
        return narrow(time_weight[0] * now + time_weight[1] * wide(before))

    prev_first = last_frame_row(0)

    partial = whole(
        partial_kernel,
        jax.ShapeDtypeStruct((SHARES * SHARE_ROWS, LANES), jnp.bfloat16),
        2 * tokens * width * 256,
        row,
        key_tokens.reshape(tokens, width),
        value_tokens.reshape(tokens, width),
    )
    held = partial.reshape(4, 2, SHARE_ROWS, LANES)
    held = wide(held[:, 0]) + wide(exchange(held[:, 1], "row", 1))
    held = held.reshape(2, 2, SHARE_ROWS, LANES)
    held = held[:, 0] + wide(exchange(narrow(held[:, 1]), "row", 2))
    held = held[0] + wide(exchange(narrow(held[1]), "row", 4))

    sent = narrow(held)
    others = [wide(ahead(sent, "x", k, True)) for k in range(1, INNER)]
    prev_last = last_frame_row(rows - 1, sent)
    prev_middle = last_frame_row(1, sent)
    plane = held + others[0] + others[1] + others[2]
    upto = held
    for k in range(1, INNER):
        upto = upto + jnp.where(x >= k, others[k - 1], 0.0)

    before = jnp.zeros_like(plane)
    for k in (1, 2, 4):
        arrived = wide(ahead(narrow(plane), "z", k))
        plane = plane + arrived
        before = before + arrived
    state = narrow(before + upto)[None]
    state = jnp.stack([state, exchange(state, "row", 4)], axis=1).reshape(2, SHARE_ROWS, LANES)
    state = jnp.stack([state, exchange(state, "row", 2)], axis=1).reshape(4, SHARE_ROWS, LANES)
    state = jnp.stack([state, exchange(state, "row", 1)], axis=1)
    attention = whole(
        mixed_kernel,
        jax.ShapeDtypeStruct((tokens, width), jnp.bfloat16),
        2 * tokens * width * 256,
        row,
        query_tokens.reshape(tokens, width),
        state.reshape(SHARES * SHARE_ROWS, LANES),
        norm_gain[None],
    ).reshape(query_tokens.shape)

    weights = jnp.concatenate(
        [time_weight, space_weight.reshape(9, channels), conv_bias[None]], axis=0
    )
    mine = hidden[frames - 1], hidden[frames - 2]
    up_edge = edge(frames - 1, 0, mine[1][0:1])
    down_edge = edge(frames - 1, rows - 1, mine[1][rows - 1 : rows])
    up_edge, down_edge, _ = lax.optimization_barrier((up_edge, down_edge, sent))
    top, bottom = ahead(down_edge, "row", 1), ahead(up_edge, "row", -1)
    ffn_out = conv_frame(hidden, frames - 1, None, top, bottom, weights)

    bottom = ahead(edge(0, 0, prev_first), "row", -1)
    top = ahead(edge(0, rows - 1, prev_last), "row", 1)
    ffn_out = conv_frame(
        hidden, 0, (prev_first, prev_middle, prev_last), top, bottom, weights, ffn_out
    )
    return (attention, ffn_out)


def solution(mesh):
    frame, row = mesh.shape["frame"], mesh.shape["row"]
    split = Mesh(mesh.devices.reshape(frame // INNER, INNER, row), ("z", "x", "row"))
    tokens = P(("z", "x"), "row", None, None)
    return jax.shard_map(
        per_device,
        mesh=split,
        in_specs=(tokens, tokens, tokens, P(), tokens, P(), P(), P()),
        out_specs=(tokens, tokens),
        check_vma=False,
    )
```

time: 436 us -> 151 us (0.35)
  the two profiles are of different devices: /device:TPU:1 before, /device:TPU:129 now
where the time goes in v1:
time: 151 us; the launch traced here: 150 us
  starting transfers between devices  65 us (43%)
  waiting for transfers between devices  44.3 us (29%)
  Pallas kernels  26.1 us (17%)
  local copies, waits for them, and re-layouts  8.33 us (6%)
  other arithmetic  5.54 us (4%)
    ppermute x13, starting transfers between devices, ahead(): return lax.ppermute(value, axis, pairs)  46.4 us
    ppermute x13, waiting for transfers between devices, ahead(): return lax.ppermute(value, axis, pairs)  38 us
    pallas_call x2, Pallas kernels, conv_frame(): pl.pallas_call(conv_kernel, out_shape=jax.ShapeDtypeStruct((frames, rows,...  23 us
    ppermute x6, starting transfers between devices, exchange(): lax.ppermute(value, axis, [(i, i ^ flip) for i in range(lax.axis_size(axi...  18.6 us
    ppermute x6, waiting for transfers between devices, exchange(): lax.ppermute(value, axis, [(i, i ^ flip) for i in range(lax.axis_size(axi...  6.29 us
    convert_element_type x6, other arithmetic, per_device(): narrow = lambda value: value.astype(jnp.bfloat16)  3.51 us
    pallas_call x2, Pallas kernels, whole(): pl.pallas_call(body, out_shape=out_shape, in_specs=specs, out_specs=pl.Bl...  3.11 us
    squeeze x1, local copies, waits for them, and re-layouts, last_frame_row(): piece = hidden[frames - 1, r:r + 1]  3.1 us
  transfers between devices with their start and end apart: 19, of which 11 were waited for; matrix products, arithmetic and copies ran while one was open for 7% of the time, Pallas kernels for 9%

profile of v1, /device:TPU:129, one launch (start us, length us, event | category | flops | bytes accessed | tf_op | source)
XLA Modules:
  0.0 150.1 jit_solution(4521243453114316471)
XLA Ops:
  0.6 1.2 copy-done
  1.9 1.2 copy-done.1
  6.1 1.4 collective-permute-start.1
  7.4 3.4 %collective-permute-done.1 = bf16[2,256,128]{2,1,0:T(8,128)(2,1)S(1)} collective-permute-done((bf16[2,256,128]{2,1,0:T(8,128)(2,1)S(1)}, bf16[2,256,128]{2,1,0:T(8,128)(2,1)S(1)}, u32[]{:S(2)}, u32[]{:S(2)}) %collective-permute-start.1) | collective-permute-done | bytes 131104 | tf_op jit(solution)/shard_map/ppermute | solution.py:249
  10.9 3.0 %collective-permute-start.2 = (bf16[256,128]{1,0:T(8,128)(2,1)S(1)}, bf16[256,128]{1,0:T(8,128)(2,1)S(1)}, u32[]{:S(2)}, u32[]{:S(2)}) collective-permute-start(bf16[256,128]{1,0:T(8,128)(2,1)S(1)} %fusion.21), channel_id=1, source_target_pairs={{0,4},{1,5},{2,6},{3,7},{4,0},{5,1},{6,2},{7,3},{8,12},{9,13},{10,... | collective-permute-start | bytes 196616 | tf_op jit(solution)/shard_map/ppermute | solution.py:249
  13.9 1.7 %collective-permute-done.2 = bf16[256,128]{1,0:T(8,128)(2,1)S(1)} collective-permute-done((bf16[256,128]{1,0:T(8,128)(2,1)S(1)}, bf16[256,128]{1,0:T(8,128)(2,1)S(1)}, u32[]{:S(2)}, u32[]{:S(2)}) %collective-permute-start.2) | collective-permute-done | bytes 65568 | tf_op jit(solution)/shard_map/ppermute | solution.py:249
  15.6 1.3 collective-permute-start.3
  16.9 2.4 %collective-permute-start.4 = (bf16[256,128]{1,0:T(8,128)(2,1)S(1)}, bf16[256,128]{1,0:T(8,128)(2,1)S(1)}, u32[]{:S(2)}, u32[]{:S(2)}) collective-permute-start(bf16[256,128]{1,0:T(8,128)(2,1)S(1)} %fusion.22), channel_id=1, source_target_pairs={{0,16},{8,24},{16,0},{24,8},{1,17},{9,25},{17,1},{25,9},{2,18},{10... | collective-permute-start | bytes 196616 | tf_op jit(solution)/shard_map/ppermute | solution.py:255
  20.5 1.2 collective-permute-done.4
  22.8 2.6 %collective-permute-start.6 = (bf16[256,128]{1,0:T(8,128)(2,1)S(1)}, bf16[256,128]{1,0:T(8,128)(2,1)S(1)}, u32[]{:S(2)}, u32[]{:S(2)}) collective-permute-start(bf16[256,128]{1,0:T(8,128)(2,1)S(1)} %get-tuple-element.10), channel_id=1, source_target_pairs={{0,32},{32,64},{64,96},{96,128},{128,160},{160,192},{192,224},{1,3... | collective-permute-start | bytes 196616 | tf_op jit(solution)/shard_map/ppermute | solution.py:255
  25.5 3.6 %collective-permute-done.6 = bf16[256,128]{1,0:T(8,128)(2,1)S(1)} collective-permute-done((bf16[256,128]{1,0:T(8,128)(2,1)S(1)}, bf16[256,128]{1,0:T(8,128)(2,1)S(1)}, u32[]{:S(2)}, u32[]{:S(2)}) %collective-permute-start.6) | collective-permute-done | bytes 65568 | tf_op jit(solution)/shard_map/ppermute | solution.py:255
  29.1 1.9 %collective-permute-start.7 = (bf16[256,128]{1,0:T(8,128)(2,1)S(1)}, bf16[256,128]{1,0:T(8,128)(2,1)S(1)}, u32[]{:S(2)}, u32[]{:S(2)}) collective-permute-start(bf16[256,128]{1,0:T(8,128)(2,1)S(1)} %fusion.18), channel_id=1, source_target_pairs={{0,64},{32,96},{64,128},{96,160},{128,192},{160,224},{1,65},{33,97... | collective-permute-start | bytes 196616 | tf_op jit(solution)/shard_map/ppermute | solution.py:255
  31.0 5.2 %collective-permute-done.7 = bf16[256,128]{1,0:T(8,128)(2,1)S(1)} collective-permute-done((bf16[256,128]{1,0:T(8,128)(2,1)S(1)}, bf16[256,128]{1,0:T(8,128)(2,1)S(1)}, u32[]{:S(2)}, u32[]{:S(2)}) %collective-permute-start.7) | collective-permute-done | bytes 65568 | tf_op jit(solution)/shard_map/ppermute | solution.py:255
  36.2 1.3 collective-permute-start.8
  37.5 7.6 %collective-permute-done.8 = bf16[256,128]{1,0:T(8,128)(2,1)S(1)} collective-permute-done((bf16[256,128]{1,0:T(8,128)(2,1)S(1)}, bf16[256,128]{1,0:T(8,128)(2,1)S(1)}, u32[]{:S(2)}, u32[]{:S(2)}) %collective-permute-start.8) | collective-permute-done | bytes 65568 | tf_op jit(solution)/shard_map/ppermute | solution.py:255
  45.3 3.0 %collective-permute-start.9 = (bf16[1,256,128]{2,1,0:T(8,128)(2,1)S(1)}, bf16[1,256,128]{2,1,0:T(8,128)(2,1)S(1)}, u32[]{:S(2)}, u32[]{:S(2)}) collective-permute-start(bf16[1,256,128]{2,1,0:T(8,128)(2,1)S(1)} %bitcast.83), channel_id=1, source_target_pairs={{0,4},{1,5},{2,6},{3,7},{4,0},{5,1},{6,2},{7,3},{8,12},{9,13},{10,... | collective-permute-start | bytes 196616 | tf_op jit(solution)/shard_map/ppermute | solution.py:249
  48.3 3.1 %slice_bitcast_fusion = (bf16[1,40,11200]{2,1,0:T(8,128)(2,1)}, bf16[1,40,11200]{2,1,0:T(8,128)(2,1)S(1)}, bf16[1,40,11200]{2,1,0:T(8,128)(2,1)}) fusion(bf16[2,3,40,11200]{3,2,1,0:T(8,128)(2,1)} %cur_ref.3), kind=kLoop, calls=%fused_computation.12 | loop fusion | bytes 5376000 | tf_op jit(solution)/shard_map/squeeze | solution.py:271
  51.4 1.9 %collective-permute-start.12 = (bf16[1,40,11200]{2,1,0:T(8,128)(2,1)}, bf16[1,40,11200]{2,1,0:T(8,128)(2,1)S(1)}, u32[]{:S(2)}, u32[]{:S(2)}) collective-permute-start(bf16[1,40,11200]{2,1,0:T(8,128)(2,1)} %get-tuple-element.18), channel_id=1, source_target_pairs={{0,8},{8,16},{16,24},{24,32},{32,40},{40,48},{48,56},{56,64},{64,7... | collective-permute-start | bytes 2688008 | tf_op jit(solution)/shard_map/ppermute | solution.py:255
  53.3 3.2 %collective-permute-start.14 = (bf16[1,40,11200]{2,1,0:T(8,128)(2,1)}, bf16[1,40,11200]{2,1,0:T(8,128)(2,1)S(1)}, u32[]{:S(2)}, u32[]{:S(2)}) collective-permute-start(bf16[1,40,11200]{2,1,0:T(8,128)(2,1)} %get-tuple-element.7), channel_id=1, source_target_pairs={{0,8},{8,16},{16,24},{24,32},{32,40},{40,48},{48,56},{56,64},{64,7... | collective-permute-start | bytes 2688008 | tf_op jit(solution)/shard_map/ppermute | solution.py:255
  58.3 1.2 reshape.307
  60.3 3.5 %collective-permute-start.13 = (bf16[1,40,11200]{2,1,0:T(8,128)(2,1)S(1)}, bf16[1,40,11200]{2,1,0:T(8,128)(2,1)S(1)}, u32[]{:S(2)}, u32[]{:S(2)}) collective-permute-start(bf16[1,40,11200]{2,1,0:T(8,128)(2,1)S(1)} %get-tuple-element.6), channel_id=1, source_target_pairs={{0,8},{8,16},{16,24},{24,32},{32,40},{40,48},{48,56},{56,64},{64,7... | collective-permute-start | bytes 2688008 | tf_op jit(solution)/shard_map/ppermute | solution.py:255
  64.9 10.0 %collective-permute-start.11 = (bf16[4,256,128]{2,1,0:T(8,128)(2,1)S(1)}, bf16[4,256,128]{2,1,0:T(8,128)(2,1)S(1)}, u32[]{:S(2)}, u32[]{:S(2)}) collective-permute-start(bf16[4,256,128]{2,1,0:T(8,128)(2,1)S(1)} %bitcast.81), channel_id=1, source_target_pairs={{0,1},{1,0},{2,3},{3,2},{4,5},{5,4},{6,7},{7,6},{8,9},{9,8},{10,11... | collective-permute-start | bytes 786440 | tf_op jit(solution)/shard_map/ppermute | solution.py:249
  74.9 14.8 %collective-permute-done.14.prev2_ref = bf16[1,40,11200]{2,1,0:T(8,128)(2,1)S(1)} collective-permute-done((bf16[1,40,11200]{2,1,0:T(8,128)(2,1)}, bf16[1,40,11200]{2,1,0:T(8,128)(2,1)S(1)}, u32[]{:S(2)}, u32[]{:S(2)}) %collective-permute-start.14) | collective-permute-done | bytes 896032 | tf_op jit(solution)/shard_map/ppermute | solution.py:255
  89.7 3.3 %fusion.7 = (bf16[1,40,11200]{2,1,0:T(8,128)(2,1)S(1)}, bf16[1,40,11200]{2,1,0:T(8,128)(2,1)S(1)}, bf16[1,40,11200]{2,1,0:T(8,128)(2,1)S(1)}, bf16[1,40,11200]{2,1,0:T(8,128)(2,1)S(1)}) fusion(f32[11200]{0:T(1024)} %bitcast.87, f32[11200]{0:T(1024)} %bitcast.86, bf16[2,3,40,11200]{3,2,1,0:T(8,128)(2,1)} %cur_ref.3, ...), kind=kLoop, calls=%fused_computation.11 | loop fusion | flops 9856000 | bytes 9049600 | tf_op jit(solution)/shard_map/convert_element_type | solution.py:267
  93.0 19.5 %collective-permute-start.17 = (bf16[1,40,11200]{2,1,0:T(8,128)(2,1)S(1)}, bf16[1,40,11200]{2,1,0:T(8,128)(2,1)S(1)}, u32[]{:S(2)}, u32[]{:S(2)}) collective-permute-start(bf16[1,40,11200]{2,1,0:T(8,128)(2,1)S(1)} %get-tuple-element.8), channel_id=1, source_target_pairs={{0,1},{1,2},{2,3},{3,4},{4,5},{5,6},{6,7},{8,9},{9,10},{10,11},{11... | collective-permute-start | bytes 2688008 | tf_op jit(solution)/shard_map/ppermute | solution.py:255
  112.6 1.9 %collective-permute-start.18 = (bf16[1,40,11200]{2,1,0:T(8,128)(2,1)S(1)}, bf16[1,40,11200]{2,1,0:T(8,128)(2,1)S(1)}, u32[]{:S(2)}, u32[]{:S(2)}) collective-permute-start(bf16[1,40,11200]{2,1,0:T(8,128)(2,1)S(1)} %get-tuple-element.9), channel_id=1, source_target_pairs={{1,0},{2,1},{3,2},{4,3},{5,4},{6,5},{7,6},{9,8},{10,9},{11,10},{12... | collective-permute-start | bytes 2688008 | tf_op jit(solution)/shard_map/ppermute | solution.py:255
  114.5 3.6 %collective-permute-start.15 = (bf16[1,40,11200]{2,1,0:T(8,128)(2,1)S(1)}, bf16[1,40,11200]{2,1,0:T(8,128)(2,1)S(1)}, u32[]{:S(2)}, u32[]{:S(2)}) collective-permute-start(bf16[1,40,11200]{2,1,0:T(8,128)(2,1)S(1)} %get-tuple-element.15), channel_id=1, source_target_pairs={{0,1},{1,2},{2,3},{3,4},{4,5},{5,6},{6,7},{8,9},{9,10},{10,11},{11... | collective-permute-start | bytes 2688008 | tf_op jit(solution)/shard_map/ppermute | solution.py:255
  118.2 1.9 %collective-permute-start.16 = (bf16[1,40,11200]{2,1,0:T(8,128)(2,1)S(1)}, bf16[1,40,11200]{2,1,0:T(8,128)(2,1)S(1)}, u32[]{:S(2)}, u32[]{:S(2)}) collective-permute-start(bf16[1,40,11200]{2,1,0:T(8,128)(2,1)S(1)} %get-tuple-element.13), channel_id=1, source_target_pairs={{1,0},{2,1},{3,2},{4,3},{5,4},{6,5},{7,6},{9,8},{10,9},{11,10},{12... | collective-permute-start | bytes 2688008 | tf_op jit(solution)/shard_map/ppermute | solution.py:255
  120.3 2.2 %mixed_kernel.1 = bf16[240,2240]{1,0:T(8,128)(2,1)} custom-call(s32[1]{0:T(128)} %bitcast.row_ref, bf16[240,2240]{1,0:T(8,128)(2,1)S(1)} %bitcast.77, bf16[2048,128]{1,0:T(8,128)(2,1)S(1)} %bitcast.72, f32[1,2240]{1,0:T(1,128)S(1)} %broadcast_in_dim.17.gain_ref), custom_call_target="tpu_custom_call" | custom-call | flops 275251200 | bytes 3145728 | tf_op jit(solution)/shard_map/mixed_kernel/pallas_call | solution.py:237
  122.7 4.4 %collective-permute-done.18.bottom_ref = bf16[1,40,11200]{2,1,0:T(8,128)(2,1)S(1)} collective-permute-done((bf16[1,40,11200]{2,1,0:T(8,128)(2,1)S(1)}, bf16[1,40,11200]{2,1,0:T(8,128)(2,1)S(1)}, u32[]{:S(2)}, u32[]{:S(2)}) %collective-permute-start.18) | collective-permute-done | bytes 896032 | tf_op jit(solution)/shard_map/ppermute | solution.py:255
  127.1 11.5 %conv_frame.2.rest_0_ = bf16[2,3,40,5600]{3,2,1,0:T(8,128)(2,1)} custom-call(bf16[2,3,40,11200]{3,2,1,0:T(8,128)(2,1)S(1)} %bitcast.71, bf16[2,3,40,11200]{3,2,1,0:T(8,128)(2,1)S(1)} %bitcast.71, bf16[2,3,40,11200]{3,2,1,0:T(8,128)(2,1)S(1)} %bitcast.71, bf16[2,3,40,11200]{3,2,1,0:T(8,128)(2,1)S(1)} %bitcast.71, ...), custom_call_target="tpu_custom_call" | custom-call | flops 53760000 | bytes 8064000 | tf_op jit(solution)/shard_map/conv_frame/pallas_call | solution.py:213
  138.6 11.5 %conv_frame.3 = bf16[2,3,40,5600]{3,2,1,0:T(8,128)(2,1)} custom-call(bf16[2,3,40,11200]{3,2,1,0:T(8,128)(2,1)S(1)} %bitcast.71, bf16[1,40,11200]{2,1,0:T(8,128)(2,1)S(1)} %collective-permute-done.12.prev0_ref, bf16[1,40,11200]{2,1,0:T(8,128)(2,1)S(1)} %collective-permute-done.13.prev1_ref, ...), custom_call_target="tpu_custom_call", output_to_operand_aliasing={{}: (7, {})} | custom-call | flops 53760000 | bytes 8064000 | tf_op jit(solution)/shard_map/conv_frame/pallas_call | solution.py:213
  (46 shorter events, 9.4 us)
Async XLA Ops:
  0.6 1.2 copy-start
  1.9 1.2 copy-start.1
  4.1 1.9 %collective-permute-start = (bf16[4,256,128]{2,1,0:T(8,128)(2,1)S(1)}, bf16[4,256,128]{2,1,0:T(8,128)(2,1)S(1)}, u32[]{:S(2)}, u32[]{:S(2)}) collective-permute-start(bf16[4,256,128]{2,1,0:T(8,128)(2,1)S(1)} %slice_bitcast_fusion.3), channel_id=1, source_target_pairs={{0,1},{1,0},{2,3},{3,2},{4,5},{5,4},{6,7},{7,6},{8,9},{9,8},{10,11... | collective-permute-start | bytes 786440 | tf_op jit(solution)/shard_map/ppermute | solution.py:249
  6.1 4.8 %collective-permute-start.1 = (bf16[2,256,128]{2,1,0:T(8,128)(2,1)S(1)}, bf16[2,256,128]{2,1,0:T(8,128)(2,1)S(1)}, u32[]{:S(2)}, u32[]{:S(2)}) collective-permute-start(bf16[2,256,128]{2,1,0:T(8,128)(2,1)S(1)} %fusion.16), channel_id=1, source_target_pairs={{0,2},{1,3},{2,0},{3,1},{4,6},{5,7},{6,4},{7,5},{8,10},{9,11},{10,... | collective-permute-start | bytes 393224 | tf_op jit(solution)/shard_map/ppermute | solution.py:249
  10.9 4.7 %collective-permute-start.2 = (bf16[256,128]{1,0:T(8,128)(2,1)S(1)}, bf16[256,128]{1,0:T(8,128)(2,1)S(1)}, u32[]{:S(2)}, u32[]{:S(2)}) collective-permute-start(bf16[256,128]{1,0:T(8,128)(2,1)S(1)} %fusion.21), channel_id=1, source_target_pairs={{0,4},{1,5},{2,6},{3,7},{4,0},{5,1},{6,2},{7,3},{8,12},{9,13},{10,... | collective-permute-start | bytes 196616 | tf_op jit(solution)/shard_map/ppermute | solution.py:249
  15.6 4.9 %collective-permute-start.3 = (bf16[256,128]{1,0:T(8,128)(2,1)S(1)}, bf16[256,128]{1,0:T(8,128)(2,1)S(1)}, u32[]{:S(2)}, u32[]{:S(2)}) collective-permute-start(bf16[256,128]{1,0:T(8,128)(2,1)S(1)} %fusion.22), channel_id=1, source_target_pairs={{0,8},{8,16},{16,24},{24,0},{1,9},{9,17},{17,25},{25,1},{2,10},{10... | collective-permute-start | bytes 196616 | tf_op jit(solution)/shard_map/ppermute | solution.py:255
  16.9 4.8 %collective-permute-start.4 = (bf16[256,128]{1,0:T(8,128)(2,1)S(1)}, bf16[256,128]{1,0:T(8,128)(2,1)S(1)}, u32[]{:S(2)}, u32[]{:S(2)}) collective-permute-start(bf16[256,128]{1,0:T(8,128)(2,1)S(1)} %fusion.22), channel_id=1, source_target_pairs={{0,16},{8,24},{16,0},{24,8},{1,17},{9,25},{17,1},{25,9},{2,18},{10... | collective-permute-start | bytes 196616 | tf_op jit(solution)/shard_map/ppermute | solution.py:255
  19.4 3.4 %collective-permute-start.5 = (bf16[256,128]{1,0:T(8,128)(2,1)S(1)}, bf16[256,128]{1,0:T(8,128)(2,1)S(1)}, u32[]{:S(2)}, u32[]{:S(2)}) collective-permute-start(bf16[256,128]{1,0:T(8,128)(2,1)S(1)} %fusion.22), channel_id=1, source_target_pairs={{0,24},{8,0},{16,8},{24,16},{1,25},{9,1},{17,9},{25,17},{2,26},{10... | collective-permute-start | bytes 196616 | tf_op jit(solution)/shard_map/ppermute | solution.py:255
  22.8 6.2 %collective-permute-start.6 = (bf16[256,128]{1,0:T(8,128)(2,1)S(1)}, bf16[256,128]{1,0:T(8,128)(2,1)S(1)}, u32[]{:S(2)}, u32[]{:S(2)}) collective-permute-start(bf16[256,128]{1,0:T(8,128)(2,1)S(1)} %get-tuple-element.10), channel_id=1, source_target_pairs={{0,32},{32,64},{64,96},{96,128},{128,160},{160,192},{192,224},{1,3... | collective-permute-start | bytes 196616 | tf_op jit(solution)/shard_map/ppermute | solution.py:255
  29.1 7.1 %collective-permute-start.7 = (bf16[256,128]{1,0:T(8,128)(2,1)S(1)}, bf16[256,128]{1,0:T(8,128)(2,1)S(1)}, u32[]{:S(2)}, u32[]{:S(2)}) collective-permute-start(bf16[256,128]{1,0:T(8,128)(2,1)S(1)} %fusion.18), channel_id=1, source_target_pairs={{0,64},{32,96},{64,128},{96,160},{128,192},{160,224},{1,65},{33,97... | collective-permute-start | bytes 196616 | tf_op jit(solution)/shard_map/ppermute | solution.py:255
  36.2 8.9 %collective-permute-start.8 = (bf16[256,128]{1,0:T(8,128)(2,1)S(1)}, bf16[256,128]{1,0:T(8,128)(2,1)S(1)}, u32[]{:S(2)}, u32[]{:S(2)}) collective-permute-start(bf16[256,128]{1,0:T(8,128)(2,1)S(1)} %fusion.15), channel_id=1, source_target_pairs={{0,128},{32,160},{64,192},{96,224},{1,129},{33,161},{65,193},{97,2... | collective-permute-start | bytes 196616 | tf_op jit(solution)/shard_map/ppermute | solution.py:255
  45.2 12.3 %copy-start.3 = (f32[2,11200]{1,0:T(2,128)S(1)}, f32[2,11200]{1,0:T(2,128)}, u32[]{:S(2)}) copy-start(f32[2,11200]{1,0:T(2,128)} %param.13) | copy-start | bytes 268804
  45.3 11.3 %collective-permute-start.9 = (bf16[1,256,128]{2,1,0:T(8,128)(2,1)S(1)}, bf16[1,256,128]{2,1,0:T(8,128)(2,1)S(1)}, u32[]{:S(2)}, u32[]{:S(2)}) collective-permute-start(bf16[1,256,128]{2,1,0:T(8,128)(2,1)S(1)} %bitcast.83), channel_id=1, source_target_pairs={{0,4},{1,5},{2,6},{3,7},{4,0},{5,1},{6,2},{7,3},{8,12},{9,13},{10,... | collective-permute-start | bytes 196616 | tf_op jit(solution)/shard_map/ppermute | solution.py:249
  51.4 23.6 %collective-permute-start.12 = (bf16[1,40,11200]{2,1,0:T(8,128)(2,1)}, bf16[1,40,11200]{2,1,0:T(8,128)(2,1)S(1)}, u32[]{:S(2)}, u32[]{:S(2)}) collective-permute-start(bf16[1,40,11200]{2,1,0:T(8,128)(2,1)} %get-tuple-element.18), channel_id=1, source_target_pairs={{0,8},{8,16},{16,24},{24,32},{32,40},{40,48},{48,56},{56,64},{64,7... | collective-permute-start | bytes 2688008 | tf_op jit(solution)/shard_map/ppermute | solution.py:255
  53.3 36.4 %collective-permute-start.14 = (bf16[1,40,11200]{2,1,0:T(8,128)(2,1)}, bf16[1,40,11200]{2,1,0:T(8,128)(2,1)S(1)}, u32[]{:S(2)}, u32[]{:S(2)}) collective-permute-start(bf16[1,40,11200]{2,1,0:T(8,128)(2,1)} %get-tuple-element.7), channel_id=1, source_target_pairs={{0,8},{8,16},{16,24},{24,32},{32,40},{40,48},{48,56},{56,64},{64,7... | collective-permute-start | bytes 2688008 | tf_op jit(solution)/shard_map/ppermute | solution.py:255
  57.2 6.6 %collective-permute-start.10 = (bf16[2,256,128]{2,1,0:T(8,128)(2,1)}, bf16[2,256,128]{2,1,0:T(8,128)(2,1)}, u32[]{:S(2)}, u32[]{:S(2)}) collective-permute-start(bf16[2,256,128]{2,1,0:T(8,128)(2,1)} %get-tuple-element.20), channel_id=1, source_target_pairs={{0,2},{1,3},{2,0},{3,1},{4,6},{5,7},{6,4},{7,5},{8,10},{9,11},{10,... | collective-permute-start | bytes 393224 | tf_op jit(solution)/shard_map/ppermute | solution.py:249
  60.3 78.3 %collective-permute-start.13 = (bf16[1,40,11200]{2,1,0:T(8,128)(2,1)S(1)}, bf16[1,40,11200]{2,1,0:T(8,128)(2,1)S(1)}, u32[]{:S(2)}, u32[]{:S(2)}) collective-permute-start(bf16[1,40,11200]{2,1,0:T(8,128)(2,1)S(1)} %get-tuple-element.6), channel_id=1, source_target_pairs={{0,8},{8,16},{16,24},{24,32},{32,40},{40,48},{48,56},{56,64},{64,7... | collective-permute-start | bytes 2688008 | tf_op jit(solution)/shard_map/ppermute | solution.py:255
  63.8 63.3 %slice-start = ((s8[5406720]{0:T(1024)(128)(4,1)}), s8[4194304]{0:T(1024)(128)(4,1)S(1)}, s32[]{:S(2)}) async-start(s8[5406720]{0:T(1024)(128)(4,1)} %bitcast.70), calls=%async_computation | async-start | bytes 8388608
  64.9 53.3 %collective-permute-start.11 = (bf16[4,256,128]{2,1,0:T(8,128)(2,1)S(1)}, bf16[4,256,128]{2,1,0:T(8,128)(2,1)S(1)}, u32[]{:S(2)}, u32[]{:S(2)}) collective-permute-start(bf16[4,256,128]{2,1,0:T(8,128)(2,1)S(1)} %bitcast.81), channel_id=1, source_target_pairs={{0,1},{1,0},{2,3},{3,2},{4,5},{5,4},{6,7},{7,6},{8,9},{9,8},{10,11... | collective-permute-start | bytes 786440 | tf_op jit(solution)/shard_map/ppermute | solution.py:249
  89.7 30.4 %copy-start.4 = (f32[2,11200]{1,0:T(2,128)S(1)}, f32[2,11200]{1,0:T(2,128)}, u32[]{:S(2)}) copy-start(f32[2,11200]{1,0:T(2,128)} %param.13) | copy-start | bytes 268804
  89.7 30.4 %copy-start.5 = (f32[11200]{0:T(1024)S(1)}, f32[11200]{0:T(1024)}, u32[]{:S(2)}) copy-start(f32[11200]{0:T(1024)} %param.15) | copy-start | bytes 134404
  89.7 37.4 %slice-start.1 = ((s8[5406720]{0:T(1024)(128)(4,1)}), s8[1212416]{0:T(1024)(128)(4,1)S(1)}, s32[]{:S(2)}) async-start(s8[5406720]{0:T(1024)(128)(4,1)} %bitcast.70), calls=%async_computation.1 | async-start | bytes 2424832
  93.0 27.3 %copy-start.2 = (bf16[2,3,40,2240]{3,2,1,0:T(8,128)(2,1)S(1)}, bf16[2,3,40,2240]{3,2,1,0:T(8,128)(2,1)}, u32[]{:S(2)}) copy-start(bf16[2,3,40,2240]{3,2,1,0:T(8,128)(2,1)} %param.8) | copy-start | bytes 3225604
  93.0 29.7 %collective-permute-start.17 = (bf16[1,40,11200]{2,1,0:T(8,128)(2,1)S(1)}, bf16[1,40,11200]{2,1,0:T(8,128)(2,1)S(1)}, u32[]{:S(2)}, u32[]{:S(2)}) collective-permute-start(bf16[1,40,11200]{2,1,0:T(8,128)(2,1)S(1)} %get-tuple-element.8), channel_id=1, source_target_pairs={{0,1},{1,2},{2,3},{3,4},{4,5},{5,6},{6,7},{8,9},{9,10},{10,11},{11... | collective-permute-start | bytes 2688008 | tf_op jit(solution)/shard_map/ppermute | solution.py:255
  112.6 14.5 %collective-permute-start.18 = (bf16[1,40,11200]{2,1,0:T(8,128)(2,1)S(1)}, bf16[1,40,11200]{2,1,0:T(8,128)(2,1)S(1)}, u32[]{:S(2)}, u32[]{:S(2)}) collective-permute-start(bf16[1,40,11200]{2,1,0:T(8,128)(2,1)S(1)} %get-tuple-element.9), channel_id=1, source_target_pairs={{1,0},{2,1},{3,2},{4,3},{5,4},{6,5},{7,6},{9,8},{10,9},{11,10},{12... | collective-permute-start | bytes 2688008 | tf_op jit(solution)/shard_map/ppermute | solution.py:255
  114.5 24.1 %collective-permute-start.15 = (bf16[1,40,11200]{2,1,0:T(8,128)(2,1)S(1)}, bf16[1,40,11200]{2,1,0:T(8,128)(2,1)S(1)}, u32[]{:S(2)}, u32[]{:S(2)}) collective-permute-start(bf16[1,40,11200]{2,1,0:T(8,128)(2,1)S(1)} %get-tuple-element.15), channel_id=1, source_target_pairs={{0,1},{1,2},{2,3},{3,4},{4,5},{5,6},{6,7},{8,9},{9,10},{10,11},{11... | collective-permute-start | bytes 2688008 | tf_op jit(solution)/shard_map/ppermute | solution.py:255
  118.2 20.4 %collective-permute-start.16 = (bf16[1,40,11200]{2,1,0:T(8,128)(2,1)S(1)}, bf16[1,40,11200]{2,1,0:T(8,128)(2,1)S(1)}, u32[]{:S(2)}, u32[]{:S(2)}) collective-permute-start(bf16[1,40,11200]{2,1,0:T(8,128)(2,1)S(1)} %get-tuple-element.13), channel_id=1, source_target_pairs={{1,0},{2,1},{3,2},{4,3},{5,4},{6,5},{7,6},{9,8},{10,9},{11,10},{12... | collective-permute-start | bytes 2688008 | tf_op jit(solution)/shard_map/ppermute | solution.py:255

commit v2 on v1

--- a/solution.py
+++ b/solution.py
@@ -116,43 +116,59 @@
         flush(old)
 
 
-def conv_kernel(cur_ref, prev0_ref, prev1_ref, prev2_ref, top_ref, bottom_ref, weight_ref, *rest):
-    out_ref, gate_ref = rest[-2:]
-    step = pl.program_id(0)
-    blocks = pl.num_programs(0)
-    block = blocks - 1 - step
+def conv_kernel(pieces, cur_ref, *refs):
+    count = sum(pieces)
+    prev_refs, (top_ref, bottom_ref, weight_ref) = refs[:count], refs[count : count + 3]
+    out_ref, gate_ref = refs[-2:]
+    block = pl.num_programs(0) - 1 - pl.program_id(0)
     first_gate = FF // BLOCK
-    prev_refs = (prev0_ref, prev1_ref, prev2_ref)
-    rows = cur_ref.shape[0]
+    rows, columns, _ = cur_ref.shape
+    groups = columns // 8
 
     def conv_tile(lanes):
         weights = weight_ref[:, lanes]
-        pick = lambda index: weights[index : index + 1]
-        columns = cur_ref.shape[1]
-        spread = [
-            (
-                pick(0) * cur_ref[r, :, lanes].astype(jnp.float32)
-                + pick(1) * prev_refs[r][:, lanes].astype(jnp.float32)
-            )
-            .astype(jnp.bfloat16)
-            .astype(jnp.float32)
-            for r in range(rows)
-        ]
-        spread = [top_ref[:, lanes].astype(jnp.float32)] + spread
-        spread = spread + [bottom_ref[:, lanes].astype(jnp.float32)]
-        column = lax.broadcasted_iota(jnp.int32, (columns, LANES), 0)
+        pick = [jnp.broadcast_to(weights[i : i + 1], (8, LANES)) for i in range(12)]
+        subrow = lax.broadcasted_iota(jnp.int32, (8, LANES), 0)
+        first, last = subrow == 0, subrow == 7
+        zero = jnp.zeros((8, LANES), jnp.float32)
+
+        def split(value):
+            return [value[8 * g : 8 * g + 8] for g in range(value.shape[0] // 8)]
+
+        spread = [split(top_ref[:, lanes].astype(jnp.float32))]
+        at = 0
+        for r in range(rows):
+            now = split(cur_ref[r, :, lanes].astype(jnp.float32))
+            old = []
+            for ref in prev_refs[at : at + pieces[r]]:
+                old += split(ref[:, lanes].astype(jnp.float32))
+            at += pieces[r]
+            blend = jnp.concatenate([pick[0] * c + pick[1] * p for c, p in zip(now, old)], axis=0)
+            spread.append(split(blend.astype(jnp.bfloat16).astype(jnp.float32)))
+        spread.append(split(bottom_ref[:, lanes].astype(jnp.float32)))
         out = []
         for r in range(rows):
             sums = []
             for b in range(3):
-                total = pick(2 + b) * spread[r]
-                for a in (1, 2):
-                    total = total + pick(2 + 3 * a + b) * spread[r + a]
-                sums.append(total)
-            left = jnp.where(column == 0, 0.0, pltpu.roll(sums[0], 1, 0))
-            right = jnp.where(column == columns - 1, 0.0, pltpu.roll(sums[2], columns - 1, 0))
-            out.append(pick(11) + sums[1] + left + right)
-        return out
+                sums.append(
+                    [
+                        pick[2 + b] * spread[r][g]
+                        + pick[5 + b] * spread[r + 1][g]
+                        + pick[8 + b] * spread[r + 2][g]
+                        for g in range(groups)
+                    ]
+                )
+            left = [zero] + [pltpu.roll(value, 1, 0) for value in sums[0]]
+            right = [pltpu.roll(value, 7, 0) for value in sums[2]] + [zero]
+            out.append(
+                [
+                    (pick[11] + sums[1][g])
+                    + jnp.where(first, left[g], left[g + 1])
+                    + jnp.where(last, right[g + 1], right[g])
+                    for g in range(groups)
+                ]
+            )
+        return [jnp.concatenate(row, axis=0) for row in out]
 
     @pl.when(block >= first_gate)
     def _():
@@ -190,9 +206,11 @@
             (pl.Squeezed(), rows, columns, BLOCK), lambda i: (frame, 0, 0, blocks - 1 - i)
         )
     ]
+    args = [hidden]
     if prev is None:
-        args = [hidden] * (1 + rows)
+        pieces = (1,) * rows
         for r in range(rows):
+            args.append(hidden)
             specs.append(
                 pl.BlockSpec(
                     (pl.Squeezed(), pl.Squeezed(), columns, BLOCK),
@@ -200,8 +218,14 @@
                 )
             )
     else:
-        args = [hidden, *prev]
-        specs += [flat] * rows
+        pieces = tuple(len(row) for row in prev)
+        for piece in [piece for row in prev for piece in row]:
+            args.append(piece)
+            specs.append(
+                pl.BlockSpec(
+                    (pl.Squeezed(), piece.shape[1], BLOCK), lambda i: (0, 0, blocks - 1 - i)
+                )
+            )
     args += [top, bottom, weights]
     specs += [flat, flat, pl.BlockSpec((weights.shape[0], BLOCK), lambda i: (0, blocks - 1 - i))]
     aliases = {}
@@ -211,7 +235,7 @@
         specs.append(pl.BlockSpec(memory_space=pl.ANY))
     elements = rows * columns * channels
     return pl.pallas_call(
-        conv_kernel,
+        functools.partial(conv_kernel, pieces),
         out_shape=jax.ShapeDtypeStruct((frames, rows, columns, FF), jnp.bfloat16),
         grid=(blocks,),
         in_specs=specs,
@@ -255,6 +279,17 @@
     return lax.ppermute(value, axis, pairs)
 
 
+def behind(value, last):
+    planes, inner = lax.axis_size("z"), lax.axis_size("x")
+    pairs = []
+    for z in range(planes):
+        for x in range(inner):
+            up = last and x == 1
+            if z + up < planes:
+                pairs.append((z * inner + x, (z + up) * inner + (x - 1) % inner))
+    return lax.ppermute(value, ("z", "x"), pairs)
+
+
 def per_device(
     query_tokens, key_tokens, value_tokens, norm_gain, hidden, time_weight, space_weight, conv_bias
 ):
@@ -267,17 +302,19 @@
     narrow = lambda value: value.astype(jnp.bfloat16)
     wide = lambda value: value.astype(jnp.float32)
 
-    def last_frame_row(r, after=None):
-        piece = hidden[frames - 1, r : r + 1]
-        if after is not None:
-            piece, _ = lax.optimization_barrier((piece, after))
-        return ahead(piece, frame_axes, 1)
-
-    def edge(frame, r, before):
-        now = wide(hidden[frame, r : r + 1])
+    def tie(value, *others):
+        return lax.optimization_barrier((value, *others))[0]
+
+    def last_frame(r, start, stop, after=None):
+        source = hidden if after is None else tie(hidden, after)
+        return source[frames - 1, r : r + 1, start:stop]
+
+    def edge(source, frame, r, before, part=slice(None)):
+        now = wide(source[frame, r : r + 1, part])
         return narrow(time_weight[0] * now + time_weight[1] * wide(before))
 
-    prev_first = last_frame_row(0)
+    cut = columns // 16 * 8 + 8
+    first_a = ahead(last_frame(0, 0, cut), frame_axes, 1)
 
     partial = whole(
         partial_kernel,
@@ -287,29 +324,59 @@
         key_tokens.reshape(tokens, width),
         value_tokens.reshape(tokens, width),
     )
+    first_b = ahead(last_frame(0, cut, columns, partial), frame_axes, 1)
+    prev_last = ahead(last_frame(rows - 1, 0, columns, partial), frame_axes, 1)
+    middle_a = behind(last_frame(1, 0, cut, partial), False)
     held = partial.reshape(4, 2, SHARE_ROWS, LANES)
     held = wide(held[:, 0]) + wide(exchange(held[:, 1], "row", 1))
     held = held.reshape(2, 2, SHARE_ROWS, LANES)
     held = held[:, 0] + wide(exchange(narrow(held[:, 1]), "row", 2))
     held = held[0] + wide(exchange(narrow(held[1]), "row", 4))
 
-    sent = narrow(held)
-    others = [wide(ahead(sent, "x", k, True)) for k in range(1, INNER)]
-    prev_last = last_frame_row(rows - 1, sent)
-    prev_middle = last_frame_row(1, sent)
-    plane = held + others[0] + others[1] + others[2]
-    upto = held
+    later = tie(hidden, held)
+    up_edge = edge(later, frames - 1, 0, later[frames - 2, 0:1])
+    down_edge = edge(later, frames - 1, rows - 1, later[frames - 2, rows - 1 : rows])
+    mine = ahead(down_edge, "row", 1), ahead(up_edge, "row", -1)
+
+    weights = jnp.concatenate(
+        [time_weight, space_weight.reshape(9, channels), conv_bias[None]], axis=0
+    )
+
+    column = held
+    before = jnp.zeros_like(held)
+    for k in (1, 2, 4):
+        sent = narrow(column)
+        if k == 1:
+            sent, first_a, middle_a = lax.optimization_barrier((sent, first_a, middle_a))
+            middle_a = behind(middle_a, False)
+        if k == 2:
+            sent, first_b = lax.optimization_barrier((sent, first_b))
+            up_edge = [
+                edge(hidden, 0, 0, first_a, slice(0, cut)),
+                edge(hidden, 0, 0, first_b, slice(cut, columns)),
+            ]
+            bottom = ahead(jnp.concatenate(up_edge, axis=1), "row", -1)
+        if k == 4:
+            sent, mine, middle_a = lax.optimization_barrier((sent, mine, middle_a))
+            ffn_out = conv_frame(hidden, frames - 1, None, *mine, weights)
+            middle_a = behind(middle_a, True)
+        arrived = wide(ahead(sent, "z", k))
+        column = column + arrived
+        before = before + arrived
+    closed, opened, prev_last, middle_a, ffn_out, bottom = lax.optimization_barrier(
+        (narrow(column), narrow(before), prev_last, middle_a, ffn_out, bottom)
+    )
+    top = ahead(edge(hidden, 0, rows - 1, prev_last), "row", 1)
+    prefix = column
     for k in range(1, INNER):
-        upto = upto + jnp.where(x >= k, others[k - 1], 0.0)
-
-    before = jnp.zeros_like(plane)
-    for k in (1, 2, 4):
-        arrived = wide(ahead(narrow(plane), "z", k))
-        plane = plane + arrived
-        before = before + arrived
-    state = narrow(before + upto)[None]
+        sent = jnp.where(x + k < INNER, closed, opened)
+        prefix = prefix + wide(ahead(sent, "x", k, True))
+    middle_b = ahead(last_frame(1, cut, columns, prefix), frame_axes, 1)
+
+    state = narrow(prefix)[None]
     state = jnp.stack([state, exchange(state, "row", 4)], axis=1).reshape(2, SHARE_ROWS, LANES)
     state = jnp.stack([state, exchange(state, "row", 2)], axis=1).reshape(4, SHARE_ROWS, LANES)
+    state, middle_b, top = lax.optimization_barrier((state, middle_b, top))
     state = jnp.stack([state, exchange(state, "row", 1)], axis=1)
     attention = whole(
         mixed_kernel,
@@ -320,21 +387,14 @@
         state.reshape(SHARES * SHARE_ROWS, LANES),
         norm_gain[None],
     ).reshape(query_tokens.shape)
-
-    weights = jnp.concatenate(
-        [time_weight, space_weight.reshape(9, channels), conv_bias[None]], axis=0
-    )
-    mine = hidden[frames - 1], hidden[frames - 2]
-    up_edge = edge(frames - 1, 0, mine[1][0:1])
-    down_edge = edge(frames - 1, rows - 1, mine[1][rows - 1 : rows])
-    up_edge, down_edge, _ = lax.optimization_barrier((up_edge, down_edge, sent))
-    top, bottom = ahead(down_edge, "row", 1), ahead(up_edge, "row", -1)
-    ffn_out = conv_frame(hidden, frames - 1, None, top, bottom, weights)
-
-    bottom = ahead(edge(0, 0, prev_first), "row", -1)
-    top = ahead(edge(0, rows - 1, prev_last), "row", 1)
     ffn_out = conv_frame(
-        hidden, 0, (prev_first, prev_middle, prev_last), top, bottom, weights, ffn_out
+        hidden,
+        0,
+        ((first_a, first_b), (middle_a, middle_b), (prev_last,)),
+        top,
+        bottom,
+        weights,
+        ffn_out,
     )
     return (attention, ffn_out)
 

time: 151 us -> 149 us (0.987)
  the two profiles are of different devices: /device:TPU:129 before, /device:TPU:1 now
where the time goes in v2:
time: 149 us; the launch traced here: 148 us
  starting transfers between devices  79.1 us (53%)
  Pallas kernels  26.8 us (18%)
  local copies, waits for them, and re-layouts  17.4 us (12%)
  waiting for transfers between devices  14.5 us (10%)
  other arithmetic  9.2 us (6%)
    ppermute x14, starting transfers between devices, ahead(): return lax.ppermute(value, axis, pairs)  48.5 us
    pallas_call x2, Pallas kernels, conv_frame(): pl.pallas_call(functools.partial(conv_kernel, pieces), out_shape=jax.Shap...  23.8 us
    ppermute x3, starting transfers between devices, behind(): return lax.ppermute(value, ('z', 'x'), pairs)  20.9 us
    ppermute x6, waiting for transfers between devices, exchange(): lax.ppermute(value, axis, [(i, i ^ flip) for i in range(lax.axis_size(axi...  14.5 us
    ppermute x6, starting transfers between devices, exchange(): lax.ppermute(value, axis, [(i, i ^ flip) for i in range(lax.axis_size(axi...  9.78 us
    unnamed x44, local copies, waits for them, and re-layouts  9.27 us
    convert_element_type x8, other arithmetic, per_device(): narrow = lambda value: value.astype(jnp.bfloat16)  6.95 us
    squeeze x5, local copies, waits for them, and re-layouts, last_frame(): return source[frames - 1, r:r + 1, start:stop]  6.95 us
  transfers between devices with their start and end apart: 23, of which 3 were waited for; matrix products, arithmetic and copies ran while one was open for 12% of the time, Pallas kernels for 16%

profile of v2, /device:TPU:1, one launch (start us, length us, event | category | flops | bytes accessed | tf_op | source)
XLA Modules:
  0.0 148.2 jit_solution(2339915189569919902)
XLA Ops:
  0.6 1.2 copy-done.1
  1.9 1.2 copy-done.2
  4.1 3.3 %collective-permute-start = (bf16[4,256,128]{2,1,0:T(8,128)(2,1)S(1)}, bf16[4,256,128]{2,1,0:T(8,128)(2,1)S(1)}, u32[]{:S(2)}, u32[]{:S(2)}) collective-permute-start(bf16[4,256,128]{2,1,0:T(8,128)(2,1)S(1)} %slice_bitcast_fusion.5), channel_id=1, source_target_pairs={{0,1},{1,0},{2,3},{3,2},{4,5},{5,4},{6,7},{7,6},{8,9},{9,8},{10,11... | collective-permute-start | bytes 786440 | tf_op jit(solution)/shard_map/ppermute | solution.py:273
  7.4 1.9 %slice_bitcast_fusion.1 = bf16[1,24,11200]{2,1,0:T(8,128)(2,1)} fusion(bf16[2,3,40,11200]{3,2,1,0:T(8,128)(2,1)} %cur_ref.3), kind=kLoop, calls=%fused_computation.20 | loop fusion | bytes 1075200 | tf_op jit(solution)/shard_map/squeeze | solution.py:310
  10.0 1.9 %slice_bitcast_fusion.2 = bf16[1,24,11200]{2,1,0:T(8,128)(2,1)} fusion(bf16[2,3,40,11200]{3,2,1,0:T(8,128)(2,1)} %cur_ref.3), kind=kLoop, calls=%fused_computation.21 | loop fusion | bytes 1075200 | tf_op jit(solution)/shard_map/squeeze | solution.py:310
  11.9 2.6 %collective-permute-start.3 = (bf16[1,24,11200]{2,1,0:T(8,128)(2,1)}, bf16[1,24,11200]{2,1,0:T(8,128)(2,1)S(1)}, u32[]{:S(2)}, u32[]{:S(2)}) collective-permute-start(bf16[1,24,11200]{2,1,0:T(8,128)(2,1)} %slice_bitcast_fusion.2), channel_id=1, source_target_pairs={{0,8},{8,16},{16,24},{24,32},{32,40},{40,48},{48,56},{56,64},{64,7... | collective-permute-start | bytes 1612808 | tf_op jit(solution)/shard_map/ppermute | solution.py:279
  15.6 2.0 %collective-permute-start.6 = (bf16[1,16,11200]{2,1,0:T(8,128)(2,1)S(1)}, bf16[1,16,11200]{2,1,0:T(8,128)(2,1)S(1)}, u32[]{:S(2)}, u32[]{:S(2)}) collective-permute-start(bf16[1,16,11200]{2,1,0:T(8,128)(2,1)S(1)} %slice_bitcast_fusion.4), channel_id=1, source_target_pairs={{0,8},{8,16},{16,24},{24,32},{32,40},{40,48},{48,56},{56,64},{64,7... | collective-permute-start | bytes 1075208 | tf_op jit(solution)/shard_map/ppermute | solution.py:279
  18.6 2.1 %slice_bitcast_fusion = bf16[1,40,11200]{2,1,0:T(8,128)(2,1)} fusion(bf16[2,3,40,11200]{3,2,1,0:T(8,128)(2,1)} %cur_ref.3), kind=kLoop, calls=%fused_computation.15 | loop fusion | bytes 1792000 | tf_op jit(solution)/shard_map/squeeze | solution.py:310
  20.7 3.1 %collective-permute-start.12 = (bf16[1,40,11200]{2,1,0:T(8,128)(2,1)}, bf16[1,40,11200]{2,1,0:T(8,128)(2,1)S(1)}, u32[]{:S(2)}, u32[]{:S(2)}) collective-permute-start(bf16[1,40,11200]{2,1,0:T(8,128)(2,1)} %slice_bitcast_fusion), channel_id=1, source_target_pairs={{0,8},{8,16},{16,24},{24,32},{32,40},{40,48},{48,56},{56,64},{64,7... | collective-permute-start | bytes 2688008 | tf_op jit(solution)/shard_map/ppermute | solution.py:279
  23.9 2.7 %collective-permute-start.2 = (bf16[256,128]{1,0:T(8,128)(2,1)S(1)}, bf16[256,128]{1,0:T(8,128)(2,1)S(1)}, u32[]{:S(2)}, u32[]{:S(2)}) collective-permute-start(bf16[256,128]{1,0:T(8,128)(2,1)S(1)} %fusion.18), channel_id=1, source_target_pairs={{0,4},{1,5},{2,6},{3,7},{4,0},{5,1},{6,2},{7,3},{8,12},{9,13},{10,... | collective-permute-start | bytes 196616 | tf_op jit(solution)/shard_map/ppermute | solution.py:273
  28.7 2.6 %fusion.3 = (bf16[1,40,11200]{2,1,0:T(8,128)(2,1)S(1)}, bf16[1,40,11200]{2,1,0:T(8,128)(2,1)S(1)}) fusion(bf16[2,3,40,11200]{3,2,1,0:T(8,128)(2,1)} %cur_ref.3, f32[11200]{0:T(1024)S(1)} %bitcast.95, f32[11200]{0:T(1024)S(1)} %bitcast.91), kind=kLoop, calls=%fused_computation.5 | loop fusion | flops 5376000 | bytes 5465600 | tf_op jit(solution)/shard_map/convert_element_type | solution.py:302
  31.3 4.5 %collective-permute-start.8 = (bf16[1,40,11200]{2,1,0:T(8,128)(2,1)S(1)}, bf16[1,40,11200]{2,1,0:T(8,128)(2,1)S(1)}, u32[]{:S(2)}, u32[]{:S(2)}) collective-permute-start(bf16[1,40,11200]{2,1,0:T(8,128)(2,1)S(1)} %get-tuple-element.47), channel_id=1, source_target_pairs={{0,1},{1,2},{2,3},{3,4},{4,5},{5,6},{6,7},{8,9},{9,10},{10,11},{11... | collective-permute-start | bytes 2688008 | tf_op jit(solution)/shard_map/ppermute | solution.py:279
  35.9 1.9 %collective-permute-start.9 = (bf16[1,40,11200]{2,1,0:T(8,128)(2,1)S(1)}, bf16[1,40,11200]{2,1,0:T(8,128)(2,1)S(1)}, u32[]{:S(2)}, u32[]{:S(2)}) collective-permute-start(bf16[1,40,11200]{2,1,0:T(8,128)(2,1)S(1)} %get-tuple-element.46), channel_id=1, source_target_pairs={{1,0},{2,1},{3,2},{4,3},{5,4},{6,5},{7,6},{9,8},{10,9},{11,10},{12... | collective-permute-start | bytes 2688008 | tf_op jit(solution)/shard_map/ppermute | solution.py:279
  37.8 3.5 %collective-permute-start.5 = (bf16[256,128]{1,0:T(8,128)(2,1)S(1)}, bf16[256,128]{1,0:T(8,128)(2,1)S(1)}, u32[]{:S(2)}, u32[]{:S(2)}) collective-permute-start(bf16[256,128]{1,0:T(8,128)(2,1)S(1)} %get-tuple-element.24), channel_id=1, source_target_pairs={{0,32},{32,64},{64,96},{96,128},{128,160},{160,192},{192,224},{1,3... | collective-permute-start | bytes 196616 | tf_op jit(solution)/shard_map/ppermute | solution.py:279
  41.3 1.3 fusion.7
  42.6 15.2 %collective-permute-start.10 = (bf16[1,24,11200]{2,1,0:T(8,128)(2,1)}, bf16[1,24,11200]{2,1,0:T(8,128)(2,1)}, u32[]{:S(2)}, u32[]{:S(2)}) collective-permute-start(bf16[1,24,11200]{2,1,0:T(8,128)(2,1)} %collective-permute-done.4), channel_id=1, source_target_pairs={{0,24},{8,0},{16,8},{24,16},{32,56},{40,32},{48,40},{56,48},{64,88... | collective-permute-start | bytes 1612808 | tf_op jit(solution)/shard_map/ppermute | solution.py:290
  57.9 5.2 %collective-permute-start.7 = (bf16[256,128]{1,0:T(8,128)(2,1)S(1)}, bf16[256,128]{1,0:T(8,128)(2,1)S(1)}, u32[]{:S(2)}, u32[]{:S(2)}) collective-permute-start(bf16[256,128]{1,0:T(8,128)(2,1)S(1)} %fusion.14), channel_id=1, source_target_pairs={{0,64},{32,96},{64,128},{96,160},{128,192},{160,224},{1,65},{33,97... | collective-permute-start | bytes 196616 | tf_op jit(solution)/shard_map/ppermute | solution.py:279
  65.2 3.9 %collective-permute-start.14 = (bf16[1,40,11200]{2,1,0:T(8,128)(2,1)}, bf16[1,40,11200]{2,1,0:T(8,128)(2,1)S(1)}, u32[]{:S(2)}, u32[]{:S(2)}) collective-permute-start(bf16[1,40,11200]{2,1,0:T(8,128)(2,1)} %pad_maximum_fusion), channel_id=1, source_target_pairs={{1,0},{2,1},{3,2},{4,3},{5,4},{6,5},{7,6},{9,8},{10,9},{11,10},{12... | collective-permute-start | bytes 2688008 | tf_op jit(solution)/shard_map/ppermute | solution.py:279
  71.6 5.0 %collective-permute-start.13 = (bf16[1,24,11200]{2,1,0:T(8,128)(2,1)}, bf16[1,24,11200]{2,1,0:T(8,128)(2,1)}, u32[]{:S(2)}, u32[]{:S(2)}) collective-permute-start(bf16[1,24,11200]{2,1,0:T(8,128)(2,1)} %collective-permute-done.10), channel_id=1, source_target_pairs={{0,24},{8,32},{16,8},{24,16},{32,56},{40,64},{48,40},{56,48},{64,8... | collective-permute-start | bytes 1612808 | tf_op jit(solution)/shard_map/ppermute | solution.py:290
  76.5 9.8 %collective-permute-start.11 = (bf16[256,128]{1,0:T(8,128)(2,1)}, bf16[256,128]{1,0:T(8,128)(2,1)}, u32[]{:S(2)}, u32[]{:S(2)}) collective-permute-start(bf16[256,128]{1,0:T(8,128)(2,1)} %fusion.19), channel_id=1, source_target_pairs={{0,128},{32,160},{64,192},{96,224},{1,129},{33,161},{65,193},{97,2... | collective-permute-start | bytes 196616 | tf_op jit(solution)/shard_map/ppermute | solution.py:279
  86.6 2.5 %copy-done = bf16[2,3,40,11200]{3,2,1,0:T(8,128)(2,1)S(1)} copy-done((bf16[2,3,40,11200]{3,2,1,0:T(8,128)(2,1)S(1)}, bf16[2,3,40,11200]{3,2,1,0:T(8,128)(2,1)}, u32[]{:S(2)}) %copy-start) | copy-done | bytes 5376024
  89.1 1.2 copy-done.5
  90.3 1.2 copy-done.7
  91.5 11.5 %conv_frame.2.refs_8_ = bf16[2,3,40,5600]{3,2,1,0:T(8,128)(2,1)} custom-call(bf16[2,3,40,11200]{3,2,1,0:T(8,128)(2,1)S(1)} %copy-done, bf16[2,3,40,11200]{3,2,1,0:T(8,128)(2,1)S(1)} %copy-done, bf16[2,3,40,11200]{3,2,1,0:T(8,128)(2,1)S(1)} %copy-done, bf16[2,3,40,11200]{3,2,1,0:T(8,128)(2,1)S(1)} %copy-done, bf16[1,40,11200]{2,1,0:T(8,128)(2,1)S(1)} %copy-done.5, ...), custom_call_target="tpu_custom_call" | custom-call | flops 53760000 | bytes 8064000 | tf_op jit(solution)/shard_map/conv_frame/pallas_call | solution.py:237
  105.2 1.5 %collective-permute-start.17 = (bf16[256,128]{1,0:T(8,128)(2,1)S(1)}, bf16[256,128]{1,0:T(8,128)(2,1)S(1)}, u32[]{:S(2)}, u32[]{:S(2)}) collective-permute-start(bf16[256,128]{1,0:T(8,128)(2,1)S(1)} %get-tuple-element.53), channel_id=1, source_target_pairs={{0,24},{8,0},{16,8},{24,16},{1,25},{9,1},{17,9},{25,17},{2,26},{10... | collective-permute-start | bytes 196616 | tf_op jit(solution)/shard_map/ppermute | solution.py:279
  107.0 6.5 %collective-permute-start.21 = (bf16[1,40,11200]{2,1,0:T(8,128)(2,1)S(1)}, bf16[1,40,11200]{2,1,0:T(8,128)(2,1)S(1)}, u32[]{:S(2)}, u32[]{:S(2)}) collective-permute-start(bf16[1,40,11200]{2,1,0:T(8,128)(2,1)S(1)} %fusion.1), channel_id=1, source_target_pairs={{0,1},{1,2},{2,3},{3,4},{4,5},{5,6},{6,7},{8,9},{9,10},{10,11},{11... | collective-permute-start | bytes 2688008 | tf_op jit(solution)/shard_map/ppermute | solution.py:279
  114.5 2.7 %collective-permute-start.18 = (bf16[1,256,128]{2,1,0:T(8,128)(2,1)S(1)}, bf16[1,256,128]{2,1,0:T(8,128)(2,1)S(1)}, u32[]{:S(2)}, u32[]{:S(2)}) collective-permute-start(bf16[1,256,128]{2,1,0:T(8,128)(2,1)S(1)} %bitcast.102), channel_id=1, source_target_pairs={{0,4},{1,5},{2,6},{3,7},{4,0},{5,1},{6,2},{7,3},{8,12},{9,13},{10,... | collective-permute-start | bytes 196616 | tf_op jit(solution)/shard_map/ppermute | solution.py:273
  117.2 2.5 %collective-permute-start.20 = (bf16[1,16,11200]{2,1,0:T(8,128)(2,1)S(1)}, bf16[1,16,11200]{2,1,0:T(8,128)(2,1)S(1)}, u32[]{:S(2)}, u32[]{:S(2)}) collective-permute-start(bf16[1,16,11200]{2,1,0:T(8,128)(2,1)S(1)} %slice_bitcast_fusion.3), channel_id=1, source_target_pairs={{0,8},{8,16},{16,24},{24,32},{32,40},{40,48},{48,56},{56,64},{64,7... | collective-permute-start | bytes 1075208 | tf_op jit(solution)/shard_map/ppermute | solution.py:279
  119.8 9.8 %collective-permute-done.18 = bf16[1,256,128]{2,1,0:T(8,128)(2,1)S(1)} collective-permute-done((bf16[1,256,128]{2,1,0:T(8,128)(2,1)S(1)}, bf16[1,256,128]{2,1,0:T(8,128)(2,1)S(1)}, u32[]{:S(2)}, u32[]{:S(2)}) %collective-permute-start.18) | collective-permute-done | bytes 65568 | tf_op jit(solution)/shard_map/ppermute | solution.py:273
  129.7 3.8 %collective-permute-done.19 = bf16[2,256,128]{2,1,0:T(8,128)(2,1)S(1)} collective-permute-done((bf16[2,256,128]{2,1,0:T(8,128)(2,1)S(1)}, bf16[2,256,128]{2,1,0:T(8,128)(2,1)S(1)}, u32[]{:S(2)}, u32[]{:S(2)}) %collective-permute-start.19) | collective-permute-done | bytes 131104 | tf_op jit(solution)/shard_map/ppermute | solution.py:273
  133.7 12.3 %conv_frame.3 = bf16[2,3,40,5600]{3,2,1,0:T(8,128)(2,1)} custom-call(bf16[2,3,40,11200]{3,2,1,0:T(8,128)(2,1)S(1)} %copy-done, bf16[1,24,11200]{2,1,0:T(8,128)(2,1)S(1)} %collective-permute-done.3.refs_0_, bf16[1,16,11200]{2,1,0:T(8,128)(2,1)S(1)} %collective-permute-done.6.refs_1_, ...), custom_call_target="tpu_custom_call", output_to_operand_aliasing={{}: (9, {})} | custom-call | flops 53760000 | bytes 8064000 | tf_op jit(solution)/shard_map/conv_frame/pallas_call | solution.py:237
  146.1 2.2 %mixed_kernel.1 = bf16[240,2240]{1,0:T(8,128)(2,1)} custom-call(s32[1]{0:T(128)} %bitcast.row_ref, bf16[240,2240]{1,0:T(8,128)(2,1)S(1)} %bitcast.88, bf16[2048,128]{1,0:T(8,128)(2,1)S(1)} %bitcast.83, f32[1,2240]{1,0:T(1,128)S(1)} %broadcast_in_dim.11.gain_ref), custom_call_target="tpu_custom_call" | custom-call | flops 275251200 | bytes 3145728 | tf_op jit(solution)/shard_map/mixed_kernel/pallas_call | solution.py:261
  (90 shorter events, 14.3 us)
Async XLA Ops:
  4.1 13.6 %collective-permute-start = (bf16[4,256,128]{2,1,0:T(8,128)(2,1)S(1)}, bf16[4,256,128]{2,1,0:T(8,128)(2,1)S(1)}, u32[]{:S(2)}, u32[]{:S(2)}) collective-permute-start(bf16[4,256,128]{2,1,0:T(8,128)(2,1)S(1)} %slice_bitcast_fusion.5), channel_id=1, source_target_pairs={{0,1},{1,0},{2,3},{3,2},{4,5},{5,4},{6,7},{7,6},{8,9},{9,8},{10,11... | collective-permute-start | bytes 786440 | tf_op jit(solution)/shard_map/ppermute | solution.py:273
  9.3 26.6 %collective-permute-start.4 = (bf16[1,24,11200]{2,1,0:T(8,128)(2,1)}, bf16[1,24,11200]{2,1,0:T(8,128)(2,1)}, u32[]{:S(2)}, u32[]{:S(2)}) collective-permute-start(bf16[1,24,11200]{2,1,0:T(8,128)(2,1)} %slice_bitcast_fusion.1), channel_id=1, source_target_pairs={{0,24},{8,0},{16,8},{24,16},{32,56},{40,32},{48,40},{56,48},{64,88... | collective-permute-start | bytes 1612808 | tf_op jit(solution)/shard_map/ppermute | solution.py:290
  11.9 25.9 %collective-permute-start.3 = (bf16[1,24,11200]{2,1,0:T(8,128)(2,1)}, bf16[1,24,11200]{2,1,0:T(8,128)(2,1)S(1)}, u32[]{:S(2)}, u32[]{:S(2)}) collective-permute-start(bf16[1,24,11200]{2,1,0:T(8,128)(2,1)} %slice_bitcast_fusion.2), channel_id=1, source_target_pairs={{0,8},{8,16},{16,24},{24,32},{32,40},{40,48},{48,56},{56,64},{64,7... | collective-permute-start | bytes 1612808 | tf_op jit(solution)/shard_map/ppermute | solution.py:279
  15.6 42.3 %collective-permute-start.6 = (bf16[1,16,11200]{2,1,0:T(8,128)(2,1)S(1)}, bf16[1,16,11200]{2,1,0:T(8,128)(2,1)S(1)}, u32[]{:S(2)}, u32[]{:S(2)}) collective-permute-start(bf16[1,16,11200]{2,1,0:T(8,128)(2,1)S(1)} %slice_bitcast_fusion.4), channel_id=1, source_target_pairs={{0,8},{8,16},{16,24},{24,32},{32,40},{40,48},{48,56},{56,64},{64,7... | collective-permute-start | bytes 1075208 | tf_op jit(solution)/shard_map/ppermute | solution.py:279
  17.7 6.1 %collective-permute-start.1 = (bf16[2,256,128]{2,1,0:T(8,128)(2,1)S(1)}, bf16[2,256,128]{2,1,0:T(8,128)(2,1)S(1)}, u32[]{:S(2)}, u32[]{:S(2)}) collective-permute-start(bf16[2,256,128]{2,1,0:T(8,128)(2,1)S(1)} %fusion.12), channel_id=1, source_target_pairs={{0,2},{1,3},{2,0},{3,1},{4,6},{5,7},{6,4},{7,5},{8,10},{9,11},{10,... | collective-permute-start | bytes 393224 | tf_op jit(solution)/shard_map/ppermute | solution.py:273
  20.7 83.1 %collective-permute-start.12 = (bf16[1,40,11200]{2,1,0:T(8,128)(2,1)}, bf16[1,40,11200]{2,1,0:T(8,128)(2,1)S(1)}, u32[]{:S(2)}, u32[]{:S(2)}) collective-permute-start(bf16[1,40,11200]{2,1,0:T(8,128)(2,1)} %slice_bitcast_fusion), channel_id=1, source_target_pairs={{0,8},{8,16},{16,24},{24,32},{32,40},{40,48},{48,56},{56,64},{64,7... | collective-permute-start | bytes 2688008 | tf_op jit(solution)/shard_map/ppermute | solution.py:279
  23.9 4.7 %collective-permute-start.2 = (bf16[256,128]{1,0:T(8,128)(2,1)S(1)}, bf16[256,128]{1,0:T(8,128)(2,1)S(1)}, u32[]{:S(2)}, u32[]{:S(2)}) collective-permute-start(bf16[256,128]{1,0:T(8,128)(2,1)S(1)} %fusion.18), channel_id=1, source_target_pairs={{0,4},{1,5},{2,6},{3,7},{4,0},{5,1},{6,2},{7,3},{8,12},{9,13},{10,... | collective-permute-start | bytes 196616 | tf_op jit(solution)/shard_map/ppermute | solution.py:273
  26.7 36.3 %copy-start.9 = (f32[1,11200]{1,0:T(1,128)}, f32[1,11200]{1,0:T(1,128)S(1)}, u32[]{:S(2)}) copy-start(f32[1,11200]{1,0:T(1,128)S(1)} %get-tuple-element.55) | copy-start | bytes 134404
  26.7 36.3 %copy-start.11 = (f32[1,11200]{1,0:T(1,128)}, f32[1,11200]{1,0:T(1,128)S(1)}, u32[]{:S(2)}) copy-start(f32[1,11200]{1,0:T(1,128)S(1)} %get-tuple-element.56) | copy-start | bytes 134404
  31.3 38.4 %collective-permute-start.8 = (bf16[1,40,11200]{2,1,0:T(8,128)(2,1)S(1)}, bf16[1,40,11200]{2,1,0:T(8,128)(2,1)S(1)}, u32[]{:S(2)}, u32[]{:S(2)}) collective-permute-start(bf16[1,40,11200]{2,1,0:T(8,128)(2,1)S(1)} %get-tuple-element.47), channel_id=1, source_target_pairs={{0,1},{1,2},{2,3},{3,4},{4,5},{5,6},{6,7},{8,9},{9,10},{10,11},{11... | collective-permute-start | bytes 2688008 | tf_op jit(solution)/shard_map/ppermute | solution.py:279
  35.9 34.8 %collective-permute-start.9 = (bf16[1,40,11200]{2,1,0:T(8,128)(2,1)S(1)}, bf16[1,40,11200]{2,1,0:T(8,128)(2,1)S(1)}, u32[]{:S(2)}, u32[]{:S(2)}) collective-permute-start(bf16[1,40,11200]{2,1,0:T(8,128)(2,1)S(1)} %get-tuple-element.46), channel_id=1, source_target_pairs={{1,0},{2,1},{3,2},{4,3},{5,4},{6,5},{7,6},{9,8},{10,9},{11,10},{12... | collective-permute-start | bytes 2688008 | tf_op jit(solution)/shard_map/ppermute | solution.py:279
  37.8 4.8 %collective-permute-start.5 = (bf16[256,128]{1,0:T(8,128)(2,1)S(1)}, bf16[256,128]{1,0:T(8,128)(2,1)S(1)}, u32[]{:S(2)}, u32[]{:S(2)}) collective-permute-start(bf16[256,128]{1,0:T(8,128)(2,1)S(1)} %get-tuple-element.24), channel_id=1, source_target_pairs={{0,32},{32,64},{64,96},{96,128},{128,160},{160,192},{192,224},{1,3... | collective-permute-start | bytes 196616 | tf_op jit(solution)/shard_map/ppermute | solution.py:279
  42.6 43.8 %copy-start.8 = (f32[9,11200]{1,0:T(8,128)S(1)}, f32[9,11200]{1,0:T(8,128)}, u32[]{:S(2)}) copy-start(f32[9,11200]{1,0:T(8,128)} %reshape.371) | copy-start | bytes 1209604
  42.6 43.8 %copy-start.19 = (f32[2,11200]{1,0:T(2,128)S(1)}, f32[2,11200]{1,0:T(2,128)}, u32[]{:S(2)}) copy-start(f32[2,11200]{1,0:T(2,128)} %param.13) | copy-start | bytes 268804
  42.6 43.8 %copy-start.20 = (f32[11200]{0:T(1024)S(1)}, f32[11200]{0:T(1024)}, u32[]{:S(2)}) copy-start(f32[11200]{0:T(1024)} %param.15) | copy-start | bytes 134404
  42.6 43.8 %copy-start.13 = (bf16[256,128]{1,0:T(8,128)(2,1)}, bf16[256,128]{1,0:T(8,128)(2,1)S(1)}, u32[]{:S(2)}) copy-start(bf16[256,128]{1,0:T(8,128)(2,1)S(1)} %collective-permute-done.5) | copy-start | bytes 196612
  42.6 27.1 %collective-permute-start.10 = (bf16[1,24,11200]{2,1,0:T(8,128)(2,1)}, bf16[1,24,11200]{2,1,0:T(8,128)(2,1)}, u32[]{:S(2)}, u32[]{:S(2)}) collective-permute-start(bf16[1,24,11200]{2,1,0:T(8,128)(2,1)} %collective-permute-done.4), channel_id=1, source_target_pairs={{0,24},{8,0},{16,8},{24,16},{32,56},{40,32},{48,40},{56,48},{64,88... | collective-permute-start | bytes 1612808 | tf_op jit(solution)/shard_map/ppermute | solution.py:290
  57.9 7.3 %collective-permute-start.7 = (bf16[256,128]{1,0:T(8,128)(2,1)S(1)}, bf16[256,128]{1,0:T(8,128)(2,1)S(1)}, u32[]{:S(2)}, u32[]{:S(2)}) collective-permute-start(bf16[256,128]{1,0:T(8,128)(2,1)S(1)} %fusion.14), channel_id=1, source_target_pairs={{0,64},{32,96},{64,128},{96,160},{128,192},{160,224},{1,65},{33,97... | collective-permute-start | bytes 196616 | tf_op jit(solution)/shard_map/ppermute | solution.py:279
  65.2 21.2 %copy-start.15 = (bf16[256,128]{1,0:T(8,128)(2,1)}, bf16[256,128]{1,0:T(8,128)(2,1)S(1)}, u32[]{:S(2)}) copy-start(bf16[256,128]{1,0:T(8,128)(2,1)S(1)} %collective-permute-done.7) | copy-start | bytes 196612
  65.2 38.7 %collective-permute-start.14 = (bf16[1,40,11200]{2,1,0:T(8,128)(2,1)}, bf16[1,40,11200]{2,1,0:T(8,128)(2,1)S(1)}, u32[]{:S(2)}, u32[]{:S(2)}) collective-permute-start(bf16[1,40,11200]{2,1,0:T(8,128)(2,1)} %pad_maximum_fusion), channel_id=1, source_target_pairs={{1,0},{2,1},{3,2},{4,3},{5,4},{6,5},{7,6},{9,8},{10,9},{11,10},{12... | collective-permute-start | bytes 2688008 | tf_op jit(solution)/shard_map/ppermute | solution.py:279
  71.6 32.3 %collective-permute-start.13 = (bf16[1,24,11200]{2,1,0:T(8,128)(2,1)}, bf16[1,24,11200]{2,1,0:T(8,128)(2,1)}, u32[]{:S(2)}, u32[]{:S(2)}) collective-permute-start(bf16[1,24,11200]{2,1,0:T(8,128)(2,1)} %collective-permute-done.10), channel_id=1, source_target_pairs={{0,24},{8,32},{16,8},{24,16},{32,56},{40,64},{48,40},{56,48},{64,8... | collective-permute-start | bytes 1612808 | tf_op jit(solution)/shard_map/ppermute | solution.py:290
  76.5 26.4 %collective-permute-start.11 = (bf16[256,128]{1,0:T(8,128)(2,1)}, bf16[256,128]{1,0:T(8,128)(2,1)}, u32[]{:S(2)}, u32[]{:S(2)}) collective-permute-start(bf16[256,128]{1,0:T(8,128)(2,1)} %fusion.19), channel_id=1, source_target_pairs={{0,128},{32,160},{64,192},{96,224},{1,129},{33,161},{65,193},{97,2... | collective-permute-start | bytes 196616 | tf_op jit(solution)/shard_map/ppermute | solution.py:279
  91.5 15.2 %copy-start.12 = (f32[1,11200]{1,0:T(1,128)S(1)}, f32[1,11200]{1,0:T(1,128)}, u32[]{:S(2)}) copy-start(f32[1,11200]{1,0:T(1,128)} %copy-done.11) | copy-start | bytes 134404
  103.9 9.7 %collective-permute-start.15 = (bf16[256,128]{1,0:T(8,128)(2,1)S(1)}, bf16[256,128]{1,0:T(8,128)(2,1)S(1)}, u32[]{:S(2)}, u32[]{:S(2)}) collective-permute-start(bf16[256,128]{1,0:T(8,128)(2,1)S(1)} %get-tuple-element.52), channel_id=1, source_target_pairs={{0,8},{8,16},{16,24},{24,0},{1,9},{9,17},{17,25},{25,1},{2,10},{10... | collective-permute-start | bytes 196616 | tf_op jit(solution)/shard_map/ppermute | solution.py:279
  104.0 9.5 %collective-permute-start.16 = (bf16[256,128]{1,0:T(8,128)(2,1)S(1)}, bf16[256,128]{1,0:T(8,128)(2,1)S(1)}, u32[]{:S(2)}, u32[]{:S(2)}) collective-permute-start(bf16[256,128]{1,0:T(8,128)(2,1)S(1)} %get-tuple-element.54), channel_id=1, source_target_pairs={{0,16},{8,24},{16,0},{24,8},{1,17},{9,25},{17,1},{25,9},{2,18},{10... | collective-permute-start | bytes 196616 | tf_op jit(solution)/shard_map/ppermute | solution.py:279
  105.2 8.4 %collective-permute-start.17 = (bf16[256,128]{1,0:T(8,128)(2,1)S(1)}, bf16[256,128]{1,0:T(8,128)(2,1)S(1)}, u32[]{:S(2)}, u32[]{:S(2)}) collective-permute-start(bf16[256,128]{1,0:T(8,128)(2,1)S(1)} %get-tuple-element.53), channel_id=1, source_target_pairs={{0,24},{8,0},{16,8},{24,16},{1,25},{9,1},{17,9},{25,17},{2,26},{10... | collective-permute-start | bytes 196616 | tf_op jit(solution)/shard_map/ppermute | solution.py:279
  107.0 26.7 %copy-start.21 = (f32[2240]{0:T(1024)S(1)}, f32[2240]{0:T(1024)}, u32[]{:S(2)}) copy-start(f32[2240]{0:T(1024)} %param.11) | copy-start | bytes 26884
  107.0 26.5 %collective-permute-start.21 = (bf16[1,40,11200]{2,1,0:T(8,128)(2,1)S(1)}, bf16[1,40,11200]{2,1,0:T(8,128)(2,1)S(1)}, u32[]{:S(2)}, u32[]{:S(2)}) collective-permute-start(bf16[1,40,11200]{2,1,0:T(8,128)(2,1)S(1)} %fusion.1), channel_id=1, source_target_pairs={{0,1},{1,2},{2,3},{3,4},{4,5},{5,6},{6,7},{8,9},{9,10},{10,11},{11... | collective-permute-start | bytes 2688008 | tf_op jit(solution)/shard_map/ppermute | solution.py:279
  114.5 15.1 %collective-permute-start.18 = (bf16[1,256,128]{2,1,0:T(8,128)(2,1)S(1)}, bf16[1,256,128]{2,1,0:T(8,128)(2,1)S(1)}, u32[]{:S(2)}, u32[]{:S(2)}) collective-permute-start(bf16[1,256,128]{2,1,0:T(8,128)(2,1)S(1)} %bitcast.102), channel_id=1, source_target_pairs={{0,4},{1,5},{2,6},{3,7},{4,0},{5,1},{6,2},{7,3},{8,12},{9,13},{10,... | collective-permute-start | bytes 196616 | tf_op jit(solution)/shard_map/ppermute | solution.py:273
  117.2 16.3 %collective-permute-start.20 = (bf16[1,16,11200]{2,1,0:T(8,128)(2,1)S(1)}, bf16[1,16,11200]{2,1,0:T(8,128)(2,1)S(1)}, u32[]{:S(2)}, u32[]{:S(2)}) collective-permute-start(bf16[1,16,11200]{2,1,0:T(8,128)(2,1)S(1)} %slice_bitcast_fusion.3), channel_id=1, source_target_pairs={{0,8},{8,16},{16,24},{24,32},{32,40},{40,48},{48,56},{56,64},{64,7... | collective-permute-start | bytes 1075208 | tf_op jit(solution)/shard_map/ppermute | solution.py:279
  129.6 3.9 %collective-permute-start.19 = (bf16[2,256,128]{2,1,0:T(8,128)(2,1)S(1)}, bf16[2,256,128]{2,1,0:T(8,128)(2,1)S(1)}, u32[]{:S(2)}, u32[]{:S(2)}) collective-permute-start(bf16[2,256,128]{2,1,0:T(8,128)(2,1)S(1)} %get-tuple-element.51), channel_id=1, source_target_pairs={{0,2},{1,3},{2,0},{3,1},{4,6},{5,7},{6,4},{7,5},{8,10},{9,11},{10,... | collective-permute-start | bytes 393224 | tf_op jit(solution)/shard_map/ppermute | solution.py:273
  133.6 12.4 %collective-permute-start.22 = (bf16[4,256,128]{2,1,0:T(8,128)(2,1)S(1)}, bf16[4,256,128]{2,1,0:T(8,128)(2,1)S(1)}, u32[]{:S(2)}, u32[]{:S(2)}) collective-permute-start(bf16[4,256,128]{2,1,0:T(8,128)(2,1)S(1)} %bitcast.100), channel_id=1, source_target_pairs={{0,1},{1,0},{2,3},{3,2},{4,5},{5,4},{6,7},{7,6},{8,9},{9,8},{10,11... | collective-permute-start | bytes 786440 | tf_op jit(solution)/shard_map/ppermute | solution.py:273
  (13 other events, 82.0 us)

commit v3 on v2

--- a/solution.py
+++ b/solution.py
@@ -32,7 +32,7 @@
     return pl.multiple_of((share ^ row) * SHARE_ROWS + inside * UNIT, UNIT)
 
 
-def partial_kernel(row_ref, key_ref, value_ref, out_ref):
+def partial_kernel(row_ref, key_ref, value_ref, token_ref, out_ref):
     row = row_ref[0]
     width = key_ref.shape[1]
     pending = {}
@@ -118,7 +118,8 @@
 
 def conv_kernel(pieces, cur_ref, *refs):
     count = sum(pieces)
-    prev_refs, (top_ref, bottom_ref, weight_ref) = refs[:count], refs[count : count + 3]
+    prev_refs, (top_ref, bottom_ref) = refs[:count], refs[count : count + 2]
+    time_ref, space_ref, bias_ref = refs[count + 2 : count + 5]
     out_ref, gate_ref = refs[-2:]
     block = pl.num_programs(0) - 1 - pl.program_id(0)
     first_gate = FF // BLOCK
@@ -126,8 +127,13 @@
     groups = columns // 8
 
     def conv_tile(lanes):
-        weights = weight_ref[:, lanes]
-        pick = [jnp.broadcast_to(weights[i : i + 1], (8, LANES)) for i in range(12)]
+        times, bias = time_ref[:, lanes], bias_ref[:, lanes]
+        lines = [times[0:1], times[1:2]]
+        for a in range(3):
+            taps = space_ref[a, :, lanes]
+            lines += [taps[b : b + 1] for b in range(3)]
+        lines.append(bias)
+        pick = [jnp.broadcast_to(line, (8, LANES)) for line in lines]
         subrow = lax.broadcasted_iota(jnp.int32, (8, LANES), 0)
         first, last = subrow == 0, subrow == 7
         zero = jnp.zeros((8, LANES), jnp.float32)
@@ -218,16 +224,24 @@
                 )
             )
     else:
-        pieces = tuple(len(row) for row in prev)
-        for piece in [piece for row in prev for piece in row]:
-            args.append(piece)
+        ends, middle = prev
+        pieces = (1,) * rows
+        args += [ends, middle, ends]
+        for at in (0, 0, 1):
             specs.append(
                 pl.BlockSpec(
-                    (pl.Squeezed(), piece.shape[1], BLOCK), lambda i: (0, 0, blocks - 1 - i)
+                    (pl.Squeezed(), columns, BLOCK),
+                    functools.partial(lambda at, i: (at, 0, blocks - 1 - i), at),
                 )
             )
-    args += [top, bottom, weights]
-    specs += [flat, flat, pl.BlockSpec((weights.shape[0], BLOCK), lambda i: (0, blocks - 1 - i))]
+    args += [top, bottom, *weights]
+    specs += [
+        flat,
+        flat,
+        pl.BlockSpec((2, BLOCK), lambda i: (0, blocks - 1 - i)),
+        pl.BlockSpec((3, 3, BLOCK), lambda i: (0, 0, blocks - 1 - i)),
+        pl.BlockSpec((1, BLOCK), lambda i: (0, blocks - 1 - i)),
+    ]
     aliases = {}
     if into is not None:
         aliases = {len(args): 0}
@@ -247,12 +261,73 @@
             pltpu.VMEM((rows, columns, (blocks - first_gate) * BLOCK + LANES), jnp.float32)
         ],
         input_output_aliases=aliases,
-        compiler_params=pltpu.CompilerParams(vmem_limit_bytes=32 << 20),
+        compiler_params=pltpu.CompilerParams(vmem_limit_bytes=14 << 20),
         cost_estimate=pl.CostEstimate(
             flops=elements * 40, bytes_accessed=elements * 6, transcendentals=elements // 2
         ),
         name="conv_frame",
-    )(*args)
+    )(*kept(args))
+
+
+def edge_kernel(now0_ref, now2_ref, old0_ref, old2_ref, time_ref, *refs):
+    up_ref, down_ref, token_ref = refs[-3:]
+    token_ref[...] = jnp.zeros_like(token_ref)
+    for now_ref, old_ref, out_ref in ((now0_ref, old0_ref, up_ref), (now2_ref, old2_ref, down_ref)):
+        now, old = now_ref[...].astype(jnp.float32), old_ref[...].astype(jnp.float32)
+        out_ref[...] = (time_ref[0:1] * now + time_ref[1:2] * old).astype(jnp.bfloat16)
+    if len(refs) > 3:
+        now1_ref, ends_ref, middle_ref = refs[:3]
+        ends_ref[0] = now0_ref[...]
+        ends_ref[1] = now2_ref[...]
+        middle_ref[...] = now1_ref[...]
+
+
+def edges(hidden, frame, old, times):
+    frames, rows, columns, channels = hidden.shape
+    size = 2 * BLOCK
+
+    def take(at, r):
+        return pl.BlockSpec(
+            (pl.Squeezed(), pl.Squeezed(), columns, size), lambda i: (at, r, 0, i)
+        )
+
+    flat = pl.BlockSpec((pl.Squeezed(), columns, size), lambda i: (0, 0, i))
+    line = jax.ShapeDtypeStruct((1, columns, channels), jnp.bfloat16)
+    args, specs = [hidden, hidden], [take(frame, 0), take(frame, rows - 1)]
+    if old is None:
+        args += [hidden, hidden]
+        specs += [take(frame - 1, 0), take(frame - 1, rows - 1)]
+    else:
+        args += [old, old]
+        specs += [flat, pl.BlockSpec((pl.Squeezed(), columns, size), lambda i: (1, 0, i))]
+    args.append(times)
+    specs.append(pl.BlockSpec((2, size), lambda i: (0, i)))
+    out_shape = [line, line, jax.ShapeDtypeStruct((8, LANES), jnp.float32)]
+    out_specs = [flat, flat, pl.BlockSpec((8, LANES), lambda i: (0, 0))]
+    if old is None:
+        args.append(hidden)
+        specs.append(take(frame, 1))
+        both = jax.ShapeDtypeStruct((2, columns, channels), jnp.bfloat16)
+        out_shape = [both, line] + out_shape
+        out_specs = [pl.BlockSpec((2, columns, size), lambda i: (0, 0, i)), flat] + out_specs
+    return pl.pallas_call(
+        edge_kernel,
+        out_shape=out_shape,
+        grid=(pl.cdiv(channels, size),),
+        in_specs=specs,
+        out_specs=out_specs,
+        compiler_params=pltpu.CompilerParams(vmem_limit_bytes=14 << 20),
+        cost_estimate=pl.CostEstimate(
+            flops=6 * columns * channels, bytes_accessed=12 * columns * channels, transcendentals=0
+        ),
+        name="edges",
+    )(*kept(args))
+
+
+def kept(args):
+    return [
+        pltpu.with_memory_space_constraint(arg, pltpu.HBM) if arg.ndim == 4 else arg for arg in args
+    ]
 
 
 def whole(body, out_shape, flops, *args):
@@ -263,7 +338,7 @@
         out_shape=out_shape,
         in_specs=specs,
         out_specs=pl.BlockSpec(memory_space=pltpu.VMEM),
-        compiler_params=pltpu.CompilerParams(vmem_limit_bytes=32 << 20),
+        compiler_params=pltpu.CompilerParams(vmem_limit_bytes=14 << 20),
         cost_estimate=pl.CostEstimate(flops=flops, bytes_accessed=3 << 20, transcendentals=0),
         name=body.__name__,
     )(*args)
@@ -277,17 +352,6 @@
     count = lax.axis_size(axis)
     pairs = [(i, (i + steps) % count) for i in range(count) if wrap or 0 <= i + steps < count]
     return lax.ppermute(value, axis, pairs)
-
-
-def behind(value, last):
-    planes, inner = lax.axis_size("z"), lax.axis_size("x")
-    pairs = []
-    for z in range(planes):
-        for x in range(inner):
-            up = last and x == 1
-            if z + up < planes:
-                pairs.append((z * inner + x, (z + up) * inner + (x - 1) % inner))
-    return lax.ppermute(value, ("z", "x"), pairs)
 
 
 def per_device(
@@ -305,17 +369,9 @@
     def tie(value, *others):
         return lax.optimization_barrier((value, *others))[0]
 
-    def last_frame(r, start, stop, after=None):
-        source = hidden if after is None else tie(hidden, after)
-        return source[frames - 1, r : r + 1, start:stop]
-
-    def edge(source, frame, r, before, part=slice(None)):
-        now = wide(source[frame, r : r + 1, part])
-        return narrow(time_weight[0] * now + time_weight[1] * wide(before))
-
-    cut = columns // 16 * 8 + 8
-    first_a = ahead(last_frame(0, 0, cut), frame_axes, 1)
-
+    weights = time_weight, space_weight, conv_bias[None]
+    ends, middle, up_edge, down_edge, token = edges(hidden, frames - 1, None, time_weight)
+    ends = ahead(ends, frame_axes, 1)
     partial = whole(
         partial_kernel,
         jax.ShapeDtypeStruct((SHARES * SHARE_ROWS, LANES), jnp.bfloat16),
@@ -323,60 +379,41 @@
         row,
         key_tokens.reshape(tokens, width),
         value_tokens.reshape(tokens, width),
+        token,
     )
-    first_b = ahead(last_frame(0, cut, columns, partial), frame_axes, 1)
-    prev_last = ahead(last_frame(rows - 1, 0, columns, partial), frame_axes, 1)
-    middle_a = behind(last_frame(1, 0, cut, partial), False)
     held = partial.reshape(4, 2, SHARE_ROWS, LANES)
     held = wide(held[:, 0]) + wide(exchange(held[:, 1], "row", 1))
     held = held.reshape(2, 2, SHARE_ROWS, LANES)
     held = held[:, 0] + wide(exchange(narrow(held[:, 1]), "row", 2))
     held = held[0] + wide(exchange(narrow(held[1]), "row", 4))
 
-    later = tie(hidden, held)
-    up_edge = edge(later, frames - 1, 0, later[frames - 2, 0:1])
-    down_edge = edge(later, frames - 1, rows - 1, later[frames - 2, rows - 1 : rows])
-    mine = ahead(down_edge, "row", 1), ahead(up_edge, "row", -1)
-
-    weights = jnp.concatenate(
-        [time_weight, space_weight.reshape(9, channels), conv_bias[None]], axis=0
-    )
+    up_edge, down_edge = lax.optimization_barrier((up_edge, down_edge, held))[:2]
+    top, bottom = ahead(down_edge, "row", 1), ahead(up_edge, "row", -1)
 
     column = held
     before = jnp.zeros_like(held)
     for k in (1, 2, 4):
         sent = narrow(column)
-        if k == 1:
-            sent, first_a, middle_a = lax.optimization_barrier((sent, first_a, middle_a))
-            middle_a = behind(middle_a, False)
-        if k == 2:
-            sent, first_b = lax.optimization_barrier((sent, first_b))
-            up_edge = [
-                edge(hidden, 0, 0, first_a, slice(0, cut)),
-                edge(hidden, 0, 0, first_b, slice(cut, columns)),
-            ]
-            bottom = ahead(jnp.concatenate(up_edge, axis=1), "row", -1)
         if k == 4:
-            sent, mine, middle_a = lax.optimization_barrier((sent, mine, middle_a))
-            ffn_out = conv_frame(hidden, frames - 1, None, *mine, weights)
-            middle_a = behind(middle_a, True)
-        arrived = wide(ahead(sent, "z", k))
+            ffn_out = conv_frame(hidden, frames - 1, None, top, bottom, weights)
+        arrived = ahead(sent, "z", k)
+        if k == 4:
+            arrived, ffn_out = lax.optimization_barrier((arrived, ffn_out))
+        arrived = wide(arrived)
         column = column + arrived
         before = before + arrived
-    closed, opened, prev_last, middle_a, ffn_out, bottom = lax.optimization_barrier(
-        (narrow(column), narrow(before), prev_last, middle_a, ffn_out, bottom)
-    )
-    top = ahead(edge(hidden, 0, rows - 1, prev_last), "row", 1)
+    closed, opened = lax.optimization_barrier((narrow(column), narrow(before), ends))[:2]
+    up_edge, down_edge, _ = edges(hidden, 0, ends, time_weight)
     prefix = column
     for k in range(1, INNER):
         sent = jnp.where(x + k < INNER, closed, opened)
         prefix = prefix + wide(ahead(sent, "x", k, True))
-    middle_b = ahead(last_frame(1, cut, columns, prefix), frame_axes, 1)
+    middle = ahead(tie(middle, prefix), frame_axes, 1)
+    top, bottom = ahead(down_edge, "row", 1), ahead(up_edge, "row", -1)
 
     state = narrow(prefix)[None]
     state = jnp.stack([state, exchange(state, "row", 4)], axis=1).reshape(2, SHARE_ROWS, LANES)
     state = jnp.stack([state, exchange(state, "row", 2)], axis=1).reshape(4, SHARE_ROWS, LANES)
-    state, middle_b, top = lax.optimization_barrier((state, middle_b, top))
     state = jnp.stack([state, exchange(state, "row", 1)], axis=1)
     attention = whole(
         mixed_kernel,
@@ -386,17 +423,9 @@
         query_tokens.reshape(tokens, width),
         state.reshape(SHARES * SHARE_ROWS, LANES),
         norm_gain[None],
-    ).reshape(query_tokens.shape)
-    ffn_out = conv_frame(
-        hidden,
-        0,
-        ((first_a, first_b), (middle_a, middle_b), (prev_last,)),
-        top,
-        bottom,
-        weights,
-        ffn_out,
     )
-    return (attention, ffn_out)
+    ffn_out = conv_frame(hidden, 0, (ends, middle), top, bottom, weights, ffn_out)
+    return (attention.reshape(query_tokens.shape), ffn_out)
 
 
 def solution(mesh):

time: 149 us -> 140 us (0.940)
  local copies, waits for them, and re-layouts: 17.4 us -> 1.92 us
  Pallas kernels: 26.8 us -> 35.7 us
  other arithmetic: 9.2 us -> 2.7 us
  waiting for transfers between devices: 14.5 us -> 19.4 us
    ppermute x3 -> x0, starting transfers between devices: 20.9 us -> none  [behind(): return lax.ppermute(value, ('z', 'x'), pairs)]
    ppermute x14 -> x12, starting transfers between devices: 48.5 us -> 65.9 us  [ahead(): return lax.ppermute(value, axis, pairs)]
    pallas_call x0 -> x2, Pallas kernels: none -> 8.37 us  [edges(): pl.pallas_call(edge_kernel, out_shape=out_shape, grid=(pl.cdiv(channels,...]
    unnamed x44 -> x28, local copies, waits for them, and re-layouts: 9.27 us -> 1.87 us
    squeeze x5 -> x0, local copies, waits for them, and re-layouts: 6.95 us -> none  [last_frame(): return source[frames - 1, r:r + 1, start:stop]]
    convert_element_type x8 -> x4, other arithmetic: 6.95 us -> 1.59 us  [per_device(): narrow = lambda value: value.astype(jnp.bfloat16)]
    ppermute x6, starting transfers between devices: 9.78 us -> 12.7 us  [exchange(): lax.ppermute(value, axis, [(i, i ^ flip) for i in range(lax.axis_size(axi...]
    ppermute x14 -> x12, waiting for transfers between devices: 0.05 us -> 2.65 us  [ahead(): return lax.ppermute(value, axis, pairs)]
  transfers between devices with their start and end apart: 23 -> 18, of which waited for: 3 -> 8; matrix products, arithmetic and copies ran while one was open for 12% -> 2% of each run, Pallas kernels for 16% -> 13%
where the time goes in v3:
time: 140 us; the launch traced here: 139 us
  starting transfers between devices  78.6 us (56%)
  Pallas kernels  35.7 us (26%)
  waiting for transfers between devices  19.4 us (14%)
  other arithmetic  2.7 us (2%)
  local copies, waits for them, and re-layouts  1.92 us (1%)
    ppermute x12, starting transfers between devices, ahead(): return lax.ppermute(value, axis, pairs)  65.9 us
    pallas_call x2, Pallas kernels, conv_frame(): pl.pallas_call(functools.partial(conv_kernel, pieces), out_shape=jax.Shap...  24.2 us
    ppermute x6, waiting for transfers between devices, exchange(): lax.ppermute(value, axis, [(i, i ^ flip) for i in range(lax.axis_size(axi...  16.8 us
    ppermute x6, starting transfers between devices, exchange(): lax.ppermute(value, axis, [(i, i ^ flip) for i in range(lax.axis_size(axi...  12.7 us
    pallas_call x2, Pallas kernels, edges(): pl.pallas_call(edge_kernel, out_shape=out_shape, grid=(pl.cdiv(channels,...  8.37 us
    pallas_call x2, Pallas kernels, whole(): pl.pallas_call(body, out_shape=out_shape, in_specs=specs, out_specs=pl.Bl...  3.11 us
  transfers between devices with their start and end apart: 18, of which 8 were waited for; matrix products, arithmetic and copies ran while one was open for 2% of the time, Pallas kernels for 13%

profile of v3, /device:TPU:1, one launch (start us, length us, event | category | flops | bytes accessed | tf_op | source)
XLA Modules:
  0.0 139.3 jit_solution(14957639605026643992)
XLA Ops:
  1.5 5.0 %edges.2 = (bf16[2,40,11200]{2,1,0:T(8,128)(2,1)}, bf16[1,40,11200]{2,1,0:T(8,128)(2,1)S(1)}, bf16[1,40,11200]{2,1,0:T(8,128)(2,1)}, bf16[1,40,11200]{2,1,0:T(8,128)(2,1)}, f32[8,128]{1,0:T(8,128)S(1)}) custom-call(bf16[2,3,40,11200]{3,2,1,0:T(8,128)(2,1)} %cur_ref.3, bf16[2,3,40,11200]{3,2,1,0:T(8,128)(2,1)} %cur_ref.3, bf16[2,3,40,11200]{3,2,1,0:T(8,128)(2,1)} %cur_ref.3, ...), custom_call_target="tpu_custom_call" | custom-call | flops 2688000 | bytes 5376000 | tf_op jit(solution)/shard_map/edges/pallas_call | solution.py:313
  6.5 0.9 copy-done.7
  7.4 0.9 partial_kernel.1
  8.4 3.3 %collective-permute-start = (bf16[4,256,128]{2,1,0:T(8,128)(2,1)S(1)}, bf16[4,256,128]{2,1,0:T(8,128)(2,1)S(1)}, u32[]{:S(2)}, u32[]{:S(2)}) collective-permute-start(bf16[4,256,128]{2,1,0:T(8,128)(2,1)S(1)} %slice_bitcast_fusion), channel_id=1, source_target_pairs={{0,1},{1,0},{2,3},{3,2},{4,5},{5,4},{6,7},{7,6},{8,9},{9,8},{10,11... | collective-permute-start | bytes 786440 | tf_op jit(solution)/shard_map/ppermute | solution.py:348
  11.7 1.2 collective-permute-done
  13.1 2.8 %collective-permute-start.8 = (bf16[2,40,11200]{2,1,0:T(8,128)(2,1)}, bf16[2,40,11200]{2,1,0:T(8,128)(2,1)S(1)}, u32[]{:S(2)}, u32[]{:S(2)}) collective-permute-start(bf16[2,40,11200]{2,1,0:T(8,128)(2,1)} %get-tuple-element.22), channel_id=1, source_target_pairs={{0,8},{8,16},{16,24},{24,32},{32,40},{40,48},{48,56},{56,64},{64,7... | collective-permute-start | bytes 5376008 | tf_op jit(solution)/shard_map/ppermute | solution.py:354
  15.8 1.9 %collective-permute-done.1 = bf16[2,256,128]{2,1,0:T(8,128)(2,1)S(1)} collective-permute-done((bf16[2,256,128]{2,1,0:T(8,128)(2,1)S(1)}, bf16[2,256,128]{2,1,0:T(8,128)(2,1)S(1)}, u32[]{:S(2)}, u32[]{:S(2)}) %collective-permute-start.1) | collective-permute-done | bytes 131104 | tf_op jit(solution)/shard_map/ppermute | solution.py:348
  17.8 1.3 collective-permute-start.2
  19.1 3.4 %collective-permute-done.2 = bf16[256,128]{1,0:T(8,128)(2,1)S(1)} collective-permute-done((bf16[256,128]{1,0:T(8,128)(2,1)S(1)}, bf16[256,128]{1,0:T(8,128)(2,1)S(1)}, u32[]{:S(2)}, u32[]{:S(2)}) %collective-permute-start.2) | collective-permute-done | bytes 65568 | tf_op jit(solution)/shard_map/ppermute | solution.py:348
  22.6 4.1 %collective-permute-start.6 = (bf16[1,40,11200]{2,1,0:T(8,128)(2,1)}, bf16[1,40,11200]{2,1,0:T(8,128)(2,1)S(1)}, u32[]{:S(2)}, u32[]{:S(2)}) collective-permute-start(bf16[1,40,11200]{2,1,0:T(8,128)(2,1)} %get-tuple-element.19), channel_id=1, source_target_pairs={{0,1},{1,2},{2,3},{3,4},{4,5},{5,6},{6,7},{8,9},{9,10},{10,11},{11... | collective-permute-start | bytes 2688008 | tf_op jit(solution)/shard_map/ppermute | solution.py:354
  26.7 1.9 %collective-permute-start.7 = (bf16[1,40,11200]{2,1,0:T(8,128)(2,1)}, bf16[1,40,11200]{2,1,0:T(8,128)(2,1)}, u32[]{:S(2)}, u32[]{:S(2)}) collective-permute-start(bf16[1,40,11200]{2,1,0:T(8,128)(2,1)} %get-tuple-element.20), channel_id=1, source_target_pairs={{1,0},{2,1},{3,2},{4,3},{5,4},{6,5},{7,6},{9,8},{10,9},{11,10},{12... | collective-permute-start | bytes 2688008 | tf_op jit(solution)/shard_map/ppermute | solution.py:354
  28.6 3.1 %collective-permute-start.3 = (bf16[256,128]{1,0:T(8,128)(2,1)S(1)}, bf16[256,128]{1,0:T(8,128)(2,1)S(1)}, u32[]{:S(2)}, u32[]{:S(2)}) collective-permute-start(bf16[256,128]{1,0:T(8,128)(2,1)S(1)} %get-tuple-element.30), channel_id=1, source_target_pairs={{0,32},{32,64},{64,96},{96,128},{128,160},{160,192},{192,224},{1,3... | collective-permute-start | bytes 196616 | tf_op jit(solution)/shard_map/ppermute | solution.py:354
  31.8 1.3 collective-permute-done.3
  33.1 5.3 %collective-permute-start.4 = (bf16[256,128]{1,0:T(8,128)(2,1)S(1)}, bf16[256,128]{1,0:T(8,128)(2,1)S(1)}, u32[]{:S(2)}, u32[]{:S(2)}) collective-permute-start(bf16[256,128]{1,0:T(8,128)(2,1)S(1)} %fusion.4), channel_id=1, source_target_pairs={{0,64},{32,96},{64,128},{96,160},{128,192},{160,224},{1,65},{33,97... | collective-permute-start | bytes 196616 | tf_op jit(solution)/shard_map/ppermute | solution.py:354
  38.4 1.3 collective-permute-done.4
  40.4 11.8 %collective-permute-start.5 = (bf16[256,128]{1,0:T(8,128)(2,1)}, bf16[256,128]{1,0:T(8,128)(2,1)}, u32[]{:S(2)}, u32[]{:S(2)}) collective-permute-start(bf16[256,128]{1,0:T(8,128)(2,1)} %fusion.9), channel_id=1, source_target_pairs={{0,128},{32,160},{64,192},{96,224},{1,129},{33,161},{65,193},{97,2... | collective-permute-start | bytes 196616 | tf_op jit(solution)/shard_map/ppermute | solution.py:354
  52.3 12.1 %conv_frame.2.refs_8_ = bf16[2,3,40,5600]{3,2,1,0:T(8,128)(2,1)} custom-call(bf16[2,3,40,11200]{3,2,1,0:T(8,128)(2,1)} %cur_ref.3, bf16[2,3,40,11200]{3,2,1,0:T(8,128)(2,1)} %cur_ref.3, bf16[2,3,40,11200]{3,2,1,0:T(8,128)(2,1)} %cur_ref.3, bf16[2,3,40,11200]{3,2,1,0:T(8,128)(2,1)} %cur_ref.3, bf16[1,40,11200]{2,1,0:T(8,128)(2,1)S(1)} %collective-permute-done.6.refs_3_, ...), custom_call_target="tpu_custom_call" | custom-call | flops 53760000 | bytes 8064000 | tf_op jit(solution)/shard_map/conv_frame/pallas_call | solution.py:251
  64.4 0.9 fusion.1
  65.4 2.3 %collective-permute-start.10 = (bf16[256,128]{1,0:T(8,128)(2,1)S(1)}, bf16[256,128]{1,0:T(8,128)(2,1)S(1)}, u32[]{:S(2)}, u32[]{:S(2)}) collective-permute-start(bf16[256,128]{1,0:T(8,128)(2,1)S(1)} %get-tuple-element.38), channel_id=1, source_target_pairs={{0,16},{8,24},{16,0},{24,8},{1,17},{9,25},{17,1},{25,9},{2,18},{10... | collective-permute-start | bytes 196616 | tf_op jit(solution)/shard_map/ppermute | solution.py:354
  67.7 23.3 %collective-permute-start.11 = (bf16[256,128]{1,0:T(8,128)(2,1)S(1)}, bf16[256,128]{1,0:T(8,128)(2,1)S(1)}, u32[]{:S(2)}, u32[]{:S(2)}) collective-permute-start(bf16[256,128]{1,0:T(8,128)(2,1)S(1)} %get-tuple-element.37), channel_id=1, source_target_pairs={{0,24},{8,0},{16,8},{24,16},{1,25},{9,1},{17,9},{25,17},{2,26},{10... | collective-permute-start | bytes 196616 | tf_op jit(solution)/shard_map/ppermute | solution.py:354
  91.5 3.4 %edges.3 = (bf16[1,40,11200]{2,1,0:T(8,128)(2,1)S(1)}, bf16[1,40,11200]{2,1,0:T(8,128)(2,1)S(1)}, f32[8,128]{1,0:T(8,128)}) custom-call(bf16[2,3,40,11200]{3,2,1,0:T(8,128)(2,1)} %cur_ref.3, bf16[2,3,40,11200]{3,2,1,0:T(8,128)(2,1)} %cur_ref.3, bf16[2,40,11200]{2,1,0:T(8,128)(2,1)S(1)} %collective-permute-done.8.old0_ref.old2_ref.refs_0_.refs_2_, ...), custom_call_target="tpu_custom_call" | custom-call | flops 2688000 | bytes 5376000 | tf_op jit(solution)/shard_map/edges/pallas_call | solution.py:313
  94.9 5.1 %collective-permute-start.16 = (bf16[1,40,11200]{2,1,0:T(8,128)(2,1)S(1)}, bf16[1,40,11200]{2,1,0:T(8,128)(2,1)S(1)}, u32[]{:S(2)}, u32[]{:S(2)}) collective-permute-start(bf16[1,40,11200]{2,1,0:T(8,128)(2,1)S(1)} %get-tuple-element.27), channel_id=1, source_target_pairs={{0,1},{1,2},{2,3},{3,4},{4,5},{5,6},{6,7},{8,9},{9,10},{10,11},{11... | collective-permute-start | bytes 2688008 | tf_op jit(solution)/shard_map/ppermute | solution.py:354
  100.0 1.9 %collective-permute-start.17 = (bf16[1,40,11200]{2,1,0:T(8,128)(2,1)S(1)}, bf16[1,40,11200]{2,1,0:T(8,128)(2,1)S(1)}, u32[]{:S(2)}, u32[]{:S(2)}) collective-permute-start(bf16[1,40,11200]{2,1,0:T(8,128)(2,1)S(1)} %get-tuple-element.28), channel_id=1, source_target_pairs={{1,0},{2,1},{3,2},{4,3},{5,4},{6,5},{7,6},{9,8},{10,9},{11,10},{12... | collective-permute-start | bytes 2688008 | tf_op jit(solution)/shard_map/ppermute | solution.py:354
  101.9 0.9 convert_add_fusion.6
  102.9 3.7 %collective-permute-start.15 = (bf16[1,40,11200]{2,1,0:T(8,128)(2,1)S(1)}, bf16[1,40,11200]{2,1,0:T(8,128)(2,1)S(1)}, u32[]{:S(2)}, u32[]{:S(2)}) collective-permute-start(bf16[1,40,11200]{2,1,0:T(8,128)(2,1)S(1)} %copy-done.8), channel_id=1, source_target_pairs={{0,8},{8,16},{16,24},{24,32},{32,40},{40,48},{48,56},{56,64},{64,7... | collective-permute-start | bytes 2688008 | tf_op jit(solution)/shard_map/ppermute | solution.py:354
  106.6 3.0 %collective-permute-start.12 = (bf16[1,256,128]{2,1,0:T(8,128)(2,1)S(1)}, bf16[1,256,128]{2,1,0:T(8,128)(2,1)S(1)}, u32[]{:S(2)}, u32[]{:S(2)}) collective-permute-start(bf16[1,256,128]{2,1,0:T(8,128)(2,1)S(1)} %bitcast.61), channel_id=1, source_target_pairs={{0,4},{1,5},{2,6},{3,7},{4,0},{5,1},{6,2},{7,3},{8,12},{9,13},{10,... | collective-permute-start | bytes 196616 | tf_op jit(solution)/shard_map/ppermute | solution.py:348
  109.6 5.3 %collective-permute-done.12 = bf16[1,256,128]{2,1,0:T(8,128)(2,1)S(1)} collective-permute-done((bf16[1,256,128]{2,1,0:T(8,128)(2,1)S(1)}, bf16[1,256,128]{2,1,0:T(8,128)(2,1)S(1)}, u32[]{:S(2)}, u32[]{:S(2)}) %collective-permute-start.12) | collective-permute-done | bytes 65568 | tf_op jit(solution)/shard_map/ppermute | solution.py:348
  115.0 3.8 %collective-permute-done.13 = bf16[2,256,128]{2,1,0:T(8,128)(2,1)S(1)} collective-permute-done((bf16[2,256,128]{2,1,0:T(8,128)(2,1)S(1)}, bf16[2,256,128]{2,1,0:T(8,128)(2,1)S(1)}, u32[]{:S(2)}, u32[]{:S(2)}) %collective-permute-start.13) | collective-permute-done | bytes 131104 | tf_op jit(solution)/shard_map/ppermute | solution.py:348
  118.8 4.9 %collective-permute-start.14 = (bf16[4,256,128]{2,1,0:T(8,128)(2,1)S(1)}, bf16[4,256,128]{2,1,0:T(8,128)(2,1)S(1)}, u32[]{:S(2)}, u32[]{:S(2)}) collective-permute-start(bf16[4,256,128]{2,1,0:T(8,128)(2,1)S(1)} %bitcast.59), channel_id=1, source_target_pairs={{0,1},{1,0},{2,3},{3,2},{4,5},{5,4},{6,7},{7,6},{8,9},{9,8},{10,11... | collective-permute-start | bytes 786440 | tf_op jit(solution)/shard_map/ppermute | solution.py:348
  123.8 1.1 collective-permute-done.14
  125.0 2.2 %mixed_kernel.1 = bf16[240,2240]{1,0:T(8,128)(2,1)} custom-call(s32[1]{0:T(128)} %bitcast.row_ref, bf16[240,2240]{1,0:T(8,128)(2,1)S(1)} %bitcast.53, bf16[2048,128]{1,0:T(8,128)(2,1)S(1)} %bitcast.48, f32[1,2240]{1,0:T(1,128)S(1)} %broadcast_in_dim.11.gain_ref), custom_call_target="tpu_custom_call" | custom-call | flops 275251200 | bytes 3145728 | tf_op jit(solution)/shard_map/mixed_kernel/pallas_call | solution.py:336
  127.2 12.1 %conv_frame.3 = bf16[2,3,40,5600]{3,2,1,0:T(8,128)(2,1)} custom-call(bf16[2,3,40,11200]{3,2,1,0:T(8,128)(2,1)} %cur_ref.3, bf16[2,40,11200]{2,1,0:T(8,128)(2,1)S(1)} %collective-permute-done.8.old0_ref.old2_ref.refs_0_.refs_2_, bf16[1,40,11200]{2,1,0:T(8,128)(2,1)S(1)} %collective-permute-done.15.refs_1_, ...), custom_call_target="tpu_custom_call", output_to_operand_aliasing={{}: (9, {})} | custom-call | flops 53760000 | bytes 8064000 | tf_op jit(solution)/shard_map/conv_frame/pallas_call | solution.py:251
  (53 shorter events, 2.6 us)
Async XLA Ops:
  0.6 0.9 copy-start.1
  1.5 5.9 %copy-start.3 = (bf16[2,3,40,2240]{3,2,1,0:T(8,128)(2,1)S(1)}, bf16[2,3,40,2240]{3,2,1,0:T(8,128)(2,1)}, u32[]{:S(2)}) copy-start(bf16[2,3,40,2240]{3,2,1,0:T(8,128)(2,1)} %param.9) | copy-start | bytes 3225604
  1.5 5.9 %copy-start.4 = (bf16[2,3,40,2240]{3,2,1,0:T(8,128)(2,1)S(1)}, bf16[2,3,40,2240]{3,2,1,0:T(8,128)(2,1)}, u32[]{:S(2)}) copy-start(bf16[2,3,40,2240]{3,2,1,0:T(8,128)(2,1)} %param.10) | copy-start | bytes 3225604
  6.5 0.9 copy-start.7
  8.3 43.9 %copy-start = (f32[3,3,11200]{2,1,0:T(4,128)S(1)}, f32[3,3,11200]{2,1,0:T(4,128)}, u32[]{:S(2)}) copy-start(f32[3,3,11200]{2,1,0:T(4,128)} %refs_6_.3) | copy-start | bytes 1209604
  8.4 43.9 %copy-start.2 = (f32[2,11200]{1,0:T(2,128)S(1)}, f32[2,11200]{1,0:T(2,128)}, u32[]{:S(2)}) copy-start(f32[2,11200]{1,0:T(2,128)} %refs_5_.3) | copy-start | bytes 268804
  8.4 43.9 %copy-start.6 = (f32[11200]{0:T(1024)S(1)}, f32[11200]{0:T(1024)}, u32[]{:S(2)}) copy-start(f32[11200]{0:T(1024)} %param.15) | copy-start | bytes 134404
  8.4 4.5 %collective-permute-start = (bf16[4,256,128]{2,1,0:T(8,128)(2,1)S(1)}, bf16[4,256,128]{2,1,0:T(8,128)(2,1)S(1)}, u32[]{:S(2)}, u32[]{:S(2)}) collective-permute-start(bf16[4,256,128]{2,1,0:T(8,128)(2,1)S(1)} %slice_bitcast_fusion), channel_id=1, source_target_pairs={{0,1},{1,0},{2,3},{3,2},{4,5},{5,4},{6,7},{7,6},{8,9},{9,8},{10,11... | collective-permute-start | bytes 786440 | tf_op jit(solution)/shard_map/ppermute | solution.py:348
  13.0 4.8 %collective-permute-start.1 = (bf16[2,256,128]{2,1,0:T(8,128)(2,1)S(1)}, bf16[2,256,128]{2,1,0:T(8,128)(2,1)S(1)}, u32[]{:S(2)}, u32[]{:S(2)}) collective-permute-start(bf16[2,256,128]{2,1,0:T(8,128)(2,1)S(1)} %fusion.2), channel_id=1, source_target_pairs={{0,2},{1,3},{2,0},{3,1},{4,6},{5,7},{6,4},{7,5},{8,10},{9,11},{10,... | collective-permute-start | bytes 393224 | tf_op jit(solution)/shard_map/ppermute | solution.py:348
  13.1 52.3 %collective-permute-start.8 = (bf16[2,40,11200]{2,1,0:T(8,128)(2,1)}, bf16[2,40,11200]{2,1,0:T(8,128)(2,1)S(1)}, u32[]{:S(2)}, u32[]{:S(2)}) collective-permute-start(bf16[2,40,11200]{2,1,0:T(8,128)(2,1)} %get-tuple-element.22), channel_id=1, source_target_pairs={{0,8},{8,16},{16,24},{24,32},{32,40},{40,48},{48,56},{56,64},{64,7... | collective-permute-start | bytes 5376008 | tf_op jit(solution)/shard_map/ppermute | solution.py:354
  17.8 4.7 %collective-permute-start.2 = (bf16[256,128]{1,0:T(8,128)(2,1)S(1)}, bf16[256,128]{1,0:T(8,128)(2,1)S(1)}, u32[]{:S(2)}, u32[]{:S(2)}) collective-permute-start(bf16[256,128]{1,0:T(8,128)(2,1)S(1)} %fusion.8), channel_id=1, source_target_pairs={{0,4},{1,5},{2,6},{3,7},{4,0},{5,1},{6,2},{7,3},{8,12},{9,13},{10,... | collective-permute-start | bytes 196616 | tf_op jit(solution)/shard_map/ppermute | solution.py:348
  22.6 29.7 %collective-permute-start.6 = (bf16[1,40,11200]{2,1,0:T(8,128)(2,1)}, bf16[1,40,11200]{2,1,0:T(8,128)(2,1)S(1)}, u32[]{:S(2)}, u32[]{:S(2)}) collective-permute-start(bf16[1,40,11200]{2,1,0:T(8,128)(2,1)} %get-tuple-element.19), channel_id=1, source_target_pairs={{0,1},{1,2},{2,3},{3,4},{4,5},{5,6},{6,7},{8,9},{9,10},{10,11},{11... | collective-permute-start | bytes 2688008 | tf_op jit(solution)/shard_map/ppermute | solution.py:354
  26.7 25.5 %collective-permute-start.7 = (bf16[1,40,11200]{2,1,0:T(8,128)(2,1)}, bf16[1,40,11200]{2,1,0:T(8,128)(2,1)}, u32[]{:S(2)}, u32[]{:S(2)}) collective-permute-start(bf16[1,40,11200]{2,1,0:T(8,128)(2,1)} %get-tuple-element.20), channel_id=1, source_target_pairs={{1,0},{2,1},{3,2},{4,3},{5,4},{6,5},{7,6},{9,8},{10,9},{11,10},{12... | collective-permute-start | bytes 2688008 | tf_op jit(solution)/shard_map/ppermute | solution.py:354
  28.6 4.4 %collective-permute-start.3 = (bf16[256,128]{1,0:T(8,128)(2,1)S(1)}, bf16[256,128]{1,0:T(8,128)(2,1)S(1)}, u32[]{:S(2)}, u32[]{:S(2)}) collective-permute-start(bf16[256,128]{1,0:T(8,128)(2,1)S(1)} %get-tuple-element.30), channel_id=1, source_target_pairs={{0,32},{32,64},{64,96},{96,128},{128,160},{160,192},{192,224},{1,3... | collective-permute-start | bytes 196616 | tf_op jit(solution)/shard_map/ppermute | solution.py:354
  33.1 6.7 %copy-start.9 = (bf16[256,128]{1,0:T(8,128)(2,1)}, bf16[256,128]{1,0:T(8,128)(2,1)S(1)}, u32[]{:S(2)}) copy-start(bf16[256,128]{1,0:T(8,128)(2,1)S(1)} %collective-permute-done.3) | copy-start | bytes 196612
  33.1 6.7 %collective-permute-start.4 = (bf16[256,128]{1,0:T(8,128)(2,1)S(1)}, bf16[256,128]{1,0:T(8,128)(2,1)S(1)}, u32[]{:S(2)}, u32[]{:S(2)}) collective-permute-start(bf16[256,128]{1,0:T(8,128)(2,1)S(1)} %fusion.4), channel_id=1, source_target_pairs={{0,64},{32,96},{64,128},{96,160},{128,192},{160,224},{1,65},{33,97... | collective-permute-start | bytes 196616 | tf_op jit(solution)/shard_map/ppermute | solution.py:354
  39.8 0.7 copy-start.11
  40.4 24.0 %collective-permute-start.5 = (bf16[256,128]{1,0:T(8,128)(2,1)}, bf16[256,128]{1,0:T(8,128)(2,1)}, u32[]{:S(2)}, u32[]{:S(2)}) collective-permute-start(bf16[256,128]{1,0:T(8,128)(2,1)} %fusion.9), channel_id=1, source_target_pairs={{0,128},{32,160},{64,192},{96,224},{1,129},{33,161},{65,193},{97,2... | collective-permute-start | bytes 196616 | tf_op jit(solution)/shard_map/ppermute | solution.py:354
  52.3 12.1 %copy-start.10 = (bf16[256,128]{1,0:T(8,128)(2,1)S(1)}, bf16[256,128]{1,0:T(8,128)(2,1)}, u32[]{:S(2)}) copy-start(bf16[256,128]{1,0:T(8,128)(2,1)} %copy-done.9) | copy-start | bytes 196612
  52.3 12.1 %copy-start.12 = (bf16[256,128]{1,0:T(8,128)(2,1)S(1)}, bf16[256,128]{1,0:T(8,128)(2,1)}, u32[]{:S(2)}) copy-start(bf16[256,128]{1,0:T(8,128)(2,1)} %copy-done.11) | copy-start | bytes 196612
  65.4 36.5 %collective-permute-start.10 = (bf16[256,128]{1,0:T(8,128)(2,1)S(1)}, bf16[256,128]{1,0:T(8,128)(2,1)S(1)}, u32[]{:S(2)}, u32[]{:S(2)}) collective-permute-start(bf16[256,128]{1,0:T(8,128)(2,1)S(1)} %get-tuple-element.38), channel_id=1, source_target_pairs={{0,16},{8,24},{16,0},{24,8},{1,17},{9,25},{17,1},{25,9},{2,18},{10... | collective-permute-start | bytes 196616 | tf_op jit(solution)/shard_map/ppermute | solution.py:354
  67.7 34.2 %collective-permute-start.11 = (bf16[256,128]{1,0:T(8,128)(2,1)S(1)}, bf16[256,128]{1,0:T(8,128)(2,1)S(1)}, u32[]{:S(2)}, u32[]{:S(2)}) collective-permute-start(bf16[256,128]{1,0:T(8,128)(2,1)S(1)} %get-tuple-element.37), channel_id=1, source_target_pairs={{0,24},{8,0},{16,8},{24,16},{1,25},{9,1},{17,9},{25,17},{2,26},{10... | collective-permute-start | bytes 196616 | tf_op jit(solution)/shard_map/ppermute | solution.py:354
  91.0 11.9 %copy-start.8 = (bf16[1,40,11200]{2,1,0:T(8,128)(2,1)S(1)}, bf16[1,40,11200]{2,1,0:T(8,128)(2,1)}, u32[]{:S(2)}) copy-start(bf16[1,40,11200]{2,1,0:T(8,128)(2,1)} %copy-done.7) | copy-start | bytes 2688004
  91.0 32.8 %copy-start.13 = (f32[2240]{0:T(1024)S(1)}, f32[2240]{0:T(1024)}, u32[]{:S(2)}) copy-start(f32[2240]{0:T(1024)} %param.11) | copy-start | bytes 26884
  91.0 10.9 %collective-permute-start.9 = (bf16[256,128]{1,0:T(8,128)(2,1)S(1)}, bf16[256,128]{1,0:T(8,128)(2,1)S(1)}, u32[]{:S(2)}, u32[]{:S(2)}) collective-permute-start(bf16[256,128]{1,0:T(8,128)(2,1)S(1)} %get-tuple-element.36), channel_id=1, source_target_pairs={{0,8},{8,16},{16,24},{24,0},{1,9},{9,17},{17,25},{25,1},{2,10},{10... | collective-permute-start | bytes 196616 | tf_op jit(solution)/shard_map/ppermute | solution.py:354
  94.9 30.1 %copy-start.5 = (bf16[2,3,40,2240]{3,2,1,0:T(8,128)(2,1)S(1)}, bf16[2,3,40,2240]{3,2,1,0:T(8,128)(2,1)}, u32[]{:S(2)}) copy-start(bf16[2,3,40,2240]{3,2,1,0:T(8,128)(2,1)} %param.8) | copy-start | bytes 3225604
  94.9 32.3 %collective-permute-start.16 = (bf16[1,40,11200]{2,1,0:T(8,128)(2,1)S(1)}, bf16[1,40,11200]{2,1,0:T(8,128)(2,1)S(1)}, u32[]{:S(2)}, u32[]{:S(2)}) collective-permute-start(bf16[1,40,11200]{2,1,0:T(8,128)(2,1)S(1)} %get-tuple-element.27), channel_id=1, source_target_pairs={{0,1},{1,2},{2,3},{3,4},{4,5},{5,6},{6,7},{8,9},{9,10},{10,11},{11... | collective-permute-start | bytes 2688008 | tf_op jit(solution)/shard_map/ppermute | solution.py:354
  100.0 27.2 %collective-permute-start.17 = (bf16[1,40,11200]{2,1,0:T(8,128)(2,1)S(1)}, bf16[1,40,11200]{2,1,0:T(8,128)(2,1)S(1)}, u32[]{:S(2)}, u32[]{:S(2)}) collective-permute-start(bf16[1,40,11200]{2,1,0:T(8,128)(2,1)S(1)} %get-tuple-element.28), channel_id=1, source_target_pairs={{1,0},{2,1},{3,2},{4,3},{5,4},{6,5},{7,6},{9,8},{10,9},{11,10},{12... | collective-permute-start | bytes 2688008 | tf_op jit(solution)/shard_map/ppermute | solution.py:354
  102.9 24.4 %collective-permute-start.15 = (bf16[1,40,11200]{2,1,0:T(8,128)(2,1)S(1)}, bf16[1,40,11200]{2,1,0:T(8,128)(2,1)S(1)}, u32[]{:S(2)}, u32[]{:S(2)}) collective-permute-start(bf16[1,40,11200]{2,1,0:T(8,128)(2,1)S(1)} %copy-done.8), channel_id=1, source_target_pairs={{0,8},{8,16},{16,24},{24,32},{32,40},{40,48},{48,56},{56,64},{64,7... | collective-permute-start | bytes 2688008 | tf_op jit(solution)/shard_map/ppermute | solution.py:354
  106.6 8.3 %collective-permute-start.12 = (bf16[1,256,128]{2,1,0:T(8,128)(2,1)S(1)}, bf16[1,256,128]{2,1,0:T(8,128)(2,1)S(1)}, u32[]{:S(2)}, u32[]{:S(2)}) collective-permute-start(bf16[1,256,128]{2,1,0:T(8,128)(2,1)S(1)} %bitcast.61), channel_id=1, source_target_pairs={{0,4},{1,5},{2,6},{3,7},{4,0},{5,1},{6,2},{7,3},{8,12},{9,13},{10,... | collective-permute-start | bytes 196616 | tf_op jit(solution)/shard_map/ppermute | solution.py:348
  114.9 3.9 %collective-permute-start.13 = (bf16[2,256,128]{2,1,0:T(8,128)(2,1)S(1)}, bf16[2,256,128]{2,1,0:T(8,128)(2,1)S(1)}, u32[]{:S(2)}, u32[]{:S(2)}) collective-permute-start(bf16[2,256,128]{2,1,0:T(8,128)(2,1)S(1)} %get-tuple-element.35), channel_id=1, source_target_pairs={{0,2},{1,3},{2,0},{3,1},{4,6},{5,7},{6,4},{7,5},{8,10},{9,11},{10,... | collective-permute-start | bytes 393224 | tf_op jit(solution)/shard_map/ppermute | solution.py:348
  118.8 6.1 %collective-permute-start.14 = (bf16[4,256,128]{2,1,0:T(8,128)(2,1)S(1)}, bf16[4,256,128]{2,1,0:T(8,128)(2,1)S(1)}, u32[]{:S(2)}, u32[]{:S(2)}) collective-permute-start(bf16[4,256,128]{2,1,0:T(8,128)(2,1)S(1)} %bitcast.59), channel_id=1, source_target_pairs={{0,1},{1,0},{2,3},{3,2},{4,5},{5,4},{6,7},{7,6},{8,9},{9,8},{10,11... | collective-permute-start | bytes 786440 | tf_op jit(solution)/shard_map/ppermute | solution.py:348

commit v4 on v1

v4 whole, which is shorter than its diff:
```python
import functools

import jax
import jax.numpy as jnp
from jax import lax
from jax.experimental import pallas as pl
from jax.experimental.pallas import tpu as pltpu
from jax.sharding import Mesh, PartitionSpec as P

HD = 112
FF = 5600
LANES = 128
UNIT = 16
SHARES = 8
SHARE_ROWS = 256
INNER = 4
PARTS = 4
epsilon = 1e-06


def windows(width):
    out = []
    for head in range(width // HD):
        tile, offset = divmod(head * HD, LANES)
        span = LANES if offset + HD <= LANES else 2 * LANES
        out.append((tile, offset, min(span, width - tile * LANES)))
    return out


def unit_row(unit, row):
    share, inside = divmod(unit, UNIT)
    place = share ^ row
    place = ((place & 1) << 2) | (place & 2) | (place >> 2)
    return pl.multiple_of(place * SHARE_ROWS + inside * UNIT, UNIT)


def partial_kernel(row_ref, key_ref, value_ref, token_ref, out_ref):
    row = row_ref[0]
    width = key_ref.shape[1]
    pending = {}

    def flush(tile):
        rounded = pending.pop(tile).astype(jnp.bfloat16)
        for piece in range(HD // UNIT):
            out_ref[pl.ds(unit_row(tile * (HD // UNIT) + piece, row), UNIT), :] = rounded[
                piece * UNIT : (piece + 1) * UNIT
            ]

    for tile, offset, span in windows(width):
        lanes = slice(tile * LANES, tile * LANES + span)
        keys = jnp.maximum(key_ref[:, lanes], 0)
        product = lax.dot_general(
            keys, value_ref[:, lanes], (((0,), (0,)), ((), ())), preferred_element_type=jnp.float32
        )
        block = product[offset : offset + HD]
        lane = lax.broadcasted_iota(jnp.int32, block.shape, 1)
        block = jnp.where((lane >= offset) & (lane < offset + HD), block, 0.0)
        for old in [done for done in pending if done < tile]:
            flush(old)
        for step in range(pl.cdiv(span, LANES)):
            part = block[:, step * LANES : min(span, (step + 1) * LANES)]
            if part.shape[1] < LANES:
                part = jnp.concatenate(
                    [part, jnp.zeros((HD, LANES - part.shape[1]), jnp.float32)], axis=1
                )
            at = tile + step
            pending[at] = pending[at] + part if at in pending else part
    tiles = max(pending) + 1
    for old in sorted(pending):
        flush(old)
    for unit in range(tiles * (HD // UNIT), SHARES * UNIT):
        out_ref[pl.ds(unit_row(unit, row), UNIT), :] = jnp.zeros((UNIT, LANES), jnp.bfloat16)


def mixed_kernel(row_ref, query_ref, state_ref, gain_ref, out_ref):
    row = row_ref[0]
    tokens, width = query_ref.shape
    pending = {}

    def state_tile(tile):
        return jnp.concatenate(
            [
                state_ref[pl.ds(unit_row(tile * (HD // UNIT) + piece, row), UNIT), :]
                for piece in range(HD // UNIT)
            ],
            axis=0,
        )

    def flush(tile):
        lanes = slice(tile * LANES, min(width, (tile + 1) * LANES))
        count = lanes.stop - lanes.start
        out_ref[:, lanes] = (pending.pop(tile)[:, :count] * gain_ref[:, lanes]).astype(jnp.bfloat16)

    for tile, offset, span in windows(width):
        lanes = slice(tile * LANES, tile * LANES + span)
        steps = pl.cdiv(span, LANES)
        block = jnp.concatenate([state_tile(tile + step) for step in range(steps)], axis=1)
        lane = lax.broadcasted_iota(jnp.int32, block.shape, 1)
        block = jnp.where((lane >= offset) & (lane < offset + HD), block, jnp.zeros_like(block))
        pieces = [block]
        if offset:
            pieces.insert(0, jnp.zeros((offset, block.shape[1]), jnp.bfloat16))
        if span - offset - HD:
            pieces.append(jnp.zeros((span - offset - HD, block.shape[1]), jnp.bfloat16))
        right = jnp.concatenate(pieces, axis=0) if len(pieces) > 1 else block
        mixed = jnp.dot(
            jnp.maximum(query_ref[:, lanes], 0), right, preferred_element_type=jnp.float32
        )
        mean_square = jnp.sum(mixed * mixed, axis=1, keepdims=True) * (1.0 / HD)
        normed = mixed * lax.rsqrt(mean_square + epsilon)
        for old in [done for done in pending if done < tile]:
            flush(old)
        for step in range(steps):
            part = normed[:, step * LANES : (step + 1) * LANES]
            at = tile + step
            pending[at] = pending[at] + part if at in pending else part
    for old in sorted(pending):
        flush(old)


def conv_kernel(frame, own_ref, *refs):
    *_, out_ref, held_ref, done_ref, sems, held_sems = refs
    if frame:
        prev_refs = [held_ref.at[0, r] for r in range(own_ref.shape[1])]
    else:
        prev_refs, refs = [ref.at[0] for ref in refs[:3]], refs[3:]
    top_ref, bottom_ref, time_ref, space_ref, bias_ref = refs[:5]
    cur_ref = held_ref.at[-1 % held_ref.shape[0]]
    rows, columns, channels = cur_ref.shape
    groups = columns // 8
    skew = FF % LANES
    lead = FF // LANES
    bounds = [lead * part // PARTS for part in range(PARTS + 1)]
    fetches = []
    for part, (start, stop) in enumerate(zip(bounds, bounds[1:])):
        gate_start = lead + start + (part > 0)
        gate_stop = min(channels, (lead + stop + 1) * LANES) if part < PARTS - 1 else channels
        spans = (start * LANES, stop * LANES), (gate_start * LANES, gate_stop)
        fetches.append(
            [
                pltpu.make_async_copy(
                    own_ref.at[pl.ds(0, held_ref.shape[0]), :, :, pl.ds(a, b - a)],
                    held_ref.at[:, :, :, pl.ds(a, b - a)],
                    held_sems.at[part, which],
                )
                for which, (a, b) in enumerate(spans)
            ]
        )
        for fetch in fetches[-1]:
            fetch.start()

    def conv_tile(lanes):
        times = time_ref[:, lanes]
        lines = [times[0:1], times[1:2]]
        for a in range(3):
            taps = space_ref[a, :, lanes]
            lines += [taps[b : b + 1] for b in range(3)]
        lines.append(bias_ref[:, lanes])
        shape = (8, lines[0].shape[1])
        pick = [jnp.broadcast_to(line, shape) for line in lines]
        subrow = lax.broadcasted_iota(jnp.int32, shape, 0)
        first, last = subrow == 0, subrow == 7
        zero = jnp.zeros(shape, jnp.float32)

        def split(value):
            return [value[8 * g : 8 * g + 8] for g in range(groups)]

        spread = [split(top_ref[0, :, lanes].astype(jnp.float32))]
        for r in range(rows):
            now = split(cur_ref[r, :, lanes].astype(jnp.float32))
            old = split(prev_refs[r][:, lanes].astype(jnp.float32))
            blend = jnp.concatenate([pick[0] * c + pick[1] * p for c, p in zip(now, old)], axis=0)
            spread.append(split(blend.astype(jnp.bfloat16).astype(jnp.float32)))
        spread.append(split(bottom_ref[0, :, lanes].astype(jnp.float32)))
        out = []
        for r in range(rows):
            sums = []
            for b in range(3):
                sums.append(
                    [
                        pick[2 + b] * spread[r][g]
                        + pick[5 + b] * spread[r + 1][g]
                        + pick[8 + b] * spread[r + 2][g]
                        for g in range(groups)
                    ]
                )
            left = [zero] + [pltpu.roll(value, 1, 0) for value in sums[0]]
            right = [pltpu.roll(value, 7, 0) for value in sums[2]] + [zero]
            out += [
                (pick[11] + sums[1][g])
                + jnp.where(first, left[g], left[g + 1])
                + jnp.where(last, right[g + 1], right[g])
                for g in range(groups)
            ]
        return out

    lane = lax.broadcasted_iota(jnp.int32, (8, LANES), 1)

    def gates(lanes):
        turned = []
        for value in conv_tile(lanes):
            value = value * (1.0 / (1.0 + jnp.exp(-value)))
            if value.shape[1] < LANES:
                rest = jnp.zeros((8, LANES - value.shape[1]), jnp.float32)
                value = jnp.concatenate([value, rest], axis=1)
            turned.append(pltpu.roll(value, LANES - skew, 1))
        return turned

    def step(lanes, near, far, width):
        values = conv_tile(lanes)
        gated = [
            value * jnp.where(lane < LANES - skew, a, b) for value, a, b in zip(values, near, far)
        ]
        for r in range(rows):
            row = jnp.concatenate(gated[r * groups : (r + 1) * groups], axis=0)
            row = row.astype(jnp.bfloat16)
            done_ref[r, :, pl.ds(lanes.start, width)] = row[:, :width]

    def tile_at(index):
        return pl.ds(pl.multiple_of(index * LANES, LANES), LANES)

    def body(tile, near):
        far = gates(tile_at(tile + lead + 1))
        step(tile_at(tile), near, far, LANES)
        return far

    near = None
    for part, (start, stop) in enumerate(zip(bounds, bounds[1:])):
        for fetch in fetches[part]:
            fetch.wait()
        if near is None:
            near = gates(pl.ds(lead * LANES, LANES))
        near = lax.fori_loop(start, stop, body, near)
    last = (lead * 2 + 1) * LANES
    far = gates(pl.ds(last, channels - last))
    step(pl.ds(lead * LANES, LANES), near, far, skew)
    copies = [
        pltpu.make_async_copy(done_ref.at[r], out_ref.at[frame, r], sems.at[r]) for r in range(rows)
    ]
    for copy in copies:
        copy.start()
    for copy in copies:
        copy.wait()


def conv_frame(hidden, frame, prev, top, bottom, weights, into=None):
    frames, rows, columns, channels = hidden.shape
    args = [hidden, *prev, top, bottom, *weights]
    specs = [pl.BlockSpec(memory_space=pltpu.VMEM)] * len(args)
    args[0] = pltpu.with_memory_space_constraint(hidden, pltpu.HBM)
    specs[0] = pl.BlockSpec(memory_space=pl.ANY)
    aliases = {}
    if into is not None:
        aliases = {len(args): 0}
        args.append(into)
        specs.append(pl.BlockSpec(memory_space=pl.ANY))
    elements = rows * columns * channels
    return pl.pallas_call(
        functools.partial(conv_kernel, frame),
        out_shape=jax.ShapeDtypeStruct((frames, rows, columns, FF), jnp.bfloat16),
        in_specs=specs,
        out_specs=pl.BlockSpec(memory_space=pl.ANY),
        scratch_shapes=[
            pltpu.VMEM((frame + 1, rows, columns, channels), jnp.bfloat16),
            pltpu.VMEM((rows, columns, FF), jnp.bfloat16),
            pltpu.SemaphoreType.DMA((rows,)),
            pltpu.SemaphoreType.DMA((PARTS, 2)),
        ],
        input_output_aliases=aliases,
        compiler_params=pltpu.CompilerParams(vmem_limit_bytes=12 << 20),
        cost_estimate=pl.CostEstimate(
            flops=elements * 40, bytes_accessed=elements * 6, transcendentals=elements // 2
        ),
        name="conv_frame",
    )(*args)


def edge_kernel(own_ref, *refs, frame):
    *old_refs, time_ref, _, up_ref, down_ref, now_ref, old_ref, sems = refs
    rows, channels = own_ref.shape[1], own_ref.shape[3]
    ends = (0, rows - 1)
    copies = []
    for at, r in enumerate(ends):
        group = [pltpu.make_async_copy(own_ref.at[frame, r], now_ref.at[at], sems.at[0, at])]
        if frame:
            source = own_ref.at[frame - 1, r]
            group.append(pltpu.make_async_copy(source, old_ref.at[at], sems.at[1, at]))
        copies.append(group)
    for copy in copies[0] + copies[1]:
        copy.start()

    for at, out_ref in enumerate((up_ref, down_ref)):
        old_view = old_ref.at[at] if frame else old_refs[at].at[0]
        for copy in copies[at]:
            copy.wait()

        def blend(lanes):
            times = time_ref[:, lanes]
            now = now_ref[at, :, lanes].astype(jnp.float32)
            old = old_view[:, lanes].astype(jnp.float32)
            out_ref[0, :, lanes] = (times[0:1] * now + times[1:2] * old).astype(jnp.bfloat16)

        wide = 4 * LANES

        @pl.loop(0, channels // wide)
        def _(tile):
            blend(pl.ds(pl.multiple_of(tile * wide, LANES), wide))

        if channels % wide:
            blend(pl.ds(channels // wide * wide, channels % wide))


def edges(hidden, frame, old, times, token):
    channels, columns = hidden.shape[3], hidden.shape[2]
    held = pl.BlockSpec(memory_space=pltpu.VMEM)
    anywhere = pl.BlockSpec(memory_space=pl.ANY)
    args = [pltpu.with_memory_space_constraint(hidden, pltpu.HBM), *old, times, token]
    line = jax.ShapeDtypeStruct((1, columns, channels), jnp.bfloat16)
    pair = pltpu.VMEM((2, columns, channels), jnp.bfloat16)
    return pl.pallas_call(
        functools.partial(edge_kernel, frame=frame),
        out_shape=(line, line),
        in_specs=[anywhere] + [held] * len(old) + [held, anywhere],
        out_specs=(held, held),
        scratch_shapes=[pair, pair, pltpu.SemaphoreType.DMA((2, 2))],
        compiler_params=pltpu.CompilerParams(vmem_limit_bytes=8 << 20),
        cost_estimate=pl.CostEstimate(
            flops=6 * columns * channels, bytes_accessed=12 * columns * channels, transcendentals=0
        ),
        name="edges",
    )(*args)


def copy_kernel(source_ref, *refs, frame, rows):
    *_, token_ref, sems = refs
    outs = refs[-2 - len(rows) : -2]
    copies = [
        pltpu.make_async_copy(source_ref.at[frame, r], out_ref.at[0], sems.at[at])
        for at, (r, out_ref) in enumerate(zip(rows, outs))
    ]
    for copy in copies:
        copy.start()
    token_ref[...] = jnp.zeros_like(token_ref)
    for copy in copies:
        copy.wait()


def copied_rows(hidden, frame, rows, *tokens):
    _, _, columns, channels = hidden.shape
    args = (pltpu.with_memory_space_constraint(hidden, pltpu.HBM), *tokens)
    anywhere = pl.BlockSpec(memory_space=pl.ANY)
    return pl.pallas_call(
        functools.partial(copy_kernel, frame=frame, rows=rows),
        out_shape=[jax.ShapeDtypeStruct((1, columns, channels), jnp.bfloat16) for _ in rows]
        + [jax.ShapeDtypeStruct((8, LANES), jnp.float32)],
        in_specs=[anywhere] * len(args),
        out_specs=[pl.BlockSpec(memory_space=pltpu.VMEM)] * (len(rows) + 1),
        scratch_shapes=[pltpu.SemaphoreType.DMA((len(rows),))],
        cost_estimate=pl.CostEstimate(
            flops=0, bytes_accessed=4 * len(rows) * columns * channels, transcendentals=0
        ),
        name="copied_rows",
    )(*args)


def whole(body, out_shape, flops, *args):
    specs = [pl.BlockSpec(memory_space=pltpu.SMEM)]
    specs += [pl.BlockSpec(memory_space=pltpu.VMEM)] * (len(args) - 1)
    return pl.pallas_call(
        body,
        out_shape=out_shape,
        in_specs=specs,
        out_specs=pl.BlockSpec(memory_space=pltpu.VMEM),
        compiler_params=pltpu.CompilerParams(vmem_limit_bytes=10 << 20),
        cost_estimate=pl.CostEstimate(flops=flops, bytes_accessed=3 << 20, transcendentals=0),
        name=body.__name__,
    )(*args)


def exchange(value, axis, flip):
    return lax.ppermute(value, axis, [(i, i ^ flip) for i in range(lax.axis_size(axis))])


def ahead(value, axis, steps, wrap=False):
    count = lax.axis_size(axis)
    pairs = [(i, (i + steps) % count) for i in range(count) if wrap or 0 <= i + steps < count]
    return lax.ppermute(value, axis, pairs)


def per_device(
    query_tokens, key_tokens, value_tokens, norm_gain, hidden, time_weight, space_weight, conv_bias
):
    frames, rows, columns, width = query_tokens.shape
    tokens = frames * rows * columns
    channels = hidden.shape[3]
    frame_axes = ("z", "x")
    row = lax.axis_index("row").astype(jnp.int32).reshape(1)
    x = lax.axis_index("x")
    narrow = lambda value: value.astype(jnp.bfloat16)
    wide = lambda value: value.astype(jnp.float32)

    weights = time_weight, space_weight, conv_bias[None]
    prev_first, prev_last, token = copied_rows(hidden, frames - 1, (0, rows - 1))
    prev_first, prev_last = ahead(prev_first, frame_axes, 1), ahead(prev_last, frame_axes, 1)
    partial = whole(
        partial_kernel,
        jax.ShapeDtypeStruct((SHARES * SHARE_ROWS, LANES), jnp.bfloat16),
        2 * tokens * width * 256,
        row,
        key_tokens.reshape(tokens, width),
        value_tokens.reshape(tokens, width),
        token,
    )
    held = partial.reshape(2, 4, SHARE_ROWS, LANES)
    held = wide(held[0]) + wide(exchange(held[1], "row", 1))
    held = held[:2] + wide(exchange(narrow(held[2:]), "row", 2))
    held = held[0] + wide(exchange(narrow(held[1]), "row", 4))

    planes = lax.axis_size("z")
    fold = [(z * INNER + INNER - 1, z * INNER + INNER - 2) for z in range(planes)]
    column = held + wide(lax.ppermute(narrow(held), frame_axes, fold))
    before = jnp.zeros_like(held)
    for k in (1, 2, 4):
        sent = narrow(column)
        if k == 2:
            sent, prev_first = lax.optimization_barrier((sent, prev_first))
        if k == 4:
            up_edge, down_edge = edges(hidden, frames - 1, (), time_weight, sent)
            top, bottom = ahead(down_edge, "row", 1), ahead(up_edge, "row", -1)
            ffn_out = conv_frame(hidden, frames - 1, (), top, bottom, weights)
        pairs = [
            (z * INNER + at, (z + k) * INNER + at)
            for z in range(planes - k)
            for at in range(INNER - 1)
        ]
        arrived = lax.ppermute(sent, frame_axes, pairs)
        column = column + wide(arrived)
        before = before + wide(arrived)
    prefix = before + held
    closed, opened = lax.optimization_barrier((narrow(prefix), narrow(before), prev_last))[:2]
    for k in range(1, INNER):
        sent = jnp.where(x + k < INNER, closed, opened)
        prefix = prefix + wide(ahead(sent, "x", k, True))
    prefix = narrow(prefix)
    prev_middle, _ = copied_rows(hidden, frames - 1, (1,), prefix)
    prev_middle = ahead(prev_middle, frame_axes, 1)

    state = jnp.concatenate([prefix, exchange(prefix, "row", 4)], axis=0)
    up_edge, down_edge = edges(hidden, 0, (prev_first, prev_last), time_weight, state)
    top_first, bottom_first = ahead(down_edge, "row", 1), ahead(up_edge, "row", -1)
    state, ffn_out = lax.optimization_barrier((state, ffn_out))
    state = jnp.concatenate([state, exchange(state, "row", 2)], axis=0)
    state, prev_middle = lax.optimization_barrier((state, prev_middle))
    state = jnp.concatenate([state, exchange(state, "row", 1)], axis=0)
    attention = whole(
        mixed_kernel,
        jax.ShapeDtypeStruct((tokens, width), jnp.bfloat16),
        2 * tokens * width * 256,
        row,
        query_tokens.reshape(tokens, width),
        state,
        norm_gain[None],
    )
    ffn_out = conv_frame(
        hidden, 0, (prev_first, prev_middle, prev_last), top_first, bottom_first, weights, ffn_out
    )
    return (attention.reshape(query_tokens.shape), ffn_out)


def solution(mesh):
    frame, row = mesh.shape["frame"], mesh.shape["row"]
    split = Mesh(mesh.devices.reshape(frame // INNER, INNER, row), ("z", "x", "row"))
    tokens = P(("z", "x"), "row", None, None)
    return jax.shard_map(
        per_device,
        mesh=split,
        in_specs=(tokens, tokens, tokens, P(), tokens, P(), P(), P()),
        out_specs=(tokens, tokens),
        check_vma=False,
    )
```

time: 151 us -> 120 us (0.79)
  the two profiles are of different devices: /device:TPU:129 before, /device:TPU:1 now
where the time goes in v4:
time: 120 us
  starting transfers between devices  57.4 us (48%)
  Pallas kernels  34.7 us (29%)
  waiting for transfers between devices  24.7 us (21%)
    ppermute x10, starting transfers between devices, ahead(): return lax.ppermute(value, axis, pairs)  25.9 us
    ppermute x3, starting transfers between devices, per_device(): arrived = lax.ppermute(sent, frame_axes, pairs)  22 us
    pallas_call x2, Pallas kernels, conv_frame(): pl.pallas_call(functools.partial(conv_kernel, frame), out_shape=jax.Shape...  20.8 us
    ppermute x6, waiting for transfers between devices, exchange(): lax.ppermute(value, axis, [(i, i ^ flip) for i in range(lax.axis_size(axi...  16 us
    ppermute x6, starting transfers between devices, exchange(): lax.ppermute(value, axis, [(i, i ^ flip) for i in range(lax.axis_size(axi...  8.88 us
    ppermute x10, waiting for transfers between devices, ahead(): return lax.ppermute(value, axis, pairs)  6.12 us
    pallas_call x2, Pallas kernels, edges(): pl.pallas_call(functools.partial(edge_kernel, frame=frame), out_shape=(li...  5.82 us
    pallas_call x2, Pallas kernels, copied_rows(): pl.pallas_call(functools.partial(copy_kernel, frame=frame, rows=rows), ou...  4.96 us
  transfers between devices with their start and end apart: 20, of which 8 were waited for; matrix products, arithmetic and copies ran while one was open for 1% of the time, Pallas kernels for 24%

profile of v4, /device:TPU:1, one launch (start us, length us, event | category | flops | bytes accessed | tf_op | source)
XLA Modules:
  0.0 119.7 jit_solution(1805654740884916294)
XLA Ops:
  0.7 2.8 %copied_rows.2 = (bf16[1,40,11200]{2,1,0:T(8,128)(2,1)}, bf16[1,40,11200]{2,1,0:T(8,128)(2,1)}, f32[8,128]{1,0:T(8,128)}) custom-call(bf16[2,3,40,11200]{3,2,1,0:T(8,128)(2,1)} %own_ref.7), custom_call_target="tpu_custom_call" | custom-call | bytes 3584000 | tf_op jit(solution)/shard_map/copied_rows/pallas_call | solution.py:352
  4.2 0.9 partial_kernel.1
  5.1 3.3 %collective-permute-start = (bf16[4,256,128]{2,1,0:T(8,128)(2,1)S(1)}, bf16[4,256,128]{2,1,0:T(8,128)(2,1)S(1)}, u32[]{:S(2)}, u32[]{:S(2)}) collective-permute-start(bf16[4,256,128]{2,1,0:T(8,128)(2,1)S(1)} %bitcast.23), channel_id=1, source_target_pairs={{0,1},{1,0},{2,3},{3,2},{4,5},{5,4},{6,7},{7,6},{8,9},{9,8},{10,11... | collective-permute-start | bytes 786440 | tf_op jit(solution)/shard_map/ppermute | solution.py:381
  8.5 1.2 collective-permute-done
  9.8 2.7 %collective-permute-start.5 = (bf16[1,40,11200]{2,1,0:T(8,128)(2,1)S(1)}, bf16[1,40,11200]{2,1,0:T(8,128)(2,1)S(1)}, u32[]{:S(2)}, u32[]{:S(2)}) collective-permute-start(bf16[1,40,11200]{2,1,0:T(8,128)(2,1)S(1)} %copy-done.9), channel_id=1, source_target_pairs={{0,8},{8,16},{16,24},{24,32},{32,40},{40,48},{48,56},{56,64},{64,7... | collective-permute-start | bytes 2688008 | tf_op jit(solution)/shard_map/ppermute | solution.py:387
  12.5 2.0 %collective-permute-done.1 = bf16[2,256,128]{2,1,0:T(8,128)(2,1)S(1)} collective-permute-done((bf16[2,256,128]{2,1,0:T(8,128)(2,1)S(1)}, bf16[2,256,128]{2,1,0:T(8,128)(2,1)S(1)}, u32[]{:S(2)}, u32[]{:S(2)}) %collective-permute-start.1) | collective-permute-done | bytes 131104 | tf_op jit(solution)/shard_map/ppermute | solution.py:381
  14.6 1.3 %collective-permute-start.2 = (bf16[256,128]{1,0:T(8,128)(2,1)S(1)}, bf16[256,128]{1,0:T(8,128)(2,1)S(1)}, u32[]{:S(2)}, u32[]{:S(2)}) collective-permute-start(bf16[256,128]{1,0:T(8,128)(2,1)S(1)} %fusion.6), channel_id=1, source_target_pairs={{0,4},{1,5},{2,6},{3,7},{4,0},{5,1},{6,2},{7,3},{8,12},{9,13},{10,... | collective-permute-start | bytes 196616 | tf_op jit(solution)/shard_map/ppermute | solution.py:381
  15.8 3.4 %collective-permute-done.2 = bf16[256,128]{1,0:T(8,128)(2,1)S(1)} collective-permute-done((bf16[256,128]{1,0:T(8,128)(2,1)S(1)}, bf16[256,128]{1,0:T(8,128)(2,1)S(1)}, u32[]{:S(2)}, u32[]{:S(2)}) %collective-permute-start.2) | collective-permute-done | bytes 65568 | tf_op jit(solution)/shard_map/ppermute | solution.py:381
  20.0 2.1 %collective-permute-start.4 = (bf16[256,128]{1,0:T(8,128)(2,1)S(1)}, bf16[256,128]{1,0:T(8,128)(2,1)S(1)}, u32[]{:S(2)}, u32[]{:S(2)}) collective-permute-start(bf16[256,128]{1,0:T(8,128)(2,1)S(1)} %fusion.3), channel_id=1, source_target_pairs={{0,32},{8,40},{16,48},{32,64},{40,72},{48,80},{64,96},{72,104},{80... | collective-permute-start | bytes 196616 | tf_op jit(solution)/shard_map/ppermute | solution.py:436
  22.1 2.9 %collective-permute-start.8 = (bf16[1,40,11200]{2,1,0:T(8,128)(2,1)}, bf16[1,40,11200]{2,1,0:T(8,128)(2,1)S(1)}, u32[]{:S(2)}, u32[]{:S(2)}) collective-permute-start(bf16[1,40,11200]{2,1,0:T(8,128)(2,1)} %get-tuple-element.21), channel_id=1, source_target_pairs={{0,8},{8,16},{16,24},{24,32},{32,40},{40,48},{48,56},{56,64},{64,7... | collective-permute-start | bytes 2688008 | tf_op jit(solution)/shard_map/ppermute | solution.py:387
  25.1 6.1 %collective-permute-done.5.refs_0_ = bf16[1,40,11200]{2,1,0:T(8,128)(2,1)S(1)} collective-permute-done((bf16[1,40,11200]{2,1,0:T(8,128)(2,1)S(1)}, bf16[1,40,11200]{2,1,0:T(8,128)(2,1)S(1)}, u32[]{:S(2)}, u32[]{:S(2)}) %collective-permute-start.5) | collective-permute-done | bytes 896032 | tf_op jit(solution)/shard_map/ppermute | solution.py:387
  31.2 8.0 %collective-permute-start.6 = (bf16[256,128]{1,0:T(8,128)(2,1)S(1)}, bf16[256,128]{1,0:T(8,128)(2,1)S(1)}, u32[]{:S(2)}, u32[]{:S(2)}) collective-permute-start(bf16[256,128]{1,0:T(8,128)(2,1)S(1)} %fusion.7), channel_id=1, source_target_pairs={{0,64},{8,72},{16,80},{32,96},{40,104},{48,112},{64,128},{72,136},... | collective-permute-start | bytes 196616 | tf_op jit(solution)/shard_map/ppermute | solution.py:436
  39.1 1.3 %collective-permute-done.6 = bf16[256,128]{1,0:T(8,128)(2,1)S(1)} collective-permute-done((bf16[256,128]{1,0:T(8,128)(2,1)S(1)}, bf16[256,128]{1,0:T(8,128)(2,1)S(1)}, u32[]{:S(2)}, u32[]{:S(2)}) %collective-permute-start.6) | collective-permute-done | bytes 65568 | tf_op jit(solution)/shard_map/ppermute | solution.py:436
  40.5 11.9 %collective-permute-start.7 = (bf16[256,128]{1,0:T(8,128)(2,1)S(1)}, bf16[256,128]{1,0:T(8,128)(2,1)S(1)}, u32[]{:S(2)}, u32[]{:S(2)}) collective-permute-start(bf16[256,128]{1,0:T(8,128)(2,1)S(1)} %fusion.1.refs_1_), channel_id=1, source_target_pairs={{0,128},{8,136},{16,144},{32,160},{40,168},{48,176},{64,192},{72,2... | collective-permute-start | bytes 196616 | tf_op jit(solution)/shard_map/ppermute | solution.py:436
  52.4 1.3 %collective-permute-done.7 = bf16[256,128]{1,0:T(8,128)(2,1)S(1)} collective-permute-done((bf16[256,128]{1,0:T(8,128)(2,1)S(1)}, bf16[256,128]{1,0:T(8,128)(2,1)S(1)}, u32[]{:S(2)}, u32[]{:S(2)}) %collective-permute-start.7) | collective-permute-done | bytes 65568 | tf_op jit(solution)/shard_map/ppermute | solution.py:436
  53.9 1.2 %collective-permute-start.11 = (bf16[256,128]{1,0:T(8,128)(2,1)S(1)}, bf16[256,128]{1,0:T(8,128)(2,1)S(1)}, u32[]{:S(2)}, u32[]{:S(2)}) collective-permute-start(bf16[256,128]{1,0:T(8,128)(2,1)S(1)} %get-tuple-element.41), channel_id=1, source_target_pairs={{0,24},{8,0},{16,8},{24,16},{1,25},{9,1},{17,9},{25,17},{2,26},{10... | collective-permute-start | bytes 196616 | tf_op jit(solution)/shard_map/ppermute | solution.py:387
  55.5 3.7 %edges.2 = (bf16[1,40,11200]{2,1,0:T(8,128)(2,1)}, bf16[1,40,11200]{2,1,0:T(8,128)(2,1)}) custom-call(bf16[2,3,40,11200]{3,2,1,0:T(8,128)(2,1)} %own_ref.7, f32[2,11200]{1,0:T(2,128)S(1)} %copy-done.1, bf16[256,128]{1,0:T(8,128)(2,1)S(1)} %fusion.1.refs_1_), custom_call_target="tpu_custom_call" | custom-call | flops 2688000 | bytes 5376000 | tf_op jit(solution)/shard_map/edges/pallas_call | solution.py:320
  59.1 6.2 %collective-permute-start.13 = (bf16[1,40,11200]{2,1,0:T(8,128)(2,1)}, bf16[1,40,11200]{2,1,0:T(8,128)(2,1)S(1)}, u32[]{:S(2)}, u32[]{:S(2)}) collective-permute-start(bf16[1,40,11200]{2,1,0:T(8,128)(2,1)} %get-tuple-element.24), channel_id=1, source_target_pairs={{0,1},{1,2},{2,3},{3,4},{4,5},{5,6},{6,7},{8,9},{9,10},{10,11},{11... | collective-permute-start | bytes 2688008 | tf_op jit(solution)/shard_map/ppermute | solution.py:387
  65.3 1.9 %collective-permute-start.14 = (bf16[1,40,11200]{2,1,0:T(8,128)(2,1)}, bf16[1,40,11200]{2,1,0:T(8,128)(2,1)}, u32[]{:S(2)}, u32[]{:S(2)}) collective-permute-start(bf16[1,40,11200]{2,1,0:T(8,128)(2,1)} %get-tuple-element.25), channel_id=1, source_target_pairs={{1,0},{2,1},{3,2},{4,3},{5,4},{6,5},{7,6},{9,8},{10,9},{11,10},{12... | collective-permute-start | bytes 2688008 | tf_op jit(solution)/shard_map/ppermute | solution.py:387
  67.3 0.7 add_convert_fusion.refs_0_
  68.0 2.1 %copied_rows.3 = (bf16[1,40,11200]{2,1,0:T(8,128)(2,1)}, f32[8,128]{1,0:T(8,128)}) custom-call(bf16[2,3,40,11200]{3,2,1,0:T(8,128)(2,1)} %own_ref.7, bf16[256,128]{1,0:T(8,128)(2,1)} %add_convert_fusion.refs_0_), custom_call_target="tpu_custom_call" | custom-call | bytes 1792000 | tf_op jit(solution)/shard_map/copied_rows/pallas_call | solution.py:352
  70.1 3.1 %collective-permute-start.16 = (bf16[1,40,11200]{2,1,0:T(8,128)(2,1)}, bf16[1,40,11200]{2,1,0:T(8,128)(2,1)S(1)}, u32[]{:S(2)}, u32[]{:S(2)}) collective-permute-start(bf16[1,40,11200]{2,1,0:T(8,128)(2,1)} %get-tuple-element.27), channel_id=1, source_target_pairs={{0,8},{8,16},{16,24},{24,32},{32,40},{40,48},{48,56},{56,64},{64,7... | collective-permute-start | bytes 2688008 | tf_op jit(solution)/shard_map/ppermute | solution.py:387
  73.2 3.0 %collective-permute-start.12 = (bf16[256,128]{1,0:T(8,128)(2,1)S(1)}, bf16[256,128]{1,0:T(8,128)(2,1)S(1)}, u32[]{:S(2)}, u32[]{:S(2)}) collective-permute-start(bf16[256,128]{1,0:T(8,128)(2,1)S(1)} %copy-done.7), channel_id=1, source_target_pairs={{0,4},{1,5},{2,6},{3,7},{4,0},{5,1},{6,2},{7,3},{8,12},{9,13},{10,... | collective-permute-start | bytes 196616 | tf_op jit(solution)/shard_map/ppermute | solution.py:381
  76.2 4.5 %collective-permute-done.12 = bf16[256,128]{1,0:T(8,128)(2,1)S(1)} collective-permute-done((bf16[256,128]{1,0:T(8,128)(2,1)S(1)}, bf16[256,128]{1,0:T(8,128)(2,1)S(1)}, u32[]{:S(2)}, u32[]{:S(2)}) %collective-permute-start.12) | collective-permute-done | bytes 65568 | tf_op jit(solution)/shard_map/ppermute | solution.py:381
  80.7 2.2 %edges.3 = (bf16[1,40,11200]{2,1,0:T(8,128)(2,1)S(1)}, bf16[1,40,11200]{2,1,0:T(8,128)(2,1)S(1)}) custom-call(bf16[2,3,40,11200]{3,2,1,0:T(8,128)(2,1)} %own_ref.7, bf16[1,40,11200]{2,1,0:T(8,128)(2,1)S(1)} %collective-permute-done.5.refs_0_, bf16[1,40,11200]{2,1,0:T(8,128)(2,1)S(1)} %collective-permute-done.8.refs_1_.refs_2_, f32[2,11200]{1,0:T(2,128)S(1)} %copy-done.1, ...), custom_call_target="tpu_custom_call" | custom-call | flops 2688000 | bytes 5376000 | tf_op jit(solution)/shard_map/edges/pallas_call | solution.py:320
  82.9 5.6 %collective-permute-start.18 = (bf16[1,40,11200]{2,1,0:T(8,128)(2,1)S(1)}, bf16[1,40,11200]{2,1,0:T(8,128)(2,1)S(1)}, u32[]{:S(2)}, u32[]{:S(2)}) collective-permute-start(bf16[1,40,11200]{2,1,0:T(8,128)(2,1)S(1)} %get-tuple-element.31), channel_id=1, source_target_pairs={{0,1},{1,2},{2,3},{3,4},{4,5},{5,6},{6,7},{8,9},{9,10},{10,11},{11... | collective-permute-start | bytes 2688008 | tf_op jit(solution)/shard_map/ppermute | solution.py:387
  88.5 1.9 %collective-permute-start.19 = (bf16[1,40,11200]{2,1,0:T(8,128)(2,1)S(1)}, bf16[1,40,11200]{2,1,0:T(8,128)(2,1)S(1)}, u32[]{:S(2)}, u32[]{:S(2)}) collective-permute-start(bf16[1,40,11200]{2,1,0:T(8,128)(2,1)S(1)} %get-tuple-element.32), channel_id=1, source_target_pairs={{1,0},{2,1},{3,2},{4,3},{5,4},{6,5},{7,6},{9,8},{10,9},{11,10},{12... | collective-permute-start | bytes 2688008 | tf_op jit(solution)/shard_map/ppermute | solution.py:387
  90.5 11.0 %conv_frame.2.refs_8_ = bf16[2,3,40,5600]{3,2,1,0:T(8,128)(2,1)} custom-call(bf16[2,3,40,11200]{3,2,1,0:T(8,128)(2,1)} %own_ref.7, bf16[1,40,11200]{2,1,0:T(8,128)(2,1)S(1)} %collective-permute-done.13.refs_0_, bf16[1,40,11200]{2,1,0:T(8,128)(2,1)} %collective-permute-done.14.refs_1_, f32[2,11200]{1,0:T(2,128)S(1)} %copy-done.1, f32[3,3,11200]{2,1,0:T(4,128)S(1)} %copy-done, ...), custom_call_target="tpu_custom_call" | custom-call | flops 53760000 | bytes 8064000 | tf_op jit(solution)/shard_map/conv_frame/pallas_call | solution.py:258
  101.7 4.9 %collective-permute-done.15 = bf16[512,128]{1,0:T(8,128)(2,1)S(1)} collective-permute-done((bf16[512,128]{1,0:T(8,128)(2,1)S(1)}, bf16[512,128]{1,0:T(8,128)(2,1)S(1)}, u32[]{:S(2)}, u32[]{:S(2)}) %collective-permute-start.15) | collective-permute-done | bytes 131104 | tf_op jit(solution)/shard_map/ppermute | solution.py:381
  106.6 1.0 collective-permute-start.17
  107.7 9.8 %conv_frame.3 = bf16[2,3,40,5600]{3,2,1,0:T(8,128)(2,1)} custom-call(bf16[2,3,40,11200]{3,2,1,0:T(8,128)(2,1)} %own_ref.7, bf16[1,40,11200]{2,1,0:T(8,128)(2,1)S(1)} %collective-permute-done.5.refs_0_, bf16[1,40,11200]{2,1,0:T(8,128)(2,1)S(1)} %collective-permute-done.16.refs_1_, ...), custom_call_target="tpu_custom_call", output_to_operand_aliasing={{}: (9, {})} | custom-call | flops 53760000 | bytes 8064000 | tf_op jit(solution)/shard_map/conv_frame/pallas_call | solution.py:258
  117.5 2.2 %mixed_kernel.1 = bf16[240,2240]{1,0:T(8,128)(2,1)} custom-call(s32[1]{0:T(128)} %bitcast.row_ref, bf16[240,2240]{1,0:T(8,128)(2,1)S(1)} %bitcast.18, bf16[2048,128]{1,0:T(8,128)(2,1)S(1)} %pad_maximum_fusion.state_ref, f32[1,2240]{1,0:T(1,128)S(1)} %broadcast_in_dim.7.gain_ref), custom_call_target="tpu_custom_call" | custom-call | flops 275251200 | bytes 3145728 | tf_op jit(solution)/shard_map/mixed_kernel/pallas_call | solution.py:369
  (52 shorter events, 2.5 us)
Async XLA Ops:
  0.6 2.9 %copy-start.2 = (bf16[2,3,40,2240]{3,2,1,0:T(8,128)(2,1)S(1)}, bf16[2,3,40,2240]{3,2,1,0:T(8,128)(2,1)}, u32[]{:S(2)}) copy-start(bf16[2,3,40,2240]{3,2,1,0:T(8,128)(2,1)} %param.9) | copy-start | bytes 3225604
  0.6 2.9 %copy-start.3 = (bf16[2,3,40,2240]{3,2,1,0:T(8,128)(2,1)S(1)}, bf16[2,3,40,2240]{3,2,1,0:T(8,128)(2,1)}, u32[]{:S(2)}) copy-start(bf16[2,3,40,2240]{3,2,1,0:T(8,128)(2,1)} %param.10) | copy-start | bytes 3225604
  3.5 0.7 copy-start.6
  5.1 4.7 %copy-start.9 = (bf16[1,40,11200]{2,1,0:T(8,128)(2,1)S(1)}, bf16[1,40,11200]{2,1,0:T(8,128)(2,1)}, u32[]{:S(2)}) copy-start(bf16[1,40,11200]{2,1,0:T(8,128)(2,1)} %get-tuple-element.19) | copy-start | bytes 2688004
  5.1 4.5 %collective-permute-start = (bf16[4,256,128]{2,1,0:T(8,128)(2,1)S(1)}, bf16[4,256,128]{2,1,0:T(8,128)(2,1)S(1)}, u32[]{:S(2)}, u32[]{:S(2)}) collective-permute-start(bf16[4,256,128]{2,1,0:T(8,128)(2,1)S(1)} %bitcast.23), channel_id=1, source_target_pairs={{0,1},{1,0},{2,3},{3,2},{4,5},{5,4},{6,7},{7,6},{8,9},{9,8},{10,11... | collective-permute-start | bytes 786440 | tf_op jit(solution)/shard_map/ppermute | solution.py:381
  9.7 4.8 %collective-permute-start.1 = (bf16[2,256,128]{2,1,0:T(8,128)(2,1)S(1)}, bf16[2,256,128]{2,1,0:T(8,128)(2,1)S(1)}, u32[]{:S(2)}, u32[]{:S(2)}) collective-permute-start(bf16[2,256,128]{2,1,0:T(8,128)(2,1)S(1)} %slice.42), channel_id=1, source_target_pairs={{0,2},{1,3},{2,0},{3,1},{4,6},{5,7},{6,4},{7,5},{8,10},{9,11},{10,... | collective-permute-start | bytes 393224 | tf_op jit(solution)/shard_map/ppermute | solution.py:381
  9.8 21.3 %collective-permute-start.5 = (bf16[1,40,11200]{2,1,0:T(8,128)(2,1)S(1)}, bf16[1,40,11200]{2,1,0:T(8,128)(2,1)S(1)}, u32[]{:S(2)}, u32[]{:S(2)}) collective-permute-start(bf16[1,40,11200]{2,1,0:T(8,128)(2,1)S(1)} %copy-done.9), channel_id=1, source_target_pairs={{0,8},{8,16},{16,24},{24,32},{32,40},{40,48},{48,56},{56,64},{64,7... | collective-permute-start | bytes 2688008 | tf_op jit(solution)/shard_map/ppermute | solution.py:387
  14.6 40.9 %copy-start.1 = (f32[2,11200]{1,0:T(2,128)S(1)}, f32[2,11200]{1,0:T(2,128)}, u32[]{:S(2)}) copy-start(f32[2,11200]{1,0:T(2,128)} %refs_5_.1) | copy-start | bytes 268804
  14.6 4.7 %collective-permute-start.2 = (bf16[256,128]{1,0:T(8,128)(2,1)S(1)}, bf16[256,128]{1,0:T(8,128)(2,1)S(1)}, u32[]{:S(2)}, u32[]{:S(2)}) collective-permute-start(bf16[256,128]{1,0:T(8,128)(2,1)S(1)} %fusion.6), channel_id=1, source_target_pairs={{0,4},{1,5},{2,6},{3,7},{4,0},{5,1},{6,2},{7,3},{8,12},{9,13},{10,... | collective-permute-start | bytes 196616 | tf_op jit(solution)/shard_map/ppermute | solution.py:381
  19.3 0.7 collective-permute-start.3
  20.0 5.0 %collective-permute-start.4 = (bf16[256,128]{1,0:T(8,128)(2,1)S(1)}, bf16[256,128]{1,0:T(8,128)(2,1)S(1)}, u32[]{:S(2)}, u32[]{:S(2)}) collective-permute-start(bf16[256,128]{1,0:T(8,128)(2,1)S(1)} %fusion.3), channel_id=1, source_target_pairs={{0,32},{8,40},{16,48},{32,64},{40,72},{48,80},{64,96},{72,104},{80... | collective-permute-start | bytes 196616 | tf_op jit(solution)/shard_map/ppermute | solution.py:436
  22.1 31.7 %collective-permute-start.8 = (bf16[1,40,11200]{2,1,0:T(8,128)(2,1)}, bf16[1,40,11200]{2,1,0:T(8,128)(2,1)S(1)}, u32[]{:S(2)}, u32[]{:S(2)}) collective-permute-start(bf16[1,40,11200]{2,1,0:T(8,128)(2,1)} %get-tuple-element.21), channel_id=1, source_target_pairs={{0,8},{8,16},{16,24},{24,32},{32,40},{40,48},{48,56},{56,64},{64,7... | collective-permute-start | bytes 2688008 | tf_op jit(solution)/shard_map/ppermute | solution.py:387
  31.2 9.3 %collective-permute-start.6 = (bf16[256,128]{1,0:T(8,128)(2,1)S(1)}, bf16[256,128]{1,0:T(8,128)(2,1)S(1)}, u32[]{:S(2)}, u32[]{:S(2)}) collective-permute-start(bf16[256,128]{1,0:T(8,128)(2,1)S(1)} %fusion.7), channel_id=1, source_target_pairs={{0,64},{8,72},{16,80},{32,96},{40,104},{48,112},{64,128},{72,136},... | collective-permute-start | bytes 196616 | tf_op jit(solution)/shard_map/ppermute | solution.py:436
  40.5 13.2 %collective-permute-start.7 = (bf16[256,128]{1,0:T(8,128)(2,1)S(1)}, bf16[256,128]{1,0:T(8,128)(2,1)S(1)}, u32[]{:S(2)}, u32[]{:S(2)}) collective-permute-start(bf16[256,128]{1,0:T(8,128)(2,1)S(1)} %fusion.1.refs_1_), channel_id=1, source_target_pairs={{0,128},{8,136},{16,144},{32,160},{40,168},{48,176},{64,192},{72,2... | collective-permute-start | bytes 196616 | tf_op jit(solution)/shard_map/ppermute | solution.py:436
  53.8 13.4 %collective-permute-start.10 = (bf16[256,128]{1,0:T(8,128)(2,1)S(1)}, bf16[256,128]{1,0:T(8,128)(2,1)S(1)}, u32[]{:S(2)}, u32[]{:S(2)}) collective-permute-start(bf16[256,128]{1,0:T(8,128)(2,1)S(1)} %get-tuple-element.42), channel_id=1, source_target_pairs={{0,16},{8,24},{16,0},{24,8},{1,17},{9,25},{17,1},{25,9},{2,18},{10... | collective-permute-start | bytes 196616 | tf_op jit(solution)/shard_map/ppermute | solution.py:387
  53.9 13.4 %collective-permute-start.11 = (bf16[256,128]{1,0:T(8,128)(2,1)S(1)}, bf16[256,128]{1,0:T(8,128)(2,1)S(1)}, u32[]{:S(2)}, u32[]{:S(2)}) collective-permute-start(bf16[256,128]{1,0:T(8,128)(2,1)S(1)} %get-tuple-element.41), channel_id=1, source_target_pairs={{0,24},{8,0},{16,8},{24,16},{1,25},{9,1},{17,9},{25,17},{2,26},{10... | collective-permute-start | bytes 196616 | tf_op jit(solution)/shard_map/ppermute | solution.py:387
  55.2 12.1 %collective-permute-start.9 = (bf16[256,128]{1,0:T(8,128)(2,1)S(1)}, bf16[256,128]{1,0:T(8,128)(2,1)S(1)}, u32[]{:S(2)}, u32[]{:S(2)}) collective-permute-start(bf16[256,128]{1,0:T(8,128)(2,1)S(1)} %get-tuple-element.40), channel_id=1, source_target_pairs={{0,8},{8,16},{16,24},{24,0},{1,9},{9,17},{17,25},{25,1},{2,10},{10... | collective-permute-start | bytes 196616 | tf_op jit(solution)/shard_map/ppermute | solution.py:387
  59.1 31.3 %collective-permute-start.13 = (bf16[1,40,11200]{2,1,0:T(8,128)(2,1)}, bf16[1,40,11200]{2,1,0:T(8,128)(2,1)S(1)}, u32[]{:S(2)}, u32[]{:S(2)}) collective-permute-start(bf16[1,40,11200]{2,1,0:T(8,128)(2,1)} %get-tuple-element.24), channel_id=1, source_target_pairs={{0,1},{1,2},{2,3},{3,4},{4,5},{5,6},{6,7},{8,9},{9,10},{10,11},{11... | collective-permute-start | bytes 2688008 | tf_op jit(solution)/shard_map/ppermute | solution.py:387
  65.3 25.1 %collective-permute-start.14 = (bf16[1,40,11200]{2,1,0:T(8,128)(2,1)}, bf16[1,40,11200]{2,1,0:T(8,128)(2,1)}, u32[]{:S(2)}, u32[]{:S(2)}) collective-permute-start(bf16[1,40,11200]{2,1,0:T(8,128)(2,1)} %get-tuple-element.25), channel_id=1, source_target_pairs={{1,0},{2,1},{3,2},{4,3},{5,4},{6,5},{7,6},{9,8},{10,9},{11,10},{12... | collective-permute-start | bytes 2688008 | tf_op jit(solution)/shard_map/ppermute | solution.py:387
  68.0 5.2 %copy-start.7 = (bf16[256,128]{1,0:T(8,128)(2,1)S(1)}, bf16[256,128]{1,0:T(8,128)(2,1)}, u32[]{:S(2)}) copy-start(bf16[256,128]{1,0:T(8,128)(2,1)} %add_convert_fusion.refs_0_) | copy-start | bytes 196612
  70.1 36.5 %collective-permute-start.16 = (bf16[1,40,11200]{2,1,0:T(8,128)(2,1)}, bf16[1,40,11200]{2,1,0:T(8,128)(2,1)S(1)}, u32[]{:S(2)}, u32[]{:S(2)}) collective-permute-start(bf16[1,40,11200]{2,1,0:T(8,128)(2,1)} %get-tuple-element.27), channel_id=1, source_target_pairs={{0,8},{8,16},{16,24},{24,32},{32,40},{40,48},{48,56},{56,64},{64,7... | collective-permute-start | bytes 2688008 | tf_op jit(solution)/shard_map/ppermute | solution.py:387
  73.2 7.5 %collective-permute-start.12 = (bf16[256,128]{1,0:T(8,128)(2,1)S(1)}, bf16[256,128]{1,0:T(8,128)(2,1)S(1)}, u32[]{:S(2)}, u32[]{:S(2)}) collective-permute-start(bf16[256,128]{1,0:T(8,128)(2,1)S(1)} %copy-done.7), channel_id=1, source_target_pairs={{0,4},{1,5},{2,6},{3,7},{4,0},{5,1},{6,2},{7,3},{8,12},{9,13},{10,... | collective-permute-start | bytes 196616 | tf_op jit(solution)/shard_map/ppermute | solution.py:381
  80.7 9.7 %copy-start = (f32[3,3,11200]{2,1,0:T(4,128)S(1)}, f32[3,3,11200]{2,1,0:T(4,128)}, u32[]{:S(2)}) copy-start(f32[3,3,11200]{2,1,0:T(4,128)} %refs_6_.1) | copy-start | bytes 1209604
  80.7 9.7 %copy-start.5 = (f32[11200]{0:T(1024)S(1)}, f32[11200]{0:T(1024)}, u32[]{:S(2)}) copy-start(f32[11200]{0:T(1024)} %param.15) | copy-start | bytes 134404
  82.9 24.7 %collective-permute-start.18 = (bf16[1,40,11200]{2,1,0:T(8,128)(2,1)S(1)}, bf16[1,40,11200]{2,1,0:T(8,128)(2,1)S(1)}, u32[]{:S(2)}, u32[]{:S(2)}) collective-permute-start(bf16[1,40,11200]{2,1,0:T(8,128)(2,1)S(1)} %get-tuple-element.31), channel_id=1, source_target_pairs={{0,1},{1,2},{2,3},{3,4},{4,5},{5,6},{6,7},{8,9},{9,10},{10,11},{11... | collective-permute-start | bytes 2688008 | tf_op jit(solution)/shard_map/ppermute | solution.py:387
  88.5 19.2 %collective-permute-start.19 = (bf16[1,40,11200]{2,1,0:T(8,128)(2,1)S(1)}, bf16[1,40,11200]{2,1,0:T(8,128)(2,1)S(1)}, u32[]{:S(2)}, u32[]{:S(2)}) collective-permute-start(bf16[1,40,11200]{2,1,0:T(8,128)(2,1)S(1)} %get-tuple-element.32), channel_id=1, source_target_pairs={{1,0},{2,1},{3,2},{4,3},{5,4},{6,5},{7,6},{9,8},{10,9},{11,10},{12... | collective-permute-start | bytes 2688008 | tf_op jit(solution)/shard_map/ppermute | solution.py:387
  90.5 17.2 %copy-start.8 = (f32[2240]{0:T(1024)S(1)}, f32[2240]{0:T(1024)}, u32[]{:S(2)}) copy-start(f32[2240]{0:T(1024)} %param.11) | copy-start | bytes 26884
  101.5 5.1 %collective-permute-start.15 = (bf16[512,128]{1,0:T(8,128)(2,1)S(1)}, bf16[512,128]{1,0:T(8,128)(2,1)S(1)}, u32[]{:S(2)}, u32[]{:S(2)}) collective-permute-start(bf16[512,128]{1,0:T(8,128)(2,1)S(1)} %pad_maximum_fusion.2.refs_3_), channel_id=1, source_target_pairs={{0,2},{1,3},{2,0},{3,1},{4,6},{5,7},{6,4},{7,5},{8,10},{9,11},{10,... | collective-permute-start | bytes 393224 | tf_op jit(solution)/shard_map/ppermute | solution.py:381
  106.6 10.8 %collective-permute-start.17 = (bf16[1024,128]{1,0:T(8,128)(2,1)S(1)}, bf16[1024,128]{1,0:T(8,128)(2,1)S(1)}, u32[]{:S(2)}, u32[]{:S(2)}) collective-permute-start(bf16[1024,128]{1,0:T(8,128)(2,1)S(1)} %pad_maximum_fusion.1), channel_id=1, source_target_pairs={{0,1},{1,0},{2,3},{3,2},{4,5},{5,4},{6,7},{7,6},{8,9},{9,8},{10,11... | collective-permute-start | bytes 786440 | tf_op jit(solution)/shard_map/ppermute | solution.py:381
  107.7 9.8 %copy-start.4 = (bf16[2,3,40,2240]{3,2,1,0:T(8,128)(2,1)S(1)}, bf16[2,3,40,2240]{3,2,1,0:T(8,128)(2,1)}, u32[]{:S(2)}) copy-start(bf16[2,3,40,2240]{3,2,1,0:T(8,128)(2,1)} %param.8) | copy-start | bytes 3225604

commit v5 on v4

--- a/solution.py
+++ b/solution.py
@@ -130,7 +130,7 @@
     groups = columns // 8
     skew = FF % LANES
     lead = FF // LANES
-    bounds = [lead * part // PARTS for part in range(PARTS + 1)]
+    bounds = [0, lead // 14, lead // 4, lead * 5 // 8, lead]
     fetches = []
     for part, (start, stop) in enumerate(zip(bounds, bounds[1:])):
         gate_start = lead + start + (part > 0)
@@ -275,16 +275,24 @@
     )(*args)
 
 
+def row_copies(source_ref, target_ref, sems):
+    return [
+        pltpu.make_async_copy(
+            source_ref.at[pl.ds(8 * g, 8)], target_ref.at[pl.ds(8 * g, 8)], sems.at[g]
+        )
+        for g in range(source_ref.shape[0] // 8)
+    ]
+
+
 def edge_kernel(own_ref, *refs, frame):
     *old_refs, time_ref, _, up_ref, down_ref, now_ref, old_ref, sems = refs
     rows, channels = own_ref.shape[1], own_ref.shape[3]
     ends = (0, rows - 1)
     copies = []
     for at, r in enumerate(ends):
-        group = [pltpu.make_async_copy(own_ref.at[frame, r], now_ref.at[at], sems.at[0, at])]
+        group = row_copies(own_ref.at[frame, r], now_ref.at[at], sems.at[0, at])
         if frame:
-            source = own_ref.at[frame - 1, r]
-            group.append(pltpu.make_async_copy(source, old_ref.at[at], sems.at[1, at]))
+            group += row_copies(own_ref.at[frame - 1, r], old_ref.at[at], sems.at[1, at])
         copies.append(group)
     for copy in copies[0] + copies[1]:
         copy.start()
@@ -322,7 +330,7 @@
         out_shape=(line, line),
         in_specs=[anywhere] + [held] * len(old) + [held, anywhere],
         out_specs=(held, held),
-        scratch_shapes=[pair, pair, pltpu.SemaphoreType.DMA((2, 2))],
+        scratch_shapes=[pair, pair, pltpu.SemaphoreType.DMA((2, 2, columns // 8))],
         compiler_params=pltpu.CompilerParams(vmem_limit_bytes=8 << 20),
         cost_estimate=pl.CostEstimate(
             flops=6 * columns * channels, bytes_accessed=12 * columns * channels, transcendentals=0
@@ -334,10 +342,9 @@
 def copy_kernel(source_ref, *refs, frame, rows):
     *_, token_ref, sems = refs
     outs = refs[-2 - len(rows) : -2]
-    copies = [
-        pltpu.make_async_copy(source_ref.at[frame, r], out_ref.at[0], sems.at[at])
-        for at, (r, out_ref) in enumerate(zip(rows, outs))
-    ]
+    copies = []
+    for at, (r, out_ref) in enumerate(zip(rows, outs)):
+        copies += row_copies(source_ref.at[frame, r], out_ref.at[0], sems.at[at])
     for copy in copies:
         copy.start()
     token_ref[...] = jnp.zeros_like(token_ref)
@@ -355,7 +362,7 @@
         + [jax.ShapeDtypeStruct((8, LANES), jnp.float32)],
         in_specs=[anywhere] * len(args),
         out_specs=[pl.BlockSpec(memory_space=pltpu.VMEM)] * (len(rows) + 1),
-        scratch_shapes=[pltpu.SemaphoreType.DMA((len(rows),))],
+        scratch_shapes=[pltpu.SemaphoreType.DMA((len(rows), columns // 8))],
         cost_estimate=pl.CostEstimate(
             flops=0, bytes_accessed=4 * len(rows) * columns * channels, transcendentals=0
         ),
@@ -363,9 +370,12 @@
     )(*args)
 
 
-def whole(body, out_shape, flops, *args):
+def whole(body, out_shape, flops, *args, token=None):
     specs = [pl.BlockSpec(memory_space=pltpu.SMEM)]
     specs += [pl.BlockSpec(memory_space=pltpu.VMEM)] * (len(args) - 1)
+    if token is not None:
+        args += (token,)
+        specs.append(pl.BlockSpec(memory_space=pl.ANY))
     return pl.pallas_call(
         body,
         out_shape=out_shape,
@@ -409,7 +419,7 @@
         row,
         key_tokens.reshape(tokens, width),
         value_tokens.reshape(tokens, width),
-        token,
+        token=token,
     )
     held = partial.reshape(2, 4, SHARE_ROWS, LANES)
     held = wide(held[0]) + wide(exchange(held[1], "row", 1))
@@ -424,7 +434,7 @@
         sent = narrow(column)
         if k == 2:
             sent, prev_first = lax.optimization_barrier((sent, prev_first))
-        if k == 4:
+        if k == 1:
             up_edge, down_edge = edges(hidden, frames - 1, (), time_weight, sent)
             top, bottom = ahead(down_edge, "row", 1), ahead(up_edge, "row", -1)
             ffn_out = conv_frame(hidden, frames - 1, (), top, bottom, weights)
@@ -434,10 +444,14 @@
             for at in range(INNER - 1)
         ]
         arrived = lax.ppermute(sent, frame_axes, pairs)
+        if k == 4:
+            arrived, ffn_out = lax.optimization_barrier((arrived, ffn_out))
         column = column + wide(arrived)
         before = before + wide(arrived)
     prefix = before + held
     closed, opened = lax.optimization_barrier((narrow(prefix), narrow(before), prev_last))[:2]
+    up_edge, down_edge = edges(hidden, 0, (prev_first, prev_last), time_weight, closed)
+    top_first, bottom_first = ahead(down_edge, "row", 1), ahead(up_edge, "row", -1)
     for k in range(1, INNER):
         sent = jnp.where(x + k < INNER, closed, opened)
         prefix = prefix + wide(ahead(sent, "x", k, True))
@@ -446,9 +460,6 @@
     prev_middle = ahead(prev_middle, frame_axes, 1)
 
     state = jnp.concatenate([prefix, exchange(prefix, "row", 4)], axis=0)
-    up_edge, down_edge = edges(hidden, 0, (prev_first, prev_last), time_weight, state)
-    top_first, bottom_first = ahead(down_edge, "row", 1), ahead(up_edge, "row", -1)
-    state, ffn_out = lax.optimization_barrier((state, ffn_out))
     state = jnp.concatenate([state, exchange(state, "row", 2)], axis=0)
     state, prev_middle = lax.optimization_barrier((state, prev_middle))
     state = jnp.concatenate([state, exchange(state, "row", 1)], axis=0)

time: 120 us -> 130 us (1.083); the launches traced: 120 us -> 128 us
  starting transfers between devices: 57.4 us -> 64.8 us
  other arithmetic: 0.99 us -> 3.32 us
  waiting for transfers between devices: 24.7 us -> 23.4 us
    ppermute x10, starting transfers between devices: 25.9 us -> 29.8 us  [ahead(): return lax.ppermute(value, axis, pairs)]
    ppermute x10, waiting for transfers between devices: 6.12 us -> 2.15 us  [ahead(): return lax.ppermute(value, axis, pairs)]
    ppermute x6, waiting for transfers between devices: 16 us -> 19.9 us  [exchange(): lax.ppermute(value, axis, [(i, i ^ flip) for i in range(lax.axis_size(axi...]
    convert_element_type x6, other arithmetic: 0.83 us -> 3.14 us  [per_device(): narrow = lambda value: value.astype(jnp.bfloat16)]
    ppermute x6, starting transfers between devices: 8.88 us -> 10.7 us  [exchange(): lax.ppermute(value, axis, [(i, i ^ flip) for i in range(lax.axis_size(axi...]
    ppermute x3, starting transfers between devices: 22 us -> 23.6 us  [per_device(): arrived = lax.ppermute(sent, frame_axes, pairs)]
  transfers between devices with their start and end apart: 20 -> 20, of which waited for: 8 -> 8; matrix products, arithmetic and copies ran while one was open for 1% -> 1% of each run, Pallas kernels for 24% -> 21%
where the time goes in v5:
time: 130 us; the launch traced here: 128 us
  starting transfers between devices  64.8 us (50%)
  Pallas kernels  34.9 us (27%)
  waiting for transfers between devices  23.4 us (18%)
  other arithmetic  3.32 us (3%)
    ppermute x10, starting transfers between devices, ahead(): return lax.ppermute(value, axis, pairs)  29.8 us
    ppermute x3, starting transfers between devices, per_device(): arrived = lax.ppermute(sent, frame_axes, pairs)  23.6 us
    pallas_call x2, Pallas kernels, conv_frame(): pl.pallas_call(functools.partial(conv_kernel, frame), out_shape=jax.Shape...  20.5 us
    ppermute x6, waiting for transfers between devices, exchange(): lax.ppermute(value, axis, [(i, i ^ flip) for i in range(lax.axis_size(axi...  19.9 us
    ppermute x6, starting transfers between devices, exchange(): lax.ppermute(value, axis, [(i, i ^ flip) for i in range(lax.axis_size(axi...  10.7 us
    pallas_call x2, Pallas kernels, edges(): pl.pallas_call(functools.partial(edge_kernel, frame=frame), out_shape=(li...  6.18 us
    pallas_call x2, Pallas kernels, copied_rows(): pl.pallas_call(functools.partial(copy_kernel, frame=frame, rows=rows), ou...  5.16 us
    convert_element_type x6, other arithmetic, per_device(): narrow = lambda value: value.astype(jnp.bfloat16)  3.14 us
  transfers between devices with their start and end apart: 20, of which 8 were waited for; matrix products, arithmetic and copies ran while one was open for 1% of the time, Pallas kernels for 21%

profile of v5, /device:TPU:1, one launch (start us, length us, event | category | flops | bytes accessed | tf_op | source)
XLA Modules:
  0.0 128.3 jit_solution(1042845821303456535)
XLA Ops:
  0.7 3.0 %copied_rows.2 = (bf16[1,40,11200]{2,1,0:T(8,128)(2,1)}, bf16[1,40,11200]{2,1,0:T(8,128)(2,1)}, f32[8,128]{1,0:T(8,128)}) custom-call(bf16[2,3,40,11200]{3,2,1,0:T(8,128)(2,1)} %own_ref.7), custom_call_target="tpu_custom_call" | custom-call | bytes 3584000 | tf_op jit(solution)/shard_map/copied_rows/pallas_call | solution.py:359
  4.3 0.9 partial_kernel.1
  5.3 3.3 %collective-permute-start = (bf16[4,256,128]{2,1,0:T(8,128)(2,1)S(1)}, bf16[4,256,128]{2,1,0:T(8,128)(2,1)S(1)}, u32[]{:S(2)}, u32[]{:S(2)}) collective-permute-start(bf16[4,256,128]{2,1,0:T(8,128)(2,1)S(1)} %bitcast.23), channel_id=1, source_target_pairs={{0,1},{1,0},{2,3},{3,2},{4,5},{5,4},{6,7},{7,6},{8,9},{9,8},{10,11... | collective-permute-start | bytes 786440 | tf_op jit(solution)/shard_map/ppermute | solution.py:391
  8.6 1.2 collective-permute-done
  10.0 4.7 %collective-permute-done.1 = bf16[2,256,128]{2,1,0:T(8,128)(2,1)S(1)} collective-permute-done((bf16[2,256,128]{2,1,0:T(8,128)(2,1)S(1)}, bf16[2,256,128]{2,1,0:T(8,128)(2,1)S(1)}, u32[]{:S(2)}, u32[]{:S(2)}) %collective-permute-start.1) | collective-permute-done | bytes 131104 | tf_op jit(solution)/shard_map/ppermute | solution.py:391
  14.7 1.3 collective-permute-start.2
  16.0 3.2 %collective-permute-start.5 = (bf16[1,40,11200]{2,1,0:T(8,128)(2,1)S(1)}, bf16[1,40,11200]{2,1,0:T(8,128)(2,1)S(1)}, u32[]{:S(2)}, u32[]{:S(2)}) collective-permute-start(bf16[1,40,11200]{2,1,0:T(8,128)(2,1)S(1)} %copy-done.13), channel_id=1, source_target_pairs={{0,8},{8,16},{16,24},{24,32},{32,40},{40,48},{48,56},{56,64},{64,7... | collective-permute-start | bytes 2688008 | tf_op jit(solution)/shard_map/ppermute | solution.py:397
  20.2 3.9 %edges.2 = (bf16[1,40,11200]{2,1,0:T(8,128)(2,1)}, bf16[1,40,11200]{2,1,0:T(8,128)(2,1)}) custom-call(bf16[2,3,40,11200]{3,2,1,0:T(8,128)(2,1)} %own_ref.7, f32[2,11200]{1,0:T(2,128)S(1)} %copy-done.1, bf16[256,128]{1,0:T(8,128)(2,1)S(1)} %fusion.3.refs_1_), custom_call_target="tpu_custom_call" | custom-call | flops 2688000 | bytes 5376000 | tf_op jit(solution)/shard_map/edges/pallas_call | solution.py:328
  24.1 4.3 %collective-permute-start.8 = (bf16[1,40,11200]{2,1,0:T(8,128)(2,1)}, bf16[1,40,11200]{2,1,0:T(8,128)(2,1)S(1)}, u32[]{:S(2)}, u32[]{:S(2)}) collective-permute-start(bf16[1,40,11200]{2,1,0:T(8,128)(2,1)} %get-tuple-element.21), channel_id=1, source_target_pairs={{0,1},{1,2},{2,3},{3,4},{4,5},{5,6},{6,7},{8,9},{9,10},{10,11},{11... | collective-permute-start | bytes 2688008 | tf_op jit(solution)/shard_map/ppermute | solution.py:397
  28.4 1.9 %collective-permute-start.9 = (bf16[1,40,11200]{2,1,0:T(8,128)(2,1)}, bf16[1,40,11200]{2,1,0:T(8,128)(2,1)}, u32[]{:S(2)}, u32[]{:S(2)}) collective-permute-start(bf16[1,40,11200]{2,1,0:T(8,128)(2,1)} %get-tuple-element.22), channel_id=1, source_target_pairs={{1,0},{2,1},{3,2},{4,3},{5,4},{6,5},{7,6},{9,8},{10,9},{11,10},{12... | collective-permute-start | bytes 2688008 | tf_op jit(solution)/shard_map/ppermute | solution.py:397
  30.3 3.1 %collective-permute-start.4 = (bf16[256,128]{1,0:T(8,128)(2,1)S(1)}, bf16[256,128]{1,0:T(8,128)(2,1)S(1)}, u32[]{:S(2)}, u32[]{:S(2)}) collective-permute-start(bf16[256,128]{1,0:T(8,128)(2,1)S(1)} %fusion.3.refs_1_), channel_id=1, source_target_pairs={{0,32},{8,40},{16,48},{32,64},{40,72},{48,80},{64,96},{72,104},{80... | collective-permute-start | bytes 196616 | tf_op jit(solution)/shard_map/ppermute | solution.py:446
  33.4 3.2 %collective-permute-start.10 = (bf16[1,40,11200]{2,1,0:T(8,128)(2,1)}, bf16[1,40,11200]{2,1,0:T(8,128)(2,1)S(1)}, u32[]{:S(2)}, u32[]{:S(2)}) collective-permute-start(bf16[1,40,11200]{2,1,0:T(8,128)(2,1)} %get-tuple-element.24), channel_id=1, source_target_pairs={{0,8},{8,16},{16,24},{24,32},{32,40},{40,48},{48,56},{56,64},{64,7... | collective-permute-start | bytes 2688008 | tf_op jit(solution)/shard_map/ppermute | solution.py:397
  36.9 8.0 %collective-permute-start.6 = (bf16[256,128]{1,0:T(8,128)(2,1)S(1)}, bf16[256,128]{1,0:T(8,128)(2,1)S(1)}, u32[]{:S(2)}, u32[]{:S(2)}) collective-permute-start(bf16[256,128]{1,0:T(8,128)(2,1)S(1)} %fusion.7), channel_id=1, source_target_pairs={{0,64},{8,72},{16,80},{32,96},{40,104},{48,112},{64,128},{72,136},... | collective-permute-start | bytes 196616 | tf_op jit(solution)/shard_map/ppermute | solution.py:446
  44.9 1.3 %collective-permute-done.6 = bf16[256,128]{1,0:T(8,128)(2,1)S(1)} collective-permute-done((bf16[256,128]{1,0:T(8,128)(2,1)S(1)}, bf16[256,128]{1,0:T(8,128)(2,1)S(1)}, u32[]{:S(2)}, u32[]{:S(2)}) %collective-permute-start.6) | collective-permute-done | bytes 65568 | tf_op jit(solution)/shard_map/ppermute | solution.py:446
  46.9 12.5 %collective-permute-start.7 = (bf16[256,128]{1,0:T(8,128)(2,1)}, bf16[256,128]{1,0:T(8,128)(2,1)}, u32[]{:S(2)}, u32[]{:S(2)}) collective-permute-start(bf16[256,128]{1,0:T(8,128)(2,1)} %fusion.1), channel_id=1, source_target_pairs={{0,128},{8,136},{16,144},{32,160},{40,168},{48,176},{64,192},{72,2... | collective-permute-start | bytes 196616 | tf_op jit(solution)/shard_map/ppermute | solution.py:446
  59.4 10.8 %conv_frame.2.refs_8_ = bf16[2,3,40,5600]{3,2,1,0:T(8,128)(2,1)} custom-call(bf16[2,3,40,11200]{3,2,1,0:T(8,128)(2,1)} %own_ref.7, bf16[1,40,11200]{2,1,0:T(8,128)(2,1)S(1)} %collective-permute-done.8.refs_0_, bf16[1,40,11200]{2,1,0:T(8,128)(2,1)} %collective-permute-done.9.refs_1_, f32[2,11200]{1,0:T(2,128)S(1)} %copy-done.1, f32[3,3,11200]{2,1,0:T(4,128)S(1)} %copy-done, ...), custom_call_target="tpu_custom_call" | custom-call | flops 53760000 | bytes 8064000 | tf_op jit(solution)/shard_map/conv_frame/pallas_call | solution.py:258
  70.3 0.9 fusion.4
  71.2 2.2 %collective-permute-start.11 = (bf16[256,128]{1,0:T(8,128)(2,1)S(1)}, bf16[256,128]{1,0:T(8,128)(2,1)S(1)}, u32[]{:S(2)}, u32[]{:S(2)}) collective-permute-start(bf16[256,128]{1,0:T(8,128)(2,1)S(1)} %get-tuple-element.40), channel_id=1, source_target_pairs={{0,8},{8,16},{16,24},{24,0},{1,9},{9,17},{17,25},{25,1},{2,10},{10... | collective-permute-start | bytes 196616 | tf_op jit(solution)/shard_map/ppermute | solution.py:397
  74.2 2.0 %collective-permute-start.13 = (bf16[256,128]{1,0:T(8,128)(2,1)S(1)}, bf16[256,128]{1,0:T(8,128)(2,1)S(1)}, u32[]{:S(2)}, u32[]{:S(2)}) collective-permute-start(bf16[256,128]{1,0:T(8,128)(2,1)S(1)} %get-tuple-element.41), channel_id=1, source_target_pairs={{0,24},{8,0},{16,8},{24,16},{1,25},{9,1},{17,9},{25,17},{2,26},{10... | collective-permute-start | bytes 196616 | tf_op jit(solution)/shard_map/ppermute | solution.py:397
  76.2 1.9 %collective-permute-done.12 = bf16[256,128]{1,0:T(8,128)(2,1)S(1)} collective-permute-done((bf16[256,128]{1,0:T(8,128)(2,1)S(1)}, bf16[256,128]{1,0:T(8,128)(2,1)S(1)}, u32[]{:S(2)}, u32[]{:S(2)}) %collective-permute-start.12) | collective-permute-done | bytes 65568 | tf_op jit(solution)/shard_map/ppermute | solution.py:397
  78.1 1.5 %add_convert_fusion.refs_0_ = bf16[256,128]{1,0:T(8,128)(2,1)} fusion(bf16[256,128]{1,0:T(8,128)(2,1)S(1)} %collective-permute-done.13, bf16[256,128]{1,0:T(8,128)(2,1)S(1)} %collective-permute-done.12, bf16[256,128]{1,0:T(8,128)(2,1)S(1)} %collective-permute-done.11, f32[256,128]{1,0:T(8,128)S(1)} %get-tuple-element.35, ...), kind=kLoop, calls=%fused_computation.14 | loop fusion | flops 425984 | bytes 589824 | tf_op jit(solution)/shard_map/convert_element_type | solution.py:409
  79.6 2.2 %copied_rows.3 = (bf16[1,40,11200]{2,1,0:T(8,128)(2,1)}, f32[8,128]{1,0:T(8,128)}) custom-call(bf16[2,3,40,11200]{3,2,1,0:T(8,128)(2,1)} %own_ref.7, bf16[256,128]{1,0:T(8,128)(2,1)} %add_convert_fusion.refs_0_), custom_call_target="tpu_custom_call" | custom-call | bytes 1792000 | tf_op jit(solution)/shard_map/copied_rows/pallas_call | solution.py:359
  81.8 2.5 %collective-permute-start.16 = (bf16[1,40,11200]{2,1,0:T(8,128)(2,1)}, bf16[1,40,11200]{2,1,0:T(8,128)(2,1)S(1)}, u32[]{:S(2)}, u32[]{:S(2)}) collective-permute-start(bf16[1,40,11200]{2,1,0:T(8,128)(2,1)} %get-tuple-element.27), channel_id=1, source_target_pairs={{0,8},{8,16},{16,24},{24,32},{32,40},{40,48},{48,56},{56,64},{64,7... | collective-permute-start | bytes 2688008 | tf_op jit(solution)/shard_map/ppermute | solution.py:397
  84.3 2.3 %edges.3 = (bf16[1,40,11200]{2,1,0:T(8,128)(2,1)S(1)}, bf16[1,40,11200]{2,1,0:T(8,128)(2,1)S(1)}) custom-call(bf16[2,3,40,11200]{3,2,1,0:T(8,128)(2,1)} %own_ref.7, bf16[1,40,11200]{2,1,0:T(8,128)(2,1)S(1)} %collective-permute-done.5.refs_0_, bf16[1,40,11200]{2,1,0:T(8,128)(2,1)S(1)} %collective-permute-done.10.refs_1_.refs_2_, f32[2,11200]{1,0:T(2,128)S(1)} %copy-done.1, ...), custom_call_target="tpu_custom_call" | custom-call | flops 2688000 | bytes 5376000 | tf_op jit(solution)/shard_map/edges/pallas_call | solution.py:328
  86.6 7.9 %collective-permute-start.18 = (bf16[1,40,11200]{2,1,0:T(8,128)(2,1)S(1)}, bf16[1,40,11200]{2,1,0:T(8,128)(2,1)S(1)}, u32[]{:S(2)}, u32[]{:S(2)}) collective-permute-start(bf16[1,40,11200]{2,1,0:T(8,128)(2,1)S(1)} %get-tuple-element.31), channel_id=1, source_target_pairs={{0,1},{1,2},{2,3},{3,4},{4,5},{5,6},{6,7},{8,9},{9,10},{10,11},{11... | collective-permute-start | bytes 2688008 | tf_op jit(solution)/shard_map/ppermute | solution.py:397
  94.6 1.9 %collective-permute-start.19 = (bf16[1,40,11200]{2,1,0:T(8,128)(2,1)S(1)}, bf16[1,40,11200]{2,1,0:T(8,128)(2,1)S(1)}, u32[]{:S(2)}, u32[]{:S(2)}) collective-permute-start(bf16[1,40,11200]{2,1,0:T(8,128)(2,1)S(1)} %get-tuple-element.32), channel_id=1, source_target_pairs={{1,0},{2,1},{3,2},{4,3},{5,4},{6,5},{7,6},{9,8},{10,9},{11,10},{12... | collective-permute-start | bytes 2688008 | tf_op jit(solution)/shard_map/ppermute | solution.py:397
  96.5 2.0 %collective-permute-start.14 = (bf16[256,128]{1,0:T(8,128)(2,1)S(1)}, bf16[256,128]{1,0:T(8,128)(2,1)S(1)}, u32[]{:S(2)}, u32[]{:S(2)}) collective-permute-start(bf16[256,128]{1,0:T(8,128)(2,1)S(1)} %copy-done.7), channel_id=1, source_target_pairs={{0,4},{1,5},{2,6},{3,7},{4,0},{5,1},{6,2},{7,3},{8,12},{9,13},{10,... | collective-permute-start | bytes 196616 | tf_op jit(solution)/shard_map/ppermute | solution.py:391
  98.5 10.0 %collective-permute-done.14 = bf16[256,128]{1,0:T(8,128)(2,1)S(1)} collective-permute-done((bf16[256,128]{1,0:T(8,128)(2,1)S(1)}, bf16[256,128]{1,0:T(8,128)(2,1)S(1)}, u32[]{:S(2)}, u32[]{:S(2)}) %collective-permute-start.14) | collective-permute-done | bytes 65568 | tf_op jit(solution)/shard_map/ppermute | solution.py:391
  108.6 3.8 %collective-permute-done.15 = bf16[512,128]{1,0:T(8,128)(2,1)S(1)} collective-permute-done((bf16[512,128]{1,0:T(8,128)(2,1)S(1)}, bf16[512,128]{1,0:T(8,128)(2,1)S(1)}, u32[]{:S(2)}, u32[]{:S(2)}) %collective-permute-start.15) | collective-permute-done | bytes 131104 | tf_op jit(solution)/shard_map/ppermute | solution.py:391
  112.4 3.9 %collective-permute-start.17 = (bf16[1024,128]{1,0:T(8,128)(2,1)S(1)}, bf16[1024,128]{1,0:T(8,128)(2,1)S(1)}, u32[]{:S(2)}, u32[]{:S(2)}) collective-permute-start(bf16[1024,128]{1,0:T(8,128)(2,1)S(1)} %pad_maximum_fusion.1), channel_id=1, source_target_pairs={{0,1},{1,0},{2,3},{3,2},{4,5},{5,4},{6,7},{7,6},{8,9},{9,8},{10,11... | collective-permute-start | bytes 786440 | tf_op jit(solution)/shard_map/ppermute | solution.py:391
  116.4 9.6 %conv_frame.3 = bf16[2,3,40,5600]{3,2,1,0:T(8,128)(2,1)} custom-call(bf16[2,3,40,11200]{3,2,1,0:T(8,128)(2,1)} %own_ref.7, bf16[1,40,11200]{2,1,0:T(8,128)(2,1)S(1)} %collective-permute-done.5.refs_0_, bf16[1,40,11200]{2,1,0:T(8,128)(2,1)S(1)} %collective-permute-done.16.refs_1_, ...), custom_call_target="tpu_custom_call", output_to_operand_aliasing={{}: (9, {})} | custom-call | flops 53760000 | bytes 8064000 | tf_op jit(solution)/shard_map/conv_frame/pallas_call | solution.py:258
  126.1 2.2 %mixed_kernel.1 = bf16[240,2240]{1,0:T(8,128)(2,1)} custom-call(s32[1]{0:T(128)} %bitcast.row_ref, bf16[240,2240]{1,0:T(8,128)(2,1)S(1)} %bitcast.18, bf16[2048,128]{1,0:T(8,128)(2,1)S(1)} %pad_maximum_fusion.state_ref, f32[1,2240]{1,0:T(1,128)S(1)} %broadcast_in_dim.7.gain_ref), custom_call_target="tpu_custom_call" | custom-call | flops 275251200 | bytes 3145728 | tf_op jit(solution)/shard_map/mixed_kernel/pallas_call | solution.py:379
  (60 shorter events, 3.9 us)
Async XLA Ops:
  0.6 3.0 %copy-start.2 = (bf16[2,3,40,2240]{3,2,1,0:T(8,128)(2,1)S(1)}, bf16[2,3,40,2240]{3,2,1,0:T(8,128)(2,1)}, u32[]{:S(2)}) copy-start(bf16[2,3,40,2240]{3,2,1,0:T(8,128)(2,1)} %param.9) | copy-start | bytes 3225604
  0.6 3.0 %copy-start.3 = (bf16[2,3,40,2240]{3,2,1,0:T(8,128)(2,1)S(1)}, bf16[2,3,40,2240]{3,2,1,0:T(8,128)(2,1)}, u32[]{:S(2)}) copy-start(bf16[2,3,40,2240]{3,2,1,0:T(8,128)(2,1)} %param.10) | copy-start | bytes 3225604
  5.3 10.7 %copy-start.13 = (bf16[1,40,11200]{2,1,0:T(8,128)(2,1)S(1)}, bf16[1,40,11200]{2,1,0:T(8,128)(2,1)}, u32[]{:S(2)}) copy-start(bf16[1,40,11200]{2,1,0:T(8,128)(2,1)} %get-tuple-element.19) | copy-start | bytes 2688004
  5.3 4.5 %collective-permute-start = (bf16[4,256,128]{2,1,0:T(8,128)(2,1)S(1)}, bf16[4,256,128]{2,1,0:T(8,128)(2,1)S(1)}, u32[]{:S(2)}, u32[]{:S(2)}) collective-permute-start(bf16[4,256,128]{2,1,0:T(8,128)(2,1)S(1)} %bitcast.23), channel_id=1, source_target_pairs={{0,1},{1,0},{2,3},{3,2},{4,5},{5,4},{6,7},{7,6},{8,9},{9,8},{10,11... | collective-permute-start | bytes 786440 | tf_op jit(solution)/shard_map/ppermute | solution.py:391
  9.8 10.3 %copy-start.1 = (f32[2,11200]{1,0:T(2,128)S(1)}, f32[2,11200]{1,0:T(2,128)}, u32[]{:S(2)}) copy-start(f32[2,11200]{1,0:T(2,128)} %refs_5_.1) | copy-start | bytes 268804
  9.9 4.8 %collective-permute-start.1 = (bf16[2,256,128]{2,1,0:T(8,128)(2,1)S(1)}, bf16[2,256,128]{2,1,0:T(8,128)(2,1)S(1)}, u32[]{:S(2)}, u32[]{:S(2)}) collective-permute-start(bf16[2,256,128]{2,1,0:T(8,128)(2,1)S(1)} %slice.42), channel_id=1, source_target_pairs={{0,2},{1,3},{2,0},{3,1},{4,6},{5,7},{6,4},{7,5},{8,10},{9,11},{10,... | collective-permute-start | bytes 393224 | tf_op jit(solution)/shard_map/ppermute | solution.py:391
  14.7 4.7 %collective-permute-start.2 = (bf16[256,128]{1,0:T(8,128)(2,1)S(1)}, bf16[256,128]{1,0:T(8,128)(2,1)S(1)}, u32[]{:S(2)}, u32[]{:S(2)}) collective-permute-start(bf16[256,128]{1,0:T(8,128)(2,1)S(1)} %fusion.6), channel_id=1, source_target_pairs={{0,4},{1,5},{2,6},{3,7},{4,0},{5,1},{6,2},{7,3},{8,12},{9,13},{10,... | collective-permute-start | bytes 196616 | tf_op jit(solution)/shard_map/ppermute | solution.py:391
  16.0 20.9 %collective-permute-start.5 = (bf16[1,40,11200]{2,1,0:T(8,128)(2,1)S(1)}, bf16[1,40,11200]{2,1,0:T(8,128)(2,1)S(1)}, u32[]{:S(2)}, u32[]{:S(2)}) collective-permute-start(bf16[1,40,11200]{2,1,0:T(8,128)(2,1)S(1)} %copy-done.13), channel_id=1, source_target_pairs={{0,8},{8,16},{16,24},{24,32},{32,40},{40,48},{48,56},{56,64},{64,7... | collective-permute-start | bytes 2688008 | tf_op jit(solution)/shard_map/ppermute | solution.py:397
  19.5 0.7 collective-permute-start.3
  20.2 39.2 %copy-start.5 = (f32[11200]{0:T(1024)S(1)}, f32[11200]{0:T(1024)}, u32[]{:S(2)}) copy-start(f32[11200]{0:T(1024)} %param.15) | copy-start | bytes 134404
  24.1 35.3 %copy-start = (f32[3,3,11200]{2,1,0:T(4,128)S(1)}, f32[3,3,11200]{2,1,0:T(4,128)}, u32[]{:S(2)}) copy-start(f32[3,3,11200]{2,1,0:T(4,128)} %refs_6_.1) | copy-start | bytes 1209604
  24.1 35.3 %collective-permute-start.8 = (bf16[1,40,11200]{2,1,0:T(8,128)(2,1)}, bf16[1,40,11200]{2,1,0:T(8,128)(2,1)S(1)}, u32[]{:S(2)}, u32[]{:S(2)}) collective-permute-start(bf16[1,40,11200]{2,1,0:T(8,128)(2,1)} %get-tuple-element.21), channel_id=1, source_target_pairs={{0,1},{1,2},{2,3},{3,4},{4,5},{5,6},{6,7},{8,9},{9,10},{10,11},{11... | collective-permute-start | bytes 2688008 | tf_op jit(solution)/shard_map/ppermute | solution.py:397
  28.4 31.0 %collective-permute-start.9 = (bf16[1,40,11200]{2,1,0:T(8,128)(2,1)}, bf16[1,40,11200]{2,1,0:T(8,128)(2,1)}, u32[]{:S(2)}, u32[]{:S(2)}) collective-permute-start(bf16[1,40,11200]{2,1,0:T(8,128)(2,1)} %get-tuple-element.22), channel_id=1, source_target_pairs={{1,0},{2,1},{3,2},{4,3},{5,4},{6,5},{7,6},{9,8},{10,9},{11,10},{12... | collective-permute-start | bytes 2688008 | tf_op jit(solution)/shard_map/ppermute | solution.py:397
  30.3 6.3 %collective-permute-start.4 = (bf16[256,128]{1,0:T(8,128)(2,1)S(1)}, bf16[256,128]{1,0:T(8,128)(2,1)S(1)}, u32[]{:S(2)}, u32[]{:S(2)}) collective-permute-start(bf16[256,128]{1,0:T(8,128)(2,1)S(1)} %fusion.3.refs_1_), channel_id=1, source_target_pairs={{0,32},{8,40},{16,48},{32,64},{40,72},{48,80},{64,96},{72,104},{80... | collective-permute-start | bytes 196616 | tf_op jit(solution)/shard_map/ppermute | solution.py:446
  33.4 37.8 %collective-permute-start.10 = (bf16[1,40,11200]{2,1,0:T(8,128)(2,1)}, bf16[1,40,11200]{2,1,0:T(8,128)(2,1)S(1)}, u32[]{:S(2)}, u32[]{:S(2)}) collective-permute-start(bf16[1,40,11200]{2,1,0:T(8,128)(2,1)} %get-tuple-element.24), channel_id=1, source_target_pairs={{0,8},{8,16},{16,24},{24,32},{32,40},{40,48},{48,56},{56,64},{64,7... | collective-permute-start | bytes 2688008 | tf_op jit(solution)/shard_map/ppermute | solution.py:397
  36.6 9.6 %copy-start.8 = (bf16[256,128]{1,0:T(8,128)(2,1)}, bf16[256,128]{1,0:T(8,128)(2,1)S(1)}, u32[]{:S(2)}) copy-start(bf16[256,128]{1,0:T(8,128)(2,1)S(1)} %collective-permute-done.4) | copy-start | bytes 196612
  36.9 9.3 %collective-permute-start.6 = (bf16[256,128]{1,0:T(8,128)(2,1)S(1)}, bf16[256,128]{1,0:T(8,128)(2,1)S(1)}, u32[]{:S(2)}, u32[]{:S(2)}) collective-permute-start(bf16[256,128]{1,0:T(8,128)(2,1)S(1)} %fusion.7), channel_id=1, source_target_pairs={{0,64},{8,72},{16,80},{32,96},{40,104},{48,112},{64,128},{72,136},... | collective-permute-start | bytes 196616 | tf_op jit(solution)/shard_map/ppermute | solution.py:446
  46.9 23.4 %collective-permute-start.7 = (bf16[256,128]{1,0:T(8,128)(2,1)}, bf16[256,128]{1,0:T(8,128)(2,1)}, u32[]{:S(2)}, u32[]{:S(2)}) collective-permute-start(bf16[256,128]{1,0:T(8,128)(2,1)} %fusion.1), channel_id=1, source_target_pairs={{0,128},{8,136},{16,144},{32,160},{40,168},{48,176},{64,192},{72,2... | collective-permute-start | bytes 196616 | tf_op jit(solution)/shard_map/ppermute | solution.py:446
  59.4 10.9 %copy-start.9 = (bf16[256,128]{1,0:T(8,128)(2,1)S(1)}, bf16[256,128]{1,0:T(8,128)(2,1)}, u32[]{:S(2)}) copy-start(bf16[256,128]{1,0:T(8,128)(2,1)} %copy-done.8) | copy-start | bytes 196612
  59.4 10.9 %copy-start.11 = (bf16[256,128]{1,0:T(8,128)(2,1)S(1)}, bf16[256,128]{1,0:T(8,128)(2,1)}, u32[]{:S(2)}) copy-start(bf16[256,128]{1,0:T(8,128)(2,1)} %copy-done.10) | copy-start | bytes 196612
  71.2 5.0 %collective-permute-start.11 = (bf16[256,128]{1,0:T(8,128)(2,1)S(1)}, bf16[256,128]{1,0:T(8,128)(2,1)S(1)}, u32[]{:S(2)}, u32[]{:S(2)}) collective-permute-start(bf16[256,128]{1,0:T(8,128)(2,1)S(1)} %get-tuple-element.40), channel_id=1, source_target_pairs={{0,8},{8,16},{16,24},{24,0},{1,9},{9,17},{17,25},{25,1},{2,10},{10... | collective-permute-start | bytes 196616 | tf_op jit(solution)/shard_map/ppermute | solution.py:397
  73.4 4.6 %collective-permute-start.12 = (bf16[256,128]{1,0:T(8,128)(2,1)S(1)}, bf16[256,128]{1,0:T(8,128)(2,1)S(1)}, u32[]{:S(2)}, u32[]{:S(2)}) collective-permute-start(bf16[256,128]{1,0:T(8,128)(2,1)S(1)} %get-tuple-element.42), channel_id=1, source_target_pairs={{0,16},{8,24},{16,0},{24,8},{1,17},{9,25},{17,1},{25,9},{2,18},{10... | collective-permute-start | bytes 196616 | tf_op jit(solution)/shard_map/ppermute | solution.py:397
  74.2 3.8 %collective-permute-start.13 = (bf16[256,128]{1,0:T(8,128)(2,1)S(1)}, bf16[256,128]{1,0:T(8,128)(2,1)S(1)}, u32[]{:S(2)}, u32[]{:S(2)}) collective-permute-start(bf16[256,128]{1,0:T(8,128)(2,1)S(1)} %get-tuple-element.41), channel_id=1, source_target_pairs={{0,24},{8,0},{16,8},{24,16},{1,25},{9,1},{17,9},{25,17},{2,26},{10... | collective-permute-start | bytes 196616 | tf_op jit(solution)/shard_map/ppermute | solution.py:397
  81.8 14.7 %copy-start.7 = (bf16[256,128]{1,0:T(8,128)(2,1)S(1)}, bf16[256,128]{1,0:T(8,128)(2,1)}, u32[]{:S(2)}) copy-start(bf16[256,128]{1,0:T(8,128)(2,1)} %add_convert_fusion.refs_0_) | copy-start | bytes 196612
  81.8 34.5 %copy-start.12 = (f32[2240]{0:T(1024)S(1)}, f32[2240]{0:T(1024)}, u32[]{:S(2)}) copy-start(f32[2240]{0:T(1024)} %param.11) | copy-start | bytes 26884
  81.8 30.6 %collective-permute-start.16 = (bf16[1,40,11200]{2,1,0:T(8,128)(2,1)}, bf16[1,40,11200]{2,1,0:T(8,128)(2,1)S(1)}, u32[]{:S(2)}, u32[]{:S(2)}) collective-permute-start(bf16[1,40,11200]{2,1,0:T(8,128)(2,1)} %get-tuple-element.27), channel_id=1, source_target_pairs={{0,8},{8,16},{16,24},{24,32},{32,40},{40,48},{48,56},{56,64},{64,7... | collective-permute-start | bytes 2688008 | tf_op jit(solution)/shard_map/ppermute | solution.py:397
  86.6 29.7 %collective-permute-start.18 = (bf16[1,40,11200]{2,1,0:T(8,128)(2,1)S(1)}, bf16[1,40,11200]{2,1,0:T(8,128)(2,1)S(1)}, u32[]{:S(2)}, u32[]{:S(2)}) collective-permute-start(bf16[1,40,11200]{2,1,0:T(8,128)(2,1)S(1)} %get-tuple-element.31), channel_id=1, source_target_pairs={{0,1},{1,2},{2,3},{3,4},{4,5},{5,6},{6,7},{8,9},{9,10},{10,11},{11... | collective-permute-start | bytes 2688008 | tf_op jit(solution)/shard_map/ppermute | solution.py:397
  94.6 21.7 %collective-permute-start.19 = (bf16[1,40,11200]{2,1,0:T(8,128)(2,1)S(1)}, bf16[1,40,11200]{2,1,0:T(8,128)(2,1)S(1)}, u32[]{:S(2)}, u32[]{:S(2)}) collective-permute-start(bf16[1,40,11200]{2,1,0:T(8,128)(2,1)S(1)} %get-tuple-element.32), channel_id=1, source_target_pairs={{1,0},{2,1},{3,2},{4,3},{5,4},{6,5},{7,6},{9,8},{10,9},{11,10},{12... | collective-permute-start | bytes 2688008 | tf_op jit(solution)/shard_map/ppermute | solution.py:397
  96.5 12.0 %collective-permute-start.14 = (bf16[256,128]{1,0:T(8,128)(2,1)S(1)}, bf16[256,128]{1,0:T(8,128)(2,1)S(1)}, u32[]{:S(2)}, u32[]{:S(2)}) collective-permute-start(bf16[256,128]{1,0:T(8,128)(2,1)S(1)} %copy-done.7), channel_id=1, source_target_pairs={{0,4},{1,5},{2,6},{3,7},{4,0},{5,1},{6,2},{7,3},{8,12},{9,13},{10,... | collective-permute-start | bytes 196616 | tf_op jit(solution)/shard_map/ppermute | solution.py:391
  108.5 3.9 %collective-permute-start.15 = (bf16[512,128]{1,0:T(8,128)(2,1)S(1)}, bf16[512,128]{1,0:T(8,128)(2,1)S(1)}, u32[]{:S(2)}, u32[]{:S(2)}) collective-permute-start(bf16[512,128]{1,0:T(8,128)(2,1)S(1)} %pad_maximum_fusion.2), channel_id=1, source_target_pairs={{0,2},{1,3},{2,0},{3,1},{4,6},{5,7},{6,4},{7,5},{8,10},{9,11},{10,... | collective-permute-start | bytes 393224 | tf_op jit(solution)/shard_map/ppermute | solution.py:391
  112.4 13.6 %collective-permute-start.17 = (bf16[1024,128]{1,0:T(8,128)(2,1)S(1)}, bf16[1024,128]{1,0:T(8,128)(2,1)S(1)}, u32[]{:S(2)}, u32[]{:S(2)}) collective-permute-start(bf16[1024,128]{1,0:T(8,128)(2,1)S(1)} %pad_maximum_fusion.1), channel_id=1, source_target_pairs={{0,1},{1,0},{2,3},{3,2},{4,5},{5,4},{6,7},{7,6},{8,9},{9,8},{10,11... | collective-permute-start | bytes 786440 | tf_op jit(solution)/shard_map/ppermute | solution.py:391
  116.3 9.7 %copy-start.4 = (bf16[2,3,40,2240]{3,2,1,0:T(8,128)(2,1)S(1)}, bf16[2,3,40,2240]{3,2,1,0:T(8,128)(2,1)}, u32[]{:S(2)}) copy-start(bf16[2,3,40,2240]{3,2,1,0:T(8,128)(2,1)} %param.8) | copy-start | bytes 3225604
  (2 other events, 1.3 us)

commit v6 on v5

--- a/solution.py
+++ b/solution.py
@@ -123,7 +123,8 @@
     if frame:
         prev_refs = [held_ref.at[0, r] for r in range(own_ref.shape[1])]
     else:
-        prev_refs, refs = [ref.at[0] for ref in refs[:3]], refs[3:]
+        ends_ref, middle_ref, *refs = refs
+        prev_refs = [ends_ref.at[0], middle_ref.at[0], ends_ref.at[1]]
     top_ref, bottom_ref, time_ref, space_ref, bias_ref = refs[:5]
     cur_ref = held_ref.at[-1 % held_ref.shape[0]]
     rows, columns, channels = cur_ref.shape
@@ -285,7 +286,9 @@
 
 
 def edge_kernel(own_ref, *refs, frame):
-    *old_refs, time_ref, _, up_ref, down_ref, now_ref, old_ref, sems = refs
+    up_ref, down_ref, token_ref, now_ref, old_ref, sems = refs[-6:]
+    ends_ref, time_ref = (None, refs[0]) if frame else refs[:2]
+    token_ref[...] = jnp.zeros_like(token_ref)
     rows, channels = own_ref.shape[1], own_ref.shape[3]
     ends = (0, rows - 1)
     copies = []
@@ -298,7 +301,7 @@
         copy.start()
 
     for at, out_ref in enumerate((up_ref, down_ref)):
-        old_view = old_ref.at[at] if frame else old_refs[at].at[0]
+        old_view = old_ref.at[at] if frame else ends_ref.at[at]
         for copy in copies[at]:
             copy.wait()
 
@@ -318,18 +321,18 @@
             blend(pl.ds(channels // wide * wide, channels % wide))
 
 
-def edges(hidden, frame, old, times, token):
+def edges(hidden, frame, old, times, *waits):
     channels, columns = hidden.shape[3], hidden.shape[2]
     held = pl.BlockSpec(memory_space=pltpu.VMEM)
     anywhere = pl.BlockSpec(memory_space=pl.ANY)
-    args = [pltpu.with_memory_space_constraint(hidden, pltpu.HBM), *old, times, token]
+    args = [pltpu.with_memory_space_constraint(hidden, pltpu.HBM), *old, times, *waits]
     line = jax.ShapeDtypeStruct((1, columns, channels), jnp.bfloat16)
     pair = pltpu.VMEM((2, columns, channels), jnp.bfloat16)
     return pl.pallas_call(
         functools.partial(edge_kernel, frame=frame),
-        out_shape=(line, line),
-        in_specs=[anywhere] + [held] * len(old) + [held, anywhere],
-        out_specs=(held, held),
+        out_shape=(line, line, jax.ShapeDtypeStruct((8, LANES), jnp.float32)),
+        in_specs=[anywhere] + [held] * (len(old) + 1) + [anywhere] * len(waits),
+        out_specs=(held, held, held),
         scratch_shapes=[pair, pair, pltpu.SemaphoreType.DMA((2, 2, columns // 8))],
         compiler_params=pltpu.CompilerParams(vmem_limit_bytes=8 << 20),
         cost_estimate=pl.CostEstimate(
@@ -341,10 +344,10 @@
 
 def copy_kernel(source_ref, *refs, frame, rows):
     *_, token_ref, sems = refs
-    outs = refs[-2 - len(rows) : -2]
+    out_ref = refs[-3]
     copies = []
-    for at, (r, out_ref) in enumerate(zip(rows, outs)):
-        copies += row_copies(source_ref.at[frame, r], out_ref.at[0], sems.at[at])
+    for at, r in enumerate(rows):
+        copies += row_copies(source_ref.at[frame, r], out_ref.at[at], sems.at[at])
     for copy in copies:
         copy.start()
     token_ref[...] = jnp.zeros_like(token_ref)
@@ -358,16 +361,32 @@
     anywhere = pl.BlockSpec(memory_space=pl.ANY)
     return pl.pallas_call(
         functools.partial(copy_kernel, frame=frame, rows=rows),
-        out_shape=[jax.ShapeDtypeStruct((1, columns, channels), jnp.bfloat16) for _ in rows]
-        + [jax.ShapeDtypeStruct((8, LANES), jnp.float32)],
+        out_shape=(
+            jax.ShapeDtypeStruct((len(rows), columns, channels), jnp.bfloat16),
+            jax.ShapeDtypeStruct((8, LANES), jnp.float32),
+        ),
         in_specs=[anywhere] * len(args),
-        out_specs=[pl.BlockSpec(memory_space=pltpu.VMEM)] * (len(rows) + 1),
+        out_specs=(pl.BlockSpec(memory_space=pltpu.VMEM),) * 2,
         scratch_shapes=[pltpu.SemaphoreType.DMA((len(rows), columns // 8))],
         cost_estimate=pl.CostEstimate(
             flops=0, bytes_accessed=4 * len(rows) * columns * channels, transcendentals=0
         ),
         name="copied_rows",
     )(*args)
+
+
+def reached_kernel(*refs):
+    refs[-1][...] = jnp.zeros_like(refs[-1])
+
+
+def reached(*arrays):
+    return pl.pallas_call(
+        reached_kernel,
+        out_shape=jax.ShapeDtypeStruct((8, LANES), jnp.float32),
+        in_specs=[pl.BlockSpec(memory_space=pltpu.VMEM)] * len(arrays),
+        out_specs=pl.BlockSpec(memory_space=pltpu.VMEM),
+        name="reached",
+    )(*arrays)
 
 
 def whole(body, out_shape, flops, *args, token=None):
@@ -410,8 +429,8 @@
     wide = lambda value: value.astype(jnp.float32)
 
     weights = time_weight, space_weight, conv_bias[None]
-    prev_first, prev_last, token = copied_rows(hidden, frames - 1, (0, rows - 1))
-    prev_first, prev_last = ahead(prev_first, frame_axes, 1), ahead(prev_last, frame_axes, 1)
+    prev_ends, token = copied_rows(hidden, frames - 1, (0, rows - 1))
+    prev_ends = ahead(prev_ends, frame_axes, 1)
     partial = whole(
         partial_kernel,
         jax.ShapeDtypeStruct((SHARES * SHARE_ROWS, LANES), jnp.bfloat16),
@@ -433,35 +452,36 @@
     for k in (1, 2, 4):
         sent = narrow(column)
         if k == 2:
-            sent, prev_first = lax.optimization_barrier((sent, prev_first))
-        if k == 1:
-            up_edge, down_edge = edges(hidden, frames - 1, (), time_weight, sent)
+            up_edge, down_edge, edge_token = edges(hidden, frames - 1, (), time_weight, sent)
             top, bottom = ahead(down_edge, "row", 1), ahead(up_edge, "row", -1)
             ffn_out = conv_frame(hidden, frames - 1, (), top, bottom, weights)
+            sent, edge_token = lax.optimization_barrier((sent, edge_token))
+        if k == 4:
+            prev_middle, copy_token = copied_rows(hidden, frames - 1, (1,), sent, edge_token)
         pairs = [
             (z * INNER + at, (z + k) * INNER + at)
             for z in range(planes - k)
             for at in range(INNER - 1)
         ]
         arrived = lax.ppermute(sent, frame_axes, pairs)
-        if k == 4:
-            arrived, ffn_out = lax.optimization_barrier((arrived, ffn_out))
         column = column + wide(arrived)
         before = before + wide(arrived)
     prefix = before + held
-    closed, opened = lax.optimization_barrier((narrow(prefix), narrow(before), prev_last))[:2]
-    up_edge, down_edge = edges(hidden, 0, (prev_first, prev_last), time_weight, closed)
-    top_first, bottom_first = ahead(down_edge, "row", 1), ahead(up_edge, "row", -1)
+    edge_token = reached(top, bottom, copy_token)
+    closed, opened, prev_ends, edge_token = lax.optimization_barrier(
+        (narrow(prefix), narrow(before), prev_ends, edge_token)
+    )
     for k in range(1, INNER):
         sent = jnp.where(x + k < INNER, closed, opened)
         prefix = prefix + wide(ahead(sent, "x", k, True))
     prefix = narrow(prefix)
-    prev_middle, _ = copied_rows(hidden, frames - 1, (1,), prefix)
-    prev_middle = ahead(prev_middle, frame_axes, 1)
+    prev_middle = ahead(lax.optimization_barrier((prev_middle, prefix))[0], frame_axes, 1)
+    up_edge, down_edge, _ = edges(hidden, 0, (prev_ends,), time_weight, prefix, edge_token)
+    top_first, bottom_first = ahead(down_edge, "row", 1), ahead(up_edge, "row", -1)
 
     state = jnp.concatenate([prefix, exchange(prefix, "row", 4)], axis=0)
     state = jnp.concatenate([state, exchange(state, "row", 2)], axis=0)
-    state, prev_middle = lax.optimization_barrier((state, prev_middle))
+    state, prev_middle, ffn_out = lax.optimization_barrier((state, prev_middle, ffn_out))
     state = jnp.concatenate([state, exchange(state, "row", 1)], axis=0)
     attention = whole(
         mixed_kernel,
@@ -473,7 +493,7 @@
         norm_gain[None],
     )
     ffn_out = conv_frame(
-        hidden, 0, (prev_first, prev_middle, prev_last), top_first, bottom_first, weights, ffn_out
+        hidden, 0, (prev_ends, prev_middle), top_first, bottom_first, weights, ffn_out
     )
     return (attention.reshape(query_tokens.shape), ffn_out)
 

time: 130 us -> 127 us (0.977)
  other arithmetic: 3.32 us -> 0.37 us
  Pallas kernels: 34.9 us -> 37.5 us
  waiting for transfers between devices: 23.4 us -> 20.9 us
  local copies, waits for them, and re-layouts: 0.82 us -> 2.4 us
    ppermute x3, starting transfers between devices: 23.6 us -> 18.7 us  [per_device(): arrived = lax.ppermute(sent, frame_axes, pairs)]
    ppermute x6, waiting for transfers between devices: 19.9 us -> 16.5 us  [exchange(): lax.ppermute(value, axis, [(i, i ^ flip) for i in range(lax.axis_size(axi...]
    convert_element_type x6, other arithmetic: 3.14 us -> 0.21 us  [per_device(): narrow = lambda value: value.astype(jnp.bfloat16)]
    ppermute x10 -> x9, starting transfers between devices: 29.8 us -> 32 us  [ahead(): return lax.ppermute(value, axis, pairs)]
    ppermute x6, starting transfers between devices: 10.7 us -> 12.8 us  [exchange(): lax.ppermute(value, axis, [(i, i ^ flip) for i in range(lax.axis_size(axi...]
    pallas_call x0 -> x1, Pallas kernels: none -> 2.04 us  [reached(): pl.pallas_call(reached_kernel, out_shape=jax.ShapeDtypeStruct((8, LANES),...]
    unnamed x28 -> x26, local copies, waits for them, and re-layouts: 0.75 us -> 2.33 us
  transfers between devices with their start and end apart: 20 -> 19, of which waited for: 8 -> 7; matrix products, arithmetic and copies ran while one was open for 1% -> 0% of each run, Pallas kernels for 21% -> 25%
where the time goes in v6:
time: 127 us; the launch traced here: 126 us
  starting transfers between devices  64.1 us (50%)
  Pallas kernels  37.5 us (30%)
  waiting for transfers between devices  20.9 us (16%)
  local copies, waits for them, and re-layouts  2.4 us (2%)
    ppermute x9, starting transfers between devices, ahead(): return lax.ppermute(value, axis, pairs)  32 us
    pallas_call x2, Pallas kernels, conv_frame(): pl.pallas_call(functools.partial(conv_kernel, frame), out_shape=jax.Shape...  20.4 us
    ppermute x3, starting transfers between devices, per_device(): arrived = lax.ppermute(sent, frame_axes, pairs)  18.7 us
    ppermute x6, waiting for transfers between devices, exchange(): lax.ppermute(value, axis, [(i, i ^ flip) for i in range(lax.axis_size(axi...  16.5 us
    ppermute x6, starting transfers between devices, exchange(): lax.ppermute(value, axis, [(i, i ^ flip) for i in range(lax.axis_size(axi...  12.8 us
    pallas_call x2, Pallas kernels, edges(): pl.pallas_call(functools.partial(edge_kernel, frame=frame), out_shape=(li...  6.75 us
    pallas_call x2, Pallas kernels, copied_rows(): pl.pallas_call(functools.partial(copy_kernel, frame=frame, rows=rows), ou...  5.18 us
    pallas_call x2, Pallas kernels, whole(): pl.pallas_call(body, out_shape=out_shape, in_specs=specs, out_specs=pl.Bl...  3.13 us
  transfers between devices with their start and end apart: 19, of which 7 were waited for; matrix products, arithmetic and copies ran while one was open for 0% of the time, Pallas kernels for 25%

profile of v6, /device:TPU:1, one launch (start us, length us, event | category | flops | bytes accessed | tf_op | source)
XLA Modules:
  0.0 126.4 jit_solution(12899555996357346398)
XLA Ops:
  0.7 3.0 %copied_rows.2 = (bf16[2,40,11200]{2,1,0:T(8,128)(2,1)}, f32[8,128]{1,0:T(8,128)}) custom-call(bf16[2,3,40,11200]{3,2,1,0:T(8,128)(2,1)} %own_ref.7), custom_call_target="tpu_custom_call" | custom-call | bytes 3584000 | tf_op jit(solution)/shard_map/copied_rows/pallas_call | solution.py:362
  5.3 3.3 %collective-permute-start = (bf16[4,256,128]{2,1,0:T(8,128)(2,1)S(1)}, bf16[4,256,128]{2,1,0:T(8,128)(2,1)S(1)}, u32[]{:S(2)}, u32[]{:S(2)}) collective-permute-start(bf16[4,256,128]{2,1,0:T(8,128)(2,1)S(1)} %bitcast.23), channel_id=1, source_target_pairs={{0,1},{1,0},{2,3},{3,2},{4,5},{5,4},{6,7},{7,6},{8,9},{9,8},{10,11... | collective-permute-start | bytes 786440 | tf_op jit(solution)/shard_map/ppermute | solution.py:410
  8.6 1.2 collective-permute-done
  10.0 2.8 %collective-permute-start.7 = (bf16[2,40,11200]{2,1,0:T(8,128)(2,1)}, bf16[2,40,11200]{2,1,0:T(8,128)(2,1)S(1)}, u32[]{:S(2)}, u32[]{:S(2)}) collective-permute-start(bf16[2,40,11200]{2,1,0:T(8,128)(2,1)} %get-tuple-element.24), channel_id=1, source_target_pairs={{0,8},{8,16},{16,24},{24,32},{32,40},{40,48},{48,56},{56,64},{64,7... | collective-permute-start | bytes 5376008 | tf_op jit(solution)/shard_map/ppermute | solution.py:416
  12.7 1.9 %collective-permute-done.1 = bf16[2,256,128]{2,1,0:T(8,128)(2,1)S(1)} collective-permute-done((bf16[2,256,128]{2,1,0:T(8,128)(2,1)S(1)}, bf16[2,256,128]{2,1,0:T(8,128)(2,1)S(1)}, u32[]{:S(2)}, u32[]{:S(2)}) %collective-permute-start.1) | collective-permute-done | bytes 131104 | tf_op jit(solution)/shard_map/ppermute | solution.py:410
  14.7 1.3 collective-permute-start.2
  16.0 3.4 %collective-permute-done.2 = bf16[256,128]{1,0:T(8,128)(2,1)S(1)} collective-permute-done((bf16[256,128]{1,0:T(8,128)(2,1)S(1)}, bf16[256,128]{1,0:T(8,128)(2,1)S(1)}, u32[]{:S(2)}, u32[]{:S(2)}) %collective-permute-start.2) | collective-permute-done | bytes 65568 | tf_op jit(solution)/shard_map/ppermute | solution.py:410
  20.2 2.1 %collective-permute-start.4 = (bf16[256,128]{1,0:T(8,128)(2,1)S(1)}, bf16[256,128]{1,0:T(8,128)(2,1)S(1)}, u32[]{:S(2)}, u32[]{:S(2)}) collective-permute-start(bf16[256,128]{1,0:T(8,128)(2,1)S(1)} %fusion.3), channel_id=1, source_target_pairs={{0,32},{8,40},{16,48},{32,64},{40,72},{48,80},{64,96},{72,104},{80... | collective-permute-start | bytes 196616 | tf_op jit(solution)/shard_map/ppermute | solution.py:466
  22.3 1.3 %collective-permute-done.4 = bf16[256,128]{1,0:T(8,128)(2,1)S(1)} collective-permute-done((bf16[256,128]{1,0:T(8,128)(2,1)S(1)}, bf16[256,128]{1,0:T(8,128)(2,1)S(1)}, u32[]{:S(2)}, u32[]{:S(2)}) %collective-permute-start.4) | collective-permute-done | bytes 65568 | tf_op jit(solution)/shard_map/ppermute | solution.py:466
  23.6 3.9 %edges.2 = (bf16[1,40,11200]{2,1,0:T(8,128)(2,1)}, bf16[1,40,11200]{2,1,0:T(8,128)(2,1)}, f32[8,128]{1,0:T(8,128)S(1)}) custom-call(bf16[2,3,40,11200]{3,2,1,0:T(8,128)(2,1)} %own_ref.7, f32[2,11200]{1,0:T(2,128)S(1)} %copy-done.3, bf16[256,128]{1,0:T(8,128)(2,1)S(1)} %fusion.7.refs_1_), custom_call_target="tpu_custom_call" | custom-call | flops 2688000 | bytes 5376000 | tf_op jit(solution)/shard_map/edges/pallas_call | solution.py:331
  27.5 6.0 %collective-permute-start.8 = (bf16[1,40,11200]{2,1,0:T(8,128)(2,1)}, bf16[1,40,11200]{2,1,0:T(8,128)(2,1)S(1)}, u32[]{:S(2)}, u32[]{:S(2)}) collective-permute-start(bf16[1,40,11200]{2,1,0:T(8,128)(2,1)} %get-tuple-element.25), channel_id=1, source_target_pairs={{0,1},{1,2},{2,3},{3,4},{4,5},{5,6},{6,7},{8,9},{9,10},{10,11},{11... | collective-permute-start | bytes 2688008 | tf_op jit(solution)/shard_map/ppermute | solution.py:416
  33.5 1.9 %collective-permute-start.9 = (bf16[1,40,11200]{2,1,0:T(8,128)(2,1)}, bf16[1,40,11200]{2,1,0:T(8,128)(2,1)}, u32[]{:S(2)}, u32[]{:S(2)}) collective-permute-start(bf16[1,40,11200]{2,1,0:T(8,128)(2,1)} %get-tuple-element.26), channel_id=1, source_target_pairs={{1,0},{2,1},{3,2},{4,3},{5,4},{6,5},{7,6},{9,8},{10,9},{11,10},{12... | collective-permute-start | bytes 2688008 | tf_op jit(solution)/shard_map/ppermute | solution.py:416
  35.4 5.3 %collective-permute-start.5 = (bf16[256,128]{1,0:T(8,128)(2,1)S(1)}, bf16[256,128]{1,0:T(8,128)(2,1)S(1)}, u32[]{:S(2)}, u32[]{:S(2)}) collective-permute-start(bf16[256,128]{1,0:T(8,128)(2,1)S(1)} %fusion.7.refs_1_), channel_id=1, source_target_pairs={{0,64},{8,72},{16,80},{32,96},{40,104},{48,112},{64,128},{72,136},... | collective-permute-start | bytes 196616 | tf_op jit(solution)/shard_map/ppermute | solution.py:466
  40.8 1.3 %collective-permute-done.5 = bf16[256,128]{1,0:T(8,128)(2,1)S(1)} collective-permute-done((bf16[256,128]{1,0:T(8,128)(2,1)S(1)}, bf16[256,128]{1,0:T(8,128)(2,1)S(1)}, u32[]{:S(2)}, u32[]{:S(2)}) %collective-permute-start.5) | collective-permute-done | bytes 65568 | tf_op jit(solution)/shard_map/ppermute | solution.py:466
  42.2 11.2 %collective-permute-start.6 = (bf16[256,128]{1,0:T(8,128)(2,1)S(1)}, bf16[256,128]{1,0:T(8,128)(2,1)S(1)}, u32[]{:S(2)}, u32[]{:S(2)}) collective-permute-start(bf16[256,128]{1,0:T(8,128)(2,1)S(1)} %fusion.1.refs_0_), channel_id=1, source_target_pairs={{0,128},{8,136},{16,144},{32,160},{40,168},{48,176},{64,192},{72,2... | collective-permute-start | bytes 196616 | tf_op jit(solution)/shard_map/ppermute | solution.py:466
  53.4 2.2 %copied_rows.3 = (bf16[1,40,11200]{2,1,0:T(8,128)(2,1)}, f32[8,128]{1,0:T(8,128)}) custom-call(bf16[2,3,40,11200]{3,2,1,0:T(8,128)(2,1)} %own_ref.7, bf16[256,128]{1,0:T(8,128)(2,1)} %copy-done.11, f32[8,128]{1,0:T(8,128)} %copy-done.9), custom_call_target="tpu_custom_call" | custom-call | bytes 1792000 | tf_op jit(solution)/shard_map/copied_rows/pallas_call | solution.py:362
  55.7 0.9 copy-done
  56.6 2.0 %reached.1.refs_3_ = f32[8,128]{1,0:T(8,128)} custom-call(bf16[1,40,11200]{2,1,0:T(8,128)(2,1)} %copy-done, bf16[1,40,11200]{2,1,0:T(8,128)(2,1)} %collective-permute-done.9.refs_1_, f32[8,128]{1,0:T(8,128)} %get-tuple-element.28.refs_2_), custom_call_target="tpu_custom_call" | custom-call | tf_op jit(solution)/shard_map/reached/pallas_call | solution.py:383
  58.7 1.0 collective-permute-start.10
  59.7 7.1 %collective-permute-start.11 = (bf16[256,128]{1,0:T(8,128)(2,1)S(1)}, bf16[256,128]{1,0:T(8,128)(2,1)S(1)}, u32[]{:S(2)}, u32[]{:S(2)}) collective-permute-start(bf16[256,128]{1,0:T(8,128)(2,1)S(1)} %get-tuple-element.48), channel_id=1, source_target_pairs={{0,16},{8,24},{16,0},{24,8},{1,17},{9,25},{17,1},{25,9},{2,18},{10... | collective-permute-start | bytes 196616 | tf_op jit(solution)/shard_map/ppermute | solution.py:416
  66.8 2.0 %collective-permute-start.12 = (bf16[256,128]{1,0:T(8,128)(2,1)S(1)}, bf16[256,128]{1,0:T(8,128)(2,1)S(1)}, u32[]{:S(2)}, u32[]{:S(2)}) collective-permute-start(bf16[256,128]{1,0:T(8,128)(2,1)S(1)} %get-tuple-element.47), channel_id=1, source_target_pairs={{0,24},{8,0},{16,8},{24,16},{1,25},{9,1},{17,9},{25,17},{2,26},{10... | collective-permute-start | bytes 196616 | tf_op jit(solution)/shard_map/ppermute | solution.py:416
  68.8 1.8 %collective-permute-done.11 = bf16[256,128]{1,0:T(8,128)(2,1)S(1)} collective-permute-done((bf16[256,128]{1,0:T(8,128)(2,1)S(1)}, bf16[256,128]{1,0:T(8,128)(2,1)S(1)}, u32[]{:S(2)}, u32[]{:S(2)}) %collective-permute-start.11) | collective-permute-done | bytes 65568 | tf_op jit(solution)/shard_map/ppermute | solution.py:416
  70.6 3.2 %collective-permute-start.15 = (bf16[1,40,11200]{2,1,0:T(8,128)(2,1)}, bf16[1,40,11200]{2,1,0:T(8,128)(2,1)S(1)}, u32[]{:S(2)}, u32[]{:S(2)}) collective-permute-start(bf16[1,40,11200]{2,1,0:T(8,128)(2,1)} %get-tuple-element.32), channel_id=1, source_target_pairs={{0,8},{8,16},{16,24},{24,32},{32,40},{40,48},{48,56},{56,64},{64,7... | collective-permute-start | bytes 2688008 | tf_op jit(solution)/shard_map/ppermute | solution.py:416
  74.5 2.9 %edges.3 = (bf16[1,40,11200]{2,1,0:T(8,128)(2,1)S(1)}, bf16[1,40,11200]{2,1,0:T(8,128)(2,1)S(1)}, f32[8,128]{1,0:T(8,128)}) custom-call(bf16[2,3,40,11200]{3,2,1,0:T(8,128)(2,1)} %own_ref.7, bf16[2,40,11200]{2,1,0:T(8,128)(2,1)S(1)} %collective-permute-done.7.refs_0_, f32[2,11200]{1,0:T(2,128)S(1)} %copy-done.3, ...), custom_call_target="tpu_custom_call" | custom-call | flops 2688000 | bytes 5376000 | tf_op jit(solution)/shard_map/edges/pallas_call | solution.py:331
  77.4 6.2 %collective-permute-start.17 = (bf16[1,40,11200]{2,1,0:T(8,128)(2,1)S(1)}, bf16[1,40,11200]{2,1,0:T(8,128)(2,1)S(1)}, u32[]{:S(2)}, u32[]{:S(2)}) collective-permute-start(bf16[1,40,11200]{2,1,0:T(8,128)(2,1)S(1)} %get-tuple-element.37), channel_id=1, source_target_pairs={{0,1},{1,2},{2,3},{3,4},{4,5},{5,6},{6,7},{8,9},{9,10},{10,11},{11... | collective-permute-start | bytes 2688008 | tf_op jit(solution)/shard_map/ppermute | solution.py:416
  83.6 1.9 %collective-permute-start.18 = (bf16[1,40,11200]{2,1,0:T(8,128)(2,1)S(1)}, bf16[1,40,11200]{2,1,0:T(8,128)(2,1)S(1)}, u32[]{:S(2)}, u32[]{:S(2)}) collective-permute-start(bf16[1,40,11200]{2,1,0:T(8,128)(2,1)S(1)} %get-tuple-element.38), channel_id=1, source_target_pairs={{1,0},{2,1},{3,2},{4,3},{5,4},{6,5},{7,6},{9,8},{10,9},{11,10},{12... | collective-permute-start | bytes 2688008 | tf_op jit(solution)/shard_map/ppermute | solution.py:416
  85.5 2.7 %collective-permute-start.13 = (bf16[256,128]{1,0:T(8,128)(2,1)S(1)}, bf16[256,128]{1,0:T(8,128)(2,1)S(1)}, u32[]{:S(2)}, u32[]{:S(2)}) collective-permute-start(bf16[256,128]{1,0:T(8,128)(2,1)S(1)} %add_convert_fusion.refs_2_), channel_id=1, source_target_pairs={{0,4},{1,5},{2,6},{3,7},{4,0},{5,1},{6,2},{7,3},{8,12},{9,13},{10,... | collective-permute-start | bytes 196616 | tf_op jit(solution)/shard_map/ppermute | solution.py:410
  88.2 10.0 %collective-permute-done.13 = bf16[256,128]{1,0:T(8,128)(2,1)S(1)} collective-permute-done((bf16[256,128]{1,0:T(8,128)(2,1)S(1)}, bf16[256,128]{1,0:T(8,128)(2,1)S(1)}, u32[]{:S(2)}, u32[]{:S(2)}) %collective-permute-start.13) | collective-permute-done | bytes 65568 | tf_op jit(solution)/shard_map/ppermute | solution.py:410
  98.3 10.8 %conv_frame.2.refs_7_ = bf16[2,3,40,5600]{3,2,1,0:T(8,128)(2,1)} custom-call(bf16[2,3,40,11200]{3,2,1,0:T(8,128)(2,1)} %own_ref.7, bf16[1,40,11200]{2,1,0:T(8,128)(2,1)S(1)} %copy-done.1, bf16[1,40,11200]{2,1,0:T(8,128)(2,1)} %collective-permute-done.9.refs_1_, f32[2,11200]{1,0:T(2,128)S(1)} %copy-done.3, f32[3,3,11200]{2,1,0:T(4,128)S(1)} %copy-done.2, ...), custom_call_target="tpu_custom_call" | custom-call | flops 53760000 | bytes 8064000 | tf_op jit(solution)/shard_map/conv_frame/pallas_call | solution.py:259
  109.2 5.3 %collective-permute-start.16 = (bf16[1024,128]{1,0:T(8,128)(2,1)S(1)}, bf16[1024,128]{1,0:T(8,128)(2,1)S(1)}, u32[]{:S(2)}, u32[]{:S(2)}) collective-permute-start(bf16[1024,128]{1,0:T(8,128)(2,1)S(1)} %pad_maximum_fusion.1), channel_id=1, source_target_pairs={{0,1},{1,0},{2,3},{3,2},{4,5},{5,4},{6,7},{7,6},{8,9},{9,8},{10,11... | collective-permute-start | bytes 786440 | tf_op jit(solution)/shard_map/ppermute | solution.py:410
  114.5 9.6 %conv_frame.3 = bf16[2,3,40,5600]{3,2,1,0:T(8,128)(2,1)} custom-call(bf16[2,3,40,11200]{3,2,1,0:T(8,128)(2,1)} %own_ref.7, bf16[2,40,11200]{2,1,0:T(8,128)(2,1)S(1)} %collective-permute-done.7.refs_0_, bf16[1,40,11200]{2,1,0:T(8,128)(2,1)S(1)} %collective-permute-done.15.refs_1_, ...), custom_call_target="tpu_custom_call", output_to_operand_aliasing={{}: (8, {})} | custom-call | flops 53760000 | bytes 8064000 | tf_op jit(solution)/shard_map/conv_frame/pallas_call | solution.py:259
  124.2 2.2 %mixed_kernel.1 = bf16[240,2240]{1,0:T(8,128)(2,1)} custom-call(s32[1]{0:T(128)} %bitcast.row_ref, bf16[240,2240]{1,0:T(8,128)(2,1)S(1)} %bitcast.18, bf16[2048,128]{1,0:T(8,128)(2,1)S(1)} %pad_maximum_fusion.state_ref, f32[1,2240]{1,0:T(1,128)S(1)} %broadcast_in_dim.7.gain_ref), custom_call_target="tpu_custom_call" | custom-call | flops 275251200 | bytes 3145728 | tf_op jit(solution)/shard_map/mixed_kernel/pallas_call | solution.py:398
  (57 shorter events, 3.6 us)
Async XLA Ops:
  0.6 3.0 %copy-start.4 = (bf16[2,3,40,2240]{3,2,1,0:T(8,128)(2,1)S(1)}, bf16[2,3,40,2240]{3,2,1,0:T(8,128)(2,1)}, u32[]{:S(2)}) copy-start(bf16[2,3,40,2240]{3,2,1,0:T(8,128)(2,1)} %param.9) | copy-start | bytes 3225604
  0.6 3.0 %copy-start.5 = (bf16[2,3,40,2240]{3,2,1,0:T(8,128)(2,1)S(1)}, bf16[2,3,40,2240]{3,2,1,0:T(8,128)(2,1)}, u32[]{:S(2)}) copy-start(bf16[2,3,40,2240]{3,2,1,0:T(8,128)(2,1)} %param.10) | copy-start | bytes 3225604
  3.6 0.7 copy-start.10
  5.3 18.3 %copy-start.3 = (f32[2,11200]{1,0:T(2,128)S(1)}, f32[2,11200]{1,0:T(2,128)}, u32[]{:S(2)}) copy-start(f32[2,11200]{1,0:T(2,128)} %refs_4_.1) | copy-start | bytes 268804
  5.3 4.5 %collective-permute-start = (bf16[4,256,128]{2,1,0:T(8,128)(2,1)S(1)}, bf16[4,256,128]{2,1,0:T(8,128)(2,1)S(1)}, u32[]{:S(2)}, u32[]{:S(2)}) collective-permute-start(bf16[4,256,128]{2,1,0:T(8,128)(2,1)S(1)} %bitcast.23), channel_id=1, source_target_pairs={{0,1},{1,0},{2,3},{3,2},{4,5},{5,4},{6,7},{7,6},{8,9},{9,8},{10,11... | collective-permute-start | bytes 786440 | tf_op jit(solution)/shard_map/ppermute | solution.py:410
  9.9 4.8 %collective-permute-start.1 = (bf16[2,256,128]{2,1,0:T(8,128)(2,1)S(1)}, bf16[2,256,128]{2,1,0:T(8,128)(2,1)S(1)}, u32[]{:S(2)}, u32[]{:S(2)}) collective-permute-start(bf16[2,256,128]{2,1,0:T(8,128)(2,1)S(1)} %slice.42), channel_id=1, source_target_pairs={{0,2},{1,3},{2,0},{3,1},{4,6},{5,7},{6,4},{7,5},{8,10},{9,11},{10,... | collective-permute-start | bytes 393224 | tf_op jit(solution)/shard_map/ppermute | solution.py:410
  10.0 48.7 %collective-permute-start.7 = (bf16[2,40,11200]{2,1,0:T(8,128)(2,1)}, bf16[2,40,11200]{2,1,0:T(8,128)(2,1)S(1)}, u32[]{:S(2)}, u32[]{:S(2)}) collective-permute-start(bf16[2,40,11200]{2,1,0:T(8,128)(2,1)} %get-tuple-element.24), channel_id=1, source_target_pairs={{0,8},{8,16},{16,24},{24,32},{32,40},{40,48},{48,56},{56,64},{64,7... | collective-permute-start | bytes 5376008 | tf_op jit(solution)/shard_map/ppermute | solution.py:416
  14.7 4.7 %collective-permute-start.2 = (bf16[256,128]{1,0:T(8,128)(2,1)S(1)}, bf16[256,128]{1,0:T(8,128)(2,1)S(1)}, u32[]{:S(2)}, u32[]{:S(2)}) collective-permute-start(bf16[256,128]{1,0:T(8,128)(2,1)S(1)} %fusion.6), channel_id=1, source_target_pairs={{0,4},{1,5},{2,6},{3,7},{4,0},{5,1},{6,2},{7,3},{8,12},{9,13},{10,... | collective-permute-start | bytes 196616 | tf_op jit(solution)/shard_map/ppermute | solution.py:410
  19.4 0.7 collective-permute-start.3
  20.2 3.4 %collective-permute-start.4 = (bf16[256,128]{1,0:T(8,128)(2,1)S(1)}, bf16[256,128]{1,0:T(8,128)(2,1)S(1)}, u32[]{:S(2)}, u32[]{:S(2)}) collective-permute-start(bf16[256,128]{1,0:T(8,128)(2,1)S(1)} %fusion.3), channel_id=1, source_target_pairs={{0,32},{8,40},{16,48},{32,64},{40,72},{48,80},{64,96},{72,104},{80... | collective-permute-start | bytes 196616 | tf_op jit(solution)/shard_map/ppermute | solution.py:466
  27.5 13.3 %copy-start.9 = (f32[8,128]{1,0:T(8,128)}, f32[8,128]{1,0:T(8,128)S(1)}, u32[]{:S(2)}) copy-start(f32[8,128]{1,0:T(8,128)S(1)} %get-tuple-element.27.refs_1_) | copy-start | bytes 12292
  27.5 28.2 %collective-permute-start.8 = (bf16[1,40,11200]{2,1,0:T(8,128)(2,1)}, bf16[1,40,11200]{2,1,0:T(8,128)(2,1)S(1)}, u32[]{:S(2)}, u32[]{:S(2)}) collective-permute-start(bf16[1,40,11200]{2,1,0:T(8,128)(2,1)} %get-tuple-element.25), channel_id=1, source_target_pairs={{0,1},{1,2},{2,3},{3,4},{4,5},{5,6},{6,7},{8,9},{9,10},{10,11},{11... | collective-permute-start | bytes 2688008 | tf_op jit(solution)/shard_map/ppermute | solution.py:416
  33.5 22.2 %collective-permute-start.9 = (bf16[1,40,11200]{2,1,0:T(8,128)(2,1)}, bf16[1,40,11200]{2,1,0:T(8,128)(2,1)}, u32[]{:S(2)}, u32[]{:S(2)}) collective-permute-start(bf16[1,40,11200]{2,1,0:T(8,128)(2,1)} %get-tuple-element.26), channel_id=1, source_target_pairs={{1,0},{2,1},{3,2},{4,3},{5,4},{6,5},{7,6},{9,8},{10,9},{11,10},{12... | collective-permute-start | bytes 2688008 | tf_op jit(solution)/shard_map/ppermute | solution.py:416
  35.4 6.7 %collective-permute-start.5 = (bf16[256,128]{1,0:T(8,128)(2,1)S(1)}, bf16[256,128]{1,0:T(8,128)(2,1)S(1)}, u32[]{:S(2)}, u32[]{:S(2)}) collective-permute-start(bf16[256,128]{1,0:T(8,128)(2,1)S(1)} %fusion.7.refs_1_), channel_id=1, source_target_pairs={{0,64},{8,72},{16,80},{32,96},{40,104},{48,112},{64,128},{72,136},... | collective-permute-start | bytes 196616 | tf_op jit(solution)/shard_map/ppermute | solution.py:466
  42.1 11.3 %copy-start.11 = (bf16[256,128]{1,0:T(8,128)(2,1)}, bf16[256,128]{1,0:T(8,128)(2,1)S(1)}, u32[]{:S(2)}) copy-start(bf16[256,128]{1,0:T(8,128)(2,1)S(1)} %fusion.1.refs_0_) | copy-start | bytes 196612
  42.2 13.5 %collective-permute-start.6 = (bf16[256,128]{1,0:T(8,128)(2,1)S(1)}, bf16[256,128]{1,0:T(8,128)(2,1)S(1)}, u32[]{:S(2)}, u32[]{:S(2)}) collective-permute-start(bf16[256,128]{1,0:T(8,128)(2,1)S(1)} %fusion.1.refs_0_), channel_id=1, source_target_pairs={{0,128},{8,136},{16,144},{32,160},{40,168},{48,176},{64,192},{72,2... | collective-permute-start | bytes 196616 | tf_op jit(solution)/shard_map/ppermute | solution.py:466
  55.7 0.9 copy-start
  58.7 10.1 %collective-permute-start.10 = (bf16[256,128]{1,0:T(8,128)(2,1)S(1)}, bf16[256,128]{1,0:T(8,128)(2,1)S(1)}, u32[]{:S(2)}, u32[]{:S(2)}) collective-permute-start(bf16[256,128]{1,0:T(8,128)(2,1)S(1)} %get-tuple-element.46), channel_id=1, source_target_pairs={{0,8},{8,16},{16,24},{24,0},{1,9},{9,17},{17,25},{25,1},{2,10},{10... | collective-permute-start | bytes 196616 | tf_op jit(solution)/shard_map/ppermute | solution.py:416
  59.7 10.8 %collective-permute-start.11 = (bf16[256,128]{1,0:T(8,128)(2,1)S(1)}, bf16[256,128]{1,0:T(8,128)(2,1)S(1)}, u32[]{:S(2)}, u32[]{:S(2)}) collective-permute-start(bf16[256,128]{1,0:T(8,128)(2,1)S(1)} %get-tuple-element.48), channel_id=1, source_target_pairs={{0,16},{8,24},{16,0},{24,8},{1,17},{9,25},{17,1},{25,9},{2,18},{10... | collective-permute-start | bytes 196616 | tf_op jit(solution)/shard_map/ppermute | solution.py:416
  66.8 3.7 %collective-permute-start.12 = (bf16[256,128]{1,0:T(8,128)(2,1)S(1)}, bf16[256,128]{1,0:T(8,128)(2,1)S(1)}, u32[]{:S(2)}, u32[]{:S(2)}) collective-permute-start(bf16[256,128]{1,0:T(8,128)(2,1)S(1)} %get-tuple-element.47), channel_id=1, source_target_pairs={{0,24},{8,0},{16,8},{24,16},{1,25},{9,1},{17,9},{25,17},{2,26},{10... | collective-permute-start | bytes 196616 | tf_op jit(solution)/shard_map/ppermute | solution.py:416
  70.6 27.7 %copy-start.1 = (bf16[1,40,11200]{2,1,0:T(8,128)(2,1)S(1)}, bf16[1,40,11200]{2,1,0:T(8,128)(2,1)}, u32[]{:S(2)}) copy-start(bf16[1,40,11200]{2,1,0:T(8,128)(2,1)} %copy-done) | copy-start | bytes 2688004
  70.6 27.7 %copy-start.2 = (f32[3,3,11200]{2,1,0:T(4,128)S(1)}, f32[3,3,11200]{2,1,0:T(4,128)}, u32[]{:S(2)}) copy-start(f32[3,3,11200]{2,1,0:T(4,128)} %refs_5_.1) | copy-start | bytes 1209604
  70.6 27.7 %copy-start.7 = (f32[11200]{0:T(1024)S(1)}, f32[11200]{0:T(1024)}, u32[]{:S(2)}) copy-start(f32[11200]{0:T(1024)} %param.15) | copy-start | bytes 134404
  70.6 38.5 %collective-permute-start.15 = (bf16[1,40,11200]{2,1,0:T(8,128)(2,1)}, bf16[1,40,11200]{2,1,0:T(8,128)(2,1)S(1)}, u32[]{:S(2)}, u32[]{:S(2)}) collective-permute-start(bf16[1,40,11200]{2,1,0:T(8,128)(2,1)} %get-tuple-element.32), channel_id=1, source_target_pairs={{0,8},{8,16},{16,24},{24,32},{32,40},{40,48},{48,56},{56,64},{64,7... | collective-permute-start | bytes 2688008 | tf_op jit(solution)/shard_map/ppermute | solution.py:416
  73.8 0.7 copy-start.8
  77.4 37.1 %collective-permute-start.17 = (bf16[1,40,11200]{2,1,0:T(8,128)(2,1)S(1)}, bf16[1,40,11200]{2,1,0:T(8,128)(2,1)S(1)}, u32[]{:S(2)}, u32[]{:S(2)}) collective-permute-start(bf16[1,40,11200]{2,1,0:T(8,128)(2,1)S(1)} %get-tuple-element.37), channel_id=1, source_target_pairs={{0,1},{1,2},{2,3},{3,4},{4,5},{5,6},{6,7},{8,9},{9,10},{10,11},{11... | collective-permute-start | bytes 2688008 | tf_op jit(solution)/shard_map/ppermute | solution.py:416
  83.6 30.9 %collective-permute-start.18 = (bf16[1,40,11200]{2,1,0:T(8,128)(2,1)S(1)}, bf16[1,40,11200]{2,1,0:T(8,128)(2,1)S(1)}, u32[]{:S(2)}, u32[]{:S(2)}) collective-permute-start(bf16[1,40,11200]{2,1,0:T(8,128)(2,1)S(1)} %get-tuple-element.38), channel_id=1, source_target_pairs={{1,0},{2,1},{3,2},{4,3},{5,4},{6,5},{7,6},{9,8},{10,9},{11,10},{12... | collective-permute-start | bytes 2688008 | tf_op jit(solution)/shard_map/ppermute | solution.py:416
  85.5 12.7 %collective-permute-start.13 = (bf16[256,128]{1,0:T(8,128)(2,1)S(1)}, bf16[256,128]{1,0:T(8,128)(2,1)S(1)}, u32[]{:S(2)}, u32[]{:S(2)}) collective-permute-start(bf16[256,128]{1,0:T(8,128)(2,1)S(1)} %add_convert_fusion.refs_2_), channel_id=1, source_target_pairs={{0,4},{1,5},{2,6},{3,7},{4,0},{5,1},{6,2},{7,3},{8,12},{9,13},{10,... | collective-permute-start | bytes 196616 | tf_op jit(solution)/shard_map/ppermute | solution.py:410
  98.2 10.9 %collective-permute-start.14 = (bf16[512,128]{1,0:T(8,128)(2,1)S(1)}, bf16[512,128]{1,0:T(8,128)(2,1)S(1)}, u32[]{:S(2)}, u32[]{:S(2)}) collective-permute-start(bf16[512,128]{1,0:T(8,128)(2,1)S(1)} %pad_maximum_fusion.2), channel_id=1, source_target_pairs={{0,2},{1,3},{2,0},{3,1},{4,6},{5,7},{6,4},{7,5},{8,10},{9,11},{10,... | collective-permute-start | bytes 393224 | tf_op jit(solution)/shard_map/ppermute | solution.py:410
  98.3 16.2 %copy-start.12 = (f32[2240]{0:T(1024)S(1)}, f32[2240]{0:T(1024)}, u32[]{:S(2)}) copy-start(f32[2240]{0:T(1024)} %param.11) | copy-start | bytes 26884
  109.2 15.0 %collective-permute-start.16 = (bf16[1024,128]{1,0:T(8,128)(2,1)S(1)}, bf16[1024,128]{1,0:T(8,128)(2,1)S(1)}, u32[]{:S(2)}, u32[]{:S(2)}) collective-permute-start(bf16[1024,128]{1,0:T(8,128)(2,1)S(1)} %pad_maximum_fusion.1), channel_id=1, source_target_pairs={{0,1},{1,0},{2,3},{3,2},{4,5},{5,4},{6,7},{7,6},{8,9},{9,8},{10,11... | collective-permute-start | bytes 786440 | tf_op jit(solution)/shard_map/ppermute | solution.py:410
  114.5 9.7 %copy-start.6 = (bf16[2,3,40,2240]{3,2,1,0:T(8,128)(2,1)S(1)}, bf16[2,3,40,2240]{3,2,1,0:T(8,128)(2,1)}, u32[]{:S(2)}) copy-start(bf16[2,3,40,2240]{3,2,1,0:T(8,128)(2,1)} %param.8) | copy-start | bytes 3225604

commit v7 on v5

--- a/solution.py
+++ b/solution.py
@@ -285,7 +285,9 @@
 
 
 def edge_kernel(own_ref, *refs, frame):
-    *old_refs, time_ref, _, up_ref, down_ref, now_ref, old_ref, sems = refs
+    up_ref, down_ref, token_ref, now_ref, old_ref, sems = refs[-6:]
+    old_refs, time_ref = (refs[:0], refs[0]) if frame else (refs[:2], refs[2])
+    token_ref[...] = jnp.zeros_like(token_ref)
     rows, channels = own_ref.shape[1], own_ref.shape[3]
     ends = (0, rows - 1)
     copies = []
@@ -318,18 +320,18 @@
             blend(pl.ds(channels // wide * wide, channels % wide))
 
 
-def edges(hidden, frame, old, times, token):
+def edges(hidden, frame, old, times, *waits):
     channels, columns = hidden.shape[3], hidden.shape[2]
     held = pl.BlockSpec(memory_space=pltpu.VMEM)
     anywhere = pl.BlockSpec(memory_space=pl.ANY)
-    args = [pltpu.with_memory_space_constraint(hidden, pltpu.HBM), *old, times, token]
+    args = [pltpu.with_memory_space_constraint(hidden, pltpu.HBM), *old, times, *waits]
     line = jax.ShapeDtypeStruct((1, columns, channels), jnp.bfloat16)
     pair = pltpu.VMEM((2, columns, channels), jnp.bfloat16)
     return pl.pallas_call(
         functools.partial(edge_kernel, frame=frame),
-        out_shape=(line, line),
-        in_specs=[anywhere] + [held] * len(old) + [held, anywhere],
-        out_specs=(held, held),
+        out_shape=(line, line, jax.ShapeDtypeStruct((8, LANES), jnp.float32)),
+        in_specs=[anywhere] + [held] * (len(old) + 1) + [anywhere] * len(waits),
+        out_specs=(held, held, held),
         scratch_shapes=[pair, pair, pltpu.SemaphoreType.DMA((2, 2, columns // 8))],
         compiler_params=pltpu.CompilerParams(vmem_limit_bytes=8 << 20),
         cost_estimate=pl.CostEstimate(
@@ -434,34 +436,36 @@
         sent = narrow(column)
         if k == 2:
             sent, prev_first = lax.optimization_barrier((sent, prev_first))
-        if k == 1:
-            up_edge, down_edge = edges(hidden, frames - 1, (), time_weight, sent)
+        if k == 2:
+            up_edge, down_edge, edge_token = edges(hidden, frames - 1, (), time_weight, sent)
             top, bottom = ahead(down_edge, "row", 1), ahead(up_edge, "row", -1)
             ffn_out = conv_frame(hidden, frames - 1, (), top, bottom, weights)
+            sent, prev_first, edge_token = lax.optimization_barrier((sent, prev_first, edge_token))
+        if k == 4:
+            prev_middle, copy_token = copied_rows(hidden, frames - 1, (1,), sent, edge_token)
         pairs = [
             (z * INNER + at, (z + k) * INNER + at)
             for z in range(planes - k)
             for at in range(INNER - 1)
         ]
         arrived = lax.ppermute(sent, frame_axes, pairs)
-        if k == 4:
-            arrived, ffn_out = lax.optimization_barrier((arrived, ffn_out))
         column = column + wide(arrived)
         before = before + wide(arrived)
     prefix = before + held
-    closed, opened = lax.optimization_barrier((narrow(prefix), narrow(before), prev_last))[:2]
-    up_edge, down_edge = edges(hidden, 0, (prev_first, prev_last), time_weight, closed)
-    top_first, bottom_first = ahead(down_edge, "row", 1), ahead(up_edge, "row", -1)
+    closed, opened, prev_last, copy_token = lax.optimization_barrier(
+        (narrow(prefix), narrow(before), prev_last, copy_token)
+    )
     for k in range(1, INNER):
         sent = jnp.where(x + k < INNER, closed, opened)
         prefix = prefix + wide(ahead(sent, "x", k, True))
     prefix = narrow(prefix)
-    prev_middle, _ = copied_rows(hidden, frames - 1, (1,), prefix)
-    prev_middle = ahead(prev_middle, frame_axes, 1)
+    prev_middle = ahead(lax.optimization_barrier((prev_middle, prefix))[0], frame_axes, 1)
+    up_edge, down_edge, _ = edges(hidden, 0, (prev_first, prev_last), time_weight, prefix, copy_token)
+    top_first, bottom_first = ahead(down_edge, "row", 1), ahead(up_edge, "row", -1)
 
     state = jnp.concatenate([prefix, exchange(prefix, "row", 4)], axis=0)
     state = jnp.concatenate([state, exchange(state, "row", 2)], axis=0)
-    state, prev_middle = lax.optimization_barrier((state, prev_middle))
+    state, prev_middle, ffn_out = lax.optimization_barrier((state, prev_middle, ffn_out))
     state = jnp.concatenate([state, exchange(state, "row", 1)], axis=0)
     attention = whole(
         mixed_kernel,

time: 130 us -> 116 us (0.89)
  starting transfers between devices: 64.8 us -> 58.1 us
  waiting for transfers between devices: 23.4 us -> 20.4 us
  other arithmetic: 3.32 us -> 0.4 us
  Pallas kernels: 34.9 us -> 33.1 us
  local copies, waits for them, and re-layouts: 0.82 us -> 2.31 us
    ppermute x6, waiting for transfers between devices: 19.9 us -> 9 us  [exchange(): lax.ppermute(value, axis, [(i, i ^ flip) for i in range(lax.axis_size(axi...]
    ppermute x10, waiting for transfers between devices: 2.15 us -> 10.1 us  [ahead(): return lax.ppermute(value, axis, pairs)]
    convert_element_type x6, other arithmetic: 3.14 us -> 0.22 us  [per_device(): narrow = lambda value: value.astype(jnp.bfloat16)]
    ppermute x6, starting transfers between devices: 10.7 us -> 7.74 us  [exchange(): lax.ppermute(value, axis, [(i, i ^ flip) for i in range(lax.axis_size(axi...]
    ppermute x10, starting transfers between devices: 29.8 us -> 27.7 us  [ahead(): return lax.ppermute(value, axis, pairs)]
    ppermute x3, starting transfers between devices: 23.6 us -> 22 us  [per_device(): arrived = lax.ppermute(sent, frame_axes, pairs)]
    unnamed x28, local copies, waits for them, and re-layouts: 0.75 us -> 2.24 us
  transfers between devices with their start and end apart: 20 -> 20, of which waited for: 8 -> 9; matrix products, arithmetic and copies ran while one was open for 1% -> 0% of each run, Pallas kernels for 21% -> 23%
where the time goes in v7:
time: 116 us; the launch traced here: 115 us
  starting transfers between devices  58.1 us (50%)
  Pallas kernels  33.1 us (29%)
  waiting for transfers between devices  20.4 us (18%)
  local copies, waits for them, and re-layouts  2.31 us (2%)
    ppermute x10, starting transfers between devices, ahead(): return lax.ppermute(value, axis, pairs)  27.7 us
    ppermute x3, starting transfers between devices, per_device(): arrived = lax.ppermute(sent, frame_axes, pairs)  22 us
    pallas_call x2, Pallas kernels, conv_frame(): pl.pallas_call(functools.partial(conv_kernel, frame), out_shape=jax.Shape...  19.3 us
    ppermute x10, waiting for transfers between devices, ahead(): return lax.ppermute(value, axis, pairs)  10.1 us
    ppermute x6, waiting for transfers between devices, exchange(): lax.ppermute(value, axis, [(i, i ^ flip) for i in range(lax.axis_size(axi...  9 us
    ppermute x6, starting transfers between devices, exchange(): lax.ppermute(value, axis, [(i, i ^ flip) for i in range(lax.axis_size(axi...  7.74 us
    pallas_call x2, Pallas kernels, edges(): pl.pallas_call(functools.partial(edge_kernel, frame=frame), out_shape=(li...  5.54 us
    pallas_call x2, Pallas kernels, copied_rows(): pl.pallas_call(functools.partial(copy_kernel, frame=frame, rows=rows), ou...  5.17 us
  transfers between devices with their start and end apart: 20, of which 9 were waited for; matrix products, arithmetic and copies ran while one was open for 0% of the time, Pallas kernels for 23%

profile of v7, /device:TPU:1, one launch (start us, length us, event | category | flops | bytes accessed | tf_op | source)
XLA Modules:
  0.0 115.4 jit_solution(5279252327654490393)
XLA Ops:
  0.7 3.0 %copied_rows.2 = (bf16[1,40,11200]{2,1,0:T(8,128)(2,1)}, bf16[1,40,11200]{2,1,0:T(8,128)(2,1)}, f32[8,128]{1,0:T(8,128)}) custom-call(bf16[2,3,40,11200]{3,2,1,0:T(8,128)(2,1)} %own_ref.7), custom_call_target="tpu_custom_call" | custom-call | bytes 3584000 | tf_op jit(solution)/shard_map/copied_rows/pallas_call | solution.py:361
  3.7 0.7 copy-done.8
  4.3 0.9 partial_kernel.1
  5.3 3.3 %collective-permute-start = (bf16[4,256,128]{2,1,0:T(8,128)(2,1)S(1)}, bf16[4,256,128]{2,1,0:T(8,128)(2,1)S(1)}, u32[]{:S(2)}, u32[]{:S(2)}) collective-permute-start(bf16[4,256,128]{2,1,0:T(8,128)(2,1)S(1)} %bitcast.23), channel_id=1, source_target_pairs={{0,1},{1,0},{2,3},{3,2},{4,5},{5,4},{6,7},{7,6},{8,9},{9,8},{10,11... | collective-permute-start | bytes 786440 | tf_op jit(solution)/shard_map/ppermute | solution.py:393
  8.6 1.2 %collective-permute-done = bf16[4,256,128]{2,1,0:T(8,128)(2,1)S(1)} collective-permute-done((bf16[4,256,128]{2,1,0:T(8,128)(2,1)S(1)}, bf16[4,256,128]{2,1,0:T(8,128)(2,1)S(1)}, u32[]{:S(2)}, u32[]{:S(2)}) %collective-permute-start) | collective-permute-done | bytes 262176 | tf_op jit(solution)/shard_map/ppermute | solution.py:393
  10.0 2.7 %collective-permute-start.5 = (bf16[1,40,11200]{2,1,0:T(8,128)(2,1)S(1)}, bf16[1,40,11200]{2,1,0:T(8,128)(2,1)S(1)}, u32[]{:S(2)}, u32[]{:S(2)}) collective-permute-start(bf16[1,40,11200]{2,1,0:T(8,128)(2,1)S(1)} %copy-done.13), channel_id=1, source_target_pairs={{0,8},{8,16},{16,24},{24,32},{32,40},{40,48},{48,56},{56,64},{64,7... | collective-permute-start | bytes 2688008 | tf_op jit(solution)/shard_map/ppermute | solution.py:399
  12.7 2.0 %collective-permute-done.1 = bf16[2,256,128]{2,1,0:T(8,128)(2,1)S(1)} collective-permute-done((bf16[2,256,128]{2,1,0:T(8,128)(2,1)S(1)}, bf16[2,256,128]{2,1,0:T(8,128)(2,1)S(1)}, u32[]{:S(2)}, u32[]{:S(2)}) %collective-permute-start.1) | collective-permute-done | bytes 131104 | tf_op jit(solution)/shard_map/ppermute | solution.py:393
  14.7 1.3 %collective-permute-start.2 = (bf16[256,128]{1,0:T(8,128)(2,1)S(1)}, bf16[256,128]{1,0:T(8,128)(2,1)S(1)}, u32[]{:S(2)}, u32[]{:S(2)}) collective-permute-start(bf16[256,128]{1,0:T(8,128)(2,1)S(1)} %fusion.6), channel_id=1, source_target_pairs={{0,4},{1,5},{2,6},{3,7},{4,0},{5,1},{6,2},{7,3},{8,12},{9,13},{10,... | collective-permute-start | bytes 196616 | tf_op jit(solution)/shard_map/ppermute | solution.py:393
  16.0 3.4 %collective-permute-done.2 = bf16[256,128]{1,0:T(8,128)(2,1)S(1)} collective-permute-done((bf16[256,128]{1,0:T(8,128)(2,1)S(1)}, bf16[256,128]{1,0:T(8,128)(2,1)S(1)}, u32[]{:S(2)}, u32[]{:S(2)}) %collective-permute-start.2) | collective-permute-done | bytes 65568 | tf_op jit(solution)/shard_map/ppermute | solution.py:393
  19.4 0.7 collective-permute-start.3
  20.1 2.1 %collective-permute-start.4 = (bf16[256,128]{1,0:T(8,128)(2,1)S(1)}, bf16[256,128]{1,0:T(8,128)(2,1)S(1)}, u32[]{:S(2)}, u32[]{:S(2)}) collective-permute-start(bf16[256,128]{1,0:T(8,128)(2,1)S(1)} %fusion.3), channel_id=1, source_target_pairs={{0,32},{8,40},{16,48},{32,64},{40,72},{48,80},{64,96},{72,104},{80... | collective-permute-start | bytes 196616 | tf_op jit(solution)/shard_map/ppermute | solution.py:451
  22.3 2.9 %collective-permute-start.8 = (bf16[1,40,11200]{2,1,0:T(8,128)(2,1)}, bf16[1,40,11200]{2,1,0:T(8,128)(2,1)S(1)}, u32[]{:S(2)}, u32[]{:S(2)}) collective-permute-start(bf16[1,40,11200]{2,1,0:T(8,128)(2,1)} %get-tuple-element.31), channel_id=1, source_target_pairs={{0,8},{8,16},{16,24},{24,32},{32,40},{40,48},{48,56},{56,64},{64,7... | collective-permute-start | bytes 2688008 | tf_op jit(solution)/shard_map/ppermute | solution.py:399
  25.2 6.1 %collective-permute-done.5.refs_0_ = bf16[1,40,11200]{2,1,0:T(8,128)(2,1)S(1)} collective-permute-done((bf16[1,40,11200]{2,1,0:T(8,128)(2,1)S(1)}, bf16[1,40,11200]{2,1,0:T(8,128)(2,1)S(1)}, u32[]{:S(2)}, u32[]{:S(2)}) %collective-permute-start.5) | collective-permute-done | bytes 896032 | tf_op jit(solution)/shard_map/ppermute | solution.py:399
  31.3 2.7 %edges.2 = (bf16[1,40,11200]{2,1,0:T(8,128)(2,1)S(1)}, bf16[1,40,11200]{2,1,0:T(8,128)(2,1)S(1)}, f32[8,128]{1,0:T(8,128)S(1)}) custom-call(bf16[2,3,40,11200]{3,2,1,0:T(8,128)(2,1)} %own_ref.7, f32[2,11200]{1,0:T(2,128)S(1)} %copy-done.1, bf16[256,128]{1,0:T(8,128)(2,1)S(1)} %fusion.7.refs_1_), custom_call_target="tpu_custom_call" | custom-call | flops 2688000 | bytes 5376000 | tf_op jit(solution)/shard_map/edges/pallas_call | solution.py:330
  34.6 0.9 copy-done.9
  35.5 8.0 %collective-permute-start.6 = (bf16[256,128]{1,0:T(8,128)(2,1)S(1)}, bf16[256,128]{1,0:T(8,128)(2,1)S(1)}, u32[]{:S(2)}, u32[]{:S(2)}) collective-permute-start(bf16[256,128]{1,0:T(8,128)(2,1)S(1)} %fusion.7.refs_1_), channel_id=1, source_target_pairs={{0,64},{8,72},{16,80},{32,96},{40,104},{48,112},{64,128},{72,136},... | collective-permute-start | bytes 196616 | tf_op jit(solution)/shard_map/ppermute | solution.py:451
  43.5 1.3 %collective-permute-done.6 = bf16[256,128]{1,0:T(8,128)(2,1)S(1)} collective-permute-done((bf16[256,128]{1,0:T(8,128)(2,1)S(1)}, bf16[256,128]{1,0:T(8,128)(2,1)S(1)}, u32[]{:S(2)}, u32[]{:S(2)}) %collective-permute-start.6) | collective-permute-done | bytes 65568 | tf_op jit(solution)/shard_map/ppermute | solution.py:451
  44.9 11.9 %collective-permute-start.7 = (bf16[256,128]{1,0:T(8,128)(2,1)S(1)}, bf16[256,128]{1,0:T(8,128)(2,1)S(1)}, u32[]{:S(2)}, u32[]{:S(2)}) collective-permute-start(bf16[256,128]{1,0:T(8,128)(2,1)S(1)} %fusion.1.refs_0_), channel_id=1, source_target_pairs={{0,128},{8,136},{16,144},{32,160},{40,168},{48,176},{64,192},{72,2... | collective-permute-start | bytes 196616 | tf_op jit(solution)/shard_map/ppermute | solution.py:451
  56.8 2.2 %copied_rows.3 = (bf16[1,40,11200]{2,1,0:T(8,128)(2,1)}, f32[8,128]{1,0:T(8,128)}) custom-call(bf16[2,3,40,11200]{3,2,1,0:T(8,128)(2,1)} %own_ref.7, bf16[256,128]{1,0:T(8,128)(2,1)} %copy-done.11, f32[8,128]{1,0:T(8,128)} %copy-done.7), custom_call_target="tpu_custom_call" | custom-call | bytes 1792000 | tf_op jit(solution)/shard_map/copied_rows/pallas_call | solution.py:361
  59.3 1.5 %collective-permute-start.9 = (bf16[256,128]{1,0:T(8,128)(2,1)S(1)}, bf16[256,128]{1,0:T(8,128)(2,1)S(1)}, u32[]{:S(2)}, u32[]{:S(2)}) collective-permute-start(bf16[256,128]{1,0:T(8,128)(2,1)S(1)} %get-tuple-element.54), channel_id=1, source_target_pairs={{0,8},{8,16},{16,24},{24,0},{1,9},{9,17},{17,25},{25,1},{2,10},{10... | collective-permute-start | bytes 196616 | tf_op jit(solution)/shard_map/ppermute | solution.py:399
  60.8 3.1 %collective-permute-done.10 = bf16[256,128]{1,0:T(8,128)(2,1)S(1)} collective-permute-done((bf16[256,128]{1,0:T(8,128)(2,1)S(1)}, bf16[256,128]{1,0:T(8,128)(2,1)S(1)}, u32[]{:S(2)}, u32[]{:S(2)}) %collective-permute-start.10) | collective-permute-done | bytes 65568 | tf_op jit(solution)/shard_map/ppermute | solution.py:399
  64.6 2.7 %collective-permute-start.12 = (bf16[256,128]{1,0:T(8,128)(2,1)S(1)}, bf16[256,128]{1,0:T(8,128)(2,1)S(1)}, u32[]{:S(2)}, u32[]{:S(2)}) collective-permute-start(bf16[256,128]{1,0:T(8,128)(2,1)S(1)} %add_convert_fusion.refs_3_), channel_id=1, source_target_pairs={{0,4},{1,5},{2,6},{3,7},{4,0},{5,1},{6,2},{7,3},{8,12},{9,13},{10,... | collective-permute-start | bytes 196616 | tf_op jit(solution)/shard_map/ppermute | solution.py:393
  67.3 6.2 %collective-permute-start.15 = (bf16[1,40,11200]{2,1,0:T(8,128)(2,1)S(1)}, bf16[1,40,11200]{2,1,0:T(8,128)(2,1)S(1)}, u32[]{:S(2)}, u32[]{:S(2)}) collective-permute-start(bf16[1,40,11200]{2,1,0:T(8,128)(2,1)S(1)} %copy-done.10), channel_id=1, source_target_pairs={{0,1},{1,2},{2,3},{3,4},{4,5},{5,6},{6,7},{8,9},{9,10},{10,11},{11... | collective-permute-start | bytes 2688008 | tf_op jit(solution)/shard_map/ppermute | solution.py:399
  73.5 1.9 %collective-permute-start.16 = (bf16[1,40,11200]{2,1,0:T(8,128)(2,1)S(1)}, bf16[1,40,11200]{2,1,0:T(8,128)(2,1)S(1)}, u32[]{:S(2)}, u32[]{:S(2)}) collective-permute-start(bf16[1,40,11200]{2,1,0:T(8,128)(2,1)S(1)} %get-tuple-element.39), channel_id=1, source_target_pairs={{1,0},{2,1},{3,2},{4,3},{5,4},{6,5},{7,6},{9,8},{10,9},{11,10},{12... | collective-permute-start | bytes 2688008 | tf_op jit(solution)/shard_map/ppermute | solution.py:399
  75.4 1.6 %collective-permute-start.14 = (bf16[1,40,11200]{2,1,0:T(8,128)(2,1)}, bf16[1,40,11200]{2,1,0:T(8,128)(2,1)S(1)}, u32[]{:S(2)}, u32[]{:S(2)}) collective-permute-start(bf16[1,40,11200]{2,1,0:T(8,128)(2,1)} %get-tuple-element.37), channel_id=1, source_target_pairs={{0,8},{8,16},{16,24},{24,32},{32,40},{40,48},{48,56},{56,64},{64,7... | collective-permute-start | bytes 2688008 | tf_op jit(solution)/shard_map/ppermute | solution.py:399
  77.3 2.9 %edges.3 = (bf16[1,40,11200]{2,1,0:T(8,128)(2,1)S(1)}, bf16[1,40,11200]{2,1,0:T(8,128)(2,1)S(1)}, f32[8,128]{1,0:T(8,128)}) custom-call(bf16[2,3,40,11200]{3,2,1,0:T(8,128)(2,1)} %own_ref.7, bf16[1,40,11200]{2,1,0:T(8,128)(2,1)S(1)} %collective-permute-done.5.refs_0_, bf16[1,40,11200]{2,1,0:T(8,128)(2,1)S(1)} %collective-permute-done.8.refs_1_.refs_2_, ...), custom_call_target="tpu_custom_call" | custom-call | flops 2688000 | bytes 5376000 | tf_op jit(solution)/shard_map/edges/pallas_call | solution.py:330
  80.2 3.8 %collective-permute-start.18 = (bf16[1,40,11200]{2,1,0:T(8,128)(2,1)S(1)}, bf16[1,40,11200]{2,1,0:T(8,128)(2,1)S(1)}, u32[]{:S(2)}, u32[]{:S(2)}) collective-permute-start(bf16[1,40,11200]{2,1,0:T(8,128)(2,1)S(1)} %get-tuple-element.45), channel_id=1, source_target_pairs={{0,1},{1,2},{2,3},{3,4},{4,5},{5,6},{6,7},{8,9},{9,10},{10,11},{11... | collective-permute-start | bytes 2688008 | tf_op jit(solution)/shard_map/ppermute | solution.py:399
  84.0 2.4 %collective-permute-done.13 = bf16[512,128]{1,0:T(8,128)(2,1)S(1)} collective-permute-done((bf16[512,128]{1,0:T(8,128)(2,1)S(1)}, bf16[512,128]{1,0:T(8,128)(2,1)S(1)}, u32[]{:S(2)}, u32[]{:S(2)}) %collective-permute-start.13) | collective-permute-done | bytes 131104 | tf_op jit(solution)/shard_map/ppermute | solution.py:393
  86.4 7.0 %collective-permute-start.19 = (bf16[1,40,11200]{2,1,0:T(8,128)(2,1)S(1)}, bf16[1,40,11200]{2,1,0:T(8,128)(2,1)S(1)}, u32[]{:S(2)}, u32[]{:S(2)}) collective-permute-start(bf16[1,40,11200]{2,1,0:T(8,128)(2,1)S(1)} %get-tuple-element.46), channel_id=1, source_target_pairs={{1,0},{2,1},{3,2},{4,3},{5,4},{6,5},{7,6},{9,8},{10,9},{11,10},{12... | collective-permute-start | bytes 2688008 | tf_op jit(solution)/shard_map/ppermute | solution.py:399
  93.5 9.6 %conv_frame.2.refs_8_ = bf16[2,3,40,5600]{3,2,1,0:T(8,128)(2,1)} custom-call(bf16[2,3,40,11200]{3,2,1,0:T(8,128)(2,1)} %own_ref.7, bf16[1,40,11200]{2,1,0:T(8,128)(2,1)S(1)} %collective-permute-done.15.refs_0_, bf16[1,40,11200]{2,1,0:T(8,128)(2,1)S(1)} %collective-permute-done.16.refs_1_, f32[2,11200]{1,0:T(2,128)S(1)} %copy-done.1, ...), custom_call_target="tpu_custom_call" | custom-call | flops 53760000 | bytes 8064000 | tf_op jit(solution)/shard_map/conv_frame/pallas_call | solution.py:258
  103.5 9.6 %conv_frame.3 = bf16[2,3,40,5600]{3,2,1,0:T(8,128)(2,1)} custom-call(bf16[2,3,40,11200]{3,2,1,0:T(8,128)(2,1)} %own_ref.7, bf16[1,40,11200]{2,1,0:T(8,128)(2,1)S(1)} %collective-permute-done.5.refs_0_, bf16[1,40,11200]{2,1,0:T(8,128)(2,1)S(1)} %collective-permute-done.14.refs_1_, ...), custom_call_target="tpu_custom_call", output_to_operand_aliasing={{}: (9, {})} | custom-call | flops 53760000 | bytes 8064000 | tf_op jit(solution)/shard_map/conv_frame/pallas_call | solution.py:258
  113.2 2.2 %mixed_kernel.1 = bf16[240,2240]{1,0:T(8,128)(2,1)} custom-call(s32[1]{0:T(128)} %bitcast.row_ref, bf16[240,2240]{1,0:T(8,128)(2,1)S(1)} %bitcast.18, bf16[2048,128]{1,0:T(8,128)(2,1)S(1)} %pad_maximum_fusion.state_ref, f32[1,2240]{1,0:T(1,128)S(1)} %broadcast_in_dim.7.gain_ref), custom_call_target="tpu_custom_call" | custom-call | flops 275251200 | bytes 3145728 | tf_op jit(solution)/shard_map/mixed_kernel/pallas_call | solution.py:381
  (60 shorter events, 2.6 us)
Async XLA Ops:
  0.6 3.0 %copy-start.2 = (bf16[2,3,40,2240]{3,2,1,0:T(8,128)(2,1)S(1)}, bf16[2,3,40,2240]{3,2,1,0:T(8,128)(2,1)}, u32[]{:S(2)}) copy-start(bf16[2,3,40,2240]{3,2,1,0:T(8,128)(2,1)} %param.9) | copy-start | bytes 3225604
  0.6 3.0 %copy-start.3 = (bf16[2,3,40,2240]{3,2,1,0:T(8,128)(2,1)S(1)}, bf16[2,3,40,2240]{3,2,1,0:T(8,128)(2,1)}, u32[]{:S(2)}) copy-start(bf16[2,3,40,2240]{3,2,1,0:T(8,128)(2,1)} %param.10) | copy-start | bytes 3225604
  5.2 4.7 %copy-start.13 = (bf16[1,40,11200]{2,1,0:T(8,128)(2,1)S(1)}, bf16[1,40,11200]{2,1,0:T(8,128)(2,1)}, u32[]{:S(2)}) copy-start(bf16[1,40,11200]{2,1,0:T(8,128)(2,1)} %get-tuple-element.26) | copy-start | bytes 2688004
  5.3 4.5 %collective-permute-start = (bf16[4,256,128]{2,1,0:T(8,128)(2,1)S(1)}, bf16[4,256,128]{2,1,0:T(8,128)(2,1)S(1)}, u32[]{:S(2)}, u32[]{:S(2)}) collective-permute-start(bf16[4,256,128]{2,1,0:T(8,128)(2,1)S(1)} %bitcast.23), channel_id=1, source_target_pairs={{0,1},{1,0},{2,3},{3,2},{4,5},{5,4},{6,7},{7,6},{8,9},{9,8},{10,11... | collective-permute-start | bytes 786440 | tf_op jit(solution)/shard_map/ppermute | solution.py:393
  9.8 21.5 %copy-start.1 = (f32[2,11200]{1,0:T(2,128)S(1)}, f32[2,11200]{1,0:T(2,128)}, u32[]{:S(2)}) copy-start(f32[2,11200]{1,0:T(2,128)} %refs_5_.1) | copy-start | bytes 268804
  9.9 4.8 %collective-permute-start.1 = (bf16[2,256,128]{2,1,0:T(8,128)(2,1)S(1)}, bf16[2,256,128]{2,1,0:T(8,128)(2,1)S(1)}, u32[]{:S(2)}, u32[]{:S(2)}) collective-permute-start(bf16[2,256,128]{2,1,0:T(8,128)(2,1)S(1)} %slice.42), channel_id=1, source_target_pairs={{0,2},{1,3},{2,0},{3,1},{4,6},{5,7},{6,4},{7,5},{8,10},{9,11},{10,... | collective-permute-start | bytes 393224 | tf_op jit(solution)/shard_map/ppermute | solution.py:393
  10.0 21.3 %collective-permute-start.5 = (bf16[1,40,11200]{2,1,0:T(8,128)(2,1)S(1)}, bf16[1,40,11200]{2,1,0:T(8,128)(2,1)S(1)}, u32[]{:S(2)}, u32[]{:S(2)}) collective-permute-start(bf16[1,40,11200]{2,1,0:T(8,128)(2,1)S(1)} %copy-done.13), channel_id=1, source_target_pairs={{0,8},{8,16},{16,24},{24,32},{32,40},{40,48},{48,56},{56,64},{64,7... | collective-permute-start | bytes 2688008 | tf_op jit(solution)/shard_map/ppermute | solution.py:399
  14.7 4.7 %collective-permute-start.2 = (bf16[256,128]{1,0:T(8,128)(2,1)S(1)}, bf16[256,128]{1,0:T(8,128)(2,1)S(1)}, u32[]{:S(2)}, u32[]{:S(2)}) collective-permute-start(bf16[256,128]{1,0:T(8,128)(2,1)S(1)} %fusion.6), channel_id=1, source_target_pairs={{0,4},{1,5},{2,6},{3,7},{4,0},{5,1},{6,2},{7,3},{8,12},{9,13},{10,... | collective-permute-start | bytes 196616 | tf_op jit(solution)/shard_map/ppermute | solution.py:393
  19.4 0.7 collective-permute-start.3
  20.1 5.0 %collective-permute-start.4 = (bf16[256,128]{1,0:T(8,128)(2,1)S(1)}, bf16[256,128]{1,0:T(8,128)(2,1)S(1)}, u32[]{:S(2)}, u32[]{:S(2)}) collective-permute-start(bf16[256,128]{1,0:T(8,128)(2,1)S(1)} %fusion.3), channel_id=1, source_target_pairs={{0,32},{8,40},{16,48},{32,64},{40,72},{48,80},{64,96},{72,104},{80... | collective-permute-start | bytes 196616 | tf_op jit(solution)/shard_map/ppermute | solution.py:451
  22.3 36.8 %collective-permute-start.8 = (bf16[1,40,11200]{2,1,0:T(8,128)(2,1)}, bf16[1,40,11200]{2,1,0:T(8,128)(2,1)S(1)}, u32[]{:S(2)}, u32[]{:S(2)}) collective-permute-start(bf16[1,40,11200]{2,1,0:T(8,128)(2,1)} %get-tuple-element.31), channel_id=1, source_target_pairs={{0,8},{8,16},{16,24},{24,32},{32,40},{40,48},{48,56},{56,64},{64,7... | collective-permute-start | bytes 2688008 | tf_op jit(solution)/shard_map/ppermute | solution.py:399
  34.6 0.9 copy-start.9
  35.5 9.3 %collective-permute-start.6 = (bf16[256,128]{1,0:T(8,128)(2,1)S(1)}, bf16[256,128]{1,0:T(8,128)(2,1)S(1)}, u32[]{:S(2)}, u32[]{:S(2)}) collective-permute-start(bf16[256,128]{1,0:T(8,128)(2,1)S(1)} %fusion.7.refs_1_), channel_id=1, source_target_pairs={{0,64},{8,72},{16,80},{32,96},{40,104},{48,112},{64,128},{72,136},... | collective-permute-start | bytes 196616 | tf_op jit(solution)/shard_map/ppermute | solution.py:451
  44.8 12.0 %copy-start.11 = (bf16[256,128]{1,0:T(8,128)(2,1)}, bf16[256,128]{1,0:T(8,128)(2,1)S(1)}, u32[]{:S(2)}) copy-start(bf16[256,128]{1,0:T(8,128)(2,1)S(1)} %fusion.1.refs_0_) | copy-start | bytes 196612
  44.9 14.2 %collective-permute-start.7 = (bf16[256,128]{1,0:T(8,128)(2,1)S(1)}, bf16[256,128]{1,0:T(8,128)(2,1)S(1)}, u32[]{:S(2)}, u32[]{:S(2)}) collective-permute-start(bf16[256,128]{1,0:T(8,128)(2,1)S(1)} %fusion.1.refs_0_), channel_id=1, source_target_pairs={{0,128},{8,136},{16,144},{32,160},{40,168},{48,176},{64,192},{72,2... | collective-permute-start | bytes 196616 | tf_op jit(solution)/shard_map/ppermute | solution.py:451
  59.0 8.3 %copy-start.10 = (bf16[1,40,11200]{2,1,0:T(8,128)(2,1)S(1)}, bf16[1,40,11200]{2,1,0:T(8,128)(2,1)}, u32[]{:S(2)}) copy-start(bf16[1,40,11200]{2,1,0:T(8,128)(2,1)} %copy-done.9) | copy-start | bytes 2688004
  59.0 18.3 %copy-start.6 = (f32[8,128]{1,0:T(8,128)S(1)}, f32[8,128]{1,0:T(8,128)}, u32[]{:S(2)}) copy-start(f32[8,128]{1,0:T(8,128)} %get-tuple-element.44.refs_4_) | copy-start | bytes 12292
  59.1 4.8 %collective-permute-start.10 = (bf16[256,128]{1,0:T(8,128)(2,1)S(1)}, bf16[256,128]{1,0:T(8,128)(2,1)S(1)}, u32[]{:S(2)}, u32[]{:S(2)}) collective-permute-start(bf16[256,128]{1,0:T(8,128)(2,1)S(1)} %get-tuple-element.56), channel_id=1, source_target_pairs={{0,16},{8,24},{16,0},{24,8},{1,17},{9,25},{17,1},{25,9},{2,18},{10... | collective-permute-start | bytes 196616 | tf_op jit(solution)/shard_map/ppermute | solution.py:399
  59.2 4.7 %collective-permute-start.11 = (bf16[256,128]{1,0:T(8,128)(2,1)S(1)}, bf16[256,128]{1,0:T(8,128)(2,1)S(1)}, u32[]{:S(2)}, u32[]{:S(2)}) collective-permute-start(bf16[256,128]{1,0:T(8,128)(2,1)S(1)} %get-tuple-element.55), channel_id=1, source_target_pairs={{0,24},{8,0},{16,8},{24,16},{1,25},{9,1},{17,9},{25,17},{2,26},{10... | collective-permute-start | bytes 196616 | tf_op jit(solution)/shard_map/ppermute | solution.py:399
  59.3 5.2 %collective-permute-start.9 = (bf16[256,128]{1,0:T(8,128)(2,1)S(1)}, bf16[256,128]{1,0:T(8,128)(2,1)S(1)}, u32[]{:S(2)}, u32[]{:S(2)}) collective-permute-start(bf16[256,128]{1,0:T(8,128)(2,1)S(1)} %get-tuple-element.54), channel_id=1, source_target_pairs={{0,8},{8,16},{16,24},{24,0},{1,9},{9,17},{17,25},{25,1},{2,10},{10... | collective-permute-start | bytes 196616 | tf_op jit(solution)/shard_map/ppermute | solution.py:399
  64.6 12.4 %collective-permute-start.12 = (bf16[256,128]{1,0:T(8,128)(2,1)S(1)}, bf16[256,128]{1,0:T(8,128)(2,1)S(1)}, u32[]{:S(2)}, u32[]{:S(2)}) collective-permute-start(bf16[256,128]{1,0:T(8,128)(2,1)S(1)} %add_convert_fusion.refs_3_), channel_id=1, source_target_pairs={{0,4},{1,5},{2,6},{3,7},{4,0},{5,1},{6,2},{7,3},{8,12},{9,13},{10,... | collective-permute-start | bytes 196616 | tf_op jit(solution)/shard_map/ppermute | solution.py:393
  67.3 26.1 %collective-permute-start.15 = (bf16[1,40,11200]{2,1,0:T(8,128)(2,1)S(1)}, bf16[1,40,11200]{2,1,0:T(8,128)(2,1)S(1)}, u32[]{:S(2)}, u32[]{:S(2)}) collective-permute-start(bf16[1,40,11200]{2,1,0:T(8,128)(2,1)S(1)} %copy-done.10), channel_id=1, source_target_pairs={{0,1},{1,2},{2,3},{3,4},{4,5},{5,6},{6,7},{8,9},{9,10},{10,11},{11... | collective-permute-start | bytes 2688008 | tf_op jit(solution)/shard_map/ppermute | solution.py:399
  73.5 20.0 %collective-permute-start.16 = (bf16[1,40,11200]{2,1,0:T(8,128)(2,1)S(1)}, bf16[1,40,11200]{2,1,0:T(8,128)(2,1)S(1)}, u32[]{:S(2)}, u32[]{:S(2)}) collective-permute-start(bf16[1,40,11200]{2,1,0:T(8,128)(2,1)S(1)} %get-tuple-element.39), channel_id=1, source_target_pairs={{1,0},{2,1},{3,2},{4,3},{5,4},{6,5},{7,6},{9,8},{10,9},{11,10},{12... | collective-permute-start | bytes 2688008 | tf_op jit(solution)/shard_map/ppermute | solution.py:399
  75.4 27.7 %collective-permute-start.14 = (bf16[1,40,11200]{2,1,0:T(8,128)(2,1)}, bf16[1,40,11200]{2,1,0:T(8,128)(2,1)S(1)}, u32[]{:S(2)}, u32[]{:S(2)}) collective-permute-start(bf16[1,40,11200]{2,1,0:T(8,128)(2,1)} %get-tuple-element.37), channel_id=1, source_target_pairs={{0,8},{8,16},{16,24},{24,32},{32,40},{40,48},{48,56},{56,64},{64,7... | collective-permute-start | bytes 2688008 | tf_op jit(solution)/shard_map/ppermute | solution.py:399
  77.1 16.4 %copy-start = (f32[3,3,11200]{2,1,0:T(4,128)S(1)}, f32[3,3,11200]{2,1,0:T(4,128)}, u32[]{:S(2)}) copy-start(f32[3,3,11200]{2,1,0:T(4,128)} %refs_6_.1) | copy-start | bytes 1209604
  77.1 16.4 %copy-start.5 = (f32[11200]{0:T(1024)S(1)}, f32[11200]{0:T(1024)}, u32[]{:S(2)}) copy-start(f32[11200]{0:T(1024)} %param.15) | copy-start | bytes 134404
  77.1 9.4 %collective-permute-start.13 = (bf16[512,128]{1,0:T(8,128)(2,1)S(1)}, bf16[512,128]{1,0:T(8,128)(2,1)S(1)}, u32[]{:S(2)}, u32[]{:S(2)}) collective-permute-start(bf16[512,128]{1,0:T(8,128)(2,1)S(1)} %pad_maximum_fusion.2), channel_id=1, source_target_pairs={{0,2},{1,3},{2,0},{3,1},{4,6},{5,7},{6,4},{7,5},{8,10},{9,11},{10,... | collective-permute-start | bytes 393224 | tf_op jit(solution)/shard_map/ppermute | solution.py:393
  80.2 23.1 %collective-permute-start.18 = (bf16[1,40,11200]{2,1,0:T(8,128)(2,1)S(1)}, bf16[1,40,11200]{2,1,0:T(8,128)(2,1)S(1)}, u32[]{:S(2)}, u32[]{:S(2)}) collective-permute-start(bf16[1,40,11200]{2,1,0:T(8,128)(2,1)S(1)} %get-tuple-element.45), channel_id=1, source_target_pairs={{0,1},{1,2},{2,3},{3,4},{4,5},{5,6},{6,7},{8,9},{9,10},{10,11},{11... | collective-permute-start | bytes 2688008 | tf_op jit(solution)/shard_map/ppermute | solution.py:399
  86.4 17.0 %collective-permute-start.19 = (bf16[1,40,11200]{2,1,0:T(8,128)(2,1)S(1)}, bf16[1,40,11200]{2,1,0:T(8,128)(2,1)S(1)}, u32[]{:S(2)}, u32[]{:S(2)}) collective-permute-start(bf16[1,40,11200]{2,1,0:T(8,128)(2,1)S(1)} %get-tuple-element.46), channel_id=1, source_target_pairs={{1,0},{2,1},{3,2},{4,3},{5,4},{6,5},{7,6},{9,8},{10,9},{11,10},{12... | collective-permute-start | bytes 2688008 | tf_op jit(solution)/shard_map/ppermute | solution.py:399
  93.5 9.8 %copy-start.12 = (f32[2240]{0:T(1024)S(1)}, f32[2240]{0:T(1024)}, u32[]{:S(2)}) copy-start(f32[2240]{0:T(1024)} %param.11) | copy-start | bytes 26884
  103.2 10.0 %collective-permute-start.17 = (bf16[1024,128]{1,0:T(8,128)(2,1)S(1)}, bf16[1024,128]{1,0:T(8,128)(2,1)S(1)}, u32[]{:S(2)}, u32[]{:S(2)}) collective-permute-start(bf16[1024,128]{1,0:T(8,128)(2,1)S(1)} %pad_maximum_fusion.1), channel_id=1, source_target_pairs={{0,1},{1,0},{2,3},{3,2},{4,5},{5,4},{6,7},{7,6},{8,9},{9,8},{10,11... | collective-permute-start | bytes 786440 | tf_op jit(solution)/shard_map/ppermute | solution.py:393
  103.5 9.7 %copy-start.4 = (bf16[2,3,40,2240]{3,2,1,0:T(8,128)(2,1)S(1)}, bf16[2,3,40,2240]{3,2,1,0:T(8,128)(2,1)}, u32[]{:S(2)}) copy-start(bf16[2,3,40,2240]{3,2,1,0:T(8,128)(2,1)} %param.8) | copy-start | bytes 3225604
  (2 other events, 1.3 us)

commit v8 on v7

--- a/solution.py
+++ b/solution.py
@@ -230,7 +230,14 @@
             fetch.wait()
         if near is None:
             near = gates(pl.ds(lead * LANES, LANES))
-        near = lax.fori_loop(start, stop, body, near)
+        pairs = (stop - start) // 2
+
+        def pair(at, near, start=start):
+            return body(start + 2 * at + 1, body(start + 2 * at, near))
+
+        near = lax.fori_loop(0, pairs, pair, near)
+        for tile in range(start + 2 * pairs, stop):
+            near = body(tile, near)
     last = (lead * 2 + 1) * LANES
     far = gates(pl.ds(last, channels - last))
     step(pl.ds(lead * LANES, LANES), near, far, skew)
@@ -426,21 +433,19 @@
     held = partial.reshape(2, 4, SHARE_ROWS, LANES)
     held = wide(held[0]) + wide(exchange(held[1], "row", 1))
     held = held[:2] + wide(exchange(narrow(held[2:]), "row", 2))
-    held = held[0] + wide(exchange(narrow(held[1]), "row", 4))
+    sent = narrow(held[1])
+    up_edge, down_edge, edge_token = edges(hidden, frames - 1, (), time_weight, sent)
+    held = held[0] + wide(exchange(sent, "row", 4))
 
     planes = lax.axis_size("z")
     fold = [(z * INNER + INNER - 1, z * INNER + INNER - 2) for z in range(planes)]
-    column = held + wide(lax.ppermute(narrow(held), frame_axes, fold))
+    sent, edge_token = lax.optimization_barrier((narrow(held), edge_token))
+    column = held + wide(lax.ppermute(sent, frame_axes, fold))
     before = jnp.zeros_like(held)
     for k in (1, 2, 4):
         sent = narrow(column)
         if k == 2:
             sent, prev_first = lax.optimization_barrier((sent, prev_first))
-        if k == 2:
-            up_edge, down_edge, edge_token = edges(hidden, frames - 1, (), time_weight, sent)
-            top, bottom = ahead(down_edge, "row", 1), ahead(up_edge, "row", -1)
-            ffn_out = conv_frame(hidden, frames - 1, (), top, bottom, weights)
-            sent, prev_first, edge_token = lax.optimization_barrier((sent, prev_first, edge_token))
         if k == 4:
             prev_middle, copy_token = copied_rows(hidden, frames - 1, (1,), sent, edge_token)
         pairs = [
@@ -452,6 +457,8 @@
         column = column + wide(arrived)
         before = before + wide(arrived)
     prefix = before + held
+    top, bottom = ahead(down_edge, "row", 1), ahead(up_edge, "row", -1)
+    ffn_out = conv_frame(hidden, frames - 1, (), top, bottom, weights)
     closed, opened, prev_last, copy_token = lax.optimization_barrier(
         (narrow(prefix), narrow(before), prev_last, copy_token)
     )

time: 116 us -> 109 us (0.940)
  waiting for transfers between devices: 20.4 us -> 8.45 us
  starting transfers between devices: 58.1 us -> 65.2 us
  Pallas kernels: 33.1 us -> 30.9 us
    ppermute x6, starting transfers between devices: 7.74 us -> 17.4 us  [exchange(): lax.ppermute(value, axis, [(i, i ^ flip) for i in range(lax.axis_size(axi...]
    ppermute x10, waiting for transfers between devices: 10.1 us -> 3.62 us  [ahead(): return lax.ppermute(value, axis, pairs)]
    ppermute x6, waiting for transfers between devices: 9 us -> 3.51 us  [exchange(): lax.ppermute(value, axis, [(i, i ^ flip) for i in range(lax.axis_size(axi...]
    ppermute x10, starting transfers between devices: 27.7 us -> 23.7 us  [ahead(): return lax.ppermute(value, axis, pairs)]
    pallas_call x2, Pallas kernels: 19.3 us -> 17.1 us  [conv_frame(): pl.pallas_call(functools.partial(conv_kernel, frame), out_shape=jax.Shape...]
    ppermute x3, starting transfers between devices: 22 us -> 23.4 us  [per_device(): arrived = lax.ppermute(sent, frame_axes, pairs)]
  transfers between devices with their start and end apart: 20 -> 20, of which waited for: 9 -> 5; matrix products, arithmetic and copies ran while one was open for 0% -> 0% of each run, Pallas kernels for 23% -> 23%
where the time goes in v8:
time: 109 us; the launch traced here: 108 us
  starting transfers between devices  65.2 us (60%)
  Pallas kernels  30.9 us (28%)
  waiting for transfers between devices  8.45 us (8%)
  local copies, waits for them, and re-layouts  2.32 us (2%)
  between operations  1.16 us (1%)
    ppermute x10, starting transfers between devices, ahead(): return lax.ppermute(value, axis, pairs)  23.7 us
    ppermute x3, starting transfers between devices, per_device(): arrived = lax.ppermute(sent, frame_axes, pairs)  23.4 us
    ppermute x6, starting transfers between devices, exchange(): lax.ppermute(value, axis, [(i, i ^ flip) for i in range(lax.axis_size(axi...  17.4 us
    pallas_call x2, Pallas kernels, conv_frame(): pl.pallas_call(functools.partial(conv_kernel, frame), out_shape=jax.Shape...  17.1 us
    pallas_call x2, Pallas kernels, edges(): pl.pallas_call(functools.partial(edge_kernel, frame=frame), out_shape=(li...  5.54 us
    pallas_call x2, Pallas kernels, copied_rows(): pl.pallas_call(functools.partial(copy_kernel, frame=frame, rows=rows), ou...  5.17 us
    ppermute x10, waiting for transfers between devices, ahead(): return lax.ppermute(value, axis, pairs)  3.62 us
    ppermute x6, waiting for transfers between devices, exchange(): lax.ppermute(value, axis, [(i, i ^ flip) for i in range(lax.axis_size(axi...  3.51 us
  transfers between devices with their start and end apart: 20, of which 5 were waited for; matrix products, arithmetic and copies ran while one was open for 0% of the time, Pallas kernels for 23%

profile of v8, /device:TPU:1, one launch (start us, length us, event | category | flops | bytes accessed | tf_op | source)
XLA Modules:
  0.0 108.4 jit_solution(892984609473766102)
XLA Ops:
  0.7 3.0 %copied_rows.2 = (bf16[1,40,11200]{2,1,0:T(8,128)(2,1)}, bf16[1,40,11200]{2,1,0:T(8,128)(2,1)}, f32[8,128]{1,0:T(8,128)}) custom-call(bf16[2,3,40,11200]{3,2,1,0:T(8,128)(2,1)} %own_ref.7), custom_call_target="tpu_custom_call" | custom-call | bytes 3584000 | tf_op jit(solution)/shard_map/copied_rows/pallas_call | solution.py:368
  3.7 0.7 copy-done.8
  4.3 0.9 partial_kernel.1
  5.3 3.3 %collective-permute-start = (bf16[4,256,128]{2,1,0:T(8,128)(2,1)S(1)}, bf16[4,256,128]{2,1,0:T(8,128)(2,1)S(1)}, u32[]{:S(2)}, u32[]{:S(2)}) collective-permute-start(bf16[4,256,128]{2,1,0:T(8,128)(2,1)S(1)} %bitcast.23), channel_id=1, source_target_pairs={{0,1},{1,0},{2,3},{3,2},{4,5},{5,4},{6,7},{7,6},{8,9},{9,8},{10,11... | collective-permute-start | bytes 786440 | tf_op jit(solution)/shard_map/ppermute | solution.py:400
  8.6 1.2 %collective-permute-done = bf16[4,256,128]{2,1,0:T(8,128)(2,1)S(1)} collective-permute-done((bf16[4,256,128]{2,1,0:T(8,128)(2,1)S(1)}, bf16[4,256,128]{2,1,0:T(8,128)(2,1)S(1)}, u32[]{:S(2)}, u32[]{:S(2)}) %collective-permute-start) | collective-permute-done | bytes 262176 | tf_op jit(solution)/shard_map/ppermute | solution.py:400
  10.0 2.7 %collective-permute-start.5 = (bf16[1,40,11200]{2,1,0:T(8,128)(2,1)S(1)}, bf16[1,40,11200]{2,1,0:T(8,128)(2,1)S(1)}, u32[]{:S(2)}, u32[]{:S(2)}) collective-permute-start(bf16[1,40,11200]{2,1,0:T(8,128)(2,1)S(1)} %copy-done.13), channel_id=1, source_target_pairs={{0,8},{8,16},{16,24},{24,32},{32,40},{40,48},{48,56},{56,64},{64,7... | collective-permute-start | bytes 2688008 | tf_op jit(solution)/shard_map/ppermute | solution.py:406
  12.7 2.0 %collective-permute-done.1 = bf16[2,256,128]{2,1,0:T(8,128)(2,1)S(1)} collective-permute-done((bf16[2,256,128]{2,1,0:T(8,128)(2,1)S(1)}, bf16[2,256,128]{2,1,0:T(8,128)(2,1)S(1)}, u32[]{:S(2)}, u32[]{:S(2)}) %collective-permute-start.1) | collective-permute-done | bytes 131104 | tf_op jit(solution)/shard_map/ppermute | solution.py:400
  14.7 1.3 %collective-permute-start.2 = (bf16[256,128]{1,0:T(8,128)(2,1)S(1)}, bf16[256,128]{1,0:T(8,128)(2,1)S(1)}, u32[]{:S(2)}, u32[]{:S(2)}) collective-permute-start(bf16[256,128]{1,0:T(8,128)(2,1)S(1)} %fusion.6.refs_1_), channel_id=1, source_target_pairs={{0,4},{1,5},{2,6},{3,7},{4,0},{5,1},{6,2},{7,3},{8,12},{9,13},{10,... | collective-permute-start | bytes 196616 | tf_op jit(solution)/shard_map/ppermute | solution.py:400
  16.0 2.7 %edges.2 = (bf16[1,40,11200]{2,1,0:T(8,128)(2,1)S(1)}, bf16[1,40,11200]{2,1,0:T(8,128)(2,1)S(1)}, f32[8,128]{1,0:T(8,128)S(1)}) custom-call(bf16[2,3,40,11200]{3,2,1,0:T(8,128)(2,1)} %own_ref.7, f32[2,11200]{1,0:T(2,128)S(1)} %copy-done.1, bf16[256,128]{1,0:T(8,128)(2,1)S(1)} %fusion.6.refs_1_), custom_call_target="tpu_custom_call" | custom-call | flops 2688000 | bytes 5376000 | tf_op jit(solution)/shard_map/edges/pallas_call | solution.py:337
  18.7 0.6 copy-done.6
  19.2 0.9 copy-done.9
  20.2 0.7 collective-permute-start.3
  20.9 3.5 %collective-permute-start.4 = (bf16[256,128]{1,0:T(8,128)(2,1)S(1)}, bf16[256,128]{1,0:T(8,128)(2,1)S(1)}, u32[]{:S(2)}, u32[]{:S(2)}) collective-permute-start(bf16[256,128]{1,0:T(8,128)(2,1)S(1)} %fusion.3), channel_id=1, source_target_pairs={{0,32},{8,40},{16,48},{32,64},{40,72},{48,80},{64,96},{72,104},{80... | collective-permute-start | bytes 196616 | tf_op jit(solution)/shard_map/ppermute | solution.py:456
  24.5 3.2 %collective-permute-start.8 = (bf16[1,40,11200]{2,1,0:T(8,128)(2,1)}, bf16[1,40,11200]{2,1,0:T(8,128)(2,1)S(1)}, u32[]{:S(2)}, u32[]{:S(2)}) collective-permute-start(bf16[1,40,11200]{2,1,0:T(8,128)(2,1)} %get-tuple-element.29), channel_id=1, source_target_pairs={{0,8},{8,16},{16,24},{24,32},{32,40},{40,48},{48,56},{56,64},{64,7... | collective-permute-start | bytes 2688008 | tf_op jit(solution)/shard_map/ppermute | solution.py:406
  27.7 3.6 %collective-permute-done.5.refs_0_ = bf16[1,40,11200]{2,1,0:T(8,128)(2,1)S(1)} collective-permute-done((bf16[1,40,11200]{2,1,0:T(8,128)(2,1)S(1)}, bf16[1,40,11200]{2,1,0:T(8,128)(2,1)S(1)}, u32[]{:S(2)}, u32[]{:S(2)}) %collective-permute-start.5) | collective-permute-done | bytes 896032 | tf_op jit(solution)/shard_map/ppermute | solution.py:406
  31.3 8.0 %collective-permute-start.6 = (bf16[256,128]{1,0:T(8,128)(2,1)S(1)}, bf16[256,128]{1,0:T(8,128)(2,1)S(1)}, u32[]{:S(2)}, u32[]{:S(2)}) collective-permute-start(bf16[256,128]{1,0:T(8,128)(2,1)S(1)} %fusion.7), channel_id=1, source_target_pairs={{0,64},{8,72},{16,80},{32,96},{40,104},{48,112},{64,128},{72,136},... | collective-permute-start | bytes 196616 | tf_op jit(solution)/shard_map/ppermute | solution.py:456
  39.3 1.3 %collective-permute-done.6 = bf16[256,128]{1,0:T(8,128)(2,1)S(1)} collective-permute-done((bf16[256,128]{1,0:T(8,128)(2,1)S(1)}, bf16[256,128]{1,0:T(8,128)(2,1)S(1)}, u32[]{:S(2)}, u32[]{:S(2)}) %collective-permute-start.6) | collective-permute-done | bytes 65568 | tf_op jit(solution)/shard_map/ppermute | solution.py:456
  40.6 11.9 %collective-permute-start.7 = (bf16[256,128]{1,0:T(8,128)(2,1)S(1)}, bf16[256,128]{1,0:T(8,128)(2,1)S(1)}, u32[]{:S(2)}, u32[]{:S(2)}) collective-permute-start(bf16[256,128]{1,0:T(8,128)(2,1)S(1)} %fusion.1.refs_0_), channel_id=1, source_target_pairs={{0,128},{8,136},{16,144},{32,160},{40,168},{48,176},{64,192},{72,2... | collective-permute-start | bytes 196616 | tf_op jit(solution)/shard_map/ppermute | solution.py:456
  52.6 2.2 %copied_rows.3 = (bf16[1,40,11200]{2,1,0:T(8,128)(2,1)}, f32[8,128]{1,0:T(8,128)}) custom-call(bf16[2,3,40,11200]{3,2,1,0:T(8,128)(2,1)} %own_ref.7, bf16[256,128]{1,0:T(8,128)(2,1)} %copy-done.10, f32[8,128]{1,0:T(8,128)} %copy-done.6), custom_call_target="tpu_custom_call" | custom-call | bytes 1792000 | tf_op jit(solution)/shard_map/copied_rows/pallas_call | solution.py:368
  55.3 1.3 %collective-permute-start.9 = (bf16[256,128]{1,0:T(8,128)(2,1)S(1)}, bf16[256,128]{1,0:T(8,128)(2,1)S(1)}, u32[]{:S(2)}, u32[]{:S(2)}) collective-permute-start(bf16[256,128]{1,0:T(8,128)(2,1)S(1)} %get-tuple-element.52), channel_id=1, source_target_pairs={{0,8},{8,16},{16,24},{24,0},{1,9},{9,17},{17,25},{25,1},{2,10},{10... | collective-permute-start | bytes 196616 | tf_op jit(solution)/shard_map/ppermute | solution.py:406
  56.6 5.8 %collective-permute-start.15 = (bf16[1,40,11200]{2,1,0:T(8,128)(2,1)}, bf16[1,40,11200]{2,1,0:T(8,128)(2,1)S(1)}, u32[]{:S(2)}, u32[]{:S(2)}) collective-permute-start(bf16[1,40,11200]{2,1,0:T(8,128)(2,1)} %copy-done.9), channel_id=1, source_target_pairs={{0,1},{1,2},{2,3},{3,4},{4,5},{5,6},{6,7},{8,9},{9,10},{10,11},{11... | collective-permute-start | bytes 2688008 | tf_op jit(solution)/shard_map/ppermute | solution.py:406
  62.4 1.9 %collective-permute-start.16 = (bf16[1,40,11200]{2,1,0:T(8,128)(2,1)S(1)}, bf16[1,40,11200]{2,1,0:T(8,128)(2,1)S(1)}, u32[]{:S(2)}, u32[]{:S(2)}) collective-permute-start(bf16[1,40,11200]{2,1,0:T(8,128)(2,1)S(1)} %get-tuple-element.37), channel_id=1, source_target_pairs={{1,0},{2,1},{3,2},{4,3},{5,4},{6,5},{7,6},{9,8},{10,9},{11,10},{12... | collective-permute-start | bytes 2688008 | tf_op jit(solution)/shard_map/ppermute | solution.py:406
  64.5 3.0 %collective-permute-start.14 = (bf16[1,40,11200]{2,1,0:T(8,128)(2,1)S(1)}, bf16[1,40,11200]{2,1,0:T(8,128)(2,1)S(1)}, u32[]{:S(2)}, u32[]{:S(2)}) collective-permute-start(bf16[1,40,11200]{2,1,0:T(8,128)(2,1)S(1)} %copy-done.12), channel_id=1, source_target_pairs={{0,8},{8,16},{16,24},{24,32},{32,40},{40,48},{48,56},{56,64},{64,7... | collective-permute-start | bytes 2688008 | tf_op jit(solution)/shard_map/ppermute | solution.py:406
  67.5 3.0 %collective-permute-start.12 = (bf16[256,128]{1,0:T(8,128)(2,1)S(1)}, bf16[256,128]{1,0:T(8,128)(2,1)S(1)}, u32[]{:S(2)}, u32[]{:S(2)}) collective-permute-start(bf16[256,128]{1,0:T(8,128)(2,1)S(1)} %add_convert_fusion.refs_3_), channel_id=1, source_target_pairs={{0,4},{1,5},{2,6},{3,7},{4,0},{5,1},{6,2},{7,3},{8,12},{9,13},{10,... | collective-permute-start | bytes 196616 | tf_op jit(solution)/shard_map/ppermute | solution.py:400
  70.4 2.9 %edges.3 = (bf16[1,40,11200]{2,1,0:T(8,128)(2,1)S(1)}, bf16[1,40,11200]{2,1,0:T(8,128)(2,1)S(1)}, f32[8,128]{1,0:T(8,128)}) custom-call(bf16[2,3,40,11200]{3,2,1,0:T(8,128)(2,1)} %own_ref.7, bf16[1,40,11200]{2,1,0:T(8,128)(2,1)S(1)} %collective-permute-done.5.refs_0_, bf16[1,40,11200]{2,1,0:T(8,128)(2,1)S(1)} %collective-permute-done.8.refs_1_.refs_2_, ...), custom_call_target="tpu_custom_call" | custom-call | flops 2688000 | bytes 5376000 | tf_op jit(solution)/shard_map/edges/pallas_call | solution.py:337
  73.3 3.6 %collective-permute-start.18 = (bf16[1,40,11200]{2,1,0:T(8,128)(2,1)S(1)}, bf16[1,40,11200]{2,1,0:T(8,128)(2,1)S(1)}, u32[]{:S(2)}, u32[]{:S(2)}) collective-permute-start(bf16[1,40,11200]{2,1,0:T(8,128)(2,1)S(1)} %get-tuple-element.43), channel_id=1, source_target_pairs={{0,1},{1,2},{2,3},{3,4},{4,5},{5,6},{6,7},{8,9},{9,10},{10,11},{11... | collective-permute-start | bytes 2688008 | tf_op jit(solution)/shard_map/ppermute | solution.py:406
  77.3 1.9 %collective-permute-start.19 = (bf16[1,40,11200]{2,1,0:T(8,128)(2,1)S(1)}, bf16[1,40,11200]{2,1,0:T(8,128)(2,1)S(1)}, u32[]{:S(2)}, u32[]{:S(2)}) collective-permute-start(bf16[1,40,11200]{2,1,0:T(8,128)(2,1)S(1)} %get-tuple-element.44), channel_id=1, source_target_pairs={{1,0},{2,1},{3,2},{4,3},{5,4},{6,5},{7,6},{9,8},{10,9},{11,10},{12... | collective-permute-start | bytes 2688008 | tf_op jit(solution)/shard_map/ppermute | solution.py:406
  79.2 3.9 %collective-permute-start.13 = (bf16[512,128]{1,0:T(8,128)(2,1)S(1)}, bf16[512,128]{1,0:T(8,128)(2,1)S(1)}, u32[]{:S(2)}, u32[]{:S(2)}) collective-permute-start(bf16[512,128]{1,0:T(8,128)(2,1)S(1)} %pad_maximum_fusion.2), channel_id=1, source_target_pairs={{0,2},{1,3},{2,0},{3,1},{4,6},{5,7},{6,4},{7,5},{8,10},{9,11},{10,... | collective-permute-start | bytes 393224 | tf_op jit(solution)/shard_map/ppermute | solution.py:400
  83.2 8.5 %conv_frame.2.refs_8_ = bf16[2,3,40,5600]{3,2,1,0:T(8,128)(2,1)} custom-call(bf16[2,3,40,11200]{3,2,1,0:T(8,128)(2,1)} %own_ref.7, bf16[1,40,11200]{2,1,0:T(8,128)(2,1)S(1)} %collective-permute-done.15.refs_0_, bf16[1,40,11200]{2,1,0:T(8,128)(2,1)S(1)} %collective-permute-done.16.refs_1_, f32[2,11200]{1,0:T(2,128)S(1)} %copy-done.1, ...), custom_call_target="tpu_custom_call" | custom-call | flops 53760000 | bytes 8064000 | tf_op jit(solution)/shard_map/conv_frame/pallas_call | solution.py:265
  91.8 5.8 %collective-permute-start.17 = (bf16[1024,128]{1,0:T(8,128)(2,1)S(1)}, bf16[1024,128]{1,0:T(8,128)(2,1)S(1)}, u32[]{:S(2)}, u32[]{:S(2)}) collective-permute-start(bf16[1024,128]{1,0:T(8,128)(2,1)S(1)} %pad_maximum_fusion.1), channel_id=1, source_target_pairs={{0,1},{1,0},{2,3},{3,2},{4,5},{5,4},{6,7},{7,6},{8,9},{9,8},{10,11... | collective-permute-start | bytes 786440 | tf_op jit(solution)/shard_map/ppermute | solution.py:400
  97.6 8.5 %conv_frame.3 = bf16[2,3,40,5600]{3,2,1,0:T(8,128)(2,1)} custom-call(bf16[2,3,40,11200]{3,2,1,0:T(8,128)(2,1)} %own_ref.7, bf16[1,40,11200]{2,1,0:T(8,128)(2,1)S(1)} %collective-permute-done.5.refs_0_, bf16[1,40,11200]{2,1,0:T(8,128)(2,1)S(1)} %collective-permute-done.14.refs_1_, ...), custom_call_target="tpu_custom_call", output_to_operand_aliasing={{}: (9, {})} | custom-call | flops 53760000 | bytes 8064000 | tf_op jit(solution)/shard_map/conv_frame/pallas_call | solution.py:265
  106.2 2.2 %mixed_kernel.1 = bf16[240,2240]{1,0:T(8,128)(2,1)} custom-call(s32[1]{0:T(128)} %bitcast.row_ref, bf16[240,2240]{1,0:T(8,128)(2,1)S(1)} %bitcast.18, bf16[2048,128]{1,0:T(8,128)(2,1)S(1)} %pad_maximum_fusion.state_ref, f32[1,2240]{1,0:T(1,128)S(1)} %broadcast_in_dim.7.gain_ref), custom_call_target="tpu_custom_call" | custom-call | flops 275251200 | bytes 3145728 | tf_op jit(solution)/shard_map/mixed_kernel/pallas_call | solution.py:388
  (60 shorter events, 1.4 us)
Async XLA Ops:
  0.6 3.0 %copy-start.2 = (bf16[2,3,40,2240]{3,2,1,0:T(8,128)(2,1)S(1)}, bf16[2,3,40,2240]{3,2,1,0:T(8,128)(2,1)}, u32[]{:S(2)}) copy-start(bf16[2,3,40,2240]{3,2,1,0:T(8,128)(2,1)} %param.9) | copy-start | bytes 3225604
  0.6 3.0 %copy-start.3 = (bf16[2,3,40,2240]{3,2,1,0:T(8,128)(2,1)S(1)}, bf16[2,3,40,2240]{3,2,1,0:T(8,128)(2,1)}, u32[]{:S(2)}) copy-start(bf16[2,3,40,2240]{3,2,1,0:T(8,128)(2,1)} %param.10) | copy-start | bytes 3225604
  5.2 4.7 %copy-start.13 = (bf16[1,40,11200]{2,1,0:T(8,128)(2,1)S(1)}, bf16[1,40,11200]{2,1,0:T(8,128)(2,1)}, u32[]{:S(2)}) copy-start(bf16[1,40,11200]{2,1,0:T(8,128)(2,1)} %get-tuple-element.27) | copy-start | bytes 2688004
  5.3 10.7 %copy-start.1 = (f32[2,11200]{1,0:T(2,128)S(1)}, f32[2,11200]{1,0:T(2,128)}, u32[]{:S(2)}) copy-start(f32[2,11200]{1,0:T(2,128)} %refs_5_.1) | copy-start | bytes 268804
  5.3 4.5 %collective-permute-start = (bf16[4,256,128]{2,1,0:T(8,128)(2,1)S(1)}, bf16[4,256,128]{2,1,0:T(8,128)(2,1)S(1)}, u32[]{:S(2)}, u32[]{:S(2)}) collective-permute-start(bf16[4,256,128]{2,1,0:T(8,128)(2,1)S(1)} %bitcast.23), channel_id=1, source_target_pairs={{0,1},{1,0},{2,3},{3,2},{4,5},{5,4},{6,7},{7,6},{8,9},{9,8},{10,11... | collective-permute-start | bytes 786440 | tf_op jit(solution)/shard_map/ppermute | solution.py:400
  9.9 4.8 %collective-permute-start.1 = (bf16[2,256,128]{2,1,0:T(8,128)(2,1)S(1)}, bf16[2,256,128]{2,1,0:T(8,128)(2,1)S(1)}, u32[]{:S(2)}, u32[]{:S(2)}) collective-permute-start(bf16[2,256,128]{2,1,0:T(8,128)(2,1)S(1)} %slice.42), channel_id=1, source_target_pairs={{0,2},{1,3},{2,0},{3,1},{4,6},{5,7},{6,4},{7,5},{8,10},{9,11},{10,... | collective-permute-start | bytes 393224 | tf_op jit(solution)/shard_map/ppermute | solution.py:400
  10.0 21.3 %collective-permute-start.5 = (bf16[1,40,11200]{2,1,0:T(8,128)(2,1)S(1)}, bf16[1,40,11200]{2,1,0:T(8,128)(2,1)S(1)}, u32[]{:S(2)}, u32[]{:S(2)}) collective-permute-start(bf16[1,40,11200]{2,1,0:T(8,128)(2,1)S(1)} %copy-done.13), channel_id=1, source_target_pairs={{0,8},{8,16},{16,24},{24,32},{32,40},{40,48},{48,56},{56,64},{64,7... | collective-permute-start | bytes 2688008 | tf_op jit(solution)/shard_map/ppermute | solution.py:406
  14.7 5.5 %collective-permute-start.2 = (bf16[256,128]{1,0:T(8,128)(2,1)S(1)}, bf16[256,128]{1,0:T(8,128)(2,1)S(1)}, u32[]{:S(2)}, u32[]{:S(2)}) collective-permute-start(bf16[256,128]{1,0:T(8,128)(2,1)S(1)} %fusion.6.refs_1_), channel_id=1, source_target_pairs={{0,4},{1,5},{2,6},{3,7},{4,0},{5,1},{6,2},{7,3},{8,12},{9,13},{10,... | collective-permute-start | bytes 196616 | tf_op jit(solution)/shard_map/ppermute | solution.py:400
  19.2 0.9 copy-start.9
  20.2 0.7 collective-permute-start.3
  20.9 6.7 %collective-permute-start.4 = (bf16[256,128]{1,0:T(8,128)(2,1)S(1)}, bf16[256,128]{1,0:T(8,128)(2,1)S(1)}, u32[]{:S(2)}, u32[]{:S(2)}) collective-permute-start(bf16[256,128]{1,0:T(8,128)(2,1)S(1)} %fusion.3), channel_id=1, source_target_pairs={{0,32},{8,40},{16,48},{32,64},{40,72},{48,80},{64,96},{72,104},{80... | collective-permute-start | bytes 196616 | tf_op jit(solution)/shard_map/ppermute | solution.py:456
  24.5 30.4 %collective-permute-start.8 = (bf16[1,40,11200]{2,1,0:T(8,128)(2,1)}, bf16[1,40,11200]{2,1,0:T(8,128)(2,1)S(1)}, u32[]{:S(2)}, u32[]{:S(2)}) collective-permute-start(bf16[1,40,11200]{2,1,0:T(8,128)(2,1)} %get-tuple-element.29), channel_id=1, source_target_pairs={{0,8},{8,16},{16,24},{24,32},{32,40},{40,48},{48,56},{56,64},{64,7... | collective-permute-start | bytes 2688008 | tf_op jit(solution)/shard_map/ppermute | solution.py:406
  31.3 9.3 %collective-permute-start.6 = (bf16[256,128]{1,0:T(8,128)(2,1)S(1)}, bf16[256,128]{1,0:T(8,128)(2,1)S(1)}, u32[]{:S(2)}, u32[]{:S(2)}) collective-permute-start(bf16[256,128]{1,0:T(8,128)(2,1)S(1)} %fusion.7), channel_id=1, source_target_pairs={{0,64},{8,72},{16,80},{32,96},{40,104},{48,112},{64,128},{72,136},... | collective-permute-start | bytes 196616 | tf_op jit(solution)/shard_map/ppermute | solution.py:456
  40.6 12.0 %copy-start.10 = (bf16[256,128]{1,0:T(8,128)(2,1)}, bf16[256,128]{1,0:T(8,128)(2,1)S(1)}, u32[]{:S(2)}) copy-start(bf16[256,128]{1,0:T(8,128)(2,1)S(1)} %fusion.1.refs_0_) | copy-start | bytes 196612
  40.6 14.2 %collective-permute-start.7 = (bf16[256,128]{1,0:T(8,128)(2,1)S(1)}, bf16[256,128]{1,0:T(8,128)(2,1)S(1)}, u32[]{:S(2)}, u32[]{:S(2)}) collective-permute-start(bf16[256,128]{1,0:T(8,128)(2,1)S(1)} %fusion.1.refs_0_), channel_id=1, source_target_pairs={{0,128},{8,136},{16,144},{32,160},{40,168},{48,176},{64,192},{72,2... | collective-permute-start | bytes 196616 | tf_op jit(solution)/shard_map/ppermute | solution.py:456
  54.8 9.6 %copy-start.12 = (bf16[1,40,11200]{2,1,0:T(8,128)(2,1)S(1)}, bf16[1,40,11200]{2,1,0:T(8,128)(2,1)}, u32[]{:S(2)}) copy-start(bf16[1,40,11200]{2,1,0:T(8,128)(2,1)} %get-tuple-element.35) | copy-start | bytes 2688004
  54.8 15.6 %copy-start.7 = (f32[8,128]{1,0:T(8,128)S(1)}, f32[8,128]{1,0:T(8,128)}, u32[]{:S(2)}) copy-start(f32[8,128]{1,0:T(8,128)} %get-tuple-element.42.refs_4_) | copy-start | bytes 12292
  54.9 9.4 %collective-permute-start.10 = (bf16[256,128]{1,0:T(8,128)(2,1)S(1)}, bf16[256,128]{1,0:T(8,128)(2,1)S(1)}, u32[]{:S(2)}, u32[]{:S(2)}) collective-permute-start(bf16[256,128]{1,0:T(8,128)(2,1)S(1)} %get-tuple-element.54), channel_id=1, source_target_pairs={{0,16},{8,24},{16,0},{24,8},{1,17},{9,25},{17,1},{25,9},{2,18},{10... | collective-permute-start | bytes 196616 | tf_op jit(solution)/shard_map/ppermute | solution.py:406
  55.0 9.3 %collective-permute-start.11 = (bf16[256,128]{1,0:T(8,128)(2,1)S(1)}, bf16[256,128]{1,0:T(8,128)(2,1)S(1)}, u32[]{:S(2)}, u32[]{:S(2)}) collective-permute-start(bf16[256,128]{1,0:T(8,128)(2,1)S(1)} %get-tuple-element.53), channel_id=1, source_target_pairs={{0,24},{8,0},{16,8},{24,16},{1,25},{9,1},{17,9},{25,17},{2,26},{10... | collective-permute-start | bytes 196616 | tf_op jit(solution)/shard_map/ppermute | solution.py:406
  55.3 9.0 %collective-permute-start.9 = (bf16[256,128]{1,0:T(8,128)(2,1)S(1)}, bf16[256,128]{1,0:T(8,128)(2,1)S(1)}, u32[]{:S(2)}, u32[]{:S(2)}) collective-permute-start(bf16[256,128]{1,0:T(8,128)(2,1)S(1)} %get-tuple-element.52), channel_id=1, source_target_pairs={{0,8},{8,16},{16,24},{24,0},{1,9},{9,17},{17,25},{25,1},{2,10},{10... | collective-permute-start | bytes 196616 | tf_op jit(solution)/shard_map/ppermute | solution.py:406
  56.6 22.6 %collective-permute-start.15 = (bf16[1,40,11200]{2,1,0:T(8,128)(2,1)}, bf16[1,40,11200]{2,1,0:T(8,128)(2,1)S(1)}, u32[]{:S(2)}, u32[]{:S(2)}) collective-permute-start(bf16[1,40,11200]{2,1,0:T(8,128)(2,1)} %copy-done.9), channel_id=1, source_target_pairs={{0,1},{1,2},{2,3},{3,4},{4,5},{5,6},{6,7},{8,9},{9,10},{10,11},{11... | collective-permute-start | bytes 2688008 | tf_op jit(solution)/shard_map/ppermute | solution.py:406
  62.4 20.8 %collective-permute-start.16 = (bf16[1,40,11200]{2,1,0:T(8,128)(2,1)S(1)}, bf16[1,40,11200]{2,1,0:T(8,128)(2,1)S(1)}, u32[]{:S(2)}, u32[]{:S(2)}) collective-permute-start(bf16[1,40,11200]{2,1,0:T(8,128)(2,1)S(1)} %get-tuple-element.37), channel_id=1, source_target_pairs={{1,0},{2,1},{3,2},{4,3},{5,4},{6,5},{7,6},{9,8},{10,9},{11,10},{12... | collective-permute-start | bytes 2688008 | tf_op jit(solution)/shard_map/ppermute | solution.py:406
  64.4 18.7 %copy-start = (f32[3,3,11200]{2,1,0:T(4,128)S(1)}, f32[3,3,11200]{2,1,0:T(4,128)}, u32[]{:S(2)}) copy-start(f32[3,3,11200]{2,1,0:T(4,128)} %refs_6_.1) | copy-start | bytes 1209604
  64.4 18.7 %copy-start.5 = (f32[11200]{0:T(1024)S(1)}, f32[11200]{0:T(1024)}, u32[]{:S(2)}) copy-start(f32[11200]{0:T(1024)} %param.15) | copy-start | bytes 134404
  64.5 27.3 %collective-permute-start.14 = (bf16[1,40,11200]{2,1,0:T(8,128)(2,1)S(1)}, bf16[1,40,11200]{2,1,0:T(8,128)(2,1)S(1)}, u32[]{:S(2)}, u32[]{:S(2)}) collective-permute-start(bf16[1,40,11200]{2,1,0:T(8,128)(2,1)S(1)} %copy-done.12), channel_id=1, source_target_pairs={{0,8},{8,16},{16,24},{24,32},{32,40},{40,48},{48,56},{56,64},{64,7... | collective-permute-start | bytes 2688008 | tf_op jit(solution)/shard_map/ppermute | solution.py:406
  67.5 9.8 %collective-permute-start.12 = (bf16[256,128]{1,0:T(8,128)(2,1)S(1)}, bf16[256,128]{1,0:T(8,128)(2,1)S(1)}, u32[]{:S(2)}, u32[]{:S(2)}) collective-permute-start(bf16[256,128]{1,0:T(8,128)(2,1)S(1)} %add_convert_fusion.refs_3_), channel_id=1, source_target_pairs={{0,4},{1,5},{2,6},{3,7},{4,0},{5,1},{6,2},{7,3},{8,12},{9,13},{10,... | collective-permute-start | bytes 196616 | tf_op jit(solution)/shard_map/ppermute | solution.py:400
  73.3 24.2 %collective-permute-start.18 = (bf16[1,40,11200]{2,1,0:T(8,128)(2,1)S(1)}, bf16[1,40,11200]{2,1,0:T(8,128)(2,1)S(1)}, u32[]{:S(2)}, u32[]{:S(2)}) collective-permute-start(bf16[1,40,11200]{2,1,0:T(8,128)(2,1)S(1)} %get-tuple-element.43), channel_id=1, source_target_pairs={{0,1},{1,2},{2,3},{3,4},{4,5},{5,6},{6,7},{8,9},{9,10},{10,11},{11... | collective-permute-start | bytes 2688008 | tf_op jit(solution)/shard_map/ppermute | solution.py:406
  77.3 20.3 %collective-permute-start.19 = (bf16[1,40,11200]{2,1,0:T(8,128)(2,1)S(1)}, bf16[1,40,11200]{2,1,0:T(8,128)(2,1)S(1)}, u32[]{:S(2)}, u32[]{:S(2)}) collective-permute-start(bf16[1,40,11200]{2,1,0:T(8,128)(2,1)S(1)} %get-tuple-element.44), channel_id=1, source_target_pairs={{1,0},{2,1},{3,2},{4,3},{5,4},{6,5},{7,6},{9,8},{10,9},{11,10},{12... | collective-permute-start | bytes 2688008 | tf_op jit(solution)/shard_map/ppermute | solution.py:406
  79.2 12.5 %collective-permute-start.13 = (bf16[512,128]{1,0:T(8,128)(2,1)S(1)}, bf16[512,128]{1,0:T(8,128)(2,1)S(1)}, u32[]{:S(2)}, u32[]{:S(2)}) collective-permute-start(bf16[512,128]{1,0:T(8,128)(2,1)S(1)} %pad_maximum_fusion.2), channel_id=1, source_target_pairs={{0,2},{1,3},{2,0},{3,1},{4,6},{5,7},{6,4},{7,5},{8,10},{9,11},{10,... | collective-permute-start | bytes 393224 | tf_op jit(solution)/shard_map/ppermute | solution.py:400
  83.2 14.4 %copy-start.11 = (f32[2240]{0:T(1024)S(1)}, f32[2240]{0:T(1024)}, u32[]{:S(2)}) copy-start(f32[2240]{0:T(1024)} %param.11) | copy-start | bytes 26884
  91.8 14.4 %collective-permute-start.17 = (bf16[1024,128]{1,0:T(8,128)(2,1)S(1)}, bf16[1024,128]{1,0:T(8,128)(2,1)S(1)}, u32[]{:S(2)}, u32[]{:S(2)}) collective-permute-start(bf16[1024,128]{1,0:T(8,128)(2,1)S(1)} %pad_maximum_fusion.1), channel_id=1, source_target_pairs={{0,1},{1,0},{2,3},{3,2},{4,5},{5,4},{6,7},{7,6},{8,9},{9,8},{10,11... | collective-permute-start | bytes 786440 | tf_op jit(solution)/shard_map/ppermute | solution.py:400
  97.6 8.6 %copy-start.4 = (bf16[2,3,40,2240]{3,2,1,0:T(8,128)(2,1)S(1)}, bf16[2,3,40,2240]{3,2,1,0:T(8,128)(2,1)}, u32[]{:S(2)}) copy-start(bf16[2,3,40,2240]{3,2,1,0:T(8,128)(2,1)} %param.8) | copy-start | bytes 3225604
  (2 other events, 1.3 us)

commit v9 on v8

--- a/solution.py
+++ b/solution.py
@@ -230,13 +230,15 @@
             fetch.wait()
         if near is None:
             near = gates(pl.ds(lead * LANES, LANES))
-        pairs = (stop - start) // 2
-
-        def pair(at, near, start=start):
-            return body(start + 2 * at + 1, body(start + 2 * at, near))
-
-        near = lax.fori_loop(0, pairs, pair, near)
-        for tile in range(start + 2 * pairs, stop):
+        trips = (stop - start) // 4
+
+        def trip(at, near, start=start):
+            for tile in range(4):
+                near = body(start + 4 * at + tile, near)
+            return near
+
+        near = lax.fori_loop(0, trips, trip, near)
+        for tile in range(start + 4 * trips, stop):
             near = body(tile, near)
     last = (lead * 2 + 1) * LANES
     far = gates(pl.ds(last, channels - last))

time: 109 us -> 109 us (level)
  no operation moved by 1% of the time
where the time goes in v9:
time: 109 us; the launch traced here: 108 us
  starting transfers between devices  65.4 us (60%)
  Pallas kernels  30.6 us (28%)
  waiting for transfers between devices  8.45 us (8%)
  local copies, waits for them, and re-layouts  2.32 us (2%)
  between operations  1.16 us (1%)
    ppermute x10, starting transfers between devices, ahead(): return lax.ppermute(value, axis, pairs)  23.7 us
    ppermute x3, starting transfers between devices, per_device(): arrived = lax.ppermute(sent, frame_axes, pairs)  23.4 us
    ppermute x6, starting transfers between devices, exchange(): lax.ppermute(value, axis, [(i, i ^ flip) for i in range(lax.axis_size(axi...  17.5 us
    pallas_call x2, Pallas kernels, conv_frame(): pl.pallas_call(functools.partial(conv_kernel, frame), out_shape=jax.Shape...  16.8 us
    pallas_call x2, Pallas kernels, edges(): pl.pallas_call(functools.partial(edge_kernel, frame=frame), out_shape=(li...  5.54 us
    pallas_call x2, Pallas kernels, copied_rows(): pl.pallas_call(functools.partial(copy_kernel, frame=frame, rows=rows), ou...  5.17 us
    ppermute x10, waiting for transfers between devices, ahead(): return lax.ppermute(value, axis, pairs)  3.62 us
    ppermute x6, waiting for transfers between devices, exchange(): lax.ppermute(value, axis, [(i, i ^ flip) for i in range(lax.axis_size(axi...  3.51 us
  transfers between devices with their start and end apart: 20, of which 5 were waited for; matrix products, arithmetic and copies ran while one was open for 0% of the time, Pallas kernels for 23%

profile of v9, /device:TPU:1, one launch (start us, length us, event | category | flops | bytes accessed | tf_op | source)
XLA Modules:
  0.0 108.3 jit_solution(11584343929679778864)
XLA Ops:
  0.7 3.0 %copied_rows.2 = (bf16[1,40,11200]{2,1,0:T(8,128)(2,1)}, bf16[1,40,11200]{2,1,0:T(8,128)(2,1)}, f32[8,128]{1,0:T(8,128)}) custom-call(bf16[2,3,40,11200]{3,2,1,0:T(8,128)(2,1)} %own_ref.7), custom_call_target="tpu_custom_call" | custom-call | bytes 3584000 | tf_op jit(solution)/shard_map/copied_rows/pallas_call | solution.py:370
  3.7 0.7 copy-done.8
  4.3 0.9 partial_kernel.1
  5.3 3.3 %collective-permute-start = (bf16[4,256,128]{2,1,0:T(8,128)(2,1)S(1)}, bf16[4,256,128]{2,1,0:T(8,128)(2,1)S(1)}, u32[]{:S(2)}, u32[]{:S(2)}) collective-permute-start(bf16[4,256,128]{2,1,0:T(8,128)(2,1)S(1)} %bitcast.23), channel_id=1, source_target_pairs={{0,1},{1,0},{2,3},{3,2},{4,5},{5,4},{6,7},{7,6},{8,9},{9,8},{10,11... | collective-permute-start | bytes 786440 | tf_op jit(solution)/shard_map/ppermute | solution.py:402
  8.6 1.2 %collective-permute-done = bf16[4,256,128]{2,1,0:T(8,128)(2,1)S(1)} collective-permute-done((bf16[4,256,128]{2,1,0:T(8,128)(2,1)S(1)}, bf16[4,256,128]{2,1,0:T(8,128)(2,1)S(1)}, u32[]{:S(2)}, u32[]{:S(2)}) %collective-permute-start) | collective-permute-done | bytes 262176 | tf_op jit(solution)/shard_map/ppermute | solution.py:402
  10.0 2.7 %collective-permute-start.5 = (bf16[1,40,11200]{2,1,0:T(8,128)(2,1)S(1)}, bf16[1,40,11200]{2,1,0:T(8,128)(2,1)S(1)}, u32[]{:S(2)}, u32[]{:S(2)}) collective-permute-start(bf16[1,40,11200]{2,1,0:T(8,128)(2,1)S(1)} %copy-done.13), channel_id=1, source_target_pairs={{0,8},{8,16},{16,24},{24,32},{32,40},{40,48},{48,56},{56,64},{64,7... | collective-permute-start | bytes 2688008 | tf_op jit(solution)/shard_map/ppermute | solution.py:408
  12.7 2.0 %collective-permute-done.1 = bf16[2,256,128]{2,1,0:T(8,128)(2,1)S(1)} collective-permute-done((bf16[2,256,128]{2,1,0:T(8,128)(2,1)S(1)}, bf16[2,256,128]{2,1,0:T(8,128)(2,1)S(1)}, u32[]{:S(2)}, u32[]{:S(2)}) %collective-permute-start.1) | collective-permute-done | bytes 131104 | tf_op jit(solution)/shard_map/ppermute | solution.py:402
  14.7 1.3 %collective-permute-start.2 = (bf16[256,128]{1,0:T(8,128)(2,1)S(1)}, bf16[256,128]{1,0:T(8,128)(2,1)S(1)}, u32[]{:S(2)}, u32[]{:S(2)}) collective-permute-start(bf16[256,128]{1,0:T(8,128)(2,1)S(1)} %fusion.6.refs_1_), channel_id=1, source_target_pairs={{0,4},{1,5},{2,6},{3,7},{4,0},{5,1},{6,2},{7,3},{8,12},{9,13},{10,... | collective-permute-start | bytes 196616 | tf_op jit(solution)/shard_map/ppermute | solution.py:402
  16.0 2.7 %edges.2 = (bf16[1,40,11200]{2,1,0:T(8,128)(2,1)S(1)}, bf16[1,40,11200]{2,1,0:T(8,128)(2,1)S(1)}, f32[8,128]{1,0:T(8,128)S(1)}) custom-call(bf16[2,3,40,11200]{3,2,1,0:T(8,128)(2,1)} %own_ref.7, f32[2,11200]{1,0:T(2,128)S(1)} %copy-done.1, bf16[256,128]{1,0:T(8,128)(2,1)S(1)} %fusion.6.refs_1_), custom_call_target="tpu_custom_call" | custom-call | flops 2688000 | bytes 5376000 | tf_op jit(solution)/shard_map/edges/pallas_call | solution.py:339
  18.7 0.6 copy-done.6
  19.2 0.9 copy-done.9
  20.2 0.7 collective-permute-start.3
  20.9 3.5 %collective-permute-start.4 = (bf16[256,128]{1,0:T(8,128)(2,1)S(1)}, bf16[256,128]{1,0:T(8,128)(2,1)S(1)}, u32[]{:S(2)}, u32[]{:S(2)}) collective-permute-start(bf16[256,128]{1,0:T(8,128)(2,1)S(1)} %fusion.3), channel_id=1, source_target_pairs={{0,32},{8,40},{16,48},{32,64},{40,72},{48,80},{64,96},{72,104},{80... | collective-permute-start | bytes 196616 | tf_op jit(solution)/shard_map/ppermute | solution.py:458
  24.5 3.2 %collective-permute-start.8 = (bf16[1,40,11200]{2,1,0:T(8,128)(2,1)}, bf16[1,40,11200]{2,1,0:T(8,128)(2,1)S(1)}, u32[]{:S(2)}, u32[]{:S(2)}) collective-permute-start(bf16[1,40,11200]{2,1,0:T(8,128)(2,1)} %get-tuple-element.29), channel_id=1, source_target_pairs={{0,8},{8,16},{16,24},{24,32},{32,40},{40,48},{48,56},{56,64},{64,7... | collective-permute-start | bytes 2688008 | tf_op jit(solution)/shard_map/ppermute | solution.py:408
  27.7 3.6 %collective-permute-done.5.refs_0_ = bf16[1,40,11200]{2,1,0:T(8,128)(2,1)S(1)} collective-permute-done((bf16[1,40,11200]{2,1,0:T(8,128)(2,1)S(1)}, bf16[1,40,11200]{2,1,0:T(8,128)(2,1)S(1)}, u32[]{:S(2)}, u32[]{:S(2)}) %collective-permute-start.5) | collective-permute-done | bytes 896032 | tf_op jit(solution)/shard_map/ppermute | solution.py:408
  31.3 8.0 %collective-permute-start.6 = (bf16[256,128]{1,0:T(8,128)(2,1)S(1)}, bf16[256,128]{1,0:T(8,128)(2,1)S(1)}, u32[]{:S(2)}, u32[]{:S(2)}) collective-permute-start(bf16[256,128]{1,0:T(8,128)(2,1)S(1)} %fusion.7), channel_id=1, source_target_pairs={{0,64},{8,72},{16,80},{32,96},{40,104},{48,112},{64,128},{72,136},... | collective-permute-start | bytes 196616 | tf_op jit(solution)/shard_map/ppermute | solution.py:458
  39.3 1.3 %collective-permute-done.6 = bf16[256,128]{1,0:T(8,128)(2,1)S(1)} collective-permute-done((bf16[256,128]{1,0:T(8,128)(2,1)S(1)}, bf16[256,128]{1,0:T(8,128)(2,1)S(1)}, u32[]{:S(2)}, u32[]{:S(2)}) %collective-permute-start.6) | collective-permute-done | bytes 65568 | tf_op jit(solution)/shard_map/ppermute | solution.py:458
  40.6 11.9 %collective-permute-start.7 = (bf16[256,128]{1,0:T(8,128)(2,1)S(1)}, bf16[256,128]{1,0:T(8,128)(2,1)S(1)}, u32[]{:S(2)}, u32[]{:S(2)}) collective-permute-start(bf16[256,128]{1,0:T(8,128)(2,1)S(1)} %fusion.1.refs_0_), channel_id=1, source_target_pairs={{0,128},{8,136},{16,144},{32,160},{40,168},{48,176},{64,192},{72,2... | collective-permute-start | bytes 196616 | tf_op jit(solution)/shard_map/ppermute | solution.py:458
  52.6 2.2 %copied_rows.3 = (bf16[1,40,11200]{2,1,0:T(8,128)(2,1)}, f32[8,128]{1,0:T(8,128)}) custom-call(bf16[2,3,40,11200]{3,2,1,0:T(8,128)(2,1)} %own_ref.7, bf16[256,128]{1,0:T(8,128)(2,1)} %copy-done.10, f32[8,128]{1,0:T(8,128)} %copy-done.6), custom_call_target="tpu_custom_call" | custom-call | bytes 1792000 | tf_op jit(solution)/shard_map/copied_rows/pallas_call | solution.py:370
  55.3 1.3 %collective-permute-start.9 = (bf16[256,128]{1,0:T(8,128)(2,1)S(1)}, bf16[256,128]{1,0:T(8,128)(2,1)S(1)}, u32[]{:S(2)}, u32[]{:S(2)}) collective-permute-start(bf16[256,128]{1,0:T(8,128)(2,1)S(1)} %get-tuple-element.52), channel_id=1, source_target_pairs={{0,8},{8,16},{16,24},{24,0},{1,9},{9,17},{17,25},{25,1},{2,10},{10... | collective-permute-start | bytes 196616 | tf_op jit(solution)/shard_map/ppermute | solution.py:408
  56.6 5.8 %collective-permute-start.15 = (bf16[1,40,11200]{2,1,0:T(8,128)(2,1)}, bf16[1,40,11200]{2,1,0:T(8,128)(2,1)S(1)}, u32[]{:S(2)}, u32[]{:S(2)}) collective-permute-start(bf16[1,40,11200]{2,1,0:T(8,128)(2,1)} %copy-done.9), channel_id=1, source_target_pairs={{0,1},{1,2},{2,3},{3,4},{4,5},{5,6},{6,7},{8,9},{9,10},{10,11},{11... | collective-permute-start | bytes 2688008 | tf_op jit(solution)/shard_map/ppermute | solution.py:408
  62.4 1.9 %collective-permute-start.16 = (bf16[1,40,11200]{2,1,0:T(8,128)(2,1)S(1)}, bf16[1,40,11200]{2,1,0:T(8,128)(2,1)S(1)}, u32[]{:S(2)}, u32[]{:S(2)}) collective-permute-start(bf16[1,40,11200]{2,1,0:T(8,128)(2,1)S(1)} %get-tuple-element.37), channel_id=1, source_target_pairs={{1,0},{2,1},{3,2},{4,3},{5,4},{6,5},{7,6},{9,8},{10,9},{11,10},{12... | collective-permute-start | bytes 2688008 | tf_op jit(solution)/shard_map/ppermute | solution.py:408
  64.5 3.0 %collective-permute-start.14 = (bf16[1,40,11200]{2,1,0:T(8,128)(2,1)S(1)}, bf16[1,40,11200]{2,1,0:T(8,128)(2,1)S(1)}, u32[]{:S(2)}, u32[]{:S(2)}) collective-permute-start(bf16[1,40,11200]{2,1,0:T(8,128)(2,1)S(1)} %copy-done.12), channel_id=1, source_target_pairs={{0,8},{8,16},{16,24},{24,32},{32,40},{40,48},{48,56},{56,64},{64,7... | collective-permute-start | bytes 2688008 | tf_op jit(solution)/shard_map/ppermute | solution.py:408
  67.5 3.0 %collective-permute-start.12 = (bf16[256,128]{1,0:T(8,128)(2,1)S(1)}, bf16[256,128]{1,0:T(8,128)(2,1)S(1)}, u32[]{:S(2)}, u32[]{:S(2)}) collective-permute-start(bf16[256,128]{1,0:T(8,128)(2,1)S(1)} %add_convert_fusion.refs_3_), channel_id=1, source_target_pairs={{0,4},{1,5},{2,6},{3,7},{4,0},{5,1},{6,2},{7,3},{8,12},{9,13},{10,... | collective-permute-start | bytes 196616 | tf_op jit(solution)/shard_map/ppermute | solution.py:402
  70.4 2.9 %edges.3 = (bf16[1,40,11200]{2,1,0:T(8,128)(2,1)S(1)}, bf16[1,40,11200]{2,1,0:T(8,128)(2,1)S(1)}, f32[8,128]{1,0:T(8,128)}) custom-call(bf16[2,3,40,11200]{3,2,1,0:T(8,128)(2,1)} %own_ref.7, bf16[1,40,11200]{2,1,0:T(8,128)(2,1)S(1)} %collective-permute-done.5.refs_0_, bf16[1,40,11200]{2,1,0:T(8,128)(2,1)S(1)} %collective-permute-done.8.refs_1_.refs_2_, ...), custom_call_target="tpu_custom_call" | custom-call | flops 2688000 | bytes 5376000 | tf_op jit(solution)/shard_map/edges/pallas_call | solution.py:339
  73.3 3.6 %collective-permute-start.18 = (bf16[1,40,11200]{2,1,0:T(8,128)(2,1)S(1)}, bf16[1,40,11200]{2,1,0:T(8,128)(2,1)S(1)}, u32[]{:S(2)}, u32[]{:S(2)}) collective-permute-start(bf16[1,40,11200]{2,1,0:T(8,128)(2,1)S(1)} %get-tuple-element.43), channel_id=1, source_target_pairs={{0,1},{1,2},{2,3},{3,4},{4,5},{5,6},{6,7},{8,9},{9,10},{10,11},{11... | collective-permute-start | bytes 2688008 | tf_op jit(solution)/shard_map/ppermute | solution.py:408
  77.3 1.9 %collective-permute-start.19 = (bf16[1,40,11200]{2,1,0:T(8,128)(2,1)S(1)}, bf16[1,40,11200]{2,1,0:T(8,128)(2,1)S(1)}, u32[]{:S(2)}, u32[]{:S(2)}) collective-permute-start(bf16[1,40,11200]{2,1,0:T(8,128)(2,1)S(1)} %get-tuple-element.44), channel_id=1, source_target_pairs={{1,0},{2,1},{3,2},{4,3},{5,4},{6,5},{7,6},{9,8},{10,9},{11,10},{12... | collective-permute-start | bytes 2688008 | tf_op jit(solution)/shard_map/ppermute | solution.py:408
  79.2 3.9 %collective-permute-start.13 = (bf16[512,128]{1,0:T(8,128)(2,1)S(1)}, bf16[512,128]{1,0:T(8,128)(2,1)S(1)}, u32[]{:S(2)}, u32[]{:S(2)}) collective-permute-start(bf16[512,128]{1,0:T(8,128)(2,1)S(1)} %pad_maximum_fusion.2), channel_id=1, source_target_pairs={{0,2},{1,3},{2,0},{3,1},{4,6},{5,7},{6,4},{7,5},{8,10},{9,11},{10,... | collective-permute-start | bytes 393224 | tf_op jit(solution)/shard_map/ppermute | solution.py:402
  83.2 8.4 %conv_frame.2.refs_8_ = bf16[2,3,40,5600]{3,2,1,0:T(8,128)(2,1)} custom-call(bf16[2,3,40,11200]{3,2,1,0:T(8,128)(2,1)} %own_ref.7, bf16[1,40,11200]{2,1,0:T(8,128)(2,1)S(1)} %collective-permute-done.15.refs_0_, bf16[1,40,11200]{2,1,0:T(8,128)(2,1)S(1)} %collective-permute-done.16.refs_1_, f32[2,11200]{1,0:T(2,128)S(1)} %copy-done.1, ...), custom_call_target="tpu_custom_call" | custom-call | flops 53760000 | bytes 8064000 | tf_op jit(solution)/shard_map/conv_frame/pallas_call | solution.py:267
  91.6 5.9 %collective-permute-start.17 = (bf16[1024,128]{1,0:T(8,128)(2,1)S(1)}, bf16[1024,128]{1,0:T(8,128)(2,1)S(1)}, u32[]{:S(2)}, u32[]{:S(2)}) collective-permute-start(bf16[1024,128]{1,0:T(8,128)(2,1)S(1)} %pad_maximum_fusion.1), channel_id=1, source_target_pairs={{0,1},{1,0},{2,3},{3,2},{4,5},{5,4},{6,7},{7,6},{8,9},{9,8},{10,11... | collective-permute-start | bytes 786440 | tf_op jit(solution)/shard_map/ppermute | solution.py:402
  97.6 8.4 %conv_frame.3 = bf16[2,3,40,5600]{3,2,1,0:T(8,128)(2,1)} custom-call(bf16[2,3,40,11200]{3,2,1,0:T(8,128)(2,1)} %own_ref.7, bf16[1,40,11200]{2,1,0:T(8,128)(2,1)S(1)} %collective-permute-done.5.refs_0_, bf16[1,40,11200]{2,1,0:T(8,128)(2,1)S(1)} %collective-permute-done.14.refs_1_, ...), custom_call_target="tpu_custom_call", output_to_operand_aliasing={{}: (9, {})} | custom-call | flops 53760000 | bytes 8064000 | tf_op jit(solution)/shard_map/conv_frame/pallas_call | solution.py:267
  106.1 2.2 %mixed_kernel.1 = bf16[240,2240]{1,0:T(8,128)(2,1)} custom-call(s32[1]{0:T(128)} %bitcast.row_ref, bf16[240,2240]{1,0:T(8,128)(2,1)S(1)} %bitcast.18, bf16[2048,128]{1,0:T(8,128)(2,1)S(1)} %pad_maximum_fusion.state_ref, f32[1,2240]{1,0:T(1,128)S(1)} %broadcast_in_dim.7.gain_ref), custom_call_target="tpu_custom_call" | custom-call | flops 275251200 | bytes 3145728 | tf_op jit(solution)/shard_map/mixed_kernel/pallas_call | solution.py:390
  (60 shorter events, 1.4 us)
Async XLA Ops:
  0.6 3.0 %copy-start.2 = (bf16[2,3,40,2240]{3,2,1,0:T(8,128)(2,1)S(1)}, bf16[2,3,40,2240]{3,2,1,0:T(8,128)(2,1)}, u32[]{:S(2)}) copy-start(bf16[2,3,40,2240]{3,2,1,0:T(8,128)(2,1)} %param.9) | copy-start | bytes 3225604
  0.6 3.0 %copy-start.3 = (bf16[2,3,40,2240]{3,2,1,0:T(8,128)(2,1)S(1)}, bf16[2,3,40,2240]{3,2,1,0:T(8,128)(2,1)}, u32[]{:S(2)}) copy-start(bf16[2,3,40,2240]{3,2,1,0:T(8,128)(2,1)} %param.10) | copy-start | bytes 3225604
  5.2 4.7 %copy-start.13 = (bf16[1,40,11200]{2,1,0:T(8,128)(2,1)S(1)}, bf16[1,40,11200]{2,1,0:T(8,128)(2,1)}, u32[]{:S(2)}) copy-start(bf16[1,40,11200]{2,1,0:T(8,128)(2,1)} %get-tuple-element.27) | copy-start | bytes 2688004
  5.3 10.7 %copy-start.1 = (f32[2,11200]{1,0:T(2,128)S(1)}, f32[2,11200]{1,0:T(2,128)}, u32[]{:S(2)}) copy-start(f32[2,11200]{1,0:T(2,128)} %refs_5_.1) | copy-start | bytes 268804
  5.3 4.5 %collective-permute-start = (bf16[4,256,128]{2,1,0:T(8,128)(2,1)S(1)}, bf16[4,256,128]{2,1,0:T(8,128)(2,1)S(1)}, u32[]{:S(2)}, u32[]{:S(2)}) collective-permute-start(bf16[4,256,128]{2,1,0:T(8,128)(2,1)S(1)} %bitcast.23), channel_id=1, source_target_pairs={{0,1},{1,0},{2,3},{3,2},{4,5},{5,4},{6,7},{7,6},{8,9},{9,8},{10,11... | collective-permute-start | bytes 786440 | tf_op jit(solution)/shard_map/ppermute | solution.py:402
  9.9 4.8 %collective-permute-start.1 = (bf16[2,256,128]{2,1,0:T(8,128)(2,1)S(1)}, bf16[2,256,128]{2,1,0:T(8,128)(2,1)S(1)}, u32[]{:S(2)}, u32[]{:S(2)}) collective-permute-start(bf16[2,256,128]{2,1,0:T(8,128)(2,1)S(1)} %slice.42), channel_id=1, source_target_pairs={{0,2},{1,3},{2,0},{3,1},{4,6},{5,7},{6,4},{7,5},{8,10},{9,11},{10,... | collective-permute-start | bytes 393224 | tf_op jit(solution)/shard_map/ppermute | solution.py:402
  10.0 21.3 %collective-permute-start.5 = (bf16[1,40,11200]{2,1,0:T(8,128)(2,1)S(1)}, bf16[1,40,11200]{2,1,0:T(8,128)(2,1)S(1)}, u32[]{:S(2)}, u32[]{:S(2)}) collective-permute-start(bf16[1,40,11200]{2,1,0:T(8,128)(2,1)S(1)} %copy-done.13), channel_id=1, source_target_pairs={{0,8},{8,16},{16,24},{24,32},{32,40},{40,48},{48,56},{56,64},{64,7... | collective-permute-start | bytes 2688008 | tf_op jit(solution)/shard_map/ppermute | solution.py:408
  14.7 5.5 %collective-permute-start.2 = (bf16[256,128]{1,0:T(8,128)(2,1)S(1)}, bf16[256,128]{1,0:T(8,128)(2,1)S(1)}, u32[]{:S(2)}, u32[]{:S(2)}) collective-permute-start(bf16[256,128]{1,0:T(8,128)(2,1)S(1)} %fusion.6.refs_1_), channel_id=1, source_target_pairs={{0,4},{1,5},{2,6},{3,7},{4,0},{5,1},{6,2},{7,3},{8,12},{9,13},{10,... | collective-permute-start | bytes 196616 | tf_op jit(solution)/shard_map/ppermute | solution.py:402
  19.2 0.9 copy-start.9
  20.2 0.7 collective-permute-start.3
  20.9 6.7 %collective-permute-start.4 = (bf16[256,128]{1,0:T(8,128)(2,1)S(1)}, bf16[256,128]{1,0:T(8,128)(2,1)S(1)}, u32[]{:S(2)}, u32[]{:S(2)}) collective-permute-start(bf16[256,128]{1,0:T(8,128)(2,1)S(1)} %fusion.3), channel_id=1, source_target_pairs={{0,32},{8,40},{16,48},{32,64},{40,72},{48,80},{64,96},{72,104},{80... | collective-permute-start | bytes 196616 | tf_op jit(solution)/shard_map/ppermute | solution.py:458
  24.5 30.4 %collective-permute-start.8 = (bf16[1,40,11200]{2,1,0:T(8,128)(2,1)}, bf16[1,40,11200]{2,1,0:T(8,128)(2,1)S(1)}, u32[]{:S(2)}, u32[]{:S(2)}) collective-permute-start(bf16[1,40,11200]{2,1,0:T(8,128)(2,1)} %get-tuple-element.29), channel_id=1, source_target_pairs={{0,8},{8,16},{16,24},{24,32},{32,40},{40,48},{48,56},{56,64},{64,7... | collective-permute-start | bytes 2688008 | tf_op jit(solution)/shard_map/ppermute | solution.py:408
  31.3 9.3 %collective-permute-start.6 = (bf16[256,128]{1,0:T(8,128)(2,1)S(1)}, bf16[256,128]{1,0:T(8,128)(2,1)S(1)}, u32[]{:S(2)}, u32[]{:S(2)}) collective-permute-start(bf16[256,128]{1,0:T(8,128)(2,1)S(1)} %fusion.7), channel_id=1, source_target_pairs={{0,64},{8,72},{16,80},{32,96},{40,104},{48,112},{64,128},{72,136},... | collective-permute-start | bytes 196616 | tf_op jit(solution)/shard_map/ppermute | solution.py:458
  40.6 12.0 %copy-start.10 = (bf16[256,128]{1,0:T(8,128)(2,1)}, bf16[256,128]{1,0:T(8,128)(2,1)S(1)}, u32[]{:S(2)}) copy-start(bf16[256,128]{1,0:T(8,128)(2,1)S(1)} %fusion.1.refs_0_) | copy-start | bytes 196612
  40.6 14.2 %collective-permute-start.7 = (bf16[256,128]{1,0:T(8,128)(2,1)S(1)}, bf16[256,128]{1,0:T(8,128)(2,1)S(1)}, u32[]{:S(2)}, u32[]{:S(2)}) collective-permute-start(bf16[256,128]{1,0:T(8,128)(2,1)S(1)} %fusion.1.refs_0_), channel_id=1, source_target_pairs={{0,128},{8,136},{16,144},{32,160},{40,168},{48,176},{64,192},{72,2... | collective-permute-start | bytes 196616 | tf_op jit(solution)/shard_map/ppermute | solution.py:458
  54.8 9.6 %copy-start.12 = (bf16[1,40,11200]{2,1,0:T(8,128)(2,1)S(1)}, bf16[1,40,11200]{2,1,0:T(8,128)(2,1)}, u32[]{:S(2)}) copy-start(bf16[1,40,11200]{2,1,0:T(8,128)(2,1)} %get-tuple-element.35) | copy-start | bytes 2688004
  54.8 15.6 %copy-start.7 = (f32[8,128]{1,0:T(8,128)S(1)}, f32[8,128]{1,0:T(8,128)}, u32[]{:S(2)}) copy-start(f32[8,128]{1,0:T(8,128)} %get-tuple-element.42.refs_4_) | copy-start | bytes 12292
  54.9 9.4 %collective-permute-start.10 = (bf16[256,128]{1,0:T(8,128)(2,1)S(1)}, bf16[256,128]{1,0:T(8,128)(2,1)S(1)}, u32[]{:S(2)}, u32[]{:S(2)}) collective-permute-start(bf16[256,128]{1,0:T(8,128)(2,1)S(1)} %get-tuple-element.54), channel_id=1, source_target_pairs={{0,16},{8,24},{16,0},{24,8},{1,17},{9,25},{17,1},{25,9},{2,18},{10... | collective-permute-start | bytes 196616 | tf_op jit(solution)/shard_map/ppermute | solution.py:408
  55.0 9.3 %collective-permute-start.11 = (bf16[256,128]{1,0:T(8,128)(2,1)S(1)}, bf16[256,128]{1,0:T(8,128)(2,1)S(1)}, u32[]{:S(2)}, u32[]{:S(2)}) collective-permute-start(bf16[256,128]{1,0:T(8,128)(2,1)S(1)} %get-tuple-element.53), channel_id=1, source_target_pairs={{0,24},{8,0},{16,8},{24,16},{1,25},{9,1},{17,9},{25,17},{2,26},{10... | collective-permute-start | bytes 196616 | tf_op jit(solution)/shard_map/ppermute | solution.py:408
  55.3 9.0 %collective-permute-start.9 = (bf16[256,128]{1,0:T(8,128)(2,1)S(1)}, bf16[256,128]{1,0:T(8,128)(2,1)S(1)}, u32[]{:S(2)}, u32[]{:S(2)}) collective-permute-start(bf16[256,128]{1,0:T(8,128)(2,1)S(1)} %get-tuple-element.52), channel_id=1, source_target_pairs={{0,8},{8,16},{16,24},{24,0},{1,9},{9,17},{17,25},{25,1},{2,10},{10... | collective-permute-start | bytes 196616 | tf_op jit(solution)/shard_map/ppermute | solution.py:408
  56.6 22.6 %collective-permute-start.15 = (bf16[1,40,11200]{2,1,0:T(8,128)(2,1)}, bf16[1,40,11200]{2,1,0:T(8,128)(2,1)S(1)}, u32[]{:S(2)}, u32[]{:S(2)}) collective-permute-start(bf16[1,40,11200]{2,1,0:T(8,128)(2,1)} %copy-done.9), channel_id=1, source_target_pairs={{0,1},{1,2},{2,3},{3,4},{4,5},{5,6},{6,7},{8,9},{9,10},{10,11},{11... | collective-permute-start | bytes 2688008 | tf_op jit(solution)/shard_map/ppermute | solution.py:408
  62.4 20.8 %collective-permute-start.16 = (bf16[1,40,11200]{2,1,0:T(8,128)(2,1)S(1)}, bf16[1,40,11200]{2,1,0:T(8,128)(2,1)S(1)}, u32[]{:S(2)}, u32[]{:S(2)}) collective-permute-start(bf16[1,40,11200]{2,1,0:T(8,128)(2,1)S(1)} %get-tuple-element.37), channel_id=1, source_target_pairs={{1,0},{2,1},{3,2},{4,3},{5,4},{6,5},{7,6},{9,8},{10,9},{11,10},{12... | collective-permute-start | bytes 2688008 | tf_op jit(solution)/shard_map/ppermute | solution.py:408
  64.4 18.7 %copy-start = (f32[3,3,11200]{2,1,0:T(4,128)S(1)}, f32[3,3,11200]{2,1,0:T(4,128)}, u32[]{:S(2)}) copy-start(f32[3,3,11200]{2,1,0:T(4,128)} %refs_6_.1) | copy-start | bytes 1209604
  64.4 18.7 %copy-start.5 = (f32[11200]{0:T(1024)S(1)}, f32[11200]{0:T(1024)}, u32[]{:S(2)}) copy-start(f32[11200]{0:T(1024)} %param.15) | copy-start | bytes 134404
  64.5 27.2 %collective-permute-start.14 = (bf16[1,40,11200]{2,1,0:T(8,128)(2,1)S(1)}, bf16[1,40,11200]{2,1,0:T(8,128)(2,1)S(1)}, u32[]{:S(2)}, u32[]{:S(2)}) collective-permute-start(bf16[1,40,11200]{2,1,0:T(8,128)(2,1)S(1)} %copy-done.12), channel_id=1, source_target_pairs={{0,8},{8,16},{16,24},{24,32},{32,40},{40,48},{48,56},{56,64},{64,7... | collective-permute-start | bytes 2688008 | tf_op jit(solution)/shard_map/ppermute | solution.py:408
  67.5 9.8 %collective-permute-start.12 = (bf16[256,128]{1,0:T(8,128)(2,1)S(1)}, bf16[256,128]{1,0:T(8,128)(2,1)S(1)}, u32[]{:S(2)}, u32[]{:S(2)}) collective-permute-start(bf16[256,128]{1,0:T(8,128)(2,1)S(1)} %add_convert_fusion.refs_3_), channel_id=1, source_target_pairs={{0,4},{1,5},{2,6},{3,7},{4,0},{5,1},{6,2},{7,3},{8,12},{9,13},{10,... | collective-permute-start | bytes 196616 | tf_op jit(solution)/shard_map/ppermute | solution.py:402
  73.3 24.2 %collective-permute-start.18 = (bf16[1,40,11200]{2,1,0:T(8,128)(2,1)S(1)}, bf16[1,40,11200]{2,1,0:T(8,128)(2,1)S(1)}, u32[]{:S(2)}, u32[]{:S(2)}) collective-permute-start(bf16[1,40,11200]{2,1,0:T(8,128)(2,1)S(1)} %get-tuple-element.43), channel_id=1, source_target_pairs={{0,1},{1,2},{2,3},{3,4},{4,5},{5,6},{6,7},{8,9},{9,10},{10,11},{11... | collective-permute-start | bytes 2688008 | tf_op jit(solution)/shard_map/ppermute | solution.py:408
  77.3 20.3 %collective-permute-start.19 = (bf16[1,40,11200]{2,1,0:T(8,128)(2,1)S(1)}, bf16[1,40,11200]{2,1,0:T(8,128)(2,1)S(1)}, u32[]{:S(2)}, u32[]{:S(2)}) collective-permute-start(bf16[1,40,11200]{2,1,0:T(8,128)(2,1)S(1)} %get-tuple-element.44), channel_id=1, source_target_pairs={{1,0},{2,1},{3,2},{4,3},{5,4},{6,5},{7,6},{9,8},{10,9},{11,10},{12... | collective-permute-start | bytes 2688008 | tf_op jit(solution)/shard_map/ppermute | solution.py:408
  79.2 12.3 %collective-permute-start.13 = (bf16[512,128]{1,0:T(8,128)(2,1)S(1)}, bf16[512,128]{1,0:T(8,128)(2,1)S(1)}, u32[]{:S(2)}, u32[]{:S(2)}) collective-permute-start(bf16[512,128]{1,0:T(8,128)(2,1)S(1)} %pad_maximum_fusion.2), channel_id=1, source_target_pairs={{0,2},{1,3},{2,0},{3,1},{4,6},{5,7},{6,4},{7,5},{8,10},{9,11},{10,... | collective-permute-start | bytes 393224 | tf_op jit(solution)/shard_map/ppermute | solution.py:402
  83.2 14.4 %copy-start.11 = (f32[2240]{0:T(1024)S(1)}, f32[2240]{0:T(1024)}, u32[]{:S(2)}) copy-start(f32[2240]{0:T(1024)} %param.11) | copy-start | bytes 26884
  91.6 14.4 %collective-permute-start.17 = (bf16[1024,128]{1,0:T(8,128)(2,1)S(1)}, bf16[1024,128]{1,0:T(8,128)(2,1)S(1)}, u32[]{:S(2)}, u32[]{:S(2)}) collective-permute-start(bf16[1024,128]{1,0:T(8,128)(2,1)S(1)} %pad_maximum_fusion.1), channel_id=1, source_target_pairs={{0,1},{1,0},{2,3},{3,2},{4,5},{5,4},{6,7},{7,6},{8,9},{9,8},{10,11... | collective-permute-start | bytes 786440 | tf_op jit(solution)/shard_map/ppermute | solution.py:402
  97.6 8.5 %copy-start.4 = (bf16[2,3,40,2240]{3,2,1,0:T(8,128)(2,1)S(1)}, bf16[2,3,40,2240]{3,2,1,0:T(8,128)(2,1)}, u32[]{:S(2)}) copy-start(bf16[2,3,40,2240]{3,2,1,0:T(8,128)(2,1)} %param.8) | copy-start | bytes 3225604
  (2 other events, 1.3 us)
